TPU v7x, 32 devices: a whole 2x2x4 slice. The times are simulated.
32 devices in a mesh: wide: 8 (over z, x), narrow: 4 (over y, core).
Axes of the slice: x: 2, y: 2, z: 4, core: 2. Of those that a mesh axis runs over, the one named last changes fastest.
Arguments:
- flow_field: bfloat16 [64, 64, 16, 512], P('wide', 'narrow'), may hold values from -48 to 48
- fluid_mask: int32 [64, 64, 16], P('wide', 'narrow'), may hold values 0 or 1
- conv_weight: float32 [27, 512], replicated, may hold values from -1 to 1
- latents: bfloat16 [1024, 512], replicated, may hold values from -6 to 6
- w_query1: bfloat16 [512, 512], replicated, may hold values from -0.25 to 0.25
- w_key1: bfloat16 [512, 512], replicated, may hold values from -0.25 to 0.25
- w_value1: bfloat16 [512, 512], replicated, may hold values from -0.25 to 0.25
- w_out1: bfloat16 [512, 512], replicated, may hold values from -0.25 to 0.25
- w_query2: bfloat16 [512, 512], replicated, may hold values from -0.25 to 0.25
- w_key2: bfloat16 [512, 512], replicated, may hold values from -0.25 to 0.25
- w_value2: bfloat16 [512, 512], replicated, may hold values from -0.25 to 0.25
- w_out2: bfloat16 [512, 512], replicated, may hold values from -0.25 to 0.25
Outputs:
- updated_field: float32 [64, 64, 16, 512], P('wide', 'narrow')
All inputs are finite; a program needn't handle non-finite values. No bound on the sum of `fluid_mask` on one device may be relied on, other than what follows from the above.
Results may differ from a plain program's by a relative error of at most 0.035.
The roundings to bfloat16 on the way count: a program that leaves them out, or rounds other values in their place, can miss the bound.
Values may be sent and summed in bfloat16 or wider, within the bound.
No kernel may reach another device: no remote copies, remote signals or barrier semaphores. Data moves between devices by JAX's collectives and lax.ppermute only.
A program may use at most 192 MiB of HBM per device.

v0:
```python
import math

import jax
import jax.numpy as jnp
from jax import lax
from jax.sharding import PartitionSpec as P

HEADS = 8


def padded_2(cells, sides, width):
    for axis, dim in sides:
        count = lax.axis_size(axis)
        ends = count - 1
        head = lax.slice_in_dim(cells, 0, width, axis=dim)
        tail = lax.slice_in_dim(cells, cells.shape[dim] - width, cells.shape[dim], axis=dim)
        cells = jnp.concatenate(
            [
                lax.ppermute(tail, axis, [(i, (i + 1) % count) for i in range(ends)]),
                cells,
                lax.ppermute(head, axis, [((i + 1) % count, i) for i in range(ends)]),
            ],
            axis=dim,
        )
    return cells


def head_block(matrix, head_index, head_size):
    return matrix[:, head_index * head_size : (head_index + 1) * head_size]


def pair_scores(queries, key_rows, head_size):
    factor = 1.8 / math.sqrt(head_size)
    return factor * lax.dot_general(
        queries, key_rows, (((1,), (1,)), ((), ())), preferred_element_type=jnp.float32
    )


def project(row_block, weight):
    return jnp.dot(row_block, weight, preferred_element_type=jnp.float32).astype(jnp.bfloat16)


def exact_dot(weights, values_block):
    return jnp.dot(
        weights, values_block, precision=lax.Precision.HIGHEST, preferred_element_type=jnp.float32
    )


def update_state(summed, totals, state_rows, w_out1, head_count):
    row_count, model_width = summed.shape
    shaped = summed.reshape(row_count, head_count, model_width // head_count) / totals[:, :, None]
    read_rows = shaped.reshape(row_count, model_width).astype(jnp.bfloat16)
    updated = state_rows.astype(jnp.float32) + jnp.dot(
        read_rows, w_out1, preferred_element_type=jnp.float32
    )
    return updated.astype(jnp.bfloat16)


def per_device(
    flow_field,
    fluid_mask,
    conv_weight,
    latents,
    w_query1,
    w_key1,
    w_value1,
    w_out1,
    w_query2,
    w_key2,
    w_value2,
    w_out2,
):
    size_x, size_y, size_z, model_width = flow_field.shape
    head_count = HEADS
    head_size = model_width // head_count
    latent_count = latents.shape[0]
    masked = flow_field * fluid_mask[:, :, :, None].astype(jnp.bfloat16)
    padded = padded_2(masked, (("wide", 0), ("narrow", 1)), 1)
    padded = jnp.pad(padded, ((0, 0), (0, 0), (1, 1), (0, 0)))
    stencil = masked.astype(jnp.float32)
    for offset_x in range(3):
        for offset_y in range(3):
            for offset_z in range(3):
                window = padded[
                    offset_x : offset_x + size_x,
                    offset_y : offset_y + size_y,
                    offset_z : offset_z + size_z,
                ]
                stencil = (
                    stencil
                    + window.astype(jnp.float32)
                    * conv_weight[9 * offset_x + 3 * offset_y + offset_z]
                )
    cell_count = size_x * size_y * size_z
    mixed_cells = stencil.astype(jnp.bfloat16).reshape(cell_count, model_width)
    flat_masked = masked.reshape(cell_count, model_width)
    keys1 = project(mixed_cells, w_key1)
    values1 = project(mixed_cells, w_value1)
    values_wide = values1.astype(jnp.float32)
    queries1 = project(latents, w_query1)
    device_count = lax.axis_size("wide") * lax.axis_size("narrow")
    sums_list = []
    totals_list = []
    tops_list = []
    for head_index in range(head_count):
        scores = pair_scores(
            head_block(queries1, head_index, head_size),
            head_block(keys1, head_index, head_size),
            head_size,
        )
        own_top = jnp.max(scores, axis=1, keepdims=True)
        weights = jnp.exp(scores - own_top)
        tops_list.append(own_top[:, 0])
        totals_list.append(jnp.sum(weights, axis=1))
        sums_list.append(exact_dot(weights, head_block(values_wide, head_index, head_size)))
    summed1 = jnp.concatenate(sums_list, axis=1)[None]
    totals1 = jnp.stack(totals_list, axis=1)[None]
    tops1 = jnp.stack(tops_list, axis=1)[None]
    part_sums, part_totals, part_tops = (
        lax.all_to_all(summed1, ("wide", "narrow"), split_axis=1, concat_axis=0, tiled=True),
        lax.all_to_all(totals1, ("wide", "narrow"), split_axis=1, concat_axis=0, tiled=True),
        lax.all_to_all(tops1, ("wide", "narrow"), split_axis=1, concat_axis=0, tiled=True),
    )
    row_count = latent_count // device_count
    largest = jnp.max(part_tops, axis=0, keepdims=True)
    factors = jnp.exp(part_tops - largest)
    totals = jnp.sum(factors * part_totals, axis=0)
    shaped = (
        part_sums.reshape(device_count, row_count, head_count, head_size) * factors[:, :, :, None]
    )
    summed = jnp.sum(shaped, axis=0).reshape(row_count, model_width)
    start = (
        lax.axis_index("wide") * lax.axis_size("narrow") + lax.axis_index("narrow")
    ) * row_count
    own_latents = lax.dynamic_slice_in_dim(latents, start, row_count, 0)
    own_state = update_state(summed, totals, own_latents, w_out1, head_count)
    latent_state = lax.all_gather(own_state, ("wide", "narrow"), axis=0, tiled=True)
    keys2 = project(latent_state, w_key2)
    values2 = project(latent_state, w_value2)
    queries2 = project(mixed_cells, w_query2)
    read_heads = []
    for head_index in range(head_count):
        scores = pair_scores(
            head_block(queries2, head_index, head_size),
            head_block(keys2, head_index, head_size),
            head_size,
        )
        top2 = jnp.max(scores, axis=1, keepdims=True)
        weights = jnp.exp(scores - top2)
        totals = jnp.sum(weights, axis=1, keepdims=True)
        summed = jnp.dot(
            weights.astype(jnp.bfloat16),
            head_block(values2, head_index, head_size),
            preferred_element_type=jnp.float32,
        )
        read_heads.append(summed / totals)
    read2 = jnp.concatenate(read_heads, axis=1).astype(jnp.bfloat16)
    result = flat_masked.astype(jnp.float32) + jnp.dot(
        read2, w_out2, preferred_element_type=jnp.float32
    )
    return result.reshape(size_x, size_y, size_z, model_width)


def solution(mesh):
    return jax.shard_map(
        per_device,
        mesh=mesh,
        in_specs=(
            P("wide", "narrow", None, None),
            P("wide", "narrow", None),
            P(),
            P(),
            P(),
            P(),
            P(),
            P(),
            P(),
            P(),
            P(),
            P(),
        ),
        out_specs=P("wide", "narrow", None, None),
        check_vma=False,
    )
```

profile of v0, /device:TPU:0, one launch (start us, length us, event | category | flops | bytes accessed | tf_op | source)
XLA Modules:
  0.0 399.7 jit_solution(2876258442550393296)
XLA Ops:
  9.5 4.9 %collective-permute-start = (bf16[1,16,16,512]{3,2,1,0:T(8,128)(2,1)S(1)}, bf16[1,16,16,512]{3,2,1,0:T(8,128)(2,1)S(1)}, u32[]{:S(2)}, u32[]{:S(2)}) collective-permute-start(bf16[1,16,16,512]{3,2,1,0:T(8,128)(2,1)S(1)} %get-tuple-element.11), channel_id=1, source_target_pairs={{0,4},{4,8},{8,12},{12,16},{16,20},{20,24},{24,28},{1,5},{5,9},{9,... | collective-permute-start | bytes 786440 | tf_op jit(solution)/shard_map/ppermute | solution.py:19
  16.6 9.0 %collective-permute-done = bf16[1,16,16,512]{3,2,1,0:T(8,128)(2,1)S(1)} collective-permute-done((bf16[1,16,16,512]{3,2,1,0:T(8,128)(2,1)S(1)}, bf16[1,16,16,512]{3,2,1,0:T(8,128)(2,1)S(1)}, u32[]{:S(2)}, u32[]{:S(2)}) %collective-permute-start) | collective-permute-done | bytes 262176 | tf_op jit(solution)/shard_map/ppermute | solution.py:19
  28.3 3.7 collective-permute-done.3
  32.0 2.8 select_maximum_fusion
  35.7 16.4 %add_convert_fusion = bf16[8,16,16,512]{3,2,1,0:T(8,128)(2,1)S(1)} fusion(bf16[8,16,16,512]{3,2,1,0:T(8,128)(2,1)S(1)} %broadcast_multiply_fusion, bf16[10,18,18,512]{3,2,1,0:T(8,128)(2,1)S(1)} %select_maximum_fusion, bf16[10,17,16,512]{3,2,1,0:T(8,128)(2,1)S(1)} %get-tuple-element.8, bf16[1,16,16,512]{3,2,1,0:T(8,128)(2,1)S(1)} %collective-permute-done.1, ...), kind=kLoop, calls=%fused_computation.91 | loop fusion | flops 88080384 | bytes 55105536 | tf_op jit(solution)/shard_map/convert_element_type | solution.py:95
  58.8 4.5 %multiply_reduce_fusion.12 = (f32[1024]{0:T(1024)S(1)}, f32[1024,2048]{1,0:T(8,128)}) fusion(bf16[2048,512]{0,1:T(8,128)(2,1)S(1)} %convolution_convert_fusion.1, bf16[1024,512]{0,1:T(8,128)(2,1)S(1)} %convolution_convert_fusion.5), kind=kOutput, calls=%fused_computation.31 | convolution fusion | flops 272628736 | bytes 8785920 | tf_op jit(solution)/shard_map/dot_general | solution.py:34
  63.3 4.5 %multiply_reduce_fusion.13 = (f32[1024]{0:T(1024)S(1)}, f32[1024,2048]{1,0:T(8,128)}) fusion(bf16[2048,512]{0,1:T(8,128)(2,1)S(1)} %convolution_convert_fusion.1, bf16[1024,512]{0,1:T(8,128)(2,1)S(1)} %convolution_convert_fusion.5), kind=kOutput, calls=%fused_computation.32 | convolution fusion | flops 272628736 | bytes 8785920 | tf_op jit(solution)/shard_map/dot_general | solution.py:34
  67.8 4.5 %multiply_reduce_fusion.14 = (f32[1024]{0:T(1024)S(1)}, f32[1024,2048]{1,0:T(8,128)}) fusion(bf16[2048,512]{0,1:T(8,128)(2,1)S(1)} %convolution_convert_fusion.1, bf16[1024,512]{0,1:T(8,128)(2,1)S(1)} %convolution_convert_fusion.5), kind=kOutput, calls=%fused_computation.33 | convolution fusion | flops 272628736 | bytes 8785920 | tf_op jit(solution)/shard_map/dot_general | solution.py:34
  72.3 4.5 %multiply_reduce_fusion.15 = (f32[1024]{0:T(1024)S(1)}, f32[1024,2048]{1,0:T(8,128)}) fusion(bf16[2048,512]{0,1:T(8,128)(2,1)S(1)} %convolution_convert_fusion.1, bf16[1024,512]{0,1:T(8,128)(2,1)S(1)} %convolution_convert_fusion.5), kind=kOutput, calls=%fused_computation.34 | convolution fusion | flops 272628736 | bytes 8785920 | tf_op jit(solution)/shard_map/dot_general | solution.py:34
  76.8 2.8 convolution_convert_fusion
  79.6 4.4 %fusion.1 = f32[1024]{0:T(1024)S(1)} fusion(f32[1024,2048]{1,0:T(8,128)} %get-tuple-element.41, f32[1024]{0:T(1024)S(1)} %get-tuple-element.40), kind=kLoop, calls=%fused_computation.35 | loop fusion | flops 6290432 | bytes 8396800 | tf_op jit(solution)/shard_map/reduce_sum | solution.py:114
  83.9 7.9 %fusion.149 = f32[1024,512]{0,1:T(8,128)S(1)} fusion(f32[1024,2048]{1,0:T(8,128)} %get-tuple-element.41, f32[1024]{0:T(1024)S(1)} %get-tuple-element.40, bf16[2048,512]{0,1:T(8,128)(2,1)} %convolution_convert_fusion), kind=kOutput, calls=%fused_computation.142 | convolution fusion | flops 1614807040 | bytes 8916992 | tf_op jit(solution)/shard_map/dot_general | solution.py:44
  91.8 4.4 %fusion.3 = f32[1024]{0:T(1024)S(1)} fusion(f32[1024,2048]{1,0:T(8,128)} %get-tuple-element.43, f32[1024]{0:T(1024)S(1)} %get-tuple-element.42), kind=kLoop, calls=%fused_computation.37 | loop fusion | flops 6290432 | bytes 8396800 | tf_op jit(solution)/shard_map/reduce_sum | solution.py:114
  96.2 8.1 %fusion.148 = f32[1024,512]{0,1:T(8,128)S(1)} fusion(f32[1024,512]{0,1:T(8,128)S(1)} %fusion.149, f32[1024,2048]{1,0:T(8,128)} %get-tuple-element.43, f32[1024]{0:T(1024)S(1)} %get-tuple-element.42, bf16[2048,512]{0,1:T(8,128)(2,1)} %convolution_convert_fusion), kind=kOutput, calls=%fused_computation.141 | convolution fusion | flops 1614807040 | bytes 8916992 | tf_op jit(solution)/shard_map/dot_general | solution.py:44
  104.3 4.4 %fusion.5 = f32[1024]{0:T(1024)S(1)} fusion(f32[1024,2048]{1,0:T(8,128)} %get-tuple-element.45, f32[1024]{0:T(1024)S(1)} %get-tuple-element.44), kind=kLoop, calls=%fused_computation.39 | loop fusion | flops 6290432 | bytes 8396800 | tf_op jit(solution)/shard_map/reduce_sum | solution.py:114
  108.7 8.1 %fusion.147 = f32[1024,512]{0,1:T(8,128)S(1)} fusion(f32[1024,512]{0,1:T(8,128)S(1)} %fusion.148, f32[1024,2048]{1,0:T(8,128)} %get-tuple-element.45, f32[1024]{0:T(1024)S(1)} %get-tuple-element.44, bf16[2048,512]{0,1:T(8,128)(2,1)} %convolution_convert_fusion), kind=kOutput, calls=%fused_computation.140 | convolution fusion | flops 1614807040 | bytes 8916992 | tf_op jit(solution)/shard_map/dot_general | solution.py:44
  116.8 4.4 %fusion.7 = f32[1024]{0:T(1024)S(1)} fusion(f32[1024,2048]{1,0:T(8,128)} %get-tuple-element.47, f32[1024]{0:T(1024)S(1)} %get-tuple-element.46), kind=kLoop, calls=%fused_computation.41 | loop fusion | flops 6290432 | bytes 8396800 | tf_op jit(solution)/shard_map/reduce_sum | solution.py:114
  121.1 8.3 %fusion.146 = f32[1024,512]{0,1:T(8,128)S(1)} fusion(f32[1024,512]{0,1:T(8,128)S(1)} %fusion.147, f32[1024,2048]{1,0:T(8,128)} %get-tuple-element.47, f32[1024]{0:T(1024)S(1)} %get-tuple-element.46, bf16[2048,512]{0,1:T(8,128)(2,1)} %convolution_convert_fusion), kind=kOutput, calls=%fused_computation.139 | convolution fusion | flops 1614807040 | bytes 8916992 | tf_op jit(solution)/shard_map/dot_general | solution.py:44
  131.4 6.5 %fusion.145 = f32[1024,512]{0,1:T(8,128)S(1)} fusion(f32[1024,512]{0,1:T(8,128)S(1)} %fusion.146, f32[1024,2048]{1,0:T(8,128)S(1)} %get-tuple-element.49, f32[1024]{0:T(1024)S(1)} %get-tuple-element.48, bf16[2048,512]{0,1:T(8,128)(2,1)} %convolution_convert_fusion), kind=kOutput, calls=%fused_computation.138 | convolution fusion | flops 1614807040 | bytes 8916992 | tf_op jit(solution)/shard_map/dot_general | solution.py:44
  137.9 2.3 fusion.11
  140.2 6.5 %fusion.144 = f32[1024,512]{0,1:T(8,128)S(1)} fusion(f32[1024,512]{0,1:T(8,128)S(1)} %fusion.145, f32[1024,2048]{1,0:T(8,128)S(1)} %get-tuple-element.51, f32[1024]{0:T(1024)S(1)} %get-tuple-element.50, bf16[2048,512]{0,1:T(8,128)(2,1)} %convolution_convert_fusion), kind=kOutput, calls=%fused_computation.137 | convolution fusion | flops 1614807040 | bytes 8916992 | tf_op jit(solution)/shard_map/dot_general | solution.py:44
  154.3 9.5 %all-to-all-start.1 = ((f32[32,1,256]{2,1,0:T(1,128)}), f32[32,1,256]{2,1,0:T(1,128)S(1)}, u32[]{:S(2)}, u32[]{:S(2)}) async-start(f32[32,1,256]{2,1,0:T(1,128)} %reshape.112), calls=%async_computation.1 | async-start | bytes 65536 | tf_op jit(solution)/shard_map/all_to_all | solution.py:122
  163.8 8.1 %fusion.143 = f32[1024,512]{0,1:T(8,128)S(1)} fusion(f32[1024,512]{0,1:T(8,128)S(1)} %fusion.144, f32[1024,2048]{1,0:T(8,128)} %copy-done.3, f32[1024]{0:T(1024)S(1)} %get-tuple-element.52, bf16[2048,512]{0,1:T(8,128)(2,1)} %convolution_convert_fusion), kind=kOutput, calls=%fused_computation.136 | convolution fusion | flops 1614807040 | bytes 8916992 | tf_op jit(solution)/shard_map/dot_general | solution.py:44
  175.1 5.9 %all-to-all-start.2 = ((f32[32,1,256]{2,1,0:T(1,128)}), f32[32,1,256]{2,1,0:T(1,128)S(1)}, u32[]{:S(2)}, u32[]{:S(2)}) async-start(f32[32,1,256]{2,1,0:T(1,128)} %reshape.114), calls=%async_computation.2 | async-start | bytes 65536 | tf_op jit(solution)/shard_map/all_to_all | solution.py:121
  181.1 8.1 %fusion.142 = f32[1024,512]{0,1:T(8,128)S(1)} fusion(f32[1024,512]{0,1:T(8,128)S(1)} %fusion.143, f32[1024,2048]{1,0:T(8,128)} %copy-done.2, f32[1024]{0:T(1024)S(1)} %get-tuple-element.54, bf16[2048,512]{0,1:T(8,128)(2,1)} %convolution_convert_fusion), kind=kOutput, calls=%fused_computation.135 | convolution fusion | flops 1614807040 | bytes 8916992 | tf_op jit(solution)/shard_map/dot_general | solution.py:44
  189.2 3.7 copy.23
  192.9 6.0 %all-to-all-start = ((f32[1,1024,512]{2,0,1:T(1,128)}), f32[1,1024,512]{2,0,1:T(1,128)}, u32[]{:S(2)}, u32[]{:S(2)}) async-start(f32[1,1024,512]{2,0,1:T(1,128)} %copy.23), calls=%async_computation | async-start | bytes 4194304 | tf_op jit(solution)/shard_map/all_to_all | solution.py:120
  203.2 2.6 mul.451
  205.8 3.6 mul.452
  209.5 38.1 %all-to-all-done = f32[1,1024,512]{2,0,1:T(1,128)} async-done(((f32[1,1024,512]{2,0,1:T(1,128)}), f32[1,1024,512]{2,0,1:T(1,128)}, u32[]{:S(2)}, u32[]{:S(2)}) %all-to-all-start) | async-done | bytes 2097184 | tf_op jit(solution)/shard_map/all_to_all | solution.py:120
  251.4 2.9 convolution_convert_fusion.2
  254.4 50.3 %all-gather.2.cloned.1.call-done = bf16[1024,512]{1,0:T(8,128)(2,1)} async-done(((bf16[32,512]{1,0:T(8,128)(2,1)}), bf16[1024,512]{1,0:T(8,128)(2,1)}) %all-gather.2.cloned.1.call-update) | async-done | bytes 1048592 | tf_op jit(solution)/shard_map/all_gather | solution.py:137
  304.7 2.0 convolution_convert_fusion.4
  310.6 4.5 %multiply_reduce_fusion.3 = (f32[2048]{0:T(1024)S(1)}, f32[2048,1024]{0,1:T(8,128)}) fusion(bf16[1024,512]{0,1:T(8,128)(2,1)S(1)} %convolution_convert_fusion.4, bf16[2048,512]{0,1:T(8,128)(2,1)S(1)} %convolution_convert_fusion.2), kind=kOutput, calls=%fused_computation.22 | convolution fusion | flops 272627712 | bytes 8790016 | tf_op jit(solution)/shard_map/dot_general | solution.py:34
  315.1 4.5 %multiply_reduce_fusion.4 = (f32[2048]{0:T(1024)S(1)}, f32[2048,1024]{0,1:T(8,128)}) fusion(bf16[1024,512]{0,1:T(8,128)(2,1)S(1)} %convolution_convert_fusion.4, bf16[2048,512]{0,1:T(8,128)(2,1)S(1)} %convolution_convert_fusion.2), kind=kOutput, calls=%fused_computation.23 | convolution fusion | flops 272627712 | bytes 8790016 | tf_op jit(solution)/shard_map/dot_general | solution.py:34
  319.6 4.5 %multiply_reduce_fusion.5 = (f32[2048]{0:T(1024)S(1)}, f32[2048,1024]{0,1:T(8,128)}) fusion(bf16[1024,512]{0,1:T(8,128)(2,1)S(1)} %convolution_convert_fusion.4, bf16[2048,512]{0,1:T(8,128)(2,1)S(1)} %convolution_convert_fusion.2), kind=kOutput, calls=%fused_computation.24 | convolution fusion | flops 272627712 | bytes 8790016 | tf_op jit(solution)/shard_map/dot_general | solution.py:34
  324.2 4.5 %multiply_reduce_fusion.6 = (f32[2048]{0:T(1024)S(1)}, f32[2048,1024]{0,1:T(8,128)}) fusion(bf16[1024,512]{0,1:T(8,128)(2,1)S(1)} %convolution_convert_fusion.4, bf16[2048,512]{0,1:T(8,128)(2,1)S(1)} %convolution_convert_fusion.2), kind=kOutput, calls=%fused_computation.25 | convolution fusion | flops 272627712 | bytes 8790016 | tf_op jit(solution)/shard_map/dot_general | solution.py:34
  328.7 5.0 %multiply_reduce_fusion.7 = (f32[2048]{0:T(1024)S(1)}, f32[2048,1024]{0,1:T(8,128)}) fusion(bf16[1024,512]{0,1:T(8,128)(2,1)S(1)} %convolution_convert_fusion.4, bf16[2048,512]{0,1:T(8,128)(2,1)S(1)} %convolution_convert_fusion.2), kind=kOutput, calls=%fused_computation.26 | convolution fusion | flops 272627712 | bytes 8790016 | tf_op jit(solution)/shard_map/dot_general | solution.py:34
  337.9 4.8 %fusion.25 = f32[2048]{0:T(1024)S(1)} fusion(f32[2048,1024]{0,1:T(8,128)} %get-tuple-element.65, f32[2048]{0:T(1024)S(1)} %get-tuple-element.64), kind=kLoop, calls=%fused_computation.59 | loop fusion | flops 6289408 | bytes 8404992 | tf_op jit(solution)/shard_map/reduce_sum | solution.py:150
  342.7 4.8 %fusion.23 = f32[2048]{0:T(1024)S(1)} fusion(f32[2048,1024]{0,1:T(8,128)} %get-tuple-element.63, f32[2048]{0:T(1024)S(1)} %get-tuple-element.62), kind=kLoop, calls=%fused_computation.57 | loop fusion | flops 6289408 | bytes 8404992 | tf_op jit(solution)/shard_map/reduce_sum | solution.py:150
  347.4 4.8 %fusion.21 = f32[2048]{0:T(1024)S(1)} fusion(f32[2048,1024]{0,1:T(8,128)} %get-tuple-element.61, f32[2048]{0:T(1024)S(1)} %get-tuple-element.60), kind=kLoop, calls=%fused_computation.55 | loop fusion | flops 6289408 | bytes 8404992 | tf_op jit(solution)/shard_map/reduce_sum | solution.py:150
  352.2 4.8 %fusion.19 = f32[2048]{0:T(1024)S(1)} fusion(f32[2048,1024]{0,1:T(8,128)} %get-tuple-element.59, f32[2048]{0:T(1024)S(1)} %get-tuple-element.58), kind=kLoop, calls=%fused_computation.53 | loop fusion | flops 6289408 | bytes 8404992 | tf_op jit(solution)/shard_map/reduce_sum | solution.py:150
  357.0 5.1 %fusion.17 = f32[2048]{0:T(1024)S(1)} fusion(f32[2048,1024]{0,1:T(8,128)} %get-tuple-element.57, f32[2048]{0:T(1024)S(1)} %get-tuple-element.56), kind=kLoop, calls=%fused_computation.51 | loop fusion | flops 6289408 | bytes 8404992 | tf_op jit(solution)/shard_map/reduce_sum | solution.py:150
  362.9 4.9 %fusion.76 = bf16[2048,512]{0,1:T(8,128)(2,1)S(1)} fusion(f32[2048,1024]{0,1:T(8,128)} %get-tuple-element.57, f32[2048]{0:T(1024)S(1)} %get-tuple-element.56, f32[2048]{0:T(1024)S(1)} %fusion.17, bf16[1024,512]{0,1:T(8,128)(2,1)S(1)} %convolution_convert_fusion.3), kind=kOutput, calls=%fused_computation.107 | convolution fusion | flops 274989056 | bytes 8798208 | tf_op jit(solution)/shard_map/dot_general | solution.py:151
  367.8 4.9 %fusion.85 = bf16[2048,512]{0,1:T(8,128)(2,1)S(1)} fusion(bf16[2048,512]{0,1:T(8,128)(2,1)S(1)} %fusion.76, f32[2048,1024]{0,1:T(8,128)} %get-tuple-element.59, f32[2048]{0:T(1024)S(1)} %get-tuple-element.58, f32[2048]{0:T(1024)S(1)} %fusion.19, bf16[1024,512]{0,1:T(8,128)(2,1)S(1)} %convolution_convert_fusion.3), kind=kOutput, calls=%fused_computation.110 | convolution fusion | flops 274989056 | bytes 8798208 | tf_op jit(solution)/shard_map/dot_general | solution.py:151
  372.8 5.1 %fusion.94 = bf16[2048,512]{0,1:T(8,128)(2,1)S(1)} fusion(bf16[2048,512]{0,1:T(8,128)(2,1)S(1)} %fusion.85, f32[2048,1024]{0,1:T(8,128)} %get-tuple-element.61, f32[2048]{0:T(1024)S(1)} %get-tuple-element.60, f32[2048]{0:T(1024)S(1)} %fusion.21, bf16[1024,512]{0,1:T(8,128)(2,1)S(1)} %convolution_convert_fusion.3), kind=kOutput, calls=%fused_computation.113 | convolution fusion | flops 274989056 | bytes 8798208 | tf_op jit(solution)/shard_map/dot_general | solution.py:151
  377.8 5.1 %fusion.103 = bf16[2048,512]{0,1:T(8,128)(2,1)S(1)} fusion(bf16[2048,512]{0,1:T(8,128)(2,1)S(1)} %fusion.94, f32[2048,1024]{0,1:T(8,128)} %get-tuple-element.63, f32[2048]{0:T(1024)S(1)} %get-tuple-element.62, f32[2048]{0:T(1024)S(1)} %fusion.23, bf16[1024,512]{0,1:T(8,128)(2,1)S(1)} %convolution_convert_fusion.3), kind=kOutput, calls=%fused_computation.116 | convolution fusion | flops 274989056 | bytes 8798208 | tf_op jit(solution)/shard_map/dot_general | solution.py:151
  389.3 3.3 bitcast_add_fusion
  (100 shorter events, 51.4 us)
Async XLA Ops:
  6.5 45.5 %copy-start = (bf16[512,512]{1,0:T(8,128)(2,1)S(1)}, bf16[512,512]{1,0:T(8,128)(2,1)}, u32[]{:S(2)}) copy-start(bf16[512,512]{1,0:T(8,128)(2,1)} %param.17) | copy-start | bytes 1572868
  6.5 9.2 %copy-start.9 = (f32[27,512]{1,0:T(8,128)S(1)}, f32[27,512]{1,0:T(8,128)}, u32[]{:S(2)}) copy-start(f32[27,512]{1,0:T(8,128)} %param.14) | copy-start | bytes 165892
  6.5 9.2 %copy-start.10 = (bf16[1024,512]{1,0:T(8,128)(2,1)S(1)}, bf16[1024,512]{1,0:T(8,128)(2,1)}, u32[]{:S(2)}) copy-start(bf16[1024,512]{1,0:T(8,128)(2,1)} %param.15) | copy-start | bytes 3145732
  6.5 9.2 %copy-start.12 = (bf16[512,512]{1,0:T(8,128)(2,1)S(1)}, bf16[512,512]{1,0:T(8,128)(2,1)}, u32[]{:S(2)}) copy-start(bf16[512,512]{1,0:T(8,128)(2,1)} %param.16) | copy-start | bytes 1572868
  9.5 26.2 %copy-start.4 = (bf16[8,16,16,512]{3,2,1,0:T(8,128)(2,1)}, bf16[8,16,16,512]{3,2,1,0:T(8,128)(2,1)S(1)}, u32[]{:S(2)}) copy-start(bf16[8,16,16,512]{3,2,1,0:T(8,128)(2,1)S(1)} %broadcast_multiply_fusion) | copy-start | bytes 6291460
  9.5 16.0 %collective-permute-start = (bf16[1,16,16,512]{3,2,1,0:T(8,128)(2,1)S(1)}, bf16[1,16,16,512]{3,2,1,0:T(8,128)(2,1)S(1)}, u32[]{:S(2)}, u32[]{:S(2)}) collective-permute-start(bf16[1,16,16,512]{3,2,1,0:T(8,128)(2,1)S(1)} %get-tuple-element.11), channel_id=1, source_target_pairs={{0,4},{4,8},{8,12},{12,16},{16,20},{20,24},{24,28},{1,5},{5,9},{9,... | collective-permute-start | bytes 786440 | tf_op jit(solution)/shard_map/ppermute | solution.py:19
  14.4 11.2 %collective-permute-start.1 = (bf16[1,16,16,512]{3,2,1,0:T(8,128)(2,1)S(1)}, bf16[1,16,16,512]{3,2,1,0:T(8,128)(2,1)S(1)}, u32[]{:S(2)}, u32[]{:S(2)}) collective-permute-start(bf16[1,16,16,512]{3,2,1,0:T(8,128)(2,1)S(1)} %get-tuple-element.12), channel_id=1, source_target_pairs={{4,0},{8,4},{12,8},{16,12},{20,16},{24,20},{28,24},{5,1},{9,5},{13... | collective-permute-start | bytes 786440 | tf_op jit(solution)/shard_map/ppermute | solution.py:21
  25.6 2.6 collective-permute-start.2
  26.9 5.0 %collective-permute-start.3 = (bf16[10,1,16,512]{3,2,1,0:T(8,128)(2,1)S(1)}, bf16[10,1,16,512]{3,2,1,0:T(8,128)(2,1)S(1)}, u32[]{:S(2)}, u32[]{:S(2)}) collective-permute-start(bf16[10,1,16,512]{3,2,1,0:T(8,128)(2,1)S(1)} %get-tuple-element.10), channel_id=1, source_target_pairs={{1,0},{2,1},{3,2},{5,4},{6,5},{7,6},{9,8},{10,9},{11,10},{13,12},{... | collective-permute-start | bytes 491528 | tf_op jit(solution)/shard_map/ppermute | solution.py:21
  52.1 24.7 %copy-start.6 = (bf16[8,16,16,512]{3,2,1,0:T(8,128)(2,1)}, bf16[8,16,16,512]{3,2,1,0:T(8,128)(2,1)S(1)}, u32[]{:S(2)}) copy-start(bf16[8,16,16,512]{3,2,1,0:T(8,128)(2,1)S(1)} %add_convert_fusion) | copy-start | bytes 6291460
  54.7 92.0 %copy-start.2 = (f32[1024,2048]{1,0:T(8,128)}, f32[1024,2048]{1,0:T(8,128)S(1)}, u32[]{:S(2)}) copy-start(f32[1024,2048]{1,0:T(8,128)S(1)} %get-tuple-element.55) | copy-start | bytes 25165828
  56.1 92.5 %copy-start.3 = (f32[1024,2048]{1,0:T(8,128)}, f32[1024,2048]{1,0:T(8,128)S(1)}, u32[]{:S(2)}) copy-start(f32[1024,2048]{1,0:T(8,128)S(1)} %get-tuple-element.53) | copy-start | bytes 25165828
  72.3 4.5 %copy-start.13 = (bf16[512,512]{1,0:T(8,128)(2,1)S(1)}, bf16[512,512]{1,0:T(8,128)(2,1)}, u32[]{:S(2)}) copy-start(bf16[512,512]{1,0:T(8,128)(2,1)} %param.18) | copy-start | bytes 1572868
  154.3 20.8 %all-to-all-start.1 = ((f32[32,1,256]{2,1,0:T(1,128)}), f32[32,1,256]{2,1,0:T(1,128)S(1)}, u32[]{:S(2)}, u32[]{:S(2)}) async-start(f32[32,1,256]{2,1,0:T(1,128)} %reshape.112), calls=%async_computation.1 | async-start | bytes 65536 | tf_op jit(solution)/shard_map/all_to_all | solution.py:122
  175.1 17.8 %all-to-all-start.2 = ((f32[32,1,256]{2,1,0:T(1,128)}), f32[32,1,256]{2,1,0:T(1,128)S(1)}, u32[]{:S(2)}, u32[]{:S(2)}) async-start(f32[32,1,256]{2,1,0:T(1,128)} %reshape.114), calls=%async_computation.2 | async-start | bytes 65536 | tf_op jit(solution)/shard_map/all_to_all | solution.py:121
  192.9 54.7 %all-to-all-start = ((f32[1,1024,512]{2,0,1:T(1,128)}), f32[1,1024,512]{2,0,1:T(1,128)}, u32[]{:S(2)}, u32[]{:S(2)}) async-start(f32[1,1024,512]{2,0,1:T(1,128)} %copy.23), calls=%async_computation | async-start | bytes 4194304 | tf_op jit(solution)/shard_map/all_to_all | solution.py:120
  198.9 105.8 %all-gather.2.cloned.1.call-start = ((), (), s32[]{:S(2)}) async-start(), calls=%async_computation.3 | async-start | bytes 1081344 | tf_op jit(solution)/shard_map/all_gather | solution.py:137
  209.4 40.4 %copy-start.8 = (bf16[512,512]{1,0:T(8,128)(2,1)S(1)}, bf16[512,512]{1,0:T(8,128)(2,1)}, u32[]{:S(2)}) copy-start(bf16[512,512]{1,0:T(8,128)(2,1)} %param.19) | copy-start | bytes 1572868
  209.5 42.0 %copy-start.14 = (bf16[512,512]{1,0:T(8,128)(2,1)S(1)}, bf16[512,512]{1,0:T(8,128)(2,1)}, u32[]{:S(2)}) copy-start(bf16[512,512]{1,0:T(8,128)(2,1)} %param.20) | copy-start | bytes 1572868
  251.4 53.2 %copy-start.15 = (bf16[512,512]{1,0:T(8,128)(2,1)S(1)}, bf16[512,512]{1,0:T(8,128)(2,1)}, u32[]{:S(2)}) copy-start(bf16[512,512]{1,0:T(8,128)(2,1)} %param.21) | copy-start | bytes 1572868
  357.0 5.1 %copy-start.11 = (bf16[1024,512]{1,0:T(8,128)(2,1)S(1)}, bf16[1024,512]{1,0:T(8,128)(2,1)}, u32[]{:S(2)}) copy-start(bf16[1024,512]{1,0:T(8,128)(2,1)} %all-gather.2.cloned.1.call-done) | copy-start | bytes 3145732
  357.0 5.1 %copy-start.16 = (bf16[512,512]{1,0:T(8,128)(2,1)S(1)}, bf16[512,512]{1,0:T(8,128)(2,1)}, u32[]{:S(2)}) copy-start(bf16[512,512]{1,0:T(8,128)(2,1)} %param.22) | copy-start | bytes 1572868
  372.7 10.2 %slice-start = ((s8[8388608]{0:T(1024)(128)(4,1)}), s8[4194304]{0:T(1024)(128)(4,1)S(1)}, s32[]{:S(2)}) async-start(s8[8388608]{0:T(1024)(128)(4,1)} %bitcast.74), calls=%async_computation.4 | async-start | bytes 8388608
  377.8 5.1 %slice-start.1 = ((s8[8388608]{0:T(1024)(128)(4,1)}), s8[4194304]{0:T(1024)(128)(4,1)S(1)}, s32[]{:S(2)}) async-start(s8[8388608]{0:T(1024)(128)(4,1)} %bitcast.74), calls=%async_computation.5 | async-start | bytes 8388608
  387.6 1.6 copy-start.5
  387.6 1.7 copy-start.7
  387.6 5.0 %copy-start.1 = (bf16[512,512]{1,0:T(8,128)(2,1)S(1)}, bf16[512,512]{1,0:T(8,128)(2,1)}, u32[]{:S(2)}) copy-start(bf16[512,512]{1,0:T(8,128)(2,1)} %param.17) | copy-start | bytes 1572868
Sparse Core Ops, SparseCore 0:
  251.5 53.0 all-gather.1
where the time goes:
time: 405 us; the launch traced here: 400 us
  matrix products  154 us (38%)
  waiting for transfers between devices  101 us (25%)
  other arithmetic  82.8 us (20%)
  starting transfers between devices  30.2 us (7%)
  local copies, waits for them, and re-layouts  17.8 us (4%)
  between operations  14.2 us (4%)
    dot_general x8, matrix products, exact_dot(): jnp.dot(weights, values_block, precision=lax.Precision.HIGHEST, preferred...  61.6 us
    dot_general x16, matrix products, pair_scores(): lax.dot_general(queries, key_rows, (((1,), (1,)), ((), ())), preferred_el...  50.3 us
    all_gather x1, waiting for transfers between devices, per_device(): lax.all_gather(own_state, ('wide', 'narrow'), axis=0, tiled=True)  50.3 us
    all_to_all x1, waiting for transfers between devices, per_device(): lax.all_to_all(summed1, ('wide', 'narrow'), split_axis=1, concat_axis=0,...  38.1 us
    reduce_sum x8, other arithmetic, per_device(): totals = jnp.sum(weights, axis=1, keepdims=True)  28.4 us
    dot_general x8, matrix products, per_device(): jnp.dot(weights.astype(jnp.bfloat16), head_block(values2, head_index, hea...  26.2 us
    reduce_sum x8, other arithmetic, per_device(): totals_list.append(jnp.sum(weights, axis=1))  25.6 us
    convert_element_type x1, other arithmetic, per_device(): mixed_cells = stencil.astype(jnp.bfloat16).reshape(cell_count, model_width)  16.4 us
  transfers between devices with their start and end apart: 8, of which 4 were waited for; matrix products, arithmetic and copies ran while one was open for 9% of the time, Pallas kernels for 0%

commit v1 on v0

v1 whole, which is shorter than its diff:
```python
import functools
import math

import jax
import jax.numpy as jnp
from jax import lax
from jax.experimental import pallas as pl
from jax.experimental.pallas import tpu as pltpu
from jax.sharding import Mesh, PartitionSpec as P

HEADS = 8
LANES = 128
ONES_ROWS = 16
VMEM_BYTES = 60 << 20
F32 = jnp.float32
BF16 = jnp.bfloat16


def dot(left, right, contract=((1,), (0,))):
    return lax.dot_general(left, right, (contract, ((), ())), preferred_element_type=F32)


def fill_padded(padded, masked, x_lo, x_hi, y_lo, y_hi, c_lo, c_hi):
    size_x, size_y = masked.shape[:2]

    def plane(i, carry):
        padded[i + 1, 1 : size_y + 1] = masked[i].astype(F32)
        padded[i + 1, 0] = y_lo[i].astype(F32)
        padded[i + 1, size_y + 1] = y_hi[i].astype(F32)
        return carry

    lax.fori_loop(0, size_x, plane, 0)
    for row, face in ((0, x_lo), (size_x + 1, x_hi)):
        padded[row, 1 : size_y + 1] = face[...].astype(F32)
    for end, row in ((0, 0), (1, size_x + 1)):
        padded[row, 0] = c_lo[end].astype(F32)
        padded[row, size_y + 1] = c_hi[end].astype(F32)


def stencil_plane(i, padded, conv, mixed, size_y, size_z):
    width = padded.shape[-1]
    row_of = lax.broadcasted_iota(jnp.int32, (size_z, LANES), 0)
    for tile in range(width // LANES):
        lanes = slice(tile * LANES, (tile + 1) * LANES)
        taps = [jnp.broadcast_to(conv[n : n + 1, lanes], (size_z, LANES)) for n in range(27)]
        for j in range(size_y):
            sums = [None] * 3
            for a in range(3):
                for b in range(3):
                    window = padded[i + a, j + b, :, lanes]
                    for c in range(3):
                        term = window * taps[9 * a + 3 * b + c]
                        sums[c] = term if sums[c] is None else sums[c] + term
            below = jnp.where(row_of == 0, 0.0, pltpu.roll(sums[0], 1, 0))
            above = jnp.where(row_of == size_z - 1, 0.0, pltpu.roll(sums[2], size_z - 1, 0))
            total = padded[i + 1, j + 1, :, lanes] + sums[1] + below + above
            start = pl.multiple_of((i * size_y + j) * size_z, size_z)
            mixed[pl.ds(start, size_z), lanes] = total.astype(BF16)


def score_weights(query_t, head_in_pair, head_size):
    factor = 1.8 / math.sqrt(head_size) * math.log2(math.e)
    scaled = query_t.astype(F32) * factor
    high = scaled.astype(BF16)
    low = (scaled - high.astype(F32)).astype(BF16)
    blank = jnp.zeros_like(high)
    if head_in_pair == 0:
        return jnp.concatenate([high, blank, low, blank], axis=0)
    return jnp.concatenate([blank, high, blank, low], axis=0)


def attention_scores(pair, head_in_pair, block, width, chunk, keys, query_t, scores):
    head_size = LANES // 2
    start = pl.multiple_of(pair * LANES, LANES) + head_in_pair * head_size
    columns = pl.ds(pl.multiple_of(block * width, width), width)
    right = score_weights(query_t[pl.ds(start, head_size), columns], head_in_pair, head_size)
    top = None
    for part in range(keys.shape[0] // chunk):
        rows = pl.ds(part * chunk, chunk)
        left = keys[rows, pl.ds(pl.multiple_of(pair * LANES, LANES), LANES)]
        piece = dot(jnp.concatenate([left, left], axis=1), right)
        scores[head_in_pair, rows, :] = piece
        largest = jnp.max(piece.reshape(chunk // 8, 8, width), axis=0)
        top = largest if top is None else jnp.maximum(top, largest)
    return jnp.max(top, axis=0, keepdims=True)


def attention_sums(head, head_in_pair, chunk, values_t, scores, top):
    total = None
    for part in range(scores.shape[1] // chunk):
        rows = pl.ds(part * chunk, chunk)
        weights = jnp.exp2(scores[head_in_pair, rows, :] - top).astype(BF16)
        piece = dot(values_t[head, :, rows], weights)
        total = piece if total is None else total + piece
    return total


def attention_loop(keys, query_t, values_t, scores, chunk, finish):
    width = scores.shape[2]
    blocks = query_t.shape[1] // width
    pairs = query_t.shape[0] // LANES
    steps = pairs * blocks

    def first(t):
        return attention_scores(t % pairs, 0, t // pairs, width, chunk, keys, query_t, scores)

    def step(t, top_even):
        pair, block = t % pairs, t // pairs
        top_odd = attention_scores(pair, 1, block, width, chunk, keys, query_t, scores)
        even = attention_sums(2 * pair, 0, chunk, values_t, scores, top_even)
        following = first(jnp.minimum(t + 1, steps - 1))
        odd = attention_sums(2 * pair + 1, 1, chunk, values_t, scores, top_odd)
        finish(pair, block, (even, odd), (top_even, top_odd))
        return following

    lax.fori_loop(0, steps, step, first(0))


def split3(value):
    high = value.astype(BF16).astype(F32)
    rest = value - high
    middle = rest.astype(BF16).astype(F32)
    return high, middle, rest - middle


def read_kernel(
    masked,
    x_lo,
    x_hi,
    y_lo,
    y_hi,
    c_lo,
    c_hi,
    conv,
    latents,
    w_query1,
    w_key1,
    w_value1,
    w_query2,
    query2_t,
    packed,
    padded,
    mixed,
    keys,
    values_t,
    query1_t,
    scores,
    stats,
):
    size_x, size_y, size_z, width = masked.shape
    head_size = width // HEADS
    fill_padded(padded, masked, x_lo, x_hi, y_lo, y_hi, c_lo, c_hi)

    def plane(i, carry):
        stencil_plane(i, padded, conv, mixed, size_y, size_z)
        return carry

    lax.fori_loop(0, size_x, plane, 0)

    cells = size_y * size_z
    lower = ((0,), (1,))
    values_t[:, head_size:, :] = jnp.ones_like(values_t[:, head_size:, :])

    def projections(i, carry):
        rows = pl.ds(pl.multiple_of(i * cells, cells), cells)
        block = mixed[rows, :]
        keys[rows, :] = dot(block, w_key1[...]).astype(BF16)
        value_t = dot(w_value1[...], block, lower).astype(BF16)
        values_t[:, :head_size, rows] = value_t.reshape(HEADS, head_size, cells)
        query2_t[:, rows] = dot(w_query2[...], block, lower).astype(BF16)
        return carry

    lax.fori_loop(0, size_x, projections, 0)
    query1_t[...] = dot(w_query1[...], latents[...], lower).astype(BF16)
    stats[...] = jnp.zeros_like(stats)

    def finish(pair, block, sums, tops):
        columns = pl.ds(pl.multiple_of(block * scores.shape[2], LANES), scores.shape[2])
        both = jnp.concatenate([part[:head_size] for part in sums], axis=0)
        lanes = pl.ds(pl.multiple_of(pair * LANES, LANES), LANES)
        packed[columns, lanes] = both.T.astype(BF16)
        for head_in_pair in range(2):
            rows = split3(tops[head_in_pair]) + split3(sums[head_in_pair][head_size : head_size + 1])[:2]
            for slot, row in enumerate(rows):
                stats[pl.ds(slot * HEADS + 2 * pair + head_in_pair, 1), columns] = row

    attention_loop(keys, query1_t, values_t, scores, 256, finish)
    packed[:, width:] = stats[...].T.astype(BF16)


def unpack_stats(tile):
    parts = [tile] + [pltpu.roll(tile, LANES - slot * HEADS, 1) for slot in range(1, 5)]
    return parts[0] + parts[1] + parts[2], parts[3] + parts[4]


def pack_stats(top, total):
    lane = lax.broadcasted_iota(jnp.int32, top.shape, 1)
    tile = jnp.zeros_like(top)
    for slot, value in enumerate(split3(top) + split3(total)[:2]):
        moved = pltpu.roll(value, slot * HEADS, 1) if slot else value
        tile = jnp.where((lane >= slot * HEADS) & (lane < (slot + 1) * HEADS), moved, tile)
    return tile


def spread(per_head, pair):
    rows = per_head.shape[0]
    lane = lax.broadcasted_iota(jnp.int32, (rows, LANES), 1)
    left = jnp.broadcast_to(per_head[:, 2 * pair : 2 * pair + 1], (rows, LANES))
    right = jnp.broadcast_to(per_head[:, 2 * pair + 1 : 2 * pair + 2], (rows, LANES))
    return jnp.where(lane < LANES // 2, left, right)


def merge_parts(loads, width):
    stats = [unpack_stats(load(slice(width, width + LANES))) for load in loads]
    top = functools.reduce(jnp.maximum, [t for t, _ in stats])
    factors = [jnp.exp2(t - top) for t, _ in stats]
    total = sum(f * l for f, (_, l) in zip(factors, stats))
    sums = []
    for pair in range(width // LANES):
        lanes = slice(pair * LANES, (pair + 1) * LANES)
        sums.append(sum(load(lanes) * spread(f, pair) for load, f in zip(loads, factors)))
    return sums, top, total


def merge_two_kernel(left, right, out):
    rows, full = left.shape
    width = full - LANES
    step = min(rows, 64)

    def body(r, carry):
        span = pl.ds(pl.multiple_of(r * step, step), step)
        loads = [lambda lanes, ref=ref: ref[span, lanes].astype(F32) for ref in (left, right)]
        sums, top, total = merge_parts(loads, width)
        for pair, value in enumerate(sums):
            out[span, pair * LANES : (pair + 1) * LANES] = value.astype(BF16)
        out[span, width:] = pack_stats(top, total).astype(BF16)
        return carry

    lax.fori_loop(0, rows // step, body, 0)


def update_kernel(parts, own, w_out1, out):
    count, rows, full = parts.shape
    width = full - LANES
    loads = [lambda lanes, g=g: parts[g, :, lanes].astype(F32) for g in range(count)]
    sums, _, total = merge_parts(loads, width)
    read = [value / spread(total, pair) for pair, value in enumerate(sums)]
    read = jnp.concatenate(read, axis=1).astype(BF16)
    out[...] = (own[...].astype(F32) + dot(read, w_out1[...])).astype(BF16)


def write_kernel(state, query2_t, masked, w_key2, w_value2, w_out2, out, keys, values_t, scores, read_t):
    width = state.shape[1]
    head_size = width // HEADS
    values_t[:, head_size:, :] = jnp.ones_like(values_t[:, head_size:, :])
    keys[...] = dot(state[...], w_key2[...]).astype(BF16)
    value_t = dot(w_value2[...], state[...], ((0,), (1,))).astype(BF16)
    values_t[:, :head_size, :] = value_t.reshape(HEADS, head_size, state.shape[0])
    span = scores.shape[2]

    def finish(pair, block, sums, tops):
        columns = pl.ds(pl.multiple_of(block * span, span), span)
        both = [part[:head_size] / part[head_size : head_size + 1] for part in sums]
        rows = pl.ds(pl.multiple_of(pair * LANES, LANES), LANES)
        read_t[rows, columns] = jnp.concatenate(both, axis=0).astype(BF16)

    attention_loop(keys, query2_t, values_t, scores, 256, finish)

    def emit(r, carry):
        rows = pl.ds(pl.multiple_of(r * span, span), span)
        change = dot(read_t[:, rows], w_out2[...], ((0,), (0,)))
        out[rows, :] = masked[rows, :].astype(F32) + change
        return carry

    lax.fori_loop(0, out.shape[0] // span, emit, 0)


def call(kernel, shapes, scratch, *operands):
    vmem = pl.BlockSpec(memory_space=pltpu.VMEM)
    many = isinstance(shapes, (list, tuple))
    return pl.pallas_call(
        kernel,
        out_shape=shapes,
        in_specs=[vmem] * len(operands),
        out_specs=[vmem] * len(shapes) if many else vmem,
        scratch_shapes=scratch,
        compiler_params=pltpu.CompilerParams(vmem_limit_bytes=VMEM_BYTES),
    )(*operands)


def exchange(low, high, axis):
    count = lax.axis_size(axis)
    up = [(i, i + 1) for i in range(count - 1)]
    down = [(i + 1, i) for i in range(count - 1)]
    return lax.ppermute(high, axis, up), lax.ppermute(low, axis, down)


def flipped(array, axis, distance):
    return lax.ppermute(array, axis, [(i, i ^ distance) for i in range(lax.axis_size(axis))])


def per_device(
    flow_field,
    fluid_mask,
    conv_weight,
    latents,
    w_query1,
    w_key1,
    w_value1,
    w_out1,
    w_query2,
    w_key2,
    w_value2,
    w_out2,
):
    size_x, size_y, size_z, width = flow_field.shape
    head_size = width // HEADS
    cells = size_x * size_y * size_z
    latent_count = latents.shape[0]
    narrow = ("ny", "nc")
    shape = jax.ShapeDtypeStruct
    masked = flow_field * fluid_mask[:, :, :, None].astype(BF16)

    x_lo, x_hi = exchange(masked[0], masked[-1], "wide")
    y_lo, y_hi = exchange(masked[:, 0], masked[:, -1], narrow)
    ends = jnp.stack([x_lo, x_hi])
    c_lo, c_hi = exchange(ends[:, 0], ends[:, -1], narrow)

    query2_t, packed = call(
        read_kernel,
        [shape((width, cells), BF16), shape((latent_count, width + LANES), BF16)],
        [
            pltpu.VMEM((size_x + 2, size_y + 2, size_z, width), F32),
            pltpu.VMEM((cells, width), BF16),
            pltpu.VMEM((cells, width), BF16),
            pltpu.VMEM((HEADS, head_size + ONES_ROWS, cells), BF16),
            pltpu.VMEM((width, latent_count), BF16),
            pltpu.VMEM((2, cells, 256), F32),
            pltpu.VMEM((LANES, latent_count), F32),
        ],
        masked,
        x_lo,
        x_hi,
        y_lo,
        y_hi,
        c_lo,
        c_hi,
        conv_weight,
        latents,
        w_query1,
        w_key1,
        w_value1,
        w_query2,
    )

    half = latent_count // 2
    core = lax.axis_index("nc")
    halves = packed.reshape(2, half, width + LANES)
    kept = lax.dynamic_index_in_dim(halves, core, 0, keepdims=False)
    given = lax.dynamic_index_in_dim(halves, 1 - core, 0, keepdims=False)
    taken = flipped(given, "nc", 1)
    merged = call(merge_two_kernel, shape((half, width + LANES), BF16), [], kept, taken)
    groups = lax.axis_size("wide") * lax.axis_size("ny")
    rows = half // groups
    parts = lax.all_to_all(
        merged.reshape(groups, rows, width + LANES), ("wide", "ny"), split_axis=0, concat_axis=0, tiled=True
    )
    group = lax.axis_index("wide") * lax.axis_size("ny") + lax.axis_index("ny")
    own = lax.dynamic_slice_in_dim(latents, core * half + group * rows, rows, 0)
    state = call(update_kernel, shape((rows, width), BF16), [], parts, own, w_out1)

    distance = lax.axis_size("wide") // 2
    while distance:
        state = jnp.concatenate([state, flipped(state, "wide", distance)], axis=0)
        distance //= 2
    for axis in narrow:
        state = jnp.concatenate([state, flipped(state, axis, 1)], axis=0)

    result = call(
        write_kernel,
        shape((cells, width), F32),
        [
            pltpu.VMEM((latent_count, width), BF16),
            pltpu.VMEM((HEADS, head_size + ONES_ROWS, latent_count), BF16),
            pltpu.VMEM((2, latent_count, 512), F32),
            pltpu.VMEM((width, cells), BF16),
        ],
        state,
        query2_t,
        masked.reshape(cells, width),
        w_key2,
        w_value2,
        w_out2,
    )
    return result.reshape(size_x, size_y, size_z, width)


def solution(mesh):
    wide, narrow = (mesh.shape[name] for name in ("wide", "narrow"))
    grid = Mesh(mesh.devices.reshape(wide, narrow // 2, 2), ("wide", "ny", "nc"))
    split = ("ny", "nc")
    return jax.shard_map(
        per_device,
        mesh=grid,
        in_specs=(P("wide", split, None, None), P("wide", split, None)) + (P(),) * 10,
        out_specs=P("wide", split, None, None),
        check_vma=False,
    )
```

time: 405 us -> 157 us (0.39); the launches traced: 400 us -> 156 us
  matrix products: 154 us -> 0 us
  other arithmetic: 82.8 us -> 5.09 us
  Pallas kernels: 0 us -> 71.7 us
  waiting for transfers between devices: 101 us -> 41.2 us
  between operations: 14.2 us -> 0.25 us
  local copies, waits for them, and re-layouts: 17.8 us -> 7.89 us
    dot_general x40 -> x0, matrix products: 154 us -> none  [the longest x8 61.6 us: exact_dot(): jnp.dot(weights, values_block, precision=lax.Precision.HIGHEST, preferred...]
    pallas_call x0 -> x4, Pallas kernels: none -> 71.7 us  [call(): pl.pallas_call(kernel, out_shape=shapes, in_specs=[vmem] * len(operands),...]
    reduce_sum x18 -> x0, other arithmetic: 54.5 us -> none  [the longest x8 28.4 us: per_device(): totals = jnp.sum(weights, axis=1, keepdims=True)]
    all_gather x1 -> x0, waiting for transfers between devices: 50.3 us -> none  [per_device(): lax.all_gather(own_state, ('wide', 'narrow'), axis=0, tiled=True)]
    all_to_all x3 -> x1, waiting for transfers between devices: 38.1 us -> 16.3 us  [per_device(): lax.all_to_all(merged.reshape(groups, rows, width + LANES), ('wide', 'ny'...]
    convert_element_type x2 -> x1, other arithmetic: 17.4 us -> 0.85 us  [per_device(): masked = flow_field * fluid_mask[:, :, :, None].astype(BF16)]
    all_to_all x3 -> x1, starting transfers between devices: 21.4 us -> 7.93 us  [per_device(): lax.all_to_all(merged.reshape(groups, rows, width + LANES), ('wide', 'ny'...]
    ppermute x4 -> x12, starting transfers between devices: 8.77 us -> 22.1 us  [the longest x6 15.5 us: exchange(): return (lax.ppermute(high, axis, up), lax.ppermute(low, axis, down))]
  transfers between devices with their start and end apart: 8 -> 13, of which waited for: 4 -> 9; matrix products, arithmetic and copies ran while one was open for 9% -> 1% of each run, Pallas kernels for 0% -> 0%
where the time goes in v1:
time: 157 us; the launch traced here: 156 us
  Pallas kernels  71.7 us (46%)
  waiting for transfers between devices  41.2 us (26%)
  starting transfers between devices  30.1 us (19%)
  local copies, waits for them, and re-layouts  7.89 us (5%)
  other arithmetic  5.09 us (3%)
    pallas_call x4, Pallas kernels, call(): pl.pallas_call(kernel, out_shape=shapes, in_specs=[vmem] * len(operands),...  71.7 us
    ppermute x6, waiting for transfers between devices, flipped(): lax.ppermute(array, axis, [(i, i ^ distance) for i in range(lax.axis_size...  18.4 us
    all_to_all x1, waiting for transfers between devices, per_device(): lax.all_to_all(merged.reshape(groups, rows, width + LANES), ('wide', 'ny'...  16.3 us
    ppermute x6, starting transfers between devices, exchange(): return (lax.ppermute(high, axis, up), lax.ppermute(low, axis, down))  15.5 us
    all_to_all x1, starting transfers between devices, per_device(): lax.all_to_all(merged.reshape(groups, rows, width + LANES), ('wide', 'ny'...  7.93 us
    ppermute x6, starting transfers between devices, flipped(): lax.ppermute(array, axis, [(i, i ^ distance) for i in range(lax.axis_size...  6.67 us
    ppermute x6, waiting for transfers between devices, exchange(): return (lax.ppermute(high, axis, up), lax.ppermute(low, axis, down))  6.51 us
    unnamed x24, local copies, waits for them, and re-layouts  4.12 us
  transfers between devices with their start and end apart: 13, of which 9 were waited for; matrix products, arithmetic and copies ran while one was open for 1% of the time, Pallas kernels for 0%

profile of v1, /device:TPU:0, one launch (start us, length us, event | category | flops | bytes accessed | tf_op | source)
XLA Modules:
  0.0 156.1 jit_solution(12316381398232785391)
XLA Ops:
  0.0 0.8 convert_element_type.4
  0.8 1.9 %broadcast_multiply_fusion.masked = bf16[8,16,16,512]{3,2,1,0:T(8,128)(2,1)S(1)} fusion(bf16[8,16,16,512]{3,2,1,0:T(8,128)(2,1)} %param.12, bf16[8,16,16]{2,1,0:T(8,128)(2,1)S(1)} %convert_element_type.4), kind=kLoop, calls=%fused_computation | loop fusion | flops 1048576 | bytes 4198400 | tf_op jit(solution)/shard_map/mul | solution.py:322
  2.8 0.0 copy-start
  2.8 1.3 collective-permute-start.1
  4.1 5.5 %collective-permute-start = (bf16[16,16,512]{2,1,0:T(8,128)(2,1)S(1)}, bf16[16,16,512]{2,1,0:T(8,128)(2,1)S(1)}, u32[]{:S(2)}, u32[]{:S(2)}) collective-permute-start(bf16[16,16,512]{2,1,0:T(8,128)(2,1)S(1)} %get-tuple-element.12), channel_id=1, source_target_pairs={{0,4},{4,8},{8,12},{12,16},{16,20},{20,24},{24,28},{1,5},{5,9},{9,... | collective-permute-start | bytes 786440 | tf_op jit(solution)/shard_map/ppermute | solution.py:295
  9.7 1.3 collective-permute-start.3
  11.0 3.0 %collective-permute-start.2 = (bf16[8,16,512]{2,1,0:T(8,128)(2,1)S(1)}, bf16[8,16,512]{2,1,0:T(8,128)(2,1)S(1)}, u32[]{:S(2)}, u32[]{:S(2)}) collective-permute-start(bf16[8,16,512]{2,1,0:T(8,128)(2,1)S(1)} %get-tuple-element.10), channel_id=1, source_target_pairs={{0,1},{1,2},{2,3},{4,5},{5,6},{6,7},{8,9},{9,10},{10,11},{12,13},{... | collective-permute-start | bytes 393224 | tf_op jit(solution)/shard_map/ppermute | solution.py:295
  14.0 0.0 collective-permute-done.1.x_hi
  14.0 0.0 copy-start.3
  14.1 5.7 %collective-permute-done.x_lo = bf16[16,16,512]{2,1,0:T(8,128)(2,1)S(1)} collective-permute-done((bf16[16,16,512]{2,1,0:T(8,128)(2,1)S(1)}, bf16[16,16,512]{2,1,0:T(8,128)(2,1)S(1)}, u32[]{:S(2)}, u32[]{:S(2)}) %collective-permute-start) | collective-permute-done | bytes 262176 | tf_op jit(solution)/shard_map/ppermute | solution.py:295
  19.8 1.3 collective-permute-start.5
  21.1 3.0 %collective-permute-start.4 = (bf16[2,16,512]{2,1,0:T(8,128)(2,1)S(1)}, bf16[2,16,512]{2,1,0:T(8,128)(2,1)S(1)}, u32[]{:S(2)}, u32[]{:S(2)}) collective-permute-start(bf16[2,16,512]{2,1,0:T(8,128)(2,1)S(1)} %get-tuple-element.16), channel_id=1, source_target_pairs={{0,1},{1,2},{2,3},{4,5},{5,6},{6,7},{8,9},{9,10},{10,11},{12,13},{... | collective-permute-start | bytes 98312 | tf_op jit(solution)/shard_map/ppermute | solution.py:295
  24.1 0.0 collective-permute-done.3.y_hi
  24.1 0.0 copy-start.6
  24.2 0.0 collective-permute-done.2.y_lo
  24.2 0.0 copy-start.7
  24.2 0.0 collective-permute-done.5.c_hi
  24.2 0.8 collective-permute-done.4.c_lo
  25.0 0.0 copy-done.3
  25.0 0.0 copy-done.6
  25.0 0.6 copy-done.9
  25.6 36.8 %shard_map.118 = (bf16[512,2048]{1,0:T(8,128)(2,1)}, bf16[1024,640]{1,0:T(8,128)(2,1)}) custom-call(bf16[8,16,16,512]{3,2,1,0:T(8,128)(2,1)} %copy-done, bf16[16,16,512]{2,1,0:T(8,128)(2,1)} %copy-done.4, bf16[16,16,512]{2,1,0:T(8,128)(2,1)} %copy-done.3, bf16[8,16,512]{2,1,0:T(8,128)(2,1)} %copy-done.7, bf16[8,16,512]{2,1,0:T(8,128)(2,1)} %copy-done.6, ...), custom_call_target="tpu_custom_call" | custom-call | tf_op jit(solution)/shard_map/pallas_call | solution.py:281
  62.4 2.3 %dynamic-slice_bitcast_fusion = (bf16[512,640]{1,0:T(8,128)(2,1)S(1)}, bf16[512,640]{1,0:T(8,128)(2,1)}) fusion(bf16[2,512,640]{2,1,0:T(8,128)(2,1)} %bitcast.26, s32[]{:T(128)S(6)} %select_n.11, s32[]{:T(128)S(6)} %select_n.10), kind=kLoop, calls=%fused_computation.1 | loop fusion | bytes 2621448 | tf_op jit(solution)/shard_map/jit(dynamic_index_in_dim)/squeeze | solution.py:360
  64.7 1.4 collective-permute-start.6
  66.1 1.7 %collective-permute-done.6.right = bf16[512,640]{1,0:T(8,128)(2,1)S(1)} collective-permute-done((bf16[512,640]{1,0:T(8,128)(2,1)S(1)}, bf16[512,640]{1,0:T(8,128)(2,1)S(1)}, u32[]{:S(2)}, u32[]{:S(2)}) %collective-permute-start.6) | collective-permute-done | bytes 655392 | tf_op jit(solution)/shard_map/ppermute | solution.py:299
  67.8 0.8 copy-done.5
  68.6 4.9 %shard_map.119 = bf16[512,640]{1,0:T(8,128)(2,1)} custom-call(bf16[512,640]{1,0:T(8,128)(2,1)} %get-tuple-element.14.left, bf16[512,640]{1,0:T(8,128)(2,1)} %copy-done.5), custom_call_target="tpu_custom_call" | custom-call | tf_op jit(solution)/shard_map/pallas_call | solution.py:281
  73.5 7.9 %all-to-all-start = ((bf16[16,32,640]{2,1,0:T(8,128)(2,1)}), bf16[16,32,640]{2,1,0:T(8,128)(2,1)S(1)}, u32[]{:S(2)}, u32[]{:S(2)}) async-start(bf16[16,32,640]{2,1,0:T(8,128)(2,1)} %bitcast.25), calls=%async_computation | async-start | bytes 1310720 | tf_op jit(solution)/shard_map/all_to_all | solution.py:365
  81.5 1.4 constant_dynamic-slice_fusion.own
  82.8 16.3 %all-to-all-done.parts = bf16[16,32,640]{2,1,0:T(8,128)(2,1)S(1)} async-done(((bf16[16,32,640]{2,1,0:T(8,128)(2,1)}), bf16[16,32,640]{2,1,0:T(8,128)(2,1)S(1)}, u32[]{:S(2)}, u32[]{:S(2)}) %all-to-all-start) | async-done | bytes 655392 | tf_op jit(solution)/shard_map/all_to_all | solution.py:365
  99.1 0.8 copy-done.1
  100.0 3.1 %shard_map.120 = bf16[32,512]{1,0:T(8,128)(2,1)} custom-call(bf16[16,32,640]{2,1,0:T(8,128)(2,1)} %copy-done.1, bf16[32,512]{1,0:T(8,128)(2,1)} %constant_dynamic-slice_fusion.own, bf16[512,512]{1,0:T(8,128)(2,1)} %w_out1.1), custom_call_target="tpu_custom_call" | custom-call | tf_op jit(solution)/shard_map/pallas_call | solution.py:281
  103.0 1.3 collective-permute-start.7
  104.3 3.7 %collective-permute-done.7 = bf16[32,512]{1,0:T(8,128)(2,1)S(1)} collective-permute-done((bf16[32,512]{1,0:T(8,128)(2,1)}, bf16[32,512]{1,0:T(8,128)(2,1)S(1)}, u32[]{:S(2)}, u32[]{:S(2)}) %collective-permute-start.7) | collective-permute-done | bytes 32800 | tf_op jit(solution)/shard_map/ppermute | solution.py:299
  108.1 0.8 pad_maximum_fusion.2
  108.8 1.8 %collective-permute-start.8 = (bf16[64,512]{1,0:T(8,128)(2,1)S(1)}, bf16[64,512]{1,0:T(8,128)(2,1)S(1)}, u32[]{:S(2)}, u32[]{:S(2)}) collective-permute-start(bf16[64,512]{1,0:T(8,128)(2,1)S(1)} %pad_maximum_fusion.2), channel_id=1, source_target_pairs={{0,8},{4,12},{8,0},{12,4},{16,24},{20,28},{24,16},{28,20},{1,9},{5... | collective-permute-start | bytes 196616 | tf_op jit(solution)/shard_map/ppermute | solution.py:299
  110.6 2.5 %collective-permute-done.8 = bf16[64,512]{1,0:T(8,128)(2,1)S(1)} collective-permute-done((bf16[64,512]{1,0:T(8,128)(2,1)S(1)}, bf16[64,512]{1,0:T(8,128)(2,1)S(1)}, u32[]{:S(2)}, u32[]{:S(2)}) %collective-permute-start.8) | collective-permute-done | bytes 65568 | tf_op jit(solution)/shard_map/ppermute | solution.py:299
  113.1 0.8 pad_maximum_fusion.1
  113.9 1.5 collective-permute-start.9
  115.4 0.8 constant_dynamic-update-slice_fusion.4
  116.1 2.8 %collective-permute-done.9 = bf16[128,512]{1,0:T(8,128)(2,1)S(1)} collective-permute-done((bf16[128,512]{1,0:T(8,128)(2,1)S(1)}, bf16[128,512]{1,0:T(8,128)(2,1)S(1)}, u32[]{:S(2)}, u32[]{:S(2)}) %collective-permute-start.9) | collective-permute-done | bytes 131104 | tf_op jit(solution)/shard_map/ppermute | solution.py:299
  118.9 0.8 pad_maximum_fusion
  119.7 0.6 collective-permute-start.10
  120.3 5.8 %collective-permute-done.10 = bf16[256,512]{1,0:T(8,128)(2,1)S(1)} collective-permute-done((bf16[256,512]{1,0:T(8,128)(2,1)S(1)}, bf16[256,512]{1,0:T(8,128)(2,1)S(1)}, u32[]{:S(2)}, u32[]{:S(2)}) %collective-permute-start.10) | collective-permute-done | bytes 262176 | tf_op jit(solution)/shard_map/ppermute | solution.py:299
  126.1 0.1 collective-permute-start.11
  126.2 1.9 %collective-permute-done.11 = bf16[512,512]{1,0:T(8,128)(2,1)S(1)} collective-permute-done((bf16[512,512]{1,0:T(8,128)(2,1)S(1)}, bf16[512,512]{1,0:T(8,128)(2,1)S(1)}, u32[]{:S(2)}, u32[]{:S(2)}) %collective-permute-start.11) | collective-permute-done | bytes 524320 | tf_op jit(solution)/shard_map/ppermute | solution.py:299
  128.2 1.0 copy-done.2
  129.2 26.9 %shard_map.121 = f32[2048,512]{1,0:T(8,128)} custom-call(bf16[1024,512]{1,0:T(8,128)(2,1)} %copy-done.2, bf16[512,2048]{1,0:T(8,128)(2,1)} %get-tuple-element.8.query2_t, bf16[2048,512]{1,0:T(8,128)(2,1)} %bitcast.24, bf16[512,512]{1,0:T(8,128)(2,1)} %w_key2.1, bf16[512,512]{1,0:T(8,128)(2,1)} %w_value2.1, bf16[512,512]{1,0:T(8,128)(2,1)} %w_out2.1), custom_call_target="tpu_custom_call" | custom-call | tf_op jit(solution)/shard_map/pallas_call | solution.py:281
  (18 shorter events, 0.2 us)
Async XLA Ops:
  2.8 22.2 %copy-start = (bf16[8,16,16,512]{3,2,1,0:T(8,128)(2,1)}, bf16[8,16,16,512]{3,2,1,0:T(8,128)(2,1)S(1)}, u32[]{:S(2)}) copy-start(bf16[8,16,16,512]{3,2,1,0:T(8,128)(2,1)S(1)} %broadcast_multiply_fusion.masked) | copy-start | bytes 6291460
  2.8 11.2 %collective-permute-start.1 = (bf16[16,16,512]{2,1,0:T(8,128)(2,1)S(1)}, bf16[16,16,512]{2,1,0:T(8,128)(2,1)S(1)}, u32[]{:S(2)}, u32[]{:S(2)}) collective-permute-start(bf16[16,16,512]{2,1,0:T(8,128)(2,1)S(1)} %get-tuple-element.11), channel_id=1, source_target_pairs={{4,0},{8,4},{12,8},{16,12},{20,16},{24,20},{28,24},{5,1},{9,5},{13... | collective-permute-start | bytes 786440 | tf_op jit(solution)/shard_map/ppermute | solution.py:295
  4.1 15.6 %collective-permute-start = (bf16[16,16,512]{2,1,0:T(8,128)(2,1)S(1)}, bf16[16,16,512]{2,1,0:T(8,128)(2,1)S(1)}, u32[]{:S(2)}, u32[]{:S(2)}) collective-permute-start(bf16[16,16,512]{2,1,0:T(8,128)(2,1)S(1)} %get-tuple-element.12), channel_id=1, source_target_pairs={{0,4},{4,8},{8,12},{12,16},{16,20},{20,24},{24,28},{1,5},{5,9},{9,... | collective-permute-start | bytes 786440 | tf_op jit(solution)/shard_map/ppermute | solution.py:295
  9.7 14.5 %collective-permute-start.3 = (bf16[8,16,512]{2,1,0:T(8,128)(2,1)S(1)}, bf16[8,16,512]{2,1,0:T(8,128)(2,1)S(1)}, u32[]{:S(2)}, u32[]{:S(2)}) collective-permute-start(bf16[8,16,512]{2,1,0:T(8,128)(2,1)S(1)} %get-tuple-element.9), channel_id=1, source_target_pairs={{1,0},{2,1},{3,2},{5,4},{6,5},{7,6},{9,8},{10,9},{11,10},{13,12},{... | collective-permute-start | bytes 393224 | tf_op jit(solution)/shard_map/ppermute | solution.py:295
  11.0 13.2 %collective-permute-start.2 = (bf16[8,16,512]{2,1,0:T(8,128)(2,1)S(1)}, bf16[8,16,512]{2,1,0:T(8,128)(2,1)S(1)}, u32[]{:S(2)}, u32[]{:S(2)}) collective-permute-start(bf16[8,16,512]{2,1,0:T(8,128)(2,1)S(1)} %get-tuple-element.10), channel_id=1, source_target_pairs={{0,1},{1,2},{2,3},{4,5},{5,6},{6,7},{8,9},{9,10},{10,11},{12,13},{... | collective-permute-start | bytes 393224 | tf_op jit(solution)/shard_map/ppermute | solution.py:295
  14.0 10.9 %copy-start.3 = (bf16[16,16,512]{2,1,0:T(8,128)(2,1)}, bf16[16,16,512]{2,1,0:T(8,128)(2,1)S(1)}, u32[]{:S(2)}) copy-start(bf16[16,16,512]{2,1,0:T(8,128)(2,1)S(1)} %collective-permute-done.1.x_hi) | copy-start | bytes 786436
  19.8 5.2 %copy-start.4 = (bf16[16,16,512]{2,1,0:T(8,128)(2,1)}, bf16[16,16,512]{2,1,0:T(8,128)(2,1)S(1)}, u32[]{:S(2)}) copy-start(bf16[16,16,512]{2,1,0:T(8,128)(2,1)S(1)} %collective-permute-done.x_lo) | copy-start | bytes 786436
  19.8 4.4 %collective-permute-start.5 = (bf16[2,16,512]{2,1,0:T(8,128)(2,1)S(1)}, bf16[2,16,512]{2,1,0:T(8,128)(2,1)S(1)}, u32[]{:S(2)}, u32[]{:S(2)}) collective-permute-start(bf16[2,16,512]{2,1,0:T(8,128)(2,1)S(1)} %get-tuple-element.15), channel_id=1, source_target_pairs={{1,0},{2,1},{3,2},{5,4},{6,5},{7,6},{9,8},{10,9},{11,10},{13,12},{... | collective-permute-start | bytes 98312 | tf_op jit(solution)/shard_map/ppermute | solution.py:295
  21.1 3.9 %collective-permute-start.4 = (bf16[2,16,512]{2,1,0:T(8,128)(2,1)S(1)}, bf16[2,16,512]{2,1,0:T(8,128)(2,1)S(1)}, u32[]{:S(2)}, u32[]{:S(2)}) collective-permute-start(bf16[2,16,512]{2,1,0:T(8,128)(2,1)S(1)} %get-tuple-element.16), channel_id=1, source_target_pairs={{0,1},{1,2},{2,3},{4,5},{5,6},{6,7},{8,9},{9,10},{10,11},{12,13},{... | collective-permute-start | bytes 98312 | tf_op jit(solution)/shard_map/ppermute | solution.py:295
  24.1 0.8 copy-start.6
  24.2 0.8 copy-start.7
  24.2 0.8 copy-start.8
  25.0 0.6 copy-start.9
  64.7 3.1 %collective-permute-start.6 = (bf16[512,640]{1,0:T(8,128)(2,1)S(1)}, bf16[512,640]{1,0:T(8,128)(2,1)S(1)}, u32[]{:S(2)}, u32[]{:S(2)}) collective-permute-start(bf16[512,640]{1,0:T(8,128)(2,1)S(1)} %get-tuple-element.13), channel_id=1, source_target_pairs={{0,1},{1,0},{2,3},{3,2},{4,5},{5,4},{6,7},{7,6},{8,9},{9,8},{10,11... | collective-permute-start | bytes 1966088 | tf_op jit(solution)/shard_map/ppermute | solution.py:299
  67.8 0.8 copy-start.5
  73.5 25.6 %all-to-all-start = ((bf16[16,32,640]{2,1,0:T(8,128)(2,1)}), bf16[16,32,640]{2,1,0:T(8,128)(2,1)S(1)}, u32[]{:S(2)}, u32[]{:S(2)}) async-start(bf16[16,32,640]{2,1,0:T(8,128)(2,1)} %bitcast.25), calls=%async_computation | async-start | bytes 1310720 | tf_op jit(solution)/shard_map/all_to_all | solution.py:365
  99.1 0.8 copy-start.1
  103.0 5.0 %collective-permute-start.7 = (bf16[32,512]{1,0:T(8,128)(2,1)}, bf16[32,512]{1,0:T(8,128)(2,1)S(1)}, u32[]{:S(2)}, u32[]{:S(2)}) collective-permute-start(bf16[32,512]{1,0:T(8,128)(2,1)} %shard_map.120), channel_id=1, source_target_pairs={{0,16},{4,20},{8,24},{12,28},{16,0},{20,4},{24,8},{28,12},{1,17},{... | collective-permute-start | bytes 98312 | tf_op jit(solution)/shard_map/ppermute | solution.py:299
  108.8 4.3 %collective-permute-start.8 = (bf16[64,512]{1,0:T(8,128)(2,1)S(1)}, bf16[64,512]{1,0:T(8,128)(2,1)S(1)}, u32[]{:S(2)}, u32[]{:S(2)}) collective-permute-start(bf16[64,512]{1,0:T(8,128)(2,1)S(1)} %pad_maximum_fusion.2), channel_id=1, source_target_pairs={{0,8},{4,12},{8,0},{12,4},{16,24},{20,28},{24,16},{28,20},{1,9},{5... | collective-permute-start | bytes 196616 | tf_op jit(solution)/shard_map/ppermute | solution.py:299
  113.9 5.0 %collective-permute-start.9 = (bf16[128,512]{1,0:T(8,128)(2,1)S(1)}, bf16[128,512]{1,0:T(8,128)(2,1)S(1)}, u32[]{:S(2)}, u32[]{:S(2)}) collective-permute-start(bf16[128,512]{1,0:T(8,128)(2,1)S(1)} %pad_maximum_fusion.1), channel_id=1, source_target_pairs={{0,4},{4,0},{8,12},{12,8},{16,20},{20,16},{24,28},{28,24},{1,5},{5... | collective-permute-start | bytes 393224 | tf_op jit(solution)/shard_map/ppermute | solution.py:299
  119.7 6.4 %collective-permute-start.10 = (bf16[256,512]{1,0:T(8,128)(2,1)S(1)}, bf16[256,512]{1,0:T(8,128)(2,1)S(1)}, u32[]{:S(2)}, u32[]{:S(2)}) collective-permute-start(bf16[256,512]{1,0:T(8,128)(2,1)S(1)} %pad_maximum_fusion), channel_id=1, source_target_pairs={{0,2},{2,0},{1,3},{3,1},{4,6},{6,4},{5,7},{7,5},{8,10},{10,8},{9,1... | collective-permute-start | bytes 786440 | tf_op jit(solution)/shard_map/ppermute | solution.py:299
  126.1 2.0 %collective-permute-start.11 = (bf16[512,512]{1,0:T(8,128)(2,1)S(1)}, bf16[512,512]{1,0:T(8,128)(2,1)S(1)}, u32[]{:S(2)}, u32[]{:S(2)}) collective-permute-start(bf16[512,512]{1,0:T(8,128)(2,1)S(1)} %get-tuple-element.17), channel_id=1, source_target_pairs={{0,1},{1,0},{2,3},{3,2},{4,5},{5,4},{6,7},{7,6},{8,9},{9,8},{10,11... | collective-permute-start | bytes 1572872 | tf_op jit(solution)/shard_map/ppermute | solution.py:299
  128.2 1.0 copy-start.2

commit v2 on v1

v2 whole, which is shorter than its diff:
```python
import functools
import math

import jax
import jax.numpy as jnp
from jax import lax
from jax.experimental import pallas as pl
from jax.experimental.pallas import tpu as pltpu
from jax.sharding import Mesh, PartitionSpec as P

HEADS = 8
LANES = 128
ONES_ROWS = 16
STAT_ROWS = 48
MIB = 1 << 20
F32 = jnp.float32
BF16 = jnp.bfloat16


def dot(left, right, contract=((1,), (0,))):
    return lax.dot_general(left, right, (contract, ((), ())), preferred_element_type=F32)


def fill_row(padded, row, plane, left, right):
    size_y = plane.shape[0]
    padded[row, 1 : size_y + 1] = plane.astype(F32)
    padded[row, 0] = left.astype(F32)
    padded[row, size_y + 1] = right.astype(F32)


def stencil_plane(base, padded, conv, mixed, start):
    size_y, size_z, width = padded.shape[1] - 2, padded.shape[2], padded.shape[3]
    row_of = lax.broadcasted_iota(jnp.int32, (size_z, LANES), 0)
    for tile in range(width // LANES):
        lanes = slice(tile * LANES, (tile + 1) * LANES)
        taps = [jnp.broadcast_to(conv[n : n + 1, lanes], (size_z, LANES)) for n in range(27)]
        for j in range(size_y):
            sums = [None] * 3
            for a in range(3):
                for b in range(3):
                    window = padded[base + a, j + b, :, lanes]
                    for c in range(3):
                        term = window * taps[9 * a + 3 * b + c]
                        sums[c] = term if sums[c] is None else sums[c] + term
            below = jnp.where(row_of == 0, 0.0, pltpu.roll(sums[0], 1, 0))
            above = jnp.where(row_of == size_z - 1, 0.0, pltpu.roll(sums[2], size_z - 1, 0))
            total = padded[base + 1, j + 1, :, lanes] + sums[1] + below + above
            mixed[pl.ds(pl.multiple_of(start + j * size_z, size_z), size_z), lanes] = total.astype(BF16)


def project_plane(start, cells, mixed, w_key1, w_value1, keys, values_t):
    head_size = mixed.shape[1] // HEADS
    rows = pl.ds(pl.multiple_of(start, cells), cells)
    block = mixed[rows, :]
    keys[rows, :] = dot(block, w_key1[...]).astype(BF16)
    value_t = dot(w_value1[...], block, ((0,), (1,))).astype(BF16)
    values_t[:, :head_size, rows] = value_t.reshape(HEADS, head_size, cells)


def inner_kernel(
    masked, y_lo, y_hi, conv, latents, w_query1, w_key1, w_value1, mixed, keys, values_t, query1_t, padded
):
    size_x, size_y, size_z, width = masked.shape
    head_size = width // HEADS
    cells = size_y * size_z

    def fill(i, carry):
        fill_row(padded, i, masked[i], y_lo[i], y_hi[i])
        return carry

    lax.fori_loop(0, size_x, fill, 0)
    query1_t[...] = dot(w_query1[...], latents[...], ((0,), (1,))).astype(BF16)
    values_t[:, head_size:, :] = jnp.ones_like(values_t[:, head_size:, :])
    stencil_plane(0, padded, conv, mixed, 0)

    def plane(i, carry):
        project_plane((i - 1) * cells, cells, mixed, w_key1, w_value1, keys, values_t)
        stencil_plane(i, padded, conv, mixed, i * cells)
        return carry

    lax.fori_loop(1, size_x - 2, plane, 0)
    project_plane((size_x - 3) * cells, cells, mixed, w_key1, w_value1, keys, values_t)


def score_weights(query_t, head_in_pair, head_size):
    factor = 1.8 / math.sqrt(head_size) * math.log2(math.e)
    scaled = query_t.astype(F32) * factor
    high = scaled.astype(BF16)
    low = (scaled - high.astype(F32)).astype(BF16)
    blank = jnp.zeros_like(high)
    if head_in_pair == 0:
        return jnp.concatenate([high, blank, low, blank], axis=0)
    return jnp.concatenate([blank, high, blank, low], axis=0)


def attention_scores(pair, head_in_pair, block, width, chunk, keys, query_t, scores):
    head_size = LANES // 2
    start = pl.multiple_of(pair * LANES, LANES) + head_in_pair * head_size
    columns = pl.ds(pl.multiple_of(block * width, width), width)
    right = score_weights(query_t[pl.ds(start, head_size), columns], head_in_pair, head_size)
    top = None
    base = 0
    for piece in keys:
        for part in range(piece.shape[0] // chunk):
            left = piece[pl.ds(part * chunk, chunk), pl.ds(pl.multiple_of(pair * LANES, LANES), LANES)]
            found = dot(jnp.concatenate([left, left], axis=1), right)
            scores[head_in_pair, pl.ds(base, chunk), :] = found
            base += chunk
            largest = jnp.max(found.reshape(chunk // 8, 8, width), axis=0)
            top = largest if top is None else jnp.maximum(top, largest)
    return jnp.max(top, axis=0, keepdims=True)


def attention_sums(head, head_in_pair, chunk, values_t, scores, top):
    total = None
    base = 0
    for piece in values_t:
        for part in range(piece.shape[2] // chunk):
            weights = jnp.exp2(scores[head_in_pair, pl.ds(base, chunk), :] - top).astype(BF16)
            base += chunk
            found = dot(piece[head, :, pl.ds(part * chunk, chunk)], weights)
            total = found if total is None else total + found
    return total


def attention_loop(keys, query_t, values_t, scores, chunk, finish):
    width = scores.shape[2]
    blocks = query_t.shape[1] // width
    pairs = query_t.shape[0] // LANES
    steps = pairs * blocks

    def first(t):
        return attention_scores(t % pairs, 0, t // pairs, width, chunk, keys, query_t, scores)

    def step(t, top_even):
        pair, block = t % pairs, t // pairs
        top_odd = attention_scores(pair, 1, block, width, chunk, keys, query_t, scores)
        even = attention_sums(2 * pair, 0, chunk, values_t, scores, top_even)
        following = first(jnp.minimum(t + 1, steps - 1))
        odd = attention_sums(2 * pair + 1, 1, chunk, values_t, scores, top_odd)
        finish(pair, block, (even, odd), (top_even, top_odd))
        return following

    lax.fori_loop(0, steps, step, first(0))


def split3(value):
    high = value.astype(BF16).astype(F32)
    rest = value - high
    middle = rest.astype(BF16).astype(F32)
    return high, middle, rest - middle


def stat_rows(top, total):
    return split3(top) + split3(total)[:2]


def read_kernel(
    position,
    masked,
    x_lo,
    x_hi,
    y_lo,
    y_hi,
    c_lo,
    c_hi,
    conv,
    w_key1,
    w_value1,
    inner_keys,
    inner_values_t,
    query1_t,
    mixed,
    kept,
    given,
    padded,
    keys,
    values_t,
    scores,
    stats,
):
    size_x, size_y, size_z, width = masked.shape
    head_size = width // HEADS
    cells = size_y * size_z
    last = size_x - 1
    fill_row(padded, 0, x_lo[...], c_lo[0], c_lo[1])
    fill_row(padded, 1, masked[0], y_lo[0], y_hi[0])
    fill_row(padded, 2, masked[1], y_lo[1], y_hi[1])
    fill_row(padded, 3, masked[last - 1], y_lo[last - 1], y_hi[last - 1])
    fill_row(padded, 4, masked[last], y_lo[last], y_hi[last])
    fill_row(padded, 5, x_hi[...], c_hi[0], c_hi[1])
    values_t[:, head_size:, :] = jnp.ones_like(values_t[:, head_size:, :])
    stats[...] = jnp.zeros_like(stats)

    def plane(i, carry):
        stencil_plane(3 * i, padded, conv, mixed, i * cells)
        project_plane(i * cells, cells, mixed, w_key1, w_value1, keys, values_t)
        return carry

    lax.fori_loop(0, 2, plane, 0)

    core = position[0]
    per_half = kept.shape[0]
    span = scores.shape[2]
    ratio = span // LANES

    def finish(pair, block, sums, tops):
        both = jnp.concatenate([part[:head_size] for part in sums], axis=0).astype(BF16)
        rows = pl.ds(pl.multiple_of(pair * LANES, LANES), LANES)
        first = block * ratio
        side = first // per_half

        def write(target):
            for k in range(ratio):
                target[first - side * per_half + k, rows, :] = both[:, k * LANES : (k + 1) * LANES]

        pl.when(side == core)(lambda: write(kept))
        pl.when(side != core)(lambda: write(given))
        columns = pl.ds(pl.multiple_of(block * span, span), span)
        for head_in_pair in range(2):
            values = stat_rows(tops[head_in_pair], sums[head_in_pair][head_size : head_size + 1])
            for slot, row in enumerate(values):
                stats[pl.ds(slot * HEADS + 2 * pair + head_in_pair, 1), columns] = row

    attention_loop([inner_keys, keys], query1_t, [inner_values_t, values_t], scores, 256, finish)
    for target, side in ((kept, core), (given, 1 - core)):
        for k in range(per_half):
            columns = pl.ds(pl.multiple_of((side * per_half + k) * LANES, LANES), LANES)
            target[k, width:, :] = stats[:, columns].astype(BF16)


def merge_blocks(blocks):
    width = blocks[0].shape[0] - STAT_ROWS
    head_size = width // HEADS
    slots = [[block[width + n * HEADS : width + (n + 1) * HEADS] for n in range(5)] for block in blocks]
    tops = [s[0] + s[1] + s[2] for s in slots]
    top = functools.reduce(jnp.maximum, tops)
    factors = [jnp.exp2(t - top) for t in tops]
    total = sum(f * (s[3] + s[4]) for f, s in zip(factors, slots))
    sums = []
    for head in range(HEADS):
        rows = slice(head * head_size, (head + 1) * head_size)
        sums.append(sum(block[rows] * f[head : head + 1] for block, f in zip(blocks, factors)))
    return sums, top, total


def all_stats(top, total, size):
    rows = list(stat_rows(top, total))
    filler = jnp.zeros((size - len(rows) * HEADS,) + top.shape[1:], F32)
    return jnp.concatenate(rows + [filler], axis=0)


def merge_pair_kernel(position, kept, taken, *outs):
    for distance, out in enumerate(outs):
        index = position[1] ^ distance
        sums, top, total = merge_blocks([ref[index].astype(F32) for ref in (kept, taken)])
        sums.append(all_stats(top, total, STAT_ROWS))
        out[...] = jnp.concatenate(sums, axis=0).astype(BF16)


def merge_group_kernel(count, position, *refs):
    blocks, outs, turned = refs[:count], refs[count:-1], refs[-1]
    sums, top, total = merge_blocks([ref[...].astype(F32) for ref in blocks])
    width = turned.shape[1] - LANES
    sums = jnp.concatenate(sums, axis=0)
    for k in range(width // LANES):
        lanes = slice(k * LANES, (k + 1) * LANES)
        turned[:, lanes] = sums[lanes].T
    turned[:, width:] = all_stats(top, total, LANES).T
    rows = outs[0].shape[0]
    for distance, out in enumerate(outs):
        index = position[2] ^ distance
        out[...] = turned[pl.ds(pl.multiple_of(index * rows, rows), rows), :].astype(BF16)


def unpack_stats(tile):
    parts = [tile] + [pltpu.roll(tile, LANES - slot * HEADS, 1) for slot in range(1, 5)]
    return parts[0] + parts[1] + parts[2], parts[3] + parts[4]


def spread(per_head, pair):
    rows = per_head.shape[0]
    lane = lax.broadcasted_iota(jnp.int32, (rows, LANES), 1)
    left = jnp.broadcast_to(per_head[:, 2 * pair : 2 * pair + 1], (rows, LANES))
    right = jnp.broadcast_to(per_head[:, 2 * pair + 1 : 2 * pair + 2], (rows, LANES))
    return jnp.where(lane < LANES // 2, left, right)


def update_kernel(own, w_out1, *refs):
    parts, out = refs[:-1], refs[-1]
    width = own.shape[1]
    stats = [unpack_stats(part[:, width:].astype(F32)) for part in parts]
    top = functools.reduce(jnp.maximum, [t for t, _ in stats])
    factors = [jnp.exp2(t - top) for t, _ in stats]
    total = sum(f * l for f, (_, l) in zip(factors, stats))
    read = []
    for pair in range(width // LANES):
        lanes = slice(pair * LANES, (pair + 1) * LANES)
        value = sum(part[:, lanes].astype(F32) * spread(f, pair) for part, f in zip(parts, factors))
        read.append(value / spread(total, pair))
    read = jnp.concatenate(read, axis=1).astype(BF16)
    out[...] = (own[...].astype(F32) + dot(read, w_out1[...])).astype(BF16)


def join_kernel(*refs):
    parts, out = refs[:-1], refs[-1]
    rows = parts[0].shape[0]
    for k, part in enumerate(parts):
        out[k * rows : (k + 1) * rows, :] = part[...]


def join(parts, name):
    rows, width = parts[0].shape
    out = jax.ShapeDtypeStruct((len(parts) * rows, width), parts[0].dtype)
    return call(join_kernel, out, [], parts, 8, 1e6, name)


def query_kernel(inner, outer, w_query2, query2_t):
    cells = outer.shape[0] // 2
    planes = inner.shape[0] // cells

    def put(block, plane):
        columns = pl.ds(pl.multiple_of(plane * cells, cells), cells)
        query2_t[:, columns] = dot(w_query2[...], block, ((0,), (1,))).astype(BF16)

    put(outer[:cells, :], 0)
    put(outer[cells:, :], planes + 1)

    def plane(i, carry):
        put(inner[pl.ds(pl.multiple_of(i * cells, cells), cells), :], i + 1)
        return carry

    lax.fori_loop(0, planes, plane, 0)


def write_kernel(
    own_state, other_state, query2_t, masked, w_key2, w_value2, w_out2, out, keys, values_t, scores, read_t
):
    half, width = own_state.shape
    head_size = width // HEADS
    values_t[:, head_size:, :] = jnp.ones_like(values_t[:, head_size:, :])
    for side, state in enumerate((own_state, other_state)):
        rows = slice(side * half, (side + 1) * half)
        keys[rows, :] = dot(state[...], w_key2[...]).astype(BF16)
        value_t = dot(w_value2[...], state[...], ((0,), (1,))).astype(BF16)
        values_t[:, :head_size, rows] = value_t.reshape(HEADS, head_size, half)
    span = scores.shape[2]

    def finish(pair, block, sums, tops):
        columns = pl.ds(pl.multiple_of(block * span, span), span)
        both = [part[:head_size] / part[head_size : head_size + 1] for part in sums]
        rows = pl.ds(pl.multiple_of(pair * LANES, LANES), LANES)
        read_t[rows, columns] = jnp.concatenate(both, axis=0).astype(BF16)

    attention_loop([keys], query2_t, [values_t], scores, 256, finish)

    def emit(r, carry):
        rows = pl.ds(pl.multiple_of(r * span, span), span)
        change = dot(read_t[:, rows], w_out2[...], ((0,), (0,)))
        out[rows, :] = masked[rows, :].astype(F32) + change
        return carry

    lax.fori_loop(0, out.shape[0] // span, emit, 0)


def call(kernel, shapes, scratch, operands, limit, flops, name, position=None):
    vmem = pl.BlockSpec(memory_space=pltpu.VMEM)
    many = isinstance(shapes, (list, tuple))
    in_specs = [vmem] * len(operands)
    if position is not None:
        in_specs = [pl.BlockSpec(memory_space=pltpu.SMEM)] + in_specs
        operands = [position] + list(operands)
    moved = sum(x.size * x.dtype.itemsize for x in operands)
    result = pl.pallas_call(
        kernel,
        out_shape=shapes,
        in_specs=in_specs,
        out_specs=[vmem] * len(shapes) if many else vmem,
        scratch_shapes=scratch,
        compiler_params=pltpu.CompilerParams(vmem_limit_bytes=limit * MIB),
        cost_estimate=pl.CostEstimate(flops=int(flops), bytes_accessed=moved, transcendentals=0),
        name=name,
    )(*operands)
    return list(result) if many else result


def exchange(low, high, axis):
    count = lax.axis_size(axis)
    up = [(i, i + 1) for i in range(count - 1)]
    down = [(i + 1, i) for i in range(count - 1)]
    return lax.ppermute(high, axis, up), lax.ppermute(low, axis, down)


def flipped(array, axis, distance):
    return lax.ppermute(array, axis, [(i, i ^ distance) for i in range(lax.axis_size(axis))])


def per_device(
    flow_field,
    fluid_mask,
    conv_weight,
    latents,
    w_query1,
    w_key1,
    w_value1,
    w_out1,
    w_query2,
    w_key2,
    w_value2,
    w_out2,
):
    size_x, size_y, size_z, width = flow_field.shape
    head_size = width // HEADS
    plane_cells = size_y * size_z
    inner_cells, outer_cells = (size_x - 2) * plane_cells, 2 * plane_cells
    cells = inner_cells + outer_cells
    latent_count = latents.shape[0]
    wide, narrow, group = ("wz", "wx"), ("ny", "nc"), ("wx", "ny")
    group_size = lax.axis_size(group)
    far = lax.axis_size("wz")
    core, member, layer = lax.axis_index("nc"), lax.axis_index(group), lax.axis_index("wz")
    position = jnp.stack([core, member, layer]).astype(jnp.int32)
    block_size = latent_count // (2 * group_size)
    rows = block_size // far
    shape = jax.ShapeDtypeStruct
    step = 1e9

    masked = flow_field * fluid_mask[:, :, :, None].astype(BF16)
    y_lo, y_hi = exchange(masked[:, 0], masked[:, -1], narrow)
    x_lo, x_hi = exchange(masked[0], masked[-1], wide)
    sides = jnp.stack([y_lo, y_hi], axis=1)
    c_lo, c_hi = exchange(sides[0], sides[-1], wide)

    inner_mixed, inner_keys, inner_values_t, query1_t = call(
        inner_kernel,
        [
            shape((inner_cells, width), BF16),
            shape((inner_cells, width), BF16),
            shape((HEADS, head_size + ONES_ROWS, inner_cells), BF16),
            shape((width, latent_count), BF16),
        ],
        [pltpu.VMEM((size_x, size_y + 2, size_z, width), F32)],
        [masked, y_lo, y_hi, conv_weight, latents, w_query1, w_key1, w_value1],
        28,
        10 * step,
        "inner",
    )
    outer_mixed, kept, given = call(
        read_kernel,
        [shape((outer_cells, width), BF16)] + [shape((group_size, width + STAT_ROWS, LANES), BF16)] * 2,
        [
            pltpu.VMEM((6, size_y + 2, size_z, width), F32),
            pltpu.VMEM((outer_cells, width), BF16),
            pltpu.VMEM((HEADS, head_size + ONES_ROWS, outer_cells), BF16),
            pltpu.VMEM((2, cells, 256), F32),
            pltpu.VMEM((STAT_ROWS, latent_count), F32),
        ],
        [
            masked,
            x_lo,
            x_hi,
            y_lo,
            y_hi,
            c_lo,
            c_hi,
            conv_weight,
            w_key1,
            w_value1,
            inner_keys,
            inner_values_t,
            query1_t,
        ],
        32,
        20 * step,
        "read",
        position,
    )
    taken = flipped(given, "nc", 1)
    block = shape((width + STAT_ROWS, LANES), BF16)
    blocks = call(merge_pair_kernel, [block] * group_size, [], [kept, taken], 16, step, "merge_pair", position)
    blocks = blocks[:1] + [flipped(blocks[d], group, d) for d in range(1, group_size)]
    parts = call(
        functools.partial(merge_group_kernel, group_size),
        [shape((rows, width + LANES), BF16)] * far,
        [pltpu.VMEM((block_size, width + LANES), F32)],
        blocks,
        16,
        step,
        "merge_group",
        position,
    )
    parts = parts[:1] + [flipped(parts[d], "wz", d) for d in range(1, far)]
    query2_t = call(
        query_kernel,
        shape((width, cells), BF16),
        [],
        [inner_mixed, outer_mixed, w_query2],
        16,
        2 * step,
        "query",
    )
    start = ((core * group_size + member) * far + layer) * rows
    own = lax.dynamic_slice_in_dim(latents, start, rows, 0)
    state = call(update_kernel, shape((rows, width), BF16), [], [own, w_out1] + parts, 16, step, "update")
    state = join([state] + [flipped(state, "wz", d) for d in range(1, far)], "join_far")
    state = join([state] + [flipped(state, group, d) for d in range(1, group_size)], "join_group")
    other = flipped(state, "nc", 1)

    result = call(
        write_kernel,
        shape((cells, width), F32),
        [
            pltpu.VMEM((latent_count, width), BF16),
            pltpu.VMEM((HEADS, head_size + ONES_ROWS, latent_count), BF16),
            pltpu.VMEM((2, latent_count, 512), F32),
            pltpu.VMEM((width, cells), BF16),
        ],
        [state, other, query2_t, masked.reshape(cells, width), w_key2, w_value2, w_out2],
        32,
        20 * step,
        "write",
    )
    return result.reshape(size_x, size_y, size_z, width)


def solution(mesh):
    wide, narrow = (mesh.shape[name] for name in ("wide", "narrow"))
    grid = Mesh(mesh.devices.reshape(wide // 2, 2, narrow // 2, 2), ("wz", "wx", "ny", "nc"))
    split = P(("wz", "wx"), ("ny", "nc"))
    return jax.shard_map(
        per_device,
        mesh=grid,
        in_specs=(split, split) + (P(),) * 10,
        out_specs=split,
        check_vma=False,
    )
```

time: 157 us -> 129 us (0.82)
  waiting for transfers between devices: 41.2 us -> 20.2 us
  Pallas kernels: 71.7 us -> 61 us
  starting transfers between devices: 30.1 us -> 35.2 us
  other arithmetic: 5.09 us -> 2.86 us
    all_to_all x1 -> x0, waiting for transfers between devices: 16.3 us -> none  [per_device(): lax.all_to_all(merged.reshape(groups, rows, width + LANES), ('wide', 'ny'...]
    pallas_call x4 -> x9, Pallas kernels: 71.7 us -> 61 us  [call(): pl.pallas_call(kernel, out_shape=shapes, in_specs=in_specs, out_specs=[vm...]
    ppermute x6 -> x14, starting transfers between devices: 6.67 us -> 17.3 us  [flipped(): lax.ppermute(array, axis, [(i, i ^ distance) for i in range(lax.axis_size...]
    all_to_all x1 -> x0, starting transfers between devices: 7.93 us -> none  [per_device(): lax.all_to_all(merged.reshape(groups, rows, width + LANES), ('wide', 'ny'...]
    ppermute x6, waiting for transfers between devices: 6.51 us -> 0.02 us  [exchange(): return (lax.ppermute(high, axis, up), lax.ppermute(low, axis, down))]
    ppermute x6, starting transfers between devices: 15.5 us -> 17.9 us  [exchange(): return (lax.ppermute(high, axis, up), lax.ppermute(low, axis, down))]
    concatenate x3 -> x0, other arithmetic: 2.3 us -> none  [per_device(): state = jnp.concatenate([state, flipped(state, 'wide', distance)], axis=0)]
    mul x0 -> x1, local copies, waits for them, and re-layouts: none -> 1.91 us  [per_device(): masked = flow_field * fluid_mask[:, :, :, None].astype(BF16)]
  transfers between devices with their start and end apart: 13 -> 20, of which waited for: 9 -> 12; matrix products, arithmetic and copies ran while one was open for 1% -> 2% of each run, Pallas kernels for 0% -> 9%
where the time goes in v2:
time: 129 us
  Pallas kernels  61 us (47%)
  starting transfers between devices  35.2 us (27%)
  waiting for transfers between devices  20.2 us (16%)
  local copies, waits for them, and re-layouts  9.41 us (7%)
  other arithmetic  2.86 us (2%)
    pallas_call x9, Pallas kernels, call(): pl.pallas_call(kernel, out_shape=shapes, in_specs=in_specs, out_specs=[vm...  61 us
    ppermute x14, waiting for transfers between devices, flipped(): lax.ppermute(array, axis, [(i, i ^ distance) for i in range(lax.axis_size...  20.2 us
    ppermute x6, starting transfers between devices, exchange(): return (lax.ppermute(high, axis, up), lax.ppermute(low, axis, down))  17.9 us
    ppermute x14, starting transfers between devices, flipped(): lax.ppermute(array, axis, [(i, i ^ distance) for i in range(lax.axis_size...  17.3 us
    unnamed x38, local copies, waits for them, and re-layouts  5.88 us
  transfers between devices with their start and end apart: 20, of which 12 were waited for; matrix products, arithmetic and copies ran while one was open for 2% of the time, Pallas kernels for 9%

profile of v2, /device:TPU:0, one launch (start us, length us, event | category | flops | bytes accessed | tf_op | source)
XLA Modules:
  0.0 128.9 jit_solution(5455883143628321)
XLA Ops:
  0.0 0.8 convert_element_type.4
  0.9 1.9 %copy_multiply_fusion = bf16[8,16,16,512]{3,2,0,1:T(8,128)(2,1)S(1)} fusion(bf16[8,16,16,512]{3,2,1,0:T(8,128)(2,1)} %param.12, bf16[8,16,16]{2,0,1:T(8,128)(2,1)S(1)} %copy.13), kind=kLoop, calls=%fused_computation | loop fusion | flops 1048576 | bytes 4198400 | tf_op jit(solution)/shard_map/mul | solution.py:428
  2.8 0.8 slice_bitcast_fusion.2
  3.6 1.3 collective-permute-start.3
  4.9 3.0 %collective-permute-start.2 = (bf16[8,16,512]{2,1,0:T(8,128)(2,1)}, bf16[8,16,512]{2,1,0:T(8,128)(2,1)S(1)}, u32[]{:S(2)}, u32[]{:S(2)}) collective-permute-start(bf16[8,16,512]{2,1,0:T(8,128)(2,1)} %get-tuple-element.36), channel_id=1, source_target_pairs={{0,1},{1,2},{2,3},{4,5},{5,6},{6,7},{8,9},{9,10},{10,11},{12,13},{... | collective-permute-start | bytes 393224 | tf_op jit(solution)/shard_map/ppermute | solution.py:391
  7.9 0.8 slice_bitcast_fusion
  8.7 1.3 collective-permute-start.1
  10.0 6.2 %collective-permute-start = (bf16[16,16,512]{2,1,0:T(8,128)(2,1)}, bf16[16,16,512]{2,1,0:T(8,128)(2,1)}, u32[]{:S(2)}, u32[]{:S(2)}) collective-permute-start(bf16[16,16,512]{2,1,0:T(8,128)(2,1)} %get-tuple-element.38), channel_id=1, source_target_pairs={{0,4},{4,8},{8,12},{12,16},{16,20},{20,24},{24,28},{1,5},{5,9},{9,... | collective-permute-start | bytes 786440 | tf_op jit(solution)/shard_map/ppermute | solution.py:391
  16.3 1.9 %copy.17.masked = bf16[8,16,16,512]{3,2,1,0:T(8,128)(2,1)S(1)} copy(bf16[8,16,16,512]{3,2,0,1:T(8,128)(2,1)} %copy-done.18) | data formatting | bytes 4194304 | tf_op jit(solution)/shard_map/mul | solution.py:428
  18.2 0.1 pad_add_fusion.position
  18.3 1.3 %collective-permute-start.5 = (bf16[2,16,512]{2,1,0:T(8,128)(2,1)S(1)}, bf16[2,16,512]{2,1,0:T(8,128)(2,1)S(1)}, u32[]{:S(2)}, u32[]{:S(2)}) collective-permute-start(bf16[2,16,512]{2,1,0:T(8,128)(2,1)S(1)} %get-tuple-element.39), channel_id=1, source_target_pairs={{4,0},{8,4},{12,8},{16,12},{20,16},{24,20},{28,24},{5,1},{9,5},{13... | collective-permute-start | bytes 98312 | tf_op jit(solution)/shard_map/ppermute | solution.py:391
  19.6 4.8 %collective-permute-start.4 = (bf16[2,16,512]{2,1,0:T(8,128)(2,1)S(1)}, bf16[2,16,512]{2,1,0:T(8,128)(2,1)S(1)}, u32[]{:S(2)}, u32[]{:S(2)}) collective-permute-start(bf16[2,16,512]{2,1,0:T(8,128)(2,1)S(1)} %get-tuple-element.40), channel_id=1, source_target_pairs={{0,4},{4,8},{8,12},{12,16},{16,20},{20,24},{24,28},{1,5},{5,9},{9,... | collective-permute-start | bytes 98312 | tf_op jit(solution)/shard_map/ppermute | solution.py:391
  24.4 1.0 copy-done.1
  25.4 1.0 copy-done.2
  26.5 1.0 copy-done.4
  27.5 8.8 %inner.1 = (bf16[1536,512]{1,0:T(8,128)(2,1)S(1)}, bf16[1536,512]{1,0:T(8,128)(2,1)S(1)}, bf16[8,80,1536]{2,1,0:T(8,128)(2,1)S(1)}, bf16[512,1024]{1,0:T(8,128)(2,1)S(1)}) custom-call(bf16[8,16,16,512]{3,2,1,0:T(8,128)(2,1)S(1)} %copy.17.masked, bf16[8,16,512]{2,1,0:T(8,128)(2,1)S(1)} %collective-permute-done.2.y_lo, ...), custom_call_target="tpu_custom_call" | custom-call | flops 10000000000 | bytes 5036032 | tf_op jit(solution)/shard_map/inner/pallas_call | solution.py:374
  36.4 1.1 copy-done.12
  37.5 22.4 %read.1 = (bf16[512,512]{1,0:T(8,128)(2,1)S(1)}, bf16[4,560,128]{2,1,0:T(8,128)(2,1)S(1)}, bf16[4,560,128]{2,1,0:T(8,128)(2,1)S(1)}) custom-call(s32[3]{0:T(128)S(1)} %pad_add_fusion.position, bf16[8,16,16,512]{3,2,1,0:T(8,128)(2,1)S(1)} %copy.17.masked, bf16[16,16,512]{2,1,0:T(8,128)(2,1)} %collective-permute-done.x_lo, ...), custom_call_target="tpu_custom_call" | custom-call | flops 20000000000 | bytes 8640524 | tf_op jit(solution)/shard_map/read/pallas_call | solution.py:374
  60.0 0.4 collective-permute-start.6
  60.4 1.6 %collective-permute-done.6.taken = bf16[4,560,128]{2,1,0:T(8,128)(2,1)S(1)} collective-permute-done((bf16[4,560,128]{2,1,0:T(8,128)(2,1)S(1)}, bf16[4,560,128]{2,1,0:T(8,128)(2,1)S(1)}, u32[]{:S(2)}, u32[]{:S(2)}) %collective-permute-start.6) | collective-permute-done | bytes 573472 | tf_op jit(solution)/shard_map/ppermute | solution.py:395
  62.0 1.4 %merge_pair.1 = (bf16[560,128]{1,0:T(8,128)(2,1)S(1)}, bf16[560,128]{1,0:T(8,128)(2,1)}, bf16[560,128]{1,0:T(8,128)(2,1)}, bf16[560,128]{1,0:T(8,128)(2,1)}) custom-call(s32[3]{0:T(128)S(1)} %pad_add_fusion.position, bf16[4,560,128]{2,1,0:T(8,128)(2,1)S(1)} %get-tuple-element.23.kept, bf16[4,560,128]{2,1,0:T(8,128)(2,1)S(1)} %collective-permute-done.6.taken), custom_call_target="tpu_custom_call" | custom-call | flops 1000000000 | bytes 1146892 | tf_op jit(solution)/shard_map/merge_pair/pallas_call | solution.py:374
  63.4 0.7 copy-done.16
  64.1 1.8 %collective-permute-start.7 = (bf16[560,128]{1,0:T(8,128)(2,1)}, bf16[560,128]{1,0:T(8,128)(2,1)S(1)}, u32[]{:S(2)}, u32[]{:S(2)}) collective-permute-start(bf16[560,128]{1,0:T(8,128)(2,1)} %get-tuple-element.26), channel_id=1, source_target_pairs={{0,2},{2,0},{4,6},{6,4},{1,3},{3,1},{5,7},{7,5},{8,10},{10,8},{12,... | collective-permute-start | bytes 430088 | tf_op jit(solution)/shard_map/ppermute | solution.py:395
  65.9 2.6 %collective-permute-start.8 = (bf16[560,128]{1,0:T(8,128)(2,1)}, bf16[560,128]{1,0:T(8,128)(2,1)S(1)}, u32[]{:S(2)}, u32[]{:S(2)}) collective-permute-start(bf16[560,128]{1,0:T(8,128)(2,1)} %get-tuple-element.27), channel_id=1, source_target_pairs={{0,4},{2,6},{4,0},{6,2},{1,5},{3,7},{5,1},{7,3},{8,12},{10,14},{12... | collective-permute-start | bytes 430088 | tf_op jit(solution)/shard_map/ppermute | solution.py:395
  68.5 1.8 %collective-permute-done.7.refs_1_ = bf16[560,128]{1,0:T(8,128)(2,1)S(1)} collective-permute-done((bf16[560,128]{1,0:T(8,128)(2,1)}, bf16[560,128]{1,0:T(8,128)(2,1)S(1)}, u32[]{:S(2)}, u32[]{:S(2)}) %collective-permute-start.7) | collective-permute-done | bytes 143392 | tf_op jit(solution)/shard_map/ppermute | solution.py:395
  70.3 3.0 %collective-permute-done.8.refs_2_ = bf16[560,128]{1,0:T(8,128)(2,1)S(1)} collective-permute-done((bf16[560,128]{1,0:T(8,128)(2,1)}, bf16[560,128]{1,0:T(8,128)(2,1)S(1)}, u32[]{:S(2)}, u32[]{:S(2)}) %collective-permute-start.8) | collective-permute-done | bytes 143392 | tf_op jit(solution)/shard_map/ppermute | solution.py:395
  73.3 2.3 %collective-permute-done.9.refs_3_ = bf16[560,128]{1,0:T(8,128)(2,1)} collective-permute-done((bf16[560,128]{1,0:T(8,128)(2,1)}, bf16[560,128]{1,0:T(8,128)(2,1)}, u32[]{:S(2)}, u32[]{:S(2)}) %collective-permute-start.9) | collective-permute-done | bytes 143392 | tf_op jit(solution)/shard_map/ppermute | solution.py:395
  75.6 0.9 copy-done.17
  76.5 1.1 merge_group.1
  77.7 1.7 %collective-permute-start.10 = (bf16[32,640]{1,0:T(8,128)(2,1)S(1)}, bf16[32,640]{1,0:T(8,128)(2,1)S(1)}, u32[]{:S(2)}, u32[]{:S(2)}) collective-permute-start(bf16[32,640]{1,0:T(8,128)(2,1)S(1)} %get-tuple-element.30), channel_id=1, source_target_pairs={{0,8},{8,0},{16,24},{24,16},{1,9},{9,1},{17,25},{25,17},{2,10},{10... | collective-permute-start | bytes 122888 | tf_op jit(solution)/shard_map/ppermute | solution.py:395
  79.3 1.7 %collective-permute-start.11 = (bf16[32,640]{1,0:T(8,128)(2,1)S(1)}, bf16[32,640]{1,0:T(8,128)(2,1)S(1)}, u32[]{:S(2)}, u32[]{:S(2)}) collective-permute-start(bf16[32,640]{1,0:T(8,128)(2,1)S(1)} %get-tuple-element.31), channel_id=1, source_target_pairs={{0,16},{8,24},{16,0},{24,8},{1,17},{9,25},{17,1},{25,9},{2,18},{10... | collective-permute-start | bytes 122888 | tf_op jit(solution)/shard_map/ppermute | solution.py:395
  81.0 1.1 collective-permute-start.12
  82.1 3.0 %collective-permute-done.11.refs_2_ = bf16[32,640]{1,0:T(8,128)(2,1)S(1)} collective-permute-done((bf16[32,640]{1,0:T(8,128)(2,1)S(1)}, bf16[32,640]{1,0:T(8,128)(2,1)S(1)}, u32[]{:S(2)}, u32[]{:S(2)}) %collective-permute-start.11) | collective-permute-done | bytes 40992 | tf_op jit(solution)/shard_map/ppermute | solution.py:395
  85.1 1.8 %collective-permute-done.12.refs_3_ = bf16[32,640]{1,0:T(8,128)(2,1)S(1)} collective-permute-done((bf16[32,640]{1,0:T(8,128)(2,1)S(1)}, bf16[32,640]{1,0:T(8,128)(2,1)S(1)}, u32[]{:S(2)}, u32[]{:S(2)}) %collective-permute-start.12) | collective-permute-done | bytes 40992 | tf_op jit(solution)/shard_map/ppermute | solution.py:395
  86.9 0.5 update.1.refs_0_
  87.4 1.2 collective-permute-start.15
  88.6 3.2 %collective-permute-start.13 = (bf16[32,512]{1,0:T(8,128)(2,1)S(1)}, bf16[32,512]{1,0:T(8,128)(2,1)S(1)}, u32[]{:S(2)}, u32[]{:S(2)}) collective-permute-start(bf16[32,512]{1,0:T(8,128)(2,1)S(1)} %update.1.refs_0_), channel_id=1, source_target_pairs={{0,8},{8,0},{16,24},{24,16},{1,9},{9,1},{17,25},{25,17},{2,10},{10... | collective-permute-start | bytes 98312 | tf_op jit(solution)/shard_map/ppermute | solution.py:395
  91.8 1.3 %collective-permute-done.15.refs_3_ = bf16[32,512]{1,0:T(8,128)(2,1)S(1)} collective-permute-done((bf16[32,512]{1,0:T(8,128)(2,1)S(1)}, bf16[32,512]{1,0:T(8,128)(2,1)S(1)}, u32[]{:S(2)}, u32[]{:S(2)}) %collective-permute-start.15) | collective-permute-done | bytes 32800 | tf_op jit(solution)/shard_map/ppermute | solution.py:395
  93.1 0.8 collective-permute-done.14.refs_2_
  93.9 0.1 collective-permute-done.13.refs_1_
  94.0 2.2 %collective-permute-start.18 = (bf16[128,512]{1,0:T(8,128)(2,1)S(1)}, bf16[128,512]{1,0:T(8,128)(2,1)S(1)}, u32[]{:S(2)}, u32[]{:S(2)}) collective-permute-start(bf16[128,512]{1,0:T(8,128)(2,1)S(1)} %join_far.1.refs_0_), channel_id=1, source_target_pairs={{0,6},{2,4},{4,2},{6,0},{1,7},{3,5},{5,3},{7,1},{8,14},{10,12},{12... | collective-permute-start | bytes 393224 | tf_op jit(solution)/shard_map/ppermute | solution.py:395
  96.2 0.9 collective-permute-start.17
  97.1 0.5 collective-permute-start.16
  97.6 2.4 %collective-permute-done.18.refs_3_ = bf16[128,512]{1,0:T(8,128)(2,1)S(1)} collective-permute-done((bf16[128,512]{1,0:T(8,128)(2,1)S(1)}, bf16[128,512]{1,0:T(8,128)(2,1)S(1)}, u32[]{:S(2)}, u32[]{:S(2)}) %collective-permute-start.18) | collective-permute-done | bytes 131104 | tf_op jit(solution)/shard_map/ppermute | solution.py:395
  100.0 1.5 %collective-permute-done.17.refs_2_ = bf16[128,512]{1,0:T(8,128)(2,1)S(1)} collective-permute-done((bf16[128,512]{1,0:T(8,128)(2,1)S(1)}, bf16[128,512]{1,0:T(8,128)(2,1)S(1)}, u32[]{:S(2)}, u32[]{:S(2)}) %collective-permute-start.17) | collective-permute-done | bytes 131104 | tf_op jit(solution)/shard_map/ppermute | solution.py:395
  101.5 0.6 collective-permute-done.16.refs_1_
  102.3 2.6 %query.1.query2_t = bf16[512,2048]{1,0:T(8,128)(2,1)S(1)} custom-call(bf16[1536,512]{1,0:T(8,128)(2,1)S(1)} %copy-done.13, bf16[512,512]{1,0:T(8,128)(2,1)S(1)} %copy-done.15, bf16[512,512]{1,0:T(8,128)(2,1)S(1)} %copy-done.7), custom_call_target="tpu_custom_call" | custom-call | flops 2000000000 | bytes 2621440 | tf_op jit(solution)/shard_map/query/pallas_call | solution.py:374
  104.9 24.0 %write.1 = f32[2048,512]{1,0:T(8,128)} custom-call(bf16[512,512]{1,0:T(8,128)(2,1)S(1)} %join_group.1.own_state, bf16[512,512]{1,0:T(8,128)(2,1)S(1)} %collective-permute-done.19.other_state, bf16[512,2048]{1,0:T(8,128)(2,1)S(1)} %query.1.query2_t, bf16[2048,512]{1,0:T(8,128)(2,1)S(1)} %bitcast.21, bf16[512,512]{1,0:T(8,128)(2,1)S(1)} %copy-done.8, ...), custom_call_target="tpu_custom_call" | custom-call | flops 20000000000 | bytes 6815744 | tf_op jit(solution)/shard_map/write/pallas_call | solution.py:374
  (48 shorter events, 0.2 us)
Async XLA Ops:
  2.8 13.5 %copy-start.18 = (bf16[8,16,16,512]{3,2,0,1:T(8,128)(2,1)}, bf16[8,16,16,512]{3,2,0,1:T(8,128)(2,1)S(1)}, u32[]{:S(2)}) copy-start(bf16[8,16,16,512]{3,2,0,1:T(8,128)(2,1)S(1)} %copy_multiply_fusion) | copy-start | bytes 6291460
  3.6 14.7 %collective-permute-start.3 = (bf16[8,16,512]{2,1,0:T(8,128)(2,1)}, bf16[8,16,512]{2,1,0:T(8,128)(2,1)S(1)}, u32[]{:S(2)}, u32[]{:S(2)}) collective-permute-start(bf16[8,16,512]{2,1,0:T(8,128)(2,1)} %get-tuple-element.35), channel_id=1, source_target_pairs={{1,0},{2,1},{3,2},{5,4},{6,5},{7,6},{9,8},{10,9},{11,10},{13,12},{... | collective-permute-start | bytes 393224 | tf_op jit(solution)/shard_map/ppermute | solution.py:391
  4.9 13.4 %collective-permute-start.2 = (bf16[8,16,512]{2,1,0:T(8,128)(2,1)}, bf16[8,16,512]{2,1,0:T(8,128)(2,1)S(1)}, u32[]{:S(2)}, u32[]{:S(2)}) collective-permute-start(bf16[8,16,512]{2,1,0:T(8,128)(2,1)} %get-tuple-element.36), channel_id=1, source_target_pairs={{0,1},{1,2},{2,3},{4,5},{5,6},{6,7},{8,9},{9,10},{10,11},{12,13},{... | collective-permute-start | bytes 393224 | tf_op jit(solution)/shard_map/ppermute | solution.py:391
  8.7 28.8 %collective-permute-start.1 = (bf16[16,16,512]{2,1,0:T(8,128)(2,1)}, bf16[16,16,512]{2,1,0:T(8,128)(2,1)}, u32[]{:S(2)}, u32[]{:S(2)}) collective-permute-start(bf16[16,16,512]{2,1,0:T(8,128)(2,1)} %get-tuple-element.37), channel_id=1, source_target_pairs={{4,0},{8,4},{12,8},{16,12},{20,16},{24,20},{28,24},{5,1},{9,5},{13... | collective-permute-start | bytes 786440 | tf_op jit(solution)/shard_map/ppermute | solution.py:391
  10.0 27.5 %collective-permute-start = (bf16[16,16,512]{2,1,0:T(8,128)(2,1)}, bf16[16,16,512]{2,1,0:T(8,128)(2,1)}, u32[]{:S(2)}, u32[]{:S(2)}) collective-permute-start(bf16[16,16,512]{2,1,0:T(8,128)(2,1)} %get-tuple-element.38), channel_id=1, source_target_pairs={{0,4},{4,8},{8,12},{12,16},{16,20},{20,24},{24,28},{1,5},{5,9},{9,... | collective-permute-start | bytes 786440 | tf_op jit(solution)/shard_map/ppermute | solution.py:391
  16.3 8.1 %copy-start = (bf16[1024,512]{1,0:T(8,128)(2,1)S(1)}, bf16[1024,512]{1,0:T(8,128)(2,1)}, u32[]{:S(2)}) copy-start(bf16[1024,512]{1,0:T(8,128)(2,1)} %latents.1) | copy-start | bytes 3145732
  16.3 8.1 %copy-start.11 = (f32[27,512]{1,0:T(8,128)S(1)}, f32[27,512]{1,0:T(8,128)}, u32[]{:S(2)}) copy-start(f32[27,512]{1,0:T(8,128)} %conv.3) | copy-start | bytes 165892
  18.3 19.2 %collective-permute-start.5 = (bf16[2,16,512]{2,1,0:T(8,128)(2,1)S(1)}, bf16[2,16,512]{2,1,0:T(8,128)(2,1)S(1)}, u32[]{:S(2)}, u32[]{:S(2)}) collective-permute-start(bf16[2,16,512]{2,1,0:T(8,128)(2,1)S(1)} %get-tuple-element.39), channel_id=1, source_target_pairs={{4,0},{8,4},{12,8},{16,12},{20,16},{24,20},{28,24},{5,1},{9,5},{13... | collective-permute-start | bytes 98312 | tf_op jit(solution)/shard_map/ppermute | solution.py:391
  19.6 17.9 %collective-permute-start.4 = (bf16[2,16,512]{2,1,0:T(8,128)(2,1)S(1)}, bf16[2,16,512]{2,1,0:T(8,128)(2,1)S(1)}, u32[]{:S(2)}, u32[]{:S(2)}) collective-permute-start(bf16[2,16,512]{2,1,0:T(8,128)(2,1)S(1)} %get-tuple-element.40), channel_id=1, source_target_pairs={{0,4},{4,8},{8,12},{12,16},{16,20},{20,24},{24,28},{1,5},{5,9},{9,... | collective-permute-start | bytes 98312 | tf_op jit(solution)/shard_map/ppermute | solution.py:391
  24.4 1.0 copy-start.1
  25.4 1.0 copy-start.2
  26.5 1.0 copy-start.4
  27.5 10.0 %copy-start.3 = (bf16[512,512]{1,0:T(8,128)(2,1)S(1)}, bf16[512,512]{1,0:T(8,128)(2,1)}, u32[]{:S(2)}) copy-start(bf16[512,512]{1,0:T(8,128)(2,1)} %w_key1.3) | copy-start | bytes 1572868
  27.5 10.0 %copy-start.5 = (bf16[512,512]{1,0:T(8,128)(2,1)S(1)}, bf16[512,512]{1,0:T(8,128)(2,1)}, u32[]{:S(2)}) copy-start(bf16[512,512]{1,0:T(8,128)(2,1)} %w_value1.3) | copy-start | bytes 1572868
  36.4 1.1 copy-start.12
  60.0 6.0 %copy-start.14 = (bf16[512,512]{1,0:T(8,128)(2,1)}, bf16[512,512]{1,0:T(8,128)(2,1)S(1)}, u32[]{:S(2)}) copy-start(bf16[512,512]{1,0:T(8,128)(2,1)S(1)} %get-tuple-element.34.outer) | copy-start | bytes 1572868
  60.0 2.0 %collective-permute-start.6 = (bf16[4,560,128]{2,1,0:T(8,128)(2,1)S(1)}, bf16[4,560,128]{2,1,0:T(8,128)(2,1)S(1)}, u32[]{:S(2)}, u32[]{:S(2)}) collective-permute-start(bf16[4,560,128]{2,1,0:T(8,128)(2,1)S(1)} %get-tuple-element.24), channel_id=1, source_target_pairs={{0,1},{1,0},{2,3},{3,2},{4,5},{5,4},{6,7},{7,6},{8,9},{9,8},{10,11... | collective-permute-start | bytes 1720328 | tf_op jit(solution)/shard_map/ppermute | solution.py:395
  63.4 0.7 copy-start.16
  64.1 6.2 %collective-permute-start.7 = (bf16[560,128]{1,0:T(8,128)(2,1)}, bf16[560,128]{1,0:T(8,128)(2,1)S(1)}, u32[]{:S(2)}, u32[]{:S(2)}) collective-permute-start(bf16[560,128]{1,0:T(8,128)(2,1)} %get-tuple-element.26), channel_id=1, source_target_pairs={{0,2},{2,0},{4,6},{6,4},{1,3},{3,1},{5,7},{7,5},{8,10},{10,8},{12,... | collective-permute-start | bytes 430088 | tf_op jit(solution)/shard_map/ppermute | solution.py:395
  65.9 7.4 %collective-permute-start.8 = (bf16[560,128]{1,0:T(8,128)(2,1)}, bf16[560,128]{1,0:T(8,128)(2,1)S(1)}, u32[]{:S(2)}, u32[]{:S(2)}) collective-permute-start(bf16[560,128]{1,0:T(8,128)(2,1)} %get-tuple-element.27), channel_id=1, source_target_pairs={{0,4},{2,6},{4,0},{6,2},{1,5},{3,7},{5,1},{7,3},{8,12},{10,14},{12... | collective-permute-start | bytes 430088 | tf_op jit(solution)/shard_map/ppermute | solution.py:395
  68.5 7.1 %collective-permute-start.9 = (bf16[560,128]{1,0:T(8,128)(2,1)}, bf16[560,128]{1,0:T(8,128)(2,1)}, u32[]{:S(2)}, u32[]{:S(2)}) collective-permute-start(bf16[560,128]{1,0:T(8,128)(2,1)} %get-tuple-element.28), channel_id=1, source_target_pairs={{0,6},{2,4},{4,2},{6,0},{1,7},{3,5},{5,3},{7,1},{8,14},{10,12},{12... | collective-permute-start | bytes 430088 | tf_op jit(solution)/shard_map/ppermute | solution.py:395
  68.5 18.4 %copy-start.6 = (bf16[512,512]{1,0:T(8,128)(2,1)S(1)}, bf16[512,512]{1,0:T(8,128)(2,1)}, u32[]{:S(2)}) copy-start(bf16[512,512]{1,0:T(8,128)(2,1)} %w_out1.1) | copy-start | bytes 1572868
  75.6 0.9 copy-start.17
  77.7 4.5 %collective-permute-start.10 = (bf16[32,640]{1,0:T(8,128)(2,1)S(1)}, bf16[32,640]{1,0:T(8,128)(2,1)S(1)}, u32[]{:S(2)}, u32[]{:S(2)}) collective-permute-start(bf16[32,640]{1,0:T(8,128)(2,1)S(1)} %get-tuple-element.30), channel_id=1, source_target_pairs={{0,8},{8,0},{16,24},{24,16},{1,9},{9,1},{17,25},{25,17},{2,10},{10... | collective-permute-start | bytes 122888 | tf_op jit(solution)/shard_map/ppermute | solution.py:395
  79.3 5.8 %collective-permute-start.11 = (bf16[32,640]{1,0:T(8,128)(2,1)S(1)}, bf16[32,640]{1,0:T(8,128)(2,1)S(1)}, u32[]{:S(2)}, u32[]{:S(2)}) collective-permute-start(bf16[32,640]{1,0:T(8,128)(2,1)S(1)} %get-tuple-element.31), channel_id=1, source_target_pairs={{0,16},{8,24},{16,0},{24,8},{1,17},{9,25},{17,1},{25,9},{2,18},{10... | collective-permute-start | bytes 122888 | tf_op jit(solution)/shard_map/ppermute | solution.py:395
  81.0 5.8 %collective-permute-start.12 = (bf16[32,640]{1,0:T(8,128)(2,1)S(1)}, bf16[32,640]{1,0:T(8,128)(2,1)S(1)}, u32[]{:S(2)}, u32[]{:S(2)}) collective-permute-start(bf16[32,640]{1,0:T(8,128)(2,1)S(1)} %get-tuple-element.32), channel_id=1, source_target_pairs={{0,24},{8,16},{16,8},{24,0},{1,25},{9,17},{17,9},{25,1},{2,26},{10... | collective-permute-start | bytes 122888 | tf_op jit(solution)/shard_map/ppermute | solution.py:395
  86.9 15.3 %copy-start.7 = (bf16[512,512]{1,0:T(8,128)(2,1)S(1)}, bf16[512,512]{1,0:T(8,128)(2,1)}, u32[]{:S(2)}) copy-start(bf16[512,512]{1,0:T(8,128)(2,1)} %w_query2.1) | copy-start | bytes 1572868
  86.9 15.3 %copy-start.13 = (bf16[1536,512]{1,0:T(8,128)(2,1)S(1)}, bf16[1536,512]{1,0:T(8,128)(2,1)}, u32[]{:S(2)}) copy-start(bf16[1536,512]{1,0:T(8,128)(2,1)} %copy-done.12) | copy-start | bytes 4718596
  86.9 15.3 %copy-start.15 = (bf16[512,512]{1,0:T(8,128)(2,1)S(1)}, bf16[512,512]{1,0:T(8,128)(2,1)}, u32[]{:S(2)}) copy-start(bf16[512,512]{1,0:T(8,128)(2,1)} %copy-done.14) | copy-start | bytes 1572868
  87.4 5.7 %collective-permute-start.15 = (bf16[32,512]{1,0:T(8,128)(2,1)S(1)}, bf16[32,512]{1,0:T(8,128)(2,1)S(1)}, u32[]{:S(2)}, u32[]{:S(2)}) collective-permute-start(bf16[32,512]{1,0:T(8,128)(2,1)S(1)} %update.1.refs_0_), channel_id=1, source_target_pairs={{0,24},{8,16},{16,8},{24,0},{1,25},{9,17},{17,9},{25,1},{2,26},{10... | collective-permute-start | bytes 98312 | tf_op jit(solution)/shard_map/ppermute | solution.py:395
  88.6 5.4 %collective-permute-start.14 = (bf16[32,512]{1,0:T(8,128)(2,1)S(1)}, bf16[32,512]{1,0:T(8,128)(2,1)S(1)}, u32[]{:S(2)}, u32[]{:S(2)}) collective-permute-start(bf16[32,512]{1,0:T(8,128)(2,1)S(1)} %update.1.refs_0_), channel_id=1, source_target_pairs={{0,16},{8,24},{16,0},{24,8},{1,17},{9,25},{17,1},{25,9},{2,18},{10... | collective-permute-start | bytes 98312 | tf_op jit(solution)/shard_map/ppermute | solution.py:395
  88.6 5.5 %collective-permute-start.13 = (bf16[32,512]{1,0:T(8,128)(2,1)S(1)}, bf16[32,512]{1,0:T(8,128)(2,1)S(1)}, u32[]{:S(2)}, u32[]{:S(2)}) collective-permute-start(bf16[32,512]{1,0:T(8,128)(2,1)S(1)} %update.1.refs_0_), channel_id=1, source_target_pairs={{0,8},{8,0},{16,24},{24,16},{1,9},{9,1},{17,25},{25,17},{2,10},{10... | collective-permute-start | bytes 98312 | tf_op jit(solution)/shard_map/ppermute | solution.py:395
  94.0 5.9 %collective-permute-start.18 = (bf16[128,512]{1,0:T(8,128)(2,1)S(1)}, bf16[128,512]{1,0:T(8,128)(2,1)S(1)}, u32[]{:S(2)}, u32[]{:S(2)}) collective-permute-start(bf16[128,512]{1,0:T(8,128)(2,1)S(1)} %join_far.1.refs_0_), channel_id=1, source_target_pairs={{0,6},{2,4},{4,2},{6,0},{1,7},{3,5},{5,3},{7,1},{8,14},{10,12},{12... | collective-permute-start | bytes 393224 | tf_op jit(solution)/shard_map/ppermute | solution.py:395
  96.2 5.2 %collective-permute-start.17 = (bf16[128,512]{1,0:T(8,128)(2,1)S(1)}, bf16[128,512]{1,0:T(8,128)(2,1)S(1)}, u32[]{:S(2)}, u32[]{:S(2)}) collective-permute-start(bf16[128,512]{1,0:T(8,128)(2,1)S(1)} %join_far.1.refs_0_), channel_id=1, source_target_pairs={{0,4},{2,6},{4,0},{6,2},{1,5},{3,7},{5,1},{7,3},{8,12},{10,14},{12... | collective-permute-start | bytes 393224 | tf_op jit(solution)/shard_map/ppermute | solution.py:395
  97.1 5.0 %collective-permute-start.16 = (bf16[128,512]{1,0:T(8,128)(2,1)S(1)}, bf16[128,512]{1,0:T(8,128)(2,1)S(1)}, u32[]{:S(2)}, u32[]{:S(2)}) collective-permute-start(bf16[128,512]{1,0:T(8,128)(2,1)S(1)} %join_far.1.refs_0_), channel_id=1, source_target_pairs={{0,2},{2,0},{4,6},{6,4},{1,3},{3,1},{5,7},{7,5},{8,10},{10,8},{12,... | collective-permute-start | bytes 393224 | tf_op jit(solution)/shard_map/ppermute | solution.py:395
  102.1 2.7 %collective-permute-start.19 = (bf16[512,512]{1,0:T(8,128)(2,1)S(1)}, bf16[512,512]{1,0:T(8,128)(2,1)S(1)}, u32[]{:S(2)}, u32[]{:S(2)}) collective-permute-start(bf16[512,512]{1,0:T(8,128)(2,1)S(1)} %join_group.1.own_state), channel_id=1, source_target_pairs={{0,1},{1,0},{2,3},{3,2},{4,5},{5,4},{6,7},{7,6},{8,9},{9,8},{10,11... | collective-permute-start | bytes 1572872 | tf_op jit(solution)/shard_map/ppermute | solution.py:395
  102.2 2.6 %copy-start.8 = (bf16[512,512]{1,0:T(8,128)(2,1)S(1)}, bf16[512,512]{1,0:T(8,128)(2,1)}, u32[]{:S(2)}) copy-start(bf16[512,512]{1,0:T(8,128)(2,1)} %w_key2.1) | copy-start | bytes 1572868
  102.2 2.6 %copy-start.9 = (bf16[512,512]{1,0:T(8,128)(2,1)S(1)}, bf16[512,512]{1,0:T(8,128)(2,1)}, u32[]{:S(2)}) copy-start(bf16[512,512]{1,0:T(8,128)(2,1)} %w_value2.1) | copy-start | bytes 1572868
  102.2 2.6 %copy-start.10 = (bf16[512,512]{1,0:T(8,128)(2,1)S(1)}, bf16[512,512]{1,0:T(8,128)(2,1)}, u32[]{:S(2)}) copy-start(bf16[512,512]{1,0:T(8,128)(2,1)} %w_out2.1) | copy-start | bytes 1572868

commit v3 on v2

--- a/solution.py
+++ b/solution.py
@@ -21,11 +21,38 @@
     return lax.dot_general(left, right, (contract, ((), ())), preferred_element_type=F32)
 
 
-def fill_row(padded, row, plane, left, right):
-    size_y = plane.shape[0]
-    padded[row, 1 : size_y + 1] = plane.astype(F32)
-    padded[row, 0] = left.astype(F32)
-    padded[row, size_y + 1] = right.astype(F32)
+def prepare_kernel(position, flow, mask, masked, first, second):
+    size_x, size_y, size_z, width = flow.shape
+
+    def plane(i, carry):
+        turned = mask[i].astype(F32).T
+        for j in range(size_y):
+            column = jnp.broadcast_to(turned[:, j : j + 1], (size_z, LANES)).astype(BF16)
+            for tile in range(width // LANES):
+                lanes = slice(tile * LANES, (tile + 1) * LANES)
+                masked[i, j, :, lanes] = flow[i, j, :, lanes] * column
+        outer = size_y - 1
+        first[i] = masked[i, outer * (1 - position[3])]
+        second[i] = masked[i, outer * position[3]]
+        return carry
+
+    lax.fori_loop(0, size_x, plane, 0)
+
+
+def edge_kernel(position, masked, y_first, y_second, first, second):
+    size_x, size_y = masked.shape[:2]
+    outer = size_y + 1
+    for face, plane in ((first, (size_x - 1) * (1 - position[4])), (second, (size_x - 1) * position[4])):
+        face[1:outer] = masked[plane]
+        face[outer * (1 - position[3])] = y_first[plane]
+        face[outer * position[3]] = y_second[plane]
+
+
+def fill_row(position, padded, row, i, masked, y_first, y_second):
+    outer = masked.shape[1] + 1
+    padded[row, 1:outer] = masked[i].astype(F32)
+    padded[row, outer * (1 - position[3])] = y_first[i].astype(F32)
+    padded[row, outer * position[3]] = y_second[i].astype(F32)
 
 
 def stencil_plane(base, padded, conv, mixed, start):
@@ -48,38 +75,69 @@
             mixed[pl.ds(pl.multiple_of(start + j * size_z, size_z), size_z), lanes] = total.astype(BF16)
 
 
-def project_plane(start, cells, mixed, w_key1, w_value1, keys, values_t):
+def project_plane(start, target, cells, mixed, weights, keys, values_t, query2_t):
+    w_key1, w_value1, w_query2 = weights
     head_size = mixed.shape[1] // HEADS
     rows = pl.ds(pl.multiple_of(start, cells), cells)
     block = mixed[rows, :]
     keys[rows, :] = dot(block, w_key1[...]).astype(BF16)
     value_t = dot(w_value1[...], block, ((0,), (1,))).astype(BF16)
     values_t[:, :head_size, rows] = value_t.reshape(HEADS, head_size, cells)
+    query2_t[:, pl.ds(pl.multiple_of(target, cells), cells)] = dot(w_query2[...], block, ((0,), (1,))).astype(BF16)
+
+
+def latent_query_kernel(latents, w_query1, query1_t):
+    query1_t[...] = dot(w_query1[...], latents[...], ((0,), (1,))).astype(BF16)
 
 
 def inner_kernel(
-    masked, y_lo, y_hi, conv, latents, w_query1, w_key1, w_value1, mixed, keys, values_t, query1_t, padded
+    position,
+    masked,
+    y_first,
+    y_second,
+    conv,
+    far_key1,
+    far_value1,
+    far_query2,
+    keys,
+    values_t,
+    query2_t,
+    padded,
+    mixed,
+    w_key1,
+    w_value1,
+    w_query2,
+    arrived,
 ):
     size_x, size_y, size_z, width = masked.shape
     head_size = width // HEADS
     cells = size_y * size_z
+    weights = (w_key1, w_value1, w_query2)
+    copies = [
+        pltpu.make_async_copy(source, target, arrived.at[n])
+        for n, (source, target) in enumerate(zip((far_key1, far_value1, far_query2), weights))
+    ]
+    for copy in copies:
+        copy.start()
 
     def fill(i, carry):
-        fill_row(padded, i, masked[i], y_lo[i], y_hi[i])
+        fill_row(position, padded, i, i, masked, y_first, y_second)
         return carry
 
     lax.fori_loop(0, size_x, fill, 0)
-    query1_t[...] = dot(w_query1[...], latents[...], ((0,), (1,))).astype(BF16)
     values_t[:, head_size:, :] = jnp.ones_like(values_t[:, head_size:, :])
     stencil_plane(0, padded, conv, mixed, 0)
+    for copy in copies:
+        copy.wait()
 
     def plane(i, carry):
-        project_plane((i - 1) * cells, cells, mixed, w_key1, w_value1, keys, values_t)
+        project_plane((i - 1) * cells, i * cells, cells, mixed, weights, keys, values_t, query2_t)
         stencil_plane(i, padded, conv, mixed, i * cells)
         return carry
 
     lax.fori_loop(1, size_x - 2, plane, 0)
-    project_plane((size_x - 3) * cells, cells, mixed, w_key1, w_value1, keys, values_t)
+    last = size_x - 3
+    project_plane(last * cells, (last + 1) * cells, cells, mixed, weights, keys, values_t, query2_t)
 
 
 def score_weights(query_t, head_in_pair, head_size):
@@ -158,22 +216,23 @@
 def read_kernel(
     position,
     masked,
-    x_lo,
-    x_hi,
-    y_lo,
-    y_hi,
-    c_lo,
-    c_hi,
+    x_first,
+    x_second,
+    y_first,
+    y_second,
     conv,
     w_key1,
     w_value1,
+    w_query2,
     inner_keys,
     inner_values_t,
     query1_t,
-    mixed,
+    inner_query2_t,
+    query2_t,
     kept,
     given,
     padded,
+    mixed,
     keys,
     values_t,
     scores,
@@ -183,18 +242,17 @@
     head_size = width // HEADS
     cells = size_y * size_z
     last = size_x - 1
-    fill_row(padded, 0, x_lo[...], c_lo[0], c_lo[1])
-    fill_row(padded, 1, masked[0], y_lo[0], y_hi[0])
-    fill_row(padded, 2, masked[1], y_lo[1], y_hi[1])
-    fill_row(padded, 3, masked[last - 1], y_lo[last - 1], y_hi[last - 1])
-    fill_row(padded, 4, masked[last], y_lo[last], y_hi[last])
-    fill_row(padded, 5, x_hi[...], c_hi[0], c_hi[1])
+    for row, i in ((1, 0), (2, 1), (3, last - 1), (4, last)):
+        fill_row(position, padded, row, i, masked, y_first, y_second)
+    padded[5 * (1 - position[4])] = x_first[...].astype(F32)
+    padded[5 * position[4]] = x_second[...].astype(F32)
     values_t[:, head_size:, :] = jnp.ones_like(values_t[:, head_size:, :])
     stats[...] = jnp.zeros_like(stats)
 
     def plane(i, carry):
         stencil_plane(3 * i, padded, conv, mixed, i * cells)
-        project_plane(i * cells, cells, mixed, w_key1, w_value1, keys, values_t)
+        weights = (w_key1, w_value1, w_query2)
+        project_plane(i * cells, i * last * cells, cells, mixed, weights, keys, values_t, query2_t)
         return carry
 
     lax.fori_loop(0, 2, plane, 0)
@@ -315,24 +373,6 @@
     return call(join_kernel, out, [], parts, 8, 1e6, name)
 
 
-def query_kernel(inner, outer, w_query2, query2_t):
-    cells = outer.shape[0] // 2
-    planes = inner.shape[0] // cells
-
-    def put(block, plane):
-        columns = pl.ds(pl.multiple_of(plane * cells, cells), cells)
-        query2_t[:, columns] = dot(w_query2[...], block, ((0,), (1,))).astype(BF16)
-
-    put(outer[:cells, :], 0)
-    put(outer[cells:, :], planes + 1)
-
-    def plane(i, carry):
-        put(inner[pl.ds(pl.multiple_of(i * cells, cells), cells), :], i + 1)
-        return carry
-
-    lax.fori_loop(0, planes, plane, 0)
-
-
 def write_kernel(
     own_state, other_state, query2_t, masked, w_key2, w_value2, w_out2, out, keys, values_t, scores, read_t
 ):
@@ -363,10 +403,11 @@
     lax.fori_loop(0, out.shape[0] // span, emit, 0)
 
 
-def call(kernel, shapes, scratch, operands, limit, flops, name, position=None):
+def call(kernel, shapes, scratch, operands, limit, flops, name, position=None, far=(), aliases=None):
     vmem = pl.BlockSpec(memory_space=pltpu.VMEM)
+    hbm = pl.BlockSpec(memory_space=pltpu.HBM)
     many = isinstance(shapes, (list, tuple))
-    in_specs = [vmem] * len(operands)
+    in_specs = [hbm if n in far else vmem for n in range(len(operands))]
     if position is not None:
         in_specs = [pl.BlockSpec(memory_space=pltpu.SMEM)] + in_specs
         operands = [position] + list(operands)
@@ -379,16 +420,18 @@
         scratch_shapes=scratch,
         compiler_params=pltpu.CompilerParams(vmem_limit_bytes=limit * MIB),
         cost_estimate=pl.CostEstimate(flops=int(flops), bytes_accessed=moved, transcendentals=0),
+        input_output_aliases=aliases or {},
         name=name,
     )(*operands)
     return list(result) if many else result
 
 
-def exchange(low, high, axis):
+def pair_exchange(first, second, axis):
     count = lax.axis_size(axis)
-    up = [(i, i + 1) for i in range(count - 1)]
-    down = [(i + 1, i) for i in range(count - 1)]
-    return lax.ppermute(high, axis, up), lax.ppermute(low, axis, down)
+    swaps = [[], []]
+    for i in range(count - 1):
+        swaps[i % 2] += [(i, i + 1), (i + 1, i)]
+    return lax.ppermute(first, axis, swaps[0]), lax.ppermute(second, axis, swaps[1])
 
 
 def flipped(array, axis, distance):
@@ -419,37 +462,68 @@
     group_size = lax.axis_size(group)
     far = lax.axis_size("wz")
     core, member, layer = lax.axis_index("nc"), lax.axis_index(group), lax.axis_index("wz")
-    position = jnp.stack([core, member, layer]).astype(jnp.int32)
+    column = lax.axis_index("wx")
+    position = jnp.stack([core, member, layer, core, column]).astype(jnp.int32)
     block_size = latent_count // (2 * group_size)
     rows = block_size // far
     shape = jax.ShapeDtypeStruct
     step = 1e9
 
-    masked = flow_field * fluid_mask[:, :, :, None].astype(BF16)
-    y_lo, y_hi = exchange(masked[:, 0], masked[:, -1], narrow)
-    x_lo, x_hi = exchange(masked[0], masked[-1], wide)
-    sides = jnp.stack([y_lo, y_hi], axis=1)
-    c_lo, c_hi = exchange(sides[0], sides[-1], wide)
-
-    inner_mixed, inner_keys, inner_values_t, query1_t = call(
+    side = shape((size_x, size_z, width), BF16)
+    masked, y_first, y_second = call(
+        prepare_kernel,
+        [shape(flow_field.shape, BF16), side, side],
+        [],
+        [flow_field, fluid_mask],
+        12,
+        step,
+        "prepare",
+        position,
+    )
+    y_first, y_second = pair_exchange(y_first, y_second, narrow)
+    query1_t = call(
+        latent_query_kernel,
+        shape((width, latent_count), BF16),
+        [],
+        [latents, w_query1],
+        12,
+        2 * step,
+        "latent_query",
+    )
+    side = shape((size_y + 2, size_z, width), BF16)
+    x_first, x_second = call(
+        edge_kernel, [side, side], [], [masked, y_first, y_second], 12, step, "edge", position
+    )
+    x_first, x_second = pair_exchange(x_first, x_second, wide)
+    weight = pltpu.VMEM((width, width), BF16)
+    inner_keys, inner_values_t, query2_t = call(
         inner_kernel,
         [
             shape((inner_cells, width), BF16),
-            shape((inner_cells, width), BF16),
             shape((HEADS, head_size + ONES_ROWS, inner_cells), BF16),
-            shape((width, latent_count), BF16),
+            shape((width, cells), BF16),
         ],
-        [pltpu.VMEM((size_x, size_y + 2, size_z, width), F32)],
-        [masked, y_lo, y_hi, conv_weight, latents, w_query1, w_key1, w_value1],
+        [
+            pltpu.VMEM((size_x, size_y + 2, size_z, width), F32),
+            pltpu.VMEM((inner_cells, width), BF16),
+            weight,
+            weight,
+            weight,
+            pltpu.SemaphoreType.DMA((3,)),
+        ],
+        [masked, y_first, y_second, conv_weight, w_key1, w_value1, w_query2],
         28,
         10 * step,
         "inner",
-    )
-    outer_mixed, kept, given = call(
+        position,
+        (4, 5, 6),
+    )
+    query2_t, kept, given = call(
         read_kernel,
-        [shape((outer_cells, width), BF16)] + [shape((group_size, width + STAT_ROWS, LANES), BF16)] * 2,
+        [shape((width, cells), BF16)] + [shape((group_size, width + STAT_ROWS, LANES), BF16)] * 2,
         [
             pltpu.VMEM((6, size_y + 2, size_z, width), F32),
+            pltpu.VMEM((outer_cells, width), BF16),
             pltpu.VMEM((outer_cells, width), BF16),
             pltpu.VMEM((HEADS, head_size + ONES_ROWS, outer_cells), BF16),
             pltpu.VMEM((2, cells, 256), F32),
@@ -457,23 +531,25 @@
         ],
         [
             masked,
-            x_lo,
-            x_hi,
-            y_lo,
-            y_hi,
-            c_lo,
-            c_hi,
+            x_first,
+            x_second,
+            y_first,
+            y_second,
             conv_weight,
             w_key1,
             w_value1,
+            w_query2,
             inner_keys,
             inner_values_t,
             query1_t,
+            query2_t,
         ],
         32,
         20 * step,
         "read",
         position,
+        (),
+        {13: 0},
     )
     taken = flipped(given, "nc", 1)
     block = shape((width + STAT_ROWS, LANES), BF16)
@@ -490,15 +566,6 @@
         position,
     )
     parts = parts[:1] + [flipped(parts[d], "wz", d) for d in range(1, far)]
-    query2_t = call(
-        query_kernel,
-        shape((width, cells), BF16),
-        [],
-        [inner_mixed, outer_mixed, w_query2],
-        16,
-        2 * step,
-        "query",
-    )
     start = ((core * group_size + member) * far + layer) * rows
     own = lax.dynamic_slice_in_dim(latents, start, rows, 0)
     state = call(update_kernel, shape((rows, width), BF16), [], [own, w_out1] + parts, 16, step, "update")

time: 129 us -> 116 us (0.90)
  starting transfers between devices: 35.2 us -> 28 us
  local copies, waits for them, and re-layouts: 9.41 us -> 2.66 us
  other arithmetic: 2.86 us -> 0 us
  waiting for transfers between devices: 20.2 us -> 22.8 us
    ppermute x6 -> x4, starting transfers between devices: 17.9 us -> 4.45 us  [the longest x2 3.12 us: pair_exchange(): lax.ppermute(first, axis, swaps[0])]
    ppermute x14, starting transfers between devices: 17.3 us -> 23.5 us  [flipped(): lax.ppermute(array, axis, [(i, i ^ distance) for i in range(lax.axis_size...]
    unnamed x38 -> x32, local copies, waits for them, and re-layouts: 5.88 us -> 2.57 us
    ppermute x14, waiting for transfers between devices: 20.2 us -> 22.8 us  [flipped(): lax.ppermute(array, axis, [(i, i ^ distance) for i in range(lax.axis_size...]
    mul x1 -> x0, other arithmetic: 1.93 us -> none  [per_device(): masked = flow_field * fluid_mask[:, :, :, None].astype(BF16)]
    mul x1 -> x0, local copies, waits for them, and re-layouts: 1.91 us -> none  [per_device(): masked = flow_field * fluid_mask[:, :, :, None].astype(BF16)]
    squeeze x2 -> x0, local copies, waits for them, and re-layouts: 1.6 us -> none  [the longest x1 0.83 us: per_device(): x_lo, x_hi = exchange(masked[0], masked[-1], wide)]
    pallas_call x9 -> x11, Pallas kernels: 61 us -> 62.2 us  [call(): pl.pallas_call(kernel, out_shape=shapes, in_specs=in_specs, out_specs=[vm...]
  transfers between devices with their start and end apart: 20 -> 18, of which waited for: 12 -> 13; matrix products, arithmetic and copies ran while one was open for 2% -> 0% of each run, Pallas kernels for 9% -> 10%
where the time goes in v3:
time: 116 us
  Pallas kernels  62.2 us (54%)
  starting transfers between devices  28 us (24%)
  waiting for transfers between devices  22.8 us (20%)
  local copies, waits for them, and re-layouts  2.66 us (2%)
    pallas_call x11, Pallas kernels, call(): pl.pallas_call(kernel, out_shape=shapes, in_specs=in_specs, out_specs=[vm...  62.2 us
    ppermute x14, starting transfers between devices, flipped(): lax.ppermute(array, axis, [(i, i ^ distance) for i in range(lax.axis_size...  23.5 us
    ppermute x14, waiting for transfers between devices, flipped(): lax.ppermute(array, axis, [(i, i ^ distance) for i in range(lax.axis_size...  22.8 us
    ppermute x2, starting transfers between devices, pair_exchange(): lax.ppermute(first, axis, swaps[0])  3.12 us
    unnamed x32, local copies, waits for them, and re-layouts  2.57 us
  transfers between devices with their start and end apart: 18, of which 13 were waited for; matrix products, arithmetic and copies ran while one was open for 0% of the time, Pallas kernels for 10%

profile of v3, /device:TPU:0, one launch (start us, length us, event | category | flops | bytes accessed | tf_op | source)
XLA Modules:
  0.0 116.0 jit_solution(11383788122782223042)
XLA Ops:
  0.0 0.1 stack.20.position
  0.1 1.7 %copy-done.1 = bf16[8,16,16,512]{3,2,1,0:T(8,128)(2,1)S(1)} copy-done((bf16[8,16,16,512]{3,2,1,0:T(8,128)(2,1)S(1)}, bf16[8,16,16,512]{3,2,1,0:T(8,128)(2,1)}, u32[]{:S(2)}) %copy-start.1) | copy-done | bytes 2097176
  1.8 0.8 copy-done.10
  2.6 2.1 %prepare.1 = (bf16[8,16,16,512]{3,2,1,0:T(8,128)(2,1)S(1)}, bf16[8,16,512]{2,1,0:T(8,128)(2,1)S(1)}, bf16[8,16,512]{2,1,0:T(8,128)(2,1)S(1)}) custom-call(s32[5]{0:T(128)S(1)} %stack.20.position, bf16[8,16,16,512]{3,2,1,0:T(8,128)(2,1)S(1)} %copy-done.1, s32[8,16,16]{2,1,0:T(8,128)S(1)} %copy-done.10), custom_call_target="tpu_custom_call" | custom-call | flops 1000000000 | bytes 2105364 | tf_op jit(solution)/shard_map/prepare/pallas_call | solution.py:415
  4.7 0.6 collective-permute-start
  5.2 0.7 collective-permute-start.1
  5.9 0.8 latent_query.1.query1_t
  6.7 0.0 copy-start.3
  6.7 0.0 copy-start.4
  6.7 0.0 copy-start.5
  6.7 0.0 copy-start.11
  6.8 0.6 edge.1
  7.3 2.6 %collective-permute-start.2 = (bf16[18,16,512]{2,1,0:T(8,128)(2,1)S(1)}, bf16[18,16,512]{2,1,0:T(8,128)(2,1)S(1)}, u32[]{:S(2)}, u32[]{:S(2)}) collective-permute-start(bf16[18,16,512]{2,1,0:T(8,128)(2,1)S(1)} %get-tuple-element.27), channel_id=1, source_target_pairs={{0,4},{4,0},{8,12},{12,8},{16,20},{20,16},{24,28},{28,24},{1,5},{5... | collective-permute-start | bytes 884744 | tf_op jit(solution)/shard_map/ppermute | solution.py:434
  9.9 0.7 collective-permute-start.3
  10.6 10.3 %inner.1 = (bf16[1536,512]{1,0:T(8,128)(2,1)S(1)}, bf16[8,80,1536]{2,1,0:T(8,128)(2,1)S(1)}, bf16[512,2048]{1,0:T(8,128)(2,1)S(1)}) custom-call(s32[5]{0:T(128)S(1)} %stack.20.position, bf16[8,16,16,512]{3,2,1,0:T(8,128)(2,1)S(1)} %get-tuple-element.24.masked, bf16[8,16,512]{2,1,0:T(8,128)(2,1)S(1)} %collective-permute-done.y_first, ...), custom_call_target="tpu_custom_call" | custom-call | flops 10000000000 | bytes 3987476 | tf_op jit(solution)/shard_map/inner/pallas_call | solution.py:415
  21.0 22.3 %read.1 = (bf16[512,2048]{1,0:T(8,128)(2,1)S(1)}, bf16[4,560,128]{2,1,0:T(8,128)(2,1)S(1)}, bf16[4,560,128]{2,1,0:T(8,128)(2,1)S(1)}) custom-call(s32[5]{0:T(128)S(1)} %stack.20.position, bf16[8,16,16,512]{3,2,1,0:T(8,128)(2,1)S(1)} %get-tuple-element.24.masked, ...), custom_call_target="tpu_custom_call", output_to_operand_aliasing={{0}: (13, {})} | custom-call | flops 20000000000 | bytes 11261972 | tf_op jit(solution)/shard_map/read/pallas_call | solution.py:415
  43.3 0.0 copy-start.14
  43.3 5.3 %collective-permute-start.4 = (bf16[4,560,128]{2,1,0:T(8,128)(2,1)S(1)}, bf16[4,560,128]{2,1,0:T(8,128)(2,1)S(1)}, u32[]{:S(2)}, u32[]{:S(2)}) collective-permute-start(bf16[4,560,128]{2,1,0:T(8,128)(2,1)S(1)} %get-tuple-element.33), channel_id=1, source_target_pairs={{0,1},{1,0},{2,3},{3,2},{4,5},{5,4},{6,7},{7,6},{8,9},{9,8},{10,11... | collective-permute-start | bytes 1720328 | tf_op jit(solution)/shard_map/ppermute | solution.py:438
  48.6 1.6 %collective-permute-done.4.taken = bf16[4,560,128]{2,1,0:T(8,128)(2,1)S(1)} collective-permute-done((bf16[4,560,128]{2,1,0:T(8,128)(2,1)S(1)}, bf16[4,560,128]{2,1,0:T(8,128)(2,1)S(1)}, u32[]{:S(2)}, u32[]{:S(2)}) %collective-permute-start.4) | collective-permute-done | bytes 573472 | tf_op jit(solution)/shard_map/ppermute | solution.py:438
  50.2 0.8 merge_pair.1
  51.0 0.0 copy-start.6
  51.0 1.5 %collective-permute-start.5 = (bf16[560,128]{1,0:T(8,128)(2,1)S(1)}, bf16[560,128]{1,0:T(8,128)(2,1)S(1)}, u32[]{:S(2)}, u32[]{:S(2)}) collective-permute-start(bf16[560,128]{1,0:T(8,128)(2,1)S(1)} %get-tuple-element.35), channel_id=1, source_target_pairs={{0,2},{2,0},{4,6},{6,4},{1,3},{3,1},{5,7},{7,5},{8,10},{10,8},{12,... | collective-permute-start | bytes 430088 | tf_op jit(solution)/shard_map/ppermute | solution.py:438
  52.5 4.3 %collective-permute-start.6 = (bf16[560,128]{1,0:T(8,128)(2,1)S(1)}, bf16[560,128]{1,0:T(8,128)(2,1)S(1)}, u32[]{:S(2)}, u32[]{:S(2)}) collective-permute-start(bf16[560,128]{1,0:T(8,128)(2,1)S(1)} %get-tuple-element.36), channel_id=1, source_target_pairs={{0,4},{2,6},{4,0},{6,2},{1,5},{3,7},{5,1},{7,3},{8,12},{10,14},{12... | collective-permute-start | bytes 430088 | tf_op jit(solution)/shard_map/ppermute | solution.py:438
  56.8 0.3 collective-permute-done.5.refs_1_
  57.1 4.3 %collective-permute-done.6.refs_2_ = bf16[560,128]{1,0:T(8,128)(2,1)S(1)} collective-permute-done((bf16[560,128]{1,0:T(8,128)(2,1)S(1)}, bf16[560,128]{1,0:T(8,128)(2,1)S(1)}, u32[]{:S(2)}, u32[]{:S(2)}) %collective-permute-start.6) | collective-permute-done | bytes 143392 | tf_op jit(solution)/shard_map/ppermute | solution.py:438
  61.4 2.2 %collective-permute-done.7.refs_3_ = bf16[560,128]{1,0:T(8,128)(2,1)S(1)} collective-permute-done((bf16[560,128]{1,0:T(8,128)(2,1)S(1)}, bf16[560,128]{1,0:T(8,128)(2,1)S(1)}, u32[]{:S(2)}, u32[]{:S(2)}) %collective-permute-start.7) | collective-permute-done | bytes 143392 | tf_op jit(solution)/shard_map/ppermute | solution.py:438
  63.7 0.8 merge_group.1
  64.4 2.8 %collective-permute-start.10 = (bf16[32,640]{1,0:T(8,128)(2,1)S(1)}, bf16[32,640]{1,0:T(8,128)(2,1)S(1)}, u32[]{:S(2)}, u32[]{:S(2)}) collective-permute-start(bf16[32,640]{1,0:T(8,128)(2,1)S(1)} %get-tuple-element.41), channel_id=1, source_target_pairs={{0,24},{8,16},{16,8},{24,0},{1,25},{9,17},{17,9},{25,1},{2,26},{10... | collective-permute-start | bytes 122888 | tf_op jit(solution)/shard_map/ppermute | solution.py:438
  67.2 0.4 collective-permute-start.8
  67.6 1.2 %collective-permute-start.9 = (bf16[32,640]{1,0:T(8,128)(2,1)S(1)}, bf16[32,640]{1,0:T(8,128)(2,1)S(1)}, u32[]{:S(2)}, u32[]{:S(2)}) collective-permute-start(bf16[32,640]{1,0:T(8,128)(2,1)S(1)} %get-tuple-element.40), channel_id=1, source_target_pairs={{0,16},{8,24},{16,0},{24,8},{1,17},{9,25},{17,1},{25,9},{2,18},{10... | collective-permute-start | bytes 122888 | tf_op jit(solution)/shard_map/ppermute | solution.py:438
  68.9 1.4 %collective-permute-done.10.refs_3_ = bf16[32,640]{1,0:T(8,128)(2,1)S(1)} collective-permute-done((bf16[32,640]{1,0:T(8,128)(2,1)S(1)}, bf16[32,640]{1,0:T(8,128)(2,1)S(1)}, u32[]{:S(2)}, u32[]{:S(2)}) %collective-permute-start.10) | collective-permute-done | bytes 40992 | tf_op jit(solution)/shard_map/ppermute | solution.py:438
  70.3 0.9 collective-permute-done.8.refs_1_
  71.2 1.3 %collective-permute-done.9.refs_2_ = bf16[32,640]{1,0:T(8,128)(2,1)S(1)} collective-permute-done((bf16[32,640]{1,0:T(8,128)(2,1)S(1)}, bf16[32,640]{1,0:T(8,128)(2,1)S(1)}, u32[]{:S(2)}, u32[]{:S(2)}) %collective-permute-start.9) | collective-permute-done | bytes 40992 | tf_op jit(solution)/shard_map/ppermute | solution.py:438
  72.6 0.5 update.1.refs_0_
  73.1 1.6 %collective-permute-start.11 = (bf16[32,512]{1,0:T(8,128)(2,1)S(1)}, bf16[32,512]{1,0:T(8,128)(2,1)S(1)}, u32[]{:S(2)}, u32[]{:S(2)}) collective-permute-start(bf16[32,512]{1,0:T(8,128)(2,1)S(1)} %update.1.refs_0_), channel_id=1, source_target_pairs={{0,8},{8,0},{16,24},{24,16},{1,9},{9,1},{17,25},{25,17},{2,10},{10... | collective-permute-start | bytes 98312 | tf_op jit(solution)/shard_map/ppermute | solution.py:438
  74.7 0.3 collective-permute-start.12
  75.0 2.5 %collective-permute-start.13 = (bf16[32,512]{1,0:T(8,128)(2,1)S(1)}, bf16[32,512]{1,0:T(8,128)(2,1)S(1)}, u32[]{:S(2)}, u32[]{:S(2)}) collective-permute-start(bf16[32,512]{1,0:T(8,128)(2,1)S(1)} %update.1.refs_0_), channel_id=1, source_target_pairs={{0,24},{8,16},{16,8},{24,0},{1,25},{9,17},{17,9},{25,1},{2,26},{10... | collective-permute-start | bytes 98312 | tf_op jit(solution)/shard_map/ppermute | solution.py:438
  77.5 2.2 %collective-permute-done.12.refs_2_ = bf16[32,512]{1,0:T(8,128)(2,1)S(1)} collective-permute-done((bf16[32,512]{1,0:T(8,128)(2,1)S(1)}, bf16[32,512]{1,0:T(8,128)(2,1)S(1)}, u32[]{:S(2)}, u32[]{:S(2)}) %collective-permute-start.12) | collective-permute-done | bytes 32800 | tf_op jit(solution)/shard_map/ppermute | solution.py:438
  79.7 1.0 collective-permute-done.13.refs_3_
  80.8 1.5 %collective-permute-start.14 = (bf16[128,512]{1,0:T(8,128)(2,1)S(1)}, bf16[128,512]{1,0:T(8,128)(2,1)S(1)}, u32[]{:S(2)}, u32[]{:S(2)}) collective-permute-start(bf16[128,512]{1,0:T(8,128)(2,1)S(1)} %join_far.1.refs_0_), channel_id=1, source_target_pairs={{0,2},{2,0},{4,6},{6,4},{1,3},{3,1},{5,7},{7,5},{8,10},{10,8},{12,... | collective-permute-start | bytes 393224 | tf_op jit(solution)/shard_map/ppermute | solution.py:438
  82.3 1.7 %collective-permute-start.15 = (bf16[128,512]{1,0:T(8,128)(2,1)S(1)}, bf16[128,512]{1,0:T(8,128)(2,1)S(1)}, u32[]{:S(2)}, u32[]{:S(2)}) collective-permute-start(bf16[128,512]{1,0:T(8,128)(2,1)S(1)} %join_far.1.refs_0_), channel_id=1, source_target_pairs={{0,4},{2,6},{4,0},{6,2},{1,5},{3,7},{5,1},{7,3},{8,12},{10,14},{12... | collective-permute-start | bytes 393224 | tf_op jit(solution)/shard_map/ppermute | solution.py:438
  84.0 0.3 collective-permute-start.16
  84.3 2.1 %collective-permute-done.14.refs_1_ = bf16[128,512]{1,0:T(8,128)(2,1)S(1)} collective-permute-done((bf16[128,512]{1,0:T(8,128)(2,1)S(1)}, bf16[128,512]{1,0:T(8,128)(2,1)S(1)}, u32[]{:S(2)}, u32[]{:S(2)}) %collective-permute-start.14) | collective-permute-done | bytes 131104 | tf_op jit(solution)/shard_map/ppermute | solution.py:438
  86.4 0.8 collective-permute-done.15.refs_2_
  87.2 2.6 %collective-permute-done.16.refs_3_ = bf16[128,512]{1,0:T(8,128)(2,1)S(1)} collective-permute-done((bf16[128,512]{1,0:T(8,128)(2,1)S(1)}, bf16[128,512]{1,0:T(8,128)(2,1)S(1)}, u32[]{:S(2)}, u32[]{:S(2)}) %collective-permute-start.16) | collective-permute-done | bytes 131104 | tf_op jit(solution)/shard_map/ppermute | solution.py:438
  89.9 0.1 collective-permute-start.17
  90.0 1.9 %collective-permute-done.17.other_state = bf16[512,512]{1,0:T(8,128)(2,1)S(1)} collective-permute-done((bf16[512,512]{1,0:T(8,128)(2,1)S(1)}, bf16[512,512]{1,0:T(8,128)(2,1)S(1)}, u32[]{:S(2)}, u32[]{:S(2)}) %collective-permute-start.17) | collective-permute-done | bytes 524320 | tf_op jit(solution)/shard_map/ppermute | solution.py:438
  91.9 24.0 %write.1 = f32[2048,512]{1,0:T(8,128)} custom-call(bf16[512,512]{1,0:T(8,128)(2,1)S(1)} %join_group.1.own_state, bf16[512,512]{1,0:T(8,128)(2,1)S(1)} %collective-permute-done.17.other_state, bf16[512,2048]{1,0:T(8,128)(2,1)S(1)} %copy-done.15, bf16[2048,512]{1,0:T(8,128)(2,1)S(1)} %bitcast.6, bf16[512,512]{1,0:T(8,128)(2,1)S(1)} %copy-done.7, ...), custom_call_target="tpu_custom_call" | custom-call | flops 20000000000 | bytes 6815744 | tf_op jit(solution)/shard_map/write/pallas_call | solution.py:415
  (33 shorter events, 0.1 us)
Async XLA Ops:
  0.0 5.9 %copy-start = (bf16[1024,512]{1,0:T(8,128)(2,1)S(1)}, bf16[1024,512]{1,0:T(8,128)(2,1)}, u32[]{:S(2)}) copy-start(bf16[1024,512]{1,0:T(8,128)(2,1)} %latents.1) | copy-start | bytes 3145732
  0.1 1.7 %copy-start.1 = (bf16[8,16,16,512]{3,2,1,0:T(8,128)(2,1)S(1)}, bf16[8,16,16,512]{3,2,1,0:T(8,128)(2,1)}, u32[]{:S(2)}) copy-start(bf16[8,16,16,512]{3,2,1,0:T(8,128)(2,1)} %flow.1) | copy-start | bytes 6291460
  1.8 0.8 copy-start.10
  2.6 3.3 %copy-start.2 = (bf16[512,512]{1,0:T(8,128)(2,1)S(1)}, bf16[512,512]{1,0:T(8,128)(2,1)}, u32[]{:S(2)}) copy-start(bf16[512,512]{1,0:T(8,128)(2,1)} %w_query1.1) | copy-start | bytes 1572868
  4.7 16.3 %copy-start.12 = (bf16[8,16,16,512]{3,2,1,0:T(8,128)(2,1)}, bf16[8,16,16,512]{3,2,1,0:T(8,128)(2,1)S(1)}, u32[]{:S(2)}) copy-start(bf16[8,16,16,512]{3,2,1,0:T(8,128)(2,1)S(1)} %get-tuple-element.24.masked) | copy-start | bytes 6291460
  4.7 2.0 %collective-permute-start = (bf16[8,16,512]{2,1,0:T(8,128)(2,1)S(1)}, bf16[8,16,512]{2,1,0:T(8,128)(2,1)S(1)}, u32[]{:S(2)}, u32[]{:S(2)}) collective-permute-start(bf16[8,16,512]{2,1,0:T(8,128)(2,1)S(1)} %get-tuple-element.25), channel_id=1, source_target_pairs={{0,1},{1,0},{2,3},{3,2},{4,5},{5,4},{6,7},{7,6},{8,9},{9,8},{10,11... | collective-permute-start | bytes 393224 | tf_op jit(solution)/shard_map/ppermute | solution.py:434
  5.2 1.5 %collective-permute-start.1 = (bf16[8,16,512]{2,1,0:T(8,128)(2,1)S(1)}, bf16[8,16,512]{2,1,0:T(8,128)(2,1)S(1)}, u32[]{:S(2)}, u32[]{:S(2)}) collective-permute-start(bf16[8,16,512]{2,1,0:T(8,128)(2,1)S(1)} %get-tuple-element.26), channel_id=1, source_target_pairs={{1,2},{2,1},{5,6},{6,5},{9,10},{10,9},{13,14},{14,13},{17,18},{18,... | collective-permute-start | bytes 393224 | tf_op jit(solution)/shard_map/ppermute | solution.py:434
  6.7 3.9 %copy-start.3 = (bf16[512,512]{1,0:T(8,128)(2,1)S(1)}, bf16[512,512]{1,0:T(8,128)(2,1)}, u32[]{:S(2)}) copy-start(bf16[512,512]{1,0:T(8,128)(2,1)} %w_key1.1) | copy-start | bytes 1572868
  6.7 3.9 %copy-start.4 = (bf16[512,512]{1,0:T(8,128)(2,1)S(1)}, bf16[512,512]{1,0:T(8,128)(2,1)}, u32[]{:S(2)}) copy-start(bf16[512,512]{1,0:T(8,128)(2,1)} %w_value1.1) | copy-start | bytes 1572868
  6.7 3.9 %copy-start.5 = (bf16[512,512]{1,0:T(8,128)(2,1)S(1)}, bf16[512,512]{1,0:T(8,128)(2,1)}, u32[]{:S(2)}) copy-start(bf16[512,512]{1,0:T(8,128)(2,1)} %w_query2.1) | copy-start | bytes 1572868
  6.7 3.9 %copy-start.11 = (f32[27,512]{1,0:T(8,128)S(1)}, f32[27,512]{1,0:T(8,128)}, u32[]{:S(2)}) copy-start(f32[27,512]{1,0:T(8,128)} %conv.3) | copy-start | bytes 165892
  7.3 13.6 %collective-permute-start.2 = (bf16[18,16,512]{2,1,0:T(8,128)(2,1)S(1)}, bf16[18,16,512]{2,1,0:T(8,128)(2,1)S(1)}, u32[]{:S(2)}, u32[]{:S(2)}) collective-permute-start(bf16[18,16,512]{2,1,0:T(8,128)(2,1)S(1)} %get-tuple-element.27), channel_id=1, source_target_pairs={{0,4},{4,0},{8,12},{12,8},{16,20},{20,16},{24,28},{28,24},{1,5},{5... | collective-permute-start | bytes 884744 | tf_op jit(solution)/shard_map/ppermute | solution.py:434
  9.9 11.0 %collective-permute-start.3 = (bf16[18,16,512]{2,1,0:T(8,128)(2,1)S(1)}, bf16[18,16,512]{2,1,0:T(8,128)(2,1)S(1)}, u32[]{:S(2)}, u32[]{:S(2)}) collective-permute-start(bf16[18,16,512]{2,1,0:T(8,128)(2,1)S(1)} %get-tuple-element.28), channel_id=1, source_target_pairs={{4,8},{8,4},{12,16},{16,12},{20,24},{24,20},{5,9},{9,5},{13,17},{1... | collective-permute-start | bytes 884744 | tf_op jit(solution)/shard_map/ppermute | solution.py:434
  43.3 13.5 %copy-start.14 = (bf16[512,2048]{1,0:T(8,128)(2,1)}, bf16[512,2048]{1,0:T(8,128)(2,1)S(1)}, u32[]{:S(2)}) copy-start(bf16[512,2048]{1,0:T(8,128)(2,1)S(1)} %get-tuple-element.42.query2_t) | copy-start | bytes 6291460
  43.3 6.9 %collective-permute-start.4 = (bf16[4,560,128]{2,1,0:T(8,128)(2,1)S(1)}, bf16[4,560,128]{2,1,0:T(8,128)(2,1)S(1)}, u32[]{:S(2)}, u32[]{:S(2)}) collective-permute-start(bf16[4,560,128]{2,1,0:T(8,128)(2,1)S(1)} %get-tuple-element.33), channel_id=1, source_target_pairs={{0,1},{1,0},{2,3},{3,2},{4,5},{5,4},{6,7},{7,6},{8,9},{9,8},{10,11... | collective-permute-start | bytes 1720328 | tf_op jit(solution)/shard_map/ppermute | solution.py:438
  51.0 21.5 %copy-start.6 = (bf16[512,512]{1,0:T(8,128)(2,1)S(1)}, bf16[512,512]{1,0:T(8,128)(2,1)}, u32[]{:S(2)}) copy-start(bf16[512,512]{1,0:T(8,128)(2,1)} %w_out1.1) | copy-start | bytes 1572868
  51.0 6.1 %collective-permute-start.5 = (bf16[560,128]{1,0:T(8,128)(2,1)S(1)}, bf16[560,128]{1,0:T(8,128)(2,1)S(1)}, u32[]{:S(2)}, u32[]{:S(2)}) collective-permute-start(bf16[560,128]{1,0:T(8,128)(2,1)S(1)} %get-tuple-element.35), channel_id=1, source_target_pairs={{0,2},{2,0},{4,6},{6,4},{1,3},{3,1},{5,7},{7,5},{8,10},{10,8},{12,... | collective-permute-start | bytes 430088 | tf_op jit(solution)/shard_map/ppermute | solution.py:438
  52.5 8.9 %collective-permute-start.6 = (bf16[560,128]{1,0:T(8,128)(2,1)S(1)}, bf16[560,128]{1,0:T(8,128)(2,1)S(1)}, u32[]{:S(2)}, u32[]{:S(2)}) collective-permute-start(bf16[560,128]{1,0:T(8,128)(2,1)S(1)} %get-tuple-element.36), channel_id=1, source_target_pairs={{0,4},{2,6},{4,0},{6,2},{1,5},{3,7},{5,1},{7,3},{8,12},{10,14},{12... | collective-permute-start | bytes 430088 | tf_op jit(solution)/shard_map/ppermute | solution.py:438
  56.8 6.8 %collective-permute-start.7 = (bf16[560,128]{1,0:T(8,128)(2,1)S(1)}, bf16[560,128]{1,0:T(8,128)(2,1)S(1)}, u32[]{:S(2)}, u32[]{:S(2)}) collective-permute-start(bf16[560,128]{1,0:T(8,128)(2,1)S(1)} %get-tuple-element.37), channel_id=1, source_target_pairs={{0,6},{2,4},{4,2},{6,0},{1,7},{3,5},{5,3},{7,1},{8,14},{10,12},{12... | collective-permute-start | bytes 430088 | tf_op jit(solution)/shard_map/ppermute | solution.py:438
  63.7 28.3 %copy-start.15 = (bf16[512,2048]{1,0:T(8,128)(2,1)S(1)}, bf16[512,2048]{1,0:T(8,128)(2,1)}, u32[]{:S(2)}) copy-start(bf16[512,2048]{1,0:T(8,128)(2,1)} %copy-done.14) | copy-start | bytes 6291460
  64.4 5.9 %collective-permute-start.10 = (bf16[32,640]{1,0:T(8,128)(2,1)S(1)}, bf16[32,640]{1,0:T(8,128)(2,1)S(1)}, u32[]{:S(2)}, u32[]{:S(2)}) collective-permute-start(bf16[32,640]{1,0:T(8,128)(2,1)S(1)} %get-tuple-element.41), channel_id=1, source_target_pairs={{0,24},{8,16},{16,8},{24,0},{1,25},{9,17},{17,9},{25,1},{2,26},{10... | collective-permute-start | bytes 122888 | tf_op jit(solution)/shard_map/ppermute | solution.py:438
  67.2 4.0 %collective-permute-start.8 = (bf16[32,640]{1,0:T(8,128)(2,1)S(1)}, bf16[32,640]{1,0:T(8,128)(2,1)S(1)}, u32[]{:S(2)}, u32[]{:S(2)}) collective-permute-start(bf16[32,640]{1,0:T(8,128)(2,1)S(1)} %get-tuple-element.39), channel_id=1, source_target_pairs={{0,8},{8,0},{16,24},{24,16},{1,9},{9,1},{17,25},{25,17},{2,10},{10... | collective-permute-start | bytes 122888 | tf_op jit(solution)/shard_map/ppermute | solution.py:438
  67.6 4.9 %collective-permute-start.9 = (bf16[32,640]{1,0:T(8,128)(2,1)S(1)}, bf16[32,640]{1,0:T(8,128)(2,1)S(1)}, u32[]{:S(2)}, u32[]{:S(2)}) collective-permute-start(bf16[32,640]{1,0:T(8,128)(2,1)S(1)} %get-tuple-element.40), channel_id=1, source_target_pairs={{0,16},{8,24},{16,0},{24,8},{1,17},{9,25},{17,1},{25,9},{2,18},{10... | collective-permute-start | bytes 122888 | tf_op jit(solution)/shard_map/ppermute | solution.py:438
  72.5 19.4 %copy-start.7 = (bf16[512,512]{1,0:T(8,128)(2,1)S(1)}, bf16[512,512]{1,0:T(8,128)(2,1)}, u32[]{:S(2)}) copy-start(bf16[512,512]{1,0:T(8,128)(2,1)} %w_key2.1) | copy-start | bytes 1572868
  72.5 19.4 %copy-start.8 = (bf16[512,512]{1,0:T(8,128)(2,1)S(1)}, bf16[512,512]{1,0:T(8,128)(2,1)}, u32[]{:S(2)}) copy-start(bf16[512,512]{1,0:T(8,128)(2,1)} %w_value2.1) | copy-start | bytes 1572868
  72.5 19.4 %copy-start.9 = (bf16[512,512]{1,0:T(8,128)(2,1)S(1)}, bf16[512,512]{1,0:T(8,128)(2,1)}, u32[]{:S(2)}) copy-start(bf16[512,512]{1,0:T(8,128)(2,1)} %w_out2.1) | copy-start | bytes 1572868
  72.5 19.4 %copy-start.13 = (bf16[8,16,16,512]{3,2,1,0:T(8,128)(2,1)S(1)}, bf16[8,16,16,512]{3,2,1,0:T(8,128)(2,1)}, u32[]{:S(2)}) copy-start(bf16[8,16,16,512]{3,2,1,0:T(8,128)(2,1)} %copy-done.12) | copy-start | bytes 6291460
  73.1 4.4 %collective-permute-start.11 = (bf16[32,512]{1,0:T(8,128)(2,1)S(1)}, bf16[32,512]{1,0:T(8,128)(2,1)S(1)}, u32[]{:S(2)}, u32[]{:S(2)}) collective-permute-start(bf16[32,512]{1,0:T(8,128)(2,1)S(1)} %update.1.refs_0_), channel_id=1, source_target_pairs={{0,8},{8,0},{16,24},{24,16},{1,9},{9,1},{17,25},{25,17},{2,10},{10... | collective-permute-start | bytes 98312 | tf_op jit(solution)/shard_map/ppermute | solution.py:438
  74.7 5.0 %collective-permute-start.12 = (bf16[32,512]{1,0:T(8,128)(2,1)S(1)}, bf16[32,512]{1,0:T(8,128)(2,1)S(1)}, u32[]{:S(2)}, u32[]{:S(2)}) collective-permute-start(bf16[32,512]{1,0:T(8,128)(2,1)S(1)} %update.1.refs_0_), channel_id=1, source_target_pairs={{0,16},{8,24},{16,0},{24,8},{1,17},{9,25},{17,1},{25,9},{2,18},{10... | collective-permute-start | bytes 98312 | tf_op jit(solution)/shard_map/ppermute | solution.py:438
  75.0 5.7 %collective-permute-start.13 = (bf16[32,512]{1,0:T(8,128)(2,1)S(1)}, bf16[32,512]{1,0:T(8,128)(2,1)S(1)}, u32[]{:S(2)}, u32[]{:S(2)}) collective-permute-start(bf16[32,512]{1,0:T(8,128)(2,1)S(1)} %update.1.refs_0_), channel_id=1, source_target_pairs={{0,24},{8,16},{16,8},{24,0},{1,25},{9,17},{17,9},{25,1},{2,26},{10... | collective-permute-start | bytes 98312 | tf_op jit(solution)/shard_map/ppermute | solution.py:438
  80.8 5.7 %collective-permute-start.14 = (bf16[128,512]{1,0:T(8,128)(2,1)S(1)}, bf16[128,512]{1,0:T(8,128)(2,1)S(1)}, u32[]{:S(2)}, u32[]{:S(2)}) collective-permute-start(bf16[128,512]{1,0:T(8,128)(2,1)S(1)} %join_far.1.refs_0_), channel_id=1, source_target_pairs={{0,2},{2,0},{4,6},{6,4},{1,3},{3,1},{5,7},{7,5},{8,10},{10,8},{12,... | collective-permute-start | bytes 393224 | tf_op jit(solution)/shard_map/ppermute | solution.py:438
  82.3 5.0 %collective-permute-start.15 = (bf16[128,512]{1,0:T(8,128)(2,1)S(1)}, bf16[128,512]{1,0:T(8,128)(2,1)S(1)}, u32[]{:S(2)}, u32[]{:S(2)}) collective-permute-start(bf16[128,512]{1,0:T(8,128)(2,1)S(1)} %join_far.1.refs_0_), channel_id=1, source_target_pairs={{0,4},{2,6},{4,0},{6,2},{1,5},{3,7},{5,1},{7,3},{8,12},{10,14},{12... | collective-permute-start | bytes 393224 | tf_op jit(solution)/shard_map/ppermute | solution.py:438
  84.0 5.9 %collective-permute-start.16 = (bf16[128,512]{1,0:T(8,128)(2,1)S(1)}, bf16[128,512]{1,0:T(8,128)(2,1)S(1)}, u32[]{:S(2)}, u32[]{:S(2)}) collective-permute-start(bf16[128,512]{1,0:T(8,128)(2,1)S(1)} %join_far.1.refs_0_), channel_id=1, source_target_pairs={{0,6},{2,4},{4,2},{6,0},{1,7},{3,5},{5,3},{7,1},{8,14},{10,12},{12... | collective-permute-start | bytes 393224 | tf_op jit(solution)/shard_map/ppermute | solution.py:438
  89.9 2.0 %collective-permute-start.17 = (bf16[512,512]{1,0:T(8,128)(2,1)S(1)}, bf16[512,512]{1,0:T(8,128)(2,1)S(1)}, u32[]{:S(2)}, u32[]{:S(2)}) collective-permute-start(bf16[512,512]{1,0:T(8,128)(2,1)S(1)} %join_group.1.own_state), channel_id=1, source_target_pairs={{0,1},{1,0},{2,3},{3,2},{4,5},{5,4},{6,7},{7,6},{8,9},{9,8},{10,11... | collective-permute-start | bytes 1572872 | tf_op jit(solution)/shard_map/ppermute | solution.py:438

commit v4 on v3

--- a/solution.py
+++ b/solution.py
@@ -21,19 +21,39 @@
     return lax.dot_general(left, right, (contract, ((), ())), preferred_element_type=F32)
 
 
-def prepare_kernel(position, flow, mask, masked, first, second):
-    size_x, size_y, size_z, width = flow.shape
+def masked_column(flow, mask_plane, i, j):
+    size_z, width = flow.shape[2:]
+    column = jnp.broadcast_to(mask_plane[:, j : j + 1], (size_z, LANES)).astype(BF16)
+    tiles = [flow[i, j, :, k * LANES : (k + 1) * LANES] * column for k in range(width // LANES)]
+    return jnp.concatenate(tiles, axis=1)
+
+
+def face_kernel(position, flow, far_mask, first, second, low, high, mask, arrived):
+    size_x, size_y = flow.shape[:2]
+    copies = []
+    for n, (j, target) in enumerate(((0, low), (size_y - 1, high))):
+        copies.append(pltpu.make_async_copy(flow.at[:, pl.ds(j, 1)], target, arrived.at[n]))
+        copies[-1].start()
+    copies.append(pltpu.make_async_copy(far_mask, mask, arrived.at[2]))
+    copies[-1].start()
+    for copy in copies:
+        copy.wait()
+    odd = position[3] == 1
+    for i in range(size_x):
+        turned = mask[i].astype(F32).T
+        bottom = masked_column(low, turned, i, 0)
+        top = masked_column(high, turned[:, size_y - 1 :], i, 0)
+        first[i] = jnp.where(odd, bottom, top)
+        second[i] = jnp.where(odd, top, bottom)
+
+
+def prepare_kernel(flow, mask, masked):
+    size_x, size_y = flow.shape[:2]
 
     def plane(i, carry):
         turned = mask[i].astype(F32).T
         for j in range(size_y):
-            column = jnp.broadcast_to(turned[:, j : j + 1], (size_z, LANES)).astype(BF16)
-            for tile in range(width // LANES):
-                lanes = slice(tile * LANES, (tile + 1) * LANES)
-                masked[i, j, :, lanes] = flow[i, j, :, lanes] * column
-        outer = size_y - 1
-        first[i] = masked[i, outer * (1 - position[3])]
-        second[i] = masked[i, outer * position[3]]
+            masked[i, j] = masked_column(flow, turned, i, j)
         return carry
 
     lax.fori_loop(0, size_x, plane, 0)
@@ -374,7 +394,20 @@
 
 
 def write_kernel(
-    own_state, other_state, query2_t, masked, w_key2, w_value2, w_out2, out, keys, values_t, scores, read_t
+    own_state,
+    other_state,
+    query2_t,
+    masked,
+    w_key2,
+    w_value2,
+    w_out2,
+    out,
+    keys,
+    values_t,
+    scores,
+    read_t,
+    buffers,
+    sent,
 ):
     half, width = own_state.shape
     head_size = width // HEADS
@@ -385,25 +418,33 @@
         value_t = dot(w_value2[...], state[...], ((0,), (1,))).astype(BF16)
         values_t[:, :head_size, rows] = value_t.reshape(HEADS, head_size, half)
     span = scores.shape[2]
+    blocks = out.shape[0] // span
+    last_pair = width // LANES - 1
+
+    def send(block):
+        slot = block % 2
+        rows = pl.ds(pl.multiple_of(block * span, span), span)
+        return pltpu.make_async_copy(buffers.at[slot], out.at[rows, :], sent.at[slot])
 
     def finish(pair, block, sums, tops):
-        columns = pl.ds(pl.multiple_of(block * span, span), span)
         both = [part[:head_size] / part[head_size : head_size + 1] for part in sums]
         rows = pl.ds(pl.multiple_of(pair * LANES, LANES), LANES)
-        read_t[rows, columns] = jnp.concatenate(both, axis=0).astype(BF16)
+        read_t[rows, :] = jnp.concatenate(both, axis=0).astype(BF16)
+
+        @pl.when(pair == last_pair)
+        def _():
+            pl.when(block >= 2)(lambda: send(block - 2).wait())
+            cells = pl.ds(pl.multiple_of(block * span, span), span)
+            change = dot(read_t[...], w_out2[...], ((0,), (0,)))
+            buffers[block % 2] = masked[cells, :].astype(F32) + change
+            send(block).start()
 
     attention_loop([keys], query2_t, [values_t], scores, 256, finish)
-
-    def emit(r, carry):
-        rows = pl.ds(pl.multiple_of(r * span, span), span)
-        change = dot(read_t[:, rows], w_out2[...], ((0,), (0,)))
-        out[rows, :] = masked[rows, :].astype(F32) + change
-        return carry
-
-    lax.fori_loop(0, out.shape[0] // span, emit, 0)
-
-
-def call(kernel, shapes, scratch, operands, limit, flops, name, position=None, far=(), aliases=None):
+    for block in range(max(blocks - 2, 0), blocks):
+        send(block).wait()
+
+
+def call(kernel, shapes, scratch, operands, limit, flops, name, position=None, far=(), aliases=None, out_space=pltpu.VMEM):
     vmem = pl.BlockSpec(memory_space=pltpu.VMEM)
     hbm = pl.BlockSpec(memory_space=pltpu.HBM)
     many = isinstance(shapes, (list, tuple))
@@ -416,7 +457,7 @@
         kernel,
         out_shape=shapes,
         in_specs=in_specs,
-        out_specs=[vmem] * len(shapes) if many else vmem,
+        out_specs=[vmem] * len(shapes) if many else pl.BlockSpec(memory_space=out_space),
         scratch_shapes=scratch,
         compiler_params=pltpu.CompilerParams(vmem_limit_bytes=limit * MIB),
         cost_estimate=pl.CostEstimate(flops=int(flops), bytes_accessed=moved, transcendentals=0),
@@ -431,7 +472,8 @@
     swaps = [[], []]
     for i in range(count - 1):
         swaps[i % 2] += [(i, i + 1), (i + 1, i)]
-    return lax.ppermute(first, axis, swaps[0]), lax.ppermute(second, axis, swaps[1])
+    other = lax.ppermute(second, axis, swaps[1])
+    return lax.ppermute(first, axis, swaps[0]), other
 
 
 def flipped(array, axis, distance):
@@ -470,17 +512,22 @@
     step = 1e9
 
     side = shape((size_x, size_z, width), BF16)
-    masked, y_first, y_second = call(
-        prepare_kernel,
-        [shape(flow_field.shape, BF16), side, side],
-        [],
+    ends = pltpu.VMEM((size_x, 1, size_z, width), BF16)
+    y_first, y_second = call(
+        face_kernel,
+        [side, side],
+        [ends, ends, pltpu.VMEM(fluid_mask.shape, jnp.int32), pltpu.SemaphoreType.DMA((3,))],
         [flow_field, fluid_mask],
-        12,
+        56,
         step,
-        "prepare",
+        "face",
         position,
+        (0, 1),
     )
     y_first, y_second = pair_exchange(y_first, y_second, narrow)
+    masked = call(
+        prepare_kernel, shape(flow_field.shape, BF16), [], [flow_field, fluid_mask], 12, 2 * step, "prepare"
+    )
     query1_t = call(
         latent_query_kernel,
         shape((width, latent_count), BF16),
@@ -526,7 +573,7 @@
             pltpu.VMEM((outer_cells, width), BF16),
             pltpu.VMEM((outer_cells, width), BF16),
             pltpu.VMEM((HEADS, head_size + ONES_ROWS, outer_cells), BF16),
-            pltpu.VMEM((2, cells, 256), F32),
+            pltpu.VMEM((2, cells, latent_count // 2), F32),
             pltpu.VMEM((STAT_ROWS, latent_count), F32),
         ],
         [
@@ -572,6 +619,7 @@
     state = join([state] + [flipped(state, "wz", d) for d in range(1, far)], "join_far")
     state = join([state] + [flipped(state, group, d) for d in range(1, group_size)], "join_group")
     other = flipped(state, "nc", 1)
+    span = 2 * plane_cells
 
     result = call(
         write_kernel,
@@ -579,13 +627,16 @@
         [
             pltpu.VMEM((latent_count, width), BF16),
             pltpu.VMEM((HEADS, head_size + ONES_ROWS, latent_count), BF16),
-            pltpu.VMEM((2, latent_count, 512), F32),
-            pltpu.VMEM((width, cells), BF16),
+            pltpu.VMEM((2, latent_count, span), F32),
+            pltpu.VMEM((width, span), BF16),
+            pltpu.VMEM((2, span, width), F32),
+            pltpu.SemaphoreType.DMA((2,)),
         ],
         [state, other, query2_t, masked.reshape(cells, width), w_key2, w_value2, w_out2],
         32,
         20 * step,
         "write",
+        out_space=pltpu.HBM,
     )
     return result.reshape(size_x, size_y, size_z, width)
 

time: 116 us -> 114 us (0.983)
  local copies, waits for them, and re-layouts: 2.66 us -> 0.67 us
  Pallas kernels: 62.2 us -> 63.6 us
  starting transfers between devices: 28 us -> 26.8 us
    unnamed x32 -> x34, local copies, waits for them, and re-layouts: 2.57 us -> 0.08 us
    pallas_call x11 -> x12, Pallas kernels: 62.2 us -> 63.6 us  [call(): pl.pallas_call(kernel, out_shape=shapes, in_specs=in_specs, out_specs=[vm...]
    ppermute x14, starting transfers between devices: 23.5 us -> 22.2 us  [flipped(): lax.ppermute(array, axis, [(i, i ^ distance) for i in range(lax.axis_size...]
  transfers between devices with their start and end apart: 18 -> 18, of which waited for: 13 -> 13; matrix products, arithmetic and copies ran while one was open for 0% -> 0% of each run, Pallas kernels for 10% -> 11%
where the time goes in v4:
time: 114 us
  Pallas kernels  63.6 us (56%)
  starting transfers between devices  26.8 us (24%)
  waiting for transfers between devices  22.8 us (20%)
    pallas_call x12, Pallas kernels, call(): pl.pallas_call(kernel, out_shape=shapes, in_specs=in_specs, out_specs=[vm...  63.6 us
    ppermute x14, waiting for transfers between devices, flipped(): lax.ppermute(array, axis, [(i, i ^ distance) for i in range(lax.axis_size...  22.8 us
    ppermute x14, starting transfers between devices, flipped(): lax.ppermute(array, axis, [(i, i ^ distance) for i in range(lax.axis_size...  22.2 us
    ppermute x2, starting transfers between devices, pair_exchange(): return (lax.ppermute(first, axis, swaps[0]), other)  3.14 us
  transfers between devices with their start and end apart: 18, of which 13 were waited for; matrix products, arithmetic and copies ran while one was open for 0% of the time, Pallas kernels for 11%

profile of v4, /device:TPU:0, one launch (start us, length us, event | category | flops | bytes accessed | tf_op | source)
XLA Modules:
  0.0 114.3 jit_solution(10322549613536907481)
XLA Ops:
  0.0 0.6 stack.20.position
  0.6 2.7 %face.1 = (bf16[8,16,512]{2,1,0:T(8,128)(2,1)}, bf16[8,16,512]{2,1,0:T(8,128)(2,1)}) custom-call(s32[5]{0:T(128)} %stack.20.position, bf16[8,16,16,512]{3,2,1,0:T(8,128)(2,1)} %flow.3, s32[8,16,16]{2,1,0:T(8,128)} %far_mask.1), custom_call_target="tpu_custom_call" | custom-call | flops 1000000000 | bytes 2105364 | tf_op jit(solution)/shard_map/face/pallas_call | solution.py:456
  3.3 0.6 collective-permute-start
  3.8 0.8 collective-permute-start.1
  4.7 1.5 %prepare.1.masked = bf16[8,16,16,512]{3,2,1,0:T(8,128)(2,1)S(1)} custom-call(bf16[8,16,16,512]{3,2,1,0:T(8,128)(2,1)S(1)} %copy-done.2, s32[8,16,16]{2,1,0:T(8,128)S(1)} %copy-done.11), custom_call_target="tpu_custom_call" | custom-call | flops 2000000000 | bytes 2105344 | tf_op jit(solution)/shard_map/prepare/pallas_call | solution.py:456
  6.2 0.8 latent_query.1.query1_t
  6.9 0.0 copy-start.4
  6.9 0.0 copy-start.5
  7.0 0.0 copy-start.6
  7.0 0.0 copy-start.12
  7.0 0.0 collective-permute-done.y_first
  7.0 0.6 edge.1
  7.6 2.6 %collective-permute-start.2 = (bf16[18,16,512]{2,1,0:T(8,128)(2,1)S(1)}, bf16[18,16,512]{2,1,0:T(8,128)(2,1)S(1)}, u32[]{:S(2)}, u32[]{:S(2)}) collective-permute-start(bf16[18,16,512]{2,1,0:T(8,128)(2,1)S(1)} %get-tuple-element.25), channel_id=1, source_target_pairs={{0,4},{4,0},{8,12},{12,8},{16,20},{20,16},{24,28},{28,24},{1,5},{5... | collective-permute-start | bytes 884744 | tf_op jit(solution)/shard_map/ppermute | solution.py:476
  10.2 0.7 collective-permute-start.3
  10.9 10.3 %inner.1 = (bf16[1536,512]{1,0:T(8,128)(2,1)S(1)}, bf16[8,80,1536]{2,1,0:T(8,128)(2,1)S(1)}, bf16[512,2048]{1,0:T(8,128)(2,1)S(1)}) custom-call(s32[5]{0:T(128)S(1)} %copy-done.1, bf16[8,16,16,512]{3,2,1,0:T(8,128)(2,1)S(1)} %prepare.1.masked, bf16[8,16,512]{2,1,0:T(8,128)(2,1)S(1)} %collective-permute-done.y_first, ...), custom_call_target="tpu_custom_call" | custom-call | flops 10000000000 | bytes 3987476 | tf_op jit(solution)/shard_map/inner/pallas_call | solution.py:456
  21.2 22.8 %read.1 = (bf16[512,2048]{1,0:T(8,128)(2,1)S(1)}, bf16[4,560,128]{2,1,0:T(8,128)(2,1)S(1)}, bf16[4,560,128]{2,1,0:T(8,128)(2,1)S(1)}) custom-call(s32[5]{0:T(128)S(1)} %copy-done.1, bf16[8,16,16,512]{3,2,1,0:T(8,128)(2,1)S(1)} %prepare.1.masked, bf16[18,16,512]{2,1,0:T(8,128)(2,1)S(1)} %collective-permute-done.2.x_first, ...), custom_call_target="tpu_custom_call", output_to_operand_aliasing={{0}: (13, {})} | custom-call | flops 20000000000 | bytes 11261972 | tf_op jit(solution)/shard_map/read/pallas_call | solution.py:456
  44.0 0.0 copy-start.15
  44.0 3.7 %collective-permute-start.4 = (bf16[4,560,128]{2,1,0:T(8,128)(2,1)S(1)}, bf16[4,560,128]{2,1,0:T(8,128)(2,1)S(1)}, u32[]{:S(2)}, u32[]{:S(2)}) collective-permute-start(bf16[4,560,128]{2,1,0:T(8,128)(2,1)S(1)} %get-tuple-element.31), channel_id=1, source_target_pairs={{0,1},{1,0},{2,3},{3,2},{4,5},{5,4},{6,7},{7,6},{8,9},{9,8},{10,11... | collective-permute-start | bytes 1720328 | tf_op jit(solution)/shard_map/ppermute | solution.py:480
  47.7 1.6 %collective-permute-done.4.taken = bf16[4,560,128]{2,1,0:T(8,128)(2,1)S(1)} collective-permute-done((bf16[4,560,128]{2,1,0:T(8,128)(2,1)S(1)}, bf16[4,560,128]{2,1,0:T(8,128)(2,1)S(1)}, u32[]{:S(2)}, u32[]{:S(2)}) %collective-permute-start.4) | collective-permute-done | bytes 573472 | tf_op jit(solution)/shard_map/ppermute | solution.py:480
  49.3 0.8 merge_pair.1
  50.1 0.0 copy-start.7
  50.1 1.8 %collective-permute-start.5 = (bf16[560,128]{1,0:T(8,128)(2,1)S(1)}, bf16[560,128]{1,0:T(8,128)(2,1)S(1)}, u32[]{:S(2)}, u32[]{:S(2)}) collective-permute-start(bf16[560,128]{1,0:T(8,128)(2,1)S(1)} %get-tuple-element.33), channel_id=1, source_target_pairs={{0,2},{2,0},{4,6},{6,4},{1,3},{3,1},{5,7},{7,5},{8,10},{10,8},{12,... | collective-permute-start | bytes 430088 | tf_op jit(solution)/shard_map/ppermute | solution.py:480
  51.9 4.3 %collective-permute-start.6 = (bf16[560,128]{1,0:T(8,128)(2,1)S(1)}, bf16[560,128]{1,0:T(8,128)(2,1)S(1)}, u32[]{:S(2)}, u32[]{:S(2)}) collective-permute-start(bf16[560,128]{1,0:T(8,128)(2,1)S(1)} %get-tuple-element.34), channel_id=1, source_target_pairs={{0,4},{2,6},{4,0},{6,2},{1,5},{3,7},{5,1},{7,3},{8,12},{10,14},{12... | collective-permute-start | bytes 430088 | tf_op jit(solution)/shard_map/ppermute | solution.py:480
  56.2 0.1 collective-permute-done.5.refs_1_
  56.2 4.5 %collective-permute-done.6.refs_2_ = bf16[560,128]{1,0:T(8,128)(2,1)S(1)} collective-permute-done((bf16[560,128]{1,0:T(8,128)(2,1)S(1)}, bf16[560,128]{1,0:T(8,128)(2,1)S(1)}, u32[]{:S(2)}, u32[]{:S(2)}) %collective-permute-start.6) | collective-permute-done | bytes 143392 | tf_op jit(solution)/shard_map/ppermute | solution.py:480
  60.8 2.0 %collective-permute-done.7.refs_3_ = bf16[560,128]{1,0:T(8,128)(2,1)S(1)} collective-permute-done((bf16[560,128]{1,0:T(8,128)(2,1)S(1)}, bf16[560,128]{1,0:T(8,128)(2,1)S(1)}, u32[]{:S(2)}, u32[]{:S(2)}) %collective-permute-start.7) | collective-permute-done | bytes 143392 | tf_op jit(solution)/shard_map/ppermute | solution.py:480
  62.8 0.8 merge_group.1
  63.6 2.8 %collective-permute-start.10 = (bf16[32,640]{1,0:T(8,128)(2,1)S(1)}, bf16[32,640]{1,0:T(8,128)(2,1)S(1)}, u32[]{:S(2)}, u32[]{:S(2)}) collective-permute-start(bf16[32,640]{1,0:T(8,128)(2,1)S(1)} %get-tuple-element.39), channel_id=1, source_target_pairs={{0,24},{8,16},{16,8},{24,0},{1,25},{9,17},{17,9},{25,1},{2,26},{10... | collective-permute-start | bytes 122888 | tf_op jit(solution)/shard_map/ppermute | solution.py:480
  66.4 0.4 collective-permute-start.8
  66.8 1.2 %collective-permute-start.9 = (bf16[32,640]{1,0:T(8,128)(2,1)S(1)}, bf16[32,640]{1,0:T(8,128)(2,1)S(1)}, u32[]{:S(2)}, u32[]{:S(2)}) collective-permute-start(bf16[32,640]{1,0:T(8,128)(2,1)S(1)} %get-tuple-element.38), channel_id=1, source_target_pairs={{0,16},{8,24},{16,0},{24,8},{1,17},{9,25},{17,1},{25,9},{2,18},{10... | collective-permute-start | bytes 122888 | tf_op jit(solution)/shard_map/ppermute | solution.py:480
  68.1 1.5 %collective-permute-done.10.refs_3_ = bf16[32,640]{1,0:T(8,128)(2,1)S(1)} collective-permute-done((bf16[32,640]{1,0:T(8,128)(2,1)S(1)}, bf16[32,640]{1,0:T(8,128)(2,1)S(1)}, u32[]{:S(2)}, u32[]{:S(2)}) %collective-permute-start.10) | collective-permute-done | bytes 40992 | tf_op jit(solution)/shard_map/ppermute | solution.py:480
  69.6 0.8 collective-permute-done.8.refs_1_
  70.4 1.3 %collective-permute-done.9.refs_2_ = bf16[32,640]{1,0:T(8,128)(2,1)S(1)} collective-permute-done((bf16[32,640]{1,0:T(8,128)(2,1)S(1)}, bf16[32,640]{1,0:T(8,128)(2,1)S(1)}, u32[]{:S(2)}, u32[]{:S(2)}) %collective-permute-start.9) | collective-permute-done | bytes 40992 | tf_op jit(solution)/shard_map/ppermute | solution.py:480
  71.7 0.5 update.1.refs_0_
  72.3 1.6 %collective-permute-start.11 = (bf16[32,512]{1,0:T(8,128)(2,1)S(1)}, bf16[32,512]{1,0:T(8,128)(2,1)S(1)}, u32[]{:S(2)}, u32[]{:S(2)}) collective-permute-start(bf16[32,512]{1,0:T(8,128)(2,1)S(1)} %update.1.refs_0_), channel_id=1, source_target_pairs={{0,8},{8,0},{16,24},{24,16},{1,9},{9,1},{17,25},{25,17},{2,10},{10... | collective-permute-start | bytes 98312 | tf_op jit(solution)/shard_map/ppermute | solution.py:480
  73.9 0.3 collective-permute-start.12
  74.2 2.5 %collective-permute-start.13 = (bf16[32,512]{1,0:T(8,128)(2,1)S(1)}, bf16[32,512]{1,0:T(8,128)(2,1)S(1)}, u32[]{:S(2)}, u32[]{:S(2)}) collective-permute-start(bf16[32,512]{1,0:T(8,128)(2,1)S(1)} %update.1.refs_0_), channel_id=1, source_target_pairs={{0,24},{8,16},{16,8},{24,0},{1,25},{9,17},{17,9},{25,1},{2,26},{10... | collective-permute-start | bytes 98312 | tf_op jit(solution)/shard_map/ppermute | solution.py:480
  76.7 2.2 %collective-permute-done.12.refs_2_ = bf16[32,512]{1,0:T(8,128)(2,1)S(1)} collective-permute-done((bf16[32,512]{1,0:T(8,128)(2,1)S(1)}, bf16[32,512]{1,0:T(8,128)(2,1)S(1)}, u32[]{:S(2)}, u32[]{:S(2)}) %collective-permute-start.12) | collective-permute-done | bytes 32800 | tf_op jit(solution)/shard_map/ppermute | solution.py:480
  78.9 1.0 collective-permute-done.13.refs_3_
  79.9 1.7 %collective-permute-start.14 = (bf16[128,512]{1,0:T(8,128)(2,1)S(1)}, bf16[128,512]{1,0:T(8,128)(2,1)S(1)}, u32[]{:S(2)}, u32[]{:S(2)}) collective-permute-start(bf16[128,512]{1,0:T(8,128)(2,1)S(1)} %join_far.1.refs_0_), channel_id=1, source_target_pairs={{0,2},{2,0},{4,6},{6,4},{1,3},{3,1},{5,7},{7,5},{8,10},{10,8},{12,... | collective-permute-start | bytes 393224 | tf_op jit(solution)/shard_map/ppermute | solution.py:480
  81.7 1.7 %collective-permute-start.15 = (bf16[128,512]{1,0:T(8,128)(2,1)S(1)}, bf16[128,512]{1,0:T(8,128)(2,1)S(1)}, u32[]{:S(2)}, u32[]{:S(2)}) collective-permute-start(bf16[128,512]{1,0:T(8,128)(2,1)S(1)} %join_far.1.refs_0_), channel_id=1, source_target_pairs={{0,4},{2,6},{4,0},{6,2},{1,5},{3,7},{5,1},{7,3},{8,12},{10,14},{12... | collective-permute-start | bytes 393224 | tf_op jit(solution)/shard_map/ppermute | solution.py:480
  83.4 0.1 collective-permute-start.16
  83.5 2.3 %collective-permute-done.14.refs_1_ = bf16[128,512]{1,0:T(8,128)(2,1)S(1)} collective-permute-done((bf16[128,512]{1,0:T(8,128)(2,1)S(1)}, bf16[128,512]{1,0:T(8,128)(2,1)S(1)}, u32[]{:S(2)}, u32[]{:S(2)}) %collective-permute-start.14) | collective-permute-done | bytes 131104 | tf_op jit(solution)/shard_map/ppermute | solution.py:480
  85.8 0.8 collective-permute-done.15.refs_2_
  86.6 2.6 %collective-permute-done.16.refs_3_ = bf16[128,512]{1,0:T(8,128)(2,1)S(1)} collective-permute-done((bf16[128,512]{1,0:T(8,128)(2,1)S(1)}, bf16[128,512]{1,0:T(8,128)(2,1)S(1)}, u32[]{:S(2)}, u32[]{:S(2)}) %collective-permute-start.16) | collective-permute-done | bytes 131104 | tf_op jit(solution)/shard_map/ppermute | solution.py:480
  89.3 0.1 collective-permute-start.17
  89.4 1.9 %collective-permute-done.17.other_state = bf16[512,512]{1,0:T(8,128)(2,1)S(1)} collective-permute-done((bf16[512,512]{1,0:T(8,128)(2,1)S(1)}, bf16[512,512]{1,0:T(8,128)(2,1)S(1)}, u32[]{:S(2)}, u32[]{:S(2)}) %collective-permute-start.17) | collective-permute-done | bytes 524320 | tf_op jit(solution)/shard_map/ppermute | solution.py:480
  91.3 22.9 %write.1 = f32[2048,512]{1,0:T(8,128)} custom-call(bf16[512,512]{1,0:T(8,128)(2,1)S(1)} %join_group.1.own_state, bf16[512,512]{1,0:T(8,128)(2,1)S(1)} %collective-permute-done.17.other_state, bf16[512,2048]{1,0:T(8,128)(2,1)S(1)} %copy-done.16, bf16[2048,512]{1,0:T(8,128)(2,1)S(1)} %bitcast.6, bf16[512,512]{1,0:T(8,128)(2,1)S(1)} %copy-done.8, ...), custom_call_target="tpu_custom_call" | custom-call | flops 20000000000 | bytes 6815744 | tf_op jit(solution)/shard_map/write/pallas_call | solution.py:456
  (36 shorter events, 0.1 us)
Async XLA Ops:
  0.0 4.6 %copy-start.2 = (bf16[8,16,16,512]{3,2,1,0:T(8,128)(2,1)S(1)}, bf16[8,16,16,512]{3,2,1,0:T(8,128)(2,1)}, u32[]{:S(2)}) copy-start(bf16[8,16,16,512]{3,2,1,0:T(8,128)(2,1)} %flow.3) | copy-start | bytes 6291460
  0.0 4.6 %copy-start.11 = (s32[8,16,16]{2,1,0:T(8,128)S(1)}, s32[8,16,16]{2,1,0:T(8,128)}, u32[]{:S(2)}) copy-start(s32[8,16,16]{2,1,0:T(8,128)} %far_mask.1) | copy-start | bytes 24580
  3.3 3.7 %collective-permute-start = (bf16[8,16,512]{2,1,0:T(8,128)(2,1)}, bf16[8,16,512]{2,1,0:T(8,128)(2,1)S(1)}, u32[]{:S(2)}, u32[]{:S(2)}) collective-permute-start(bf16[8,16,512]{2,1,0:T(8,128)(2,1)} %get-tuple-element.23), channel_id=1, source_target_pairs={{0,1},{1,0},{2,3},{3,2},{4,5},{5,4},{6,7},{7,6},{8,9},{9,8},{10,11... | collective-permute-start | bytes 393224 | tf_op jit(solution)/shard_map/ppermute | solution.py:476
  3.8 2.3 %copy-start = (bf16[1024,512]{1,0:T(8,128)(2,1)S(1)}, bf16[1024,512]{1,0:T(8,128)(2,1)}, u32[]{:S(2)}) copy-start(bf16[1024,512]{1,0:T(8,128)(2,1)} %latents.1) | copy-start | bytes 3145732
  3.8 2.3 %copy-start.3 = (bf16[512,512]{1,0:T(8,128)(2,1)S(1)}, bf16[512,512]{1,0:T(8,128)(2,1)}, u32[]{:S(2)}) copy-start(bf16[512,512]{1,0:T(8,128)(2,1)} %w_query1.1) | copy-start | bytes 1572868
  3.8 3.2 %collective-permute-start.1 = (bf16[8,16,512]{2,1,0:T(8,128)(2,1)}, bf16[8,16,512]{2,1,0:T(8,128)(2,1)S(1)}, u32[]{:S(2)}, u32[]{:S(2)}) collective-permute-start(bf16[8,16,512]{2,1,0:T(8,128)(2,1)} %get-tuple-element.24), channel_id=1, source_target_pairs={{1,2},{2,1},{5,6},{6,5},{9,10},{10,9},{13,14},{14,13},{17,18},{18,... | collective-permute-start | bytes 393224 | tf_op jit(solution)/shard_map/ppermute | solution.py:475
  6.2 15.1 %copy-start.13 = (bf16[8,16,16,512]{3,2,1,0:T(8,128)(2,1)}, bf16[8,16,16,512]{3,2,1,0:T(8,128)(2,1)S(1)}, u32[]{:S(2)}) copy-start(bf16[8,16,16,512]{3,2,1,0:T(8,128)(2,1)S(1)} %prepare.1.masked) | copy-start | bytes 6291460
  6.2 0.8 copy-start.1
  6.9 3.9 %copy-start.4 = (bf16[512,512]{1,0:T(8,128)(2,1)S(1)}, bf16[512,512]{1,0:T(8,128)(2,1)}, u32[]{:S(2)}) copy-start(bf16[512,512]{1,0:T(8,128)(2,1)} %w_key1.1) | copy-start | bytes 1572868
  6.9 3.9 %copy-start.5 = (bf16[512,512]{1,0:T(8,128)(2,1)S(1)}, bf16[512,512]{1,0:T(8,128)(2,1)}, u32[]{:S(2)}) copy-start(bf16[512,512]{1,0:T(8,128)(2,1)} %w_value1.1) | copy-start | bytes 1572868
  7.0 3.9 %copy-start.6 = (bf16[512,512]{1,0:T(8,128)(2,1)S(1)}, bf16[512,512]{1,0:T(8,128)(2,1)}, u32[]{:S(2)}) copy-start(bf16[512,512]{1,0:T(8,128)(2,1)} %w_query2.1) | copy-start | bytes 1572868
  7.0 3.9 %copy-start.12 = (f32[27,512]{1,0:T(8,128)S(1)}, f32[27,512]{1,0:T(8,128)}, u32[]{:S(2)}) copy-start(f32[27,512]{1,0:T(8,128)} %conv.3) | copy-start | bytes 165892
  7.6 13.6 %collective-permute-start.2 = (bf16[18,16,512]{2,1,0:T(8,128)(2,1)S(1)}, bf16[18,16,512]{2,1,0:T(8,128)(2,1)S(1)}, u32[]{:S(2)}, u32[]{:S(2)}) collective-permute-start(bf16[18,16,512]{2,1,0:T(8,128)(2,1)S(1)} %get-tuple-element.25), channel_id=1, source_target_pairs={{0,4},{4,0},{8,12},{12,8},{16,20},{20,16},{24,28},{28,24},{1,5},{5... | collective-permute-start | bytes 884744 | tf_op jit(solution)/shard_map/ppermute | solution.py:476
  10.2 11.0 %collective-permute-start.3 = (bf16[18,16,512]{2,1,0:T(8,128)(2,1)S(1)}, bf16[18,16,512]{2,1,0:T(8,128)(2,1)S(1)}, u32[]{:S(2)}, u32[]{:S(2)}) collective-permute-start(bf16[18,16,512]{2,1,0:T(8,128)(2,1)S(1)} %get-tuple-element.26), channel_id=1, source_target_pairs={{4,8},{8,4},{12,16},{16,12},{20,24},{24,20},{5,9},{9,5},{13,17},{1... | collective-permute-start | bytes 884744 | tf_op jit(solution)/shard_map/ppermute | solution.py:475
  44.0 12.2 %copy-start.15 = (bf16[512,2048]{1,0:T(8,128)(2,1)}, bf16[512,2048]{1,0:T(8,128)(2,1)S(1)}, u32[]{:S(2)}) copy-start(bf16[512,2048]{1,0:T(8,128)(2,1)S(1)} %get-tuple-element.40.query2_t) | copy-start | bytes 6291460
  44.0 5.3 %collective-permute-start.4 = (bf16[4,560,128]{2,1,0:T(8,128)(2,1)S(1)}, bf16[4,560,128]{2,1,0:T(8,128)(2,1)S(1)}, u32[]{:S(2)}, u32[]{:S(2)}) collective-permute-start(bf16[4,560,128]{2,1,0:T(8,128)(2,1)S(1)} %get-tuple-element.31), channel_id=1, source_target_pairs={{0,1},{1,0},{2,3},{3,2},{4,5},{5,4},{6,7},{7,6},{8,9},{9,8},{10,11... | collective-permute-start | bytes 1720328 | tf_op jit(solution)/shard_map/ppermute | solution.py:480
  50.1 21.6 %copy-start.7 = (bf16[512,512]{1,0:T(8,128)(2,1)S(1)}, bf16[512,512]{1,0:T(8,128)(2,1)}, u32[]{:S(2)}) copy-start(bf16[512,512]{1,0:T(8,128)(2,1)} %w_out1.1) | copy-start | bytes 1572868
  50.1 6.1 %collective-permute-start.5 = (bf16[560,128]{1,0:T(8,128)(2,1)S(1)}, bf16[560,128]{1,0:T(8,128)(2,1)S(1)}, u32[]{:S(2)}, u32[]{:S(2)}) collective-permute-start(bf16[560,128]{1,0:T(8,128)(2,1)S(1)} %get-tuple-element.33), channel_id=1, source_target_pairs={{0,2},{2,0},{4,6},{6,4},{1,3},{3,1},{5,7},{7,5},{8,10},{10,8},{12,... | collective-permute-start | bytes 430088 | tf_op jit(solution)/shard_map/ppermute | solution.py:480
  51.9 8.9 %collective-permute-start.6 = (bf16[560,128]{1,0:T(8,128)(2,1)S(1)}, bf16[560,128]{1,0:T(8,128)(2,1)S(1)}, u32[]{:S(2)}, u32[]{:S(2)}) collective-permute-start(bf16[560,128]{1,0:T(8,128)(2,1)S(1)} %get-tuple-element.34), channel_id=1, source_target_pairs={{0,4},{2,6},{4,0},{6,2},{1,5},{3,7},{5,1},{7,3},{8,12},{10,14},{12... | collective-permute-start | bytes 430088 | tf_op jit(solution)/shard_map/ppermute | solution.py:480
  56.2 6.6 %collective-permute-start.7 = (bf16[560,128]{1,0:T(8,128)(2,1)S(1)}, bf16[560,128]{1,0:T(8,128)(2,1)S(1)}, u32[]{:S(2)}, u32[]{:S(2)}) collective-permute-start(bf16[560,128]{1,0:T(8,128)(2,1)S(1)} %get-tuple-element.35), channel_id=1, source_target_pairs={{0,6},{2,4},{4,2},{6,0},{1,7},{3,5},{5,3},{7,1},{8,14},{10,12},{12... | collective-permute-start | bytes 430088 | tf_op jit(solution)/shard_map/ppermute | solution.py:480
  62.8 28.5 %copy-start.16 = (bf16[512,2048]{1,0:T(8,128)(2,1)S(1)}, bf16[512,2048]{1,0:T(8,128)(2,1)}, u32[]{:S(2)}) copy-start(bf16[512,2048]{1,0:T(8,128)(2,1)} %copy-done.15) | copy-start | bytes 6291460
  63.6 6.0 %collective-permute-start.10 = (bf16[32,640]{1,0:T(8,128)(2,1)S(1)}, bf16[32,640]{1,0:T(8,128)(2,1)S(1)}, u32[]{:S(2)}, u32[]{:S(2)}) collective-permute-start(bf16[32,640]{1,0:T(8,128)(2,1)S(1)} %get-tuple-element.39), channel_id=1, source_target_pairs={{0,24},{8,16},{16,8},{24,0},{1,25},{9,17},{17,9},{25,1},{2,26},{10... | collective-permute-start | bytes 122888 | tf_op jit(solution)/shard_map/ppermute | solution.py:480
  66.4 4.0 %collective-permute-start.8 = (bf16[32,640]{1,0:T(8,128)(2,1)S(1)}, bf16[32,640]{1,0:T(8,128)(2,1)S(1)}, u32[]{:S(2)}, u32[]{:S(2)}) collective-permute-start(bf16[32,640]{1,0:T(8,128)(2,1)S(1)} %get-tuple-element.37), channel_id=1, source_target_pairs={{0,8},{8,0},{16,24},{24,16},{1,9},{9,1},{17,25},{25,17},{2,10},{10... | collective-permute-start | bytes 122888 | tf_op jit(solution)/shard_map/ppermute | solution.py:480
  66.8 4.9 %collective-permute-start.9 = (bf16[32,640]{1,0:T(8,128)(2,1)S(1)}, bf16[32,640]{1,0:T(8,128)(2,1)S(1)}, u32[]{:S(2)}, u32[]{:S(2)}) collective-permute-start(bf16[32,640]{1,0:T(8,128)(2,1)S(1)} %get-tuple-element.38), channel_id=1, source_target_pairs={{0,16},{8,24},{16,0},{24,8},{1,17},{9,25},{17,1},{25,9},{2,18},{10... | collective-permute-start | bytes 122888 | tf_op jit(solution)/shard_map/ppermute | solution.py:480
  71.7 19.6 %copy-start.8 = (bf16[512,512]{1,0:T(8,128)(2,1)S(1)}, bf16[512,512]{1,0:T(8,128)(2,1)}, u32[]{:S(2)}) copy-start(bf16[512,512]{1,0:T(8,128)(2,1)} %w_key2.1) | copy-start | bytes 1572868
  71.7 19.6 %copy-start.9 = (bf16[512,512]{1,0:T(8,128)(2,1)S(1)}, bf16[512,512]{1,0:T(8,128)(2,1)}, u32[]{:S(2)}) copy-start(bf16[512,512]{1,0:T(8,128)(2,1)} %w_value2.1) | copy-start | bytes 1572868
  71.7 19.6 %copy-start.10 = (bf16[512,512]{1,0:T(8,128)(2,1)S(1)}, bf16[512,512]{1,0:T(8,128)(2,1)}, u32[]{:S(2)}) copy-start(bf16[512,512]{1,0:T(8,128)(2,1)} %w_out2.1) | copy-start | bytes 1572868
  71.7 19.6 %copy-start.14 = (bf16[8,16,16,512]{3,2,1,0:T(8,128)(2,1)S(1)}, bf16[8,16,16,512]{3,2,1,0:T(8,128)(2,1)}, u32[]{:S(2)}) copy-start(bf16[8,16,16,512]{3,2,1,0:T(8,128)(2,1)} %copy-done.13) | copy-start | bytes 6291460
  72.3 4.4 %collective-permute-start.11 = (bf16[32,512]{1,0:T(8,128)(2,1)S(1)}, bf16[32,512]{1,0:T(8,128)(2,1)S(1)}, u32[]{:S(2)}, u32[]{:S(2)}) collective-permute-start(bf16[32,512]{1,0:T(8,128)(2,1)S(1)} %update.1.refs_0_), channel_id=1, source_target_pairs={{0,8},{8,0},{16,24},{24,16},{1,9},{9,1},{17,25},{25,17},{2,10},{10... | collective-permute-start | bytes 98312 | tf_op jit(solution)/shard_map/ppermute | solution.py:480
  73.9 5.0 %collective-permute-start.12 = (bf16[32,512]{1,0:T(8,128)(2,1)S(1)}, bf16[32,512]{1,0:T(8,128)(2,1)S(1)}, u32[]{:S(2)}, u32[]{:S(2)}) collective-permute-start(bf16[32,512]{1,0:T(8,128)(2,1)S(1)} %update.1.refs_0_), channel_id=1, source_target_pairs={{0,16},{8,24},{16,0},{24,8},{1,17},{9,25},{17,1},{25,9},{2,18},{10... | collective-permute-start | bytes 98312 | tf_op jit(solution)/shard_map/ppermute | solution.py:480
  74.2 5.7 %collective-permute-start.13 = (bf16[32,512]{1,0:T(8,128)(2,1)S(1)}, bf16[32,512]{1,0:T(8,128)(2,1)S(1)}, u32[]{:S(2)}, u32[]{:S(2)}) collective-permute-start(bf16[32,512]{1,0:T(8,128)(2,1)S(1)} %update.1.refs_0_), channel_id=1, source_target_pairs={{0,24},{8,16},{16,8},{24,0},{1,25},{9,17},{17,9},{25,1},{2,26},{10... | collective-permute-start | bytes 98312 | tf_op jit(solution)/shard_map/ppermute | solution.py:480
  79.9 5.9 %collective-permute-start.14 = (bf16[128,512]{1,0:T(8,128)(2,1)S(1)}, bf16[128,512]{1,0:T(8,128)(2,1)S(1)}, u32[]{:S(2)}, u32[]{:S(2)}) collective-permute-start(bf16[128,512]{1,0:T(8,128)(2,1)S(1)} %join_far.1.refs_0_), channel_id=1, source_target_pairs={{0,2},{2,0},{4,6},{6,4},{1,3},{3,1},{5,7},{7,5},{8,10},{10,8},{12,... | collective-permute-start | bytes 393224 | tf_op jit(solution)/shard_map/ppermute | solution.py:480
  81.7 5.0 %collective-permute-start.15 = (bf16[128,512]{1,0:T(8,128)(2,1)S(1)}, bf16[128,512]{1,0:T(8,128)(2,1)S(1)}, u32[]{:S(2)}, u32[]{:S(2)}) collective-permute-start(bf16[128,512]{1,0:T(8,128)(2,1)S(1)} %join_far.1.refs_0_), channel_id=1, source_target_pairs={{0,4},{2,6},{4,0},{6,2},{1,5},{3,7},{5,1},{7,3},{8,12},{10,14},{12... | collective-permute-start | bytes 393224 | tf_op jit(solution)/shard_map/ppermute | solution.py:480
  83.4 5.9 %collective-permute-start.16 = (bf16[128,512]{1,0:T(8,128)(2,1)S(1)}, bf16[128,512]{1,0:T(8,128)(2,1)S(1)}, u32[]{:S(2)}, u32[]{:S(2)}) collective-permute-start(bf16[128,512]{1,0:T(8,128)(2,1)S(1)} %join_far.1.refs_0_), channel_id=1, source_target_pairs={{0,6},{2,4},{4,2},{6,0},{1,7},{3,5},{5,3},{7,1},{8,14},{10,12},{12... | collective-permute-start | bytes 393224 | tf_op jit(solution)/shard_map/ppermute | solution.py:480
  89.3 2.0 %collective-permute-start.17 = (bf16[512,512]{1,0:T(8,128)(2,1)S(1)}, bf16[512,512]{1,0:T(8,128)(2,1)S(1)}, u32[]{:S(2)}, u32[]{:S(2)}) collective-permute-start(bf16[512,512]{1,0:T(8,128)(2,1)S(1)} %join_group.1.own_state), channel_id=1, source_target_pairs={{0,1},{1,0},{2,3},{3,2},{4,5},{5,4},{6,7},{7,6},{8,9},{9,8},{10,11... | collective-permute-start | bytes 1572872 | tf_op jit(solution)/shard_map/ppermute | solution.py:480

commit v5 on v4

--- a/solution.py
+++ b/solution.py
@@ -28,7 +28,7 @@
     return jnp.concatenate(tiles, axis=1)
 
 
-def face_kernel(position, flow, far_mask, first, second, low, high, mask, arrived):
+def face_kernel(flow, far_mask, first, second, low, high, mask, arrived):
     size_x, size_y = flow.shape[:2]
     copies = []
     for n, (j, target) in enumerate(((0, low), (size_y - 1, high))):
@@ -38,11 +38,11 @@
     copies[-1].start()
     for copy in copies:
         copy.wait()
-    odd = position[3] == 1
+    odd = lax.axis_index("nc") == 1
+    turned = jnp.concatenate([mask[:, 0, :], mask[:, size_y - 1, :]], axis=0).astype(F32).T
     for i in range(size_x):
-        turned = mask[i].astype(F32).T
-        bottom = masked_column(low, turned, i, 0)
-        top = masked_column(high, turned[:, size_y - 1 :], i, 0)
+        bottom = masked_column(low, turned[:, i:], i, 0)
+        top = masked_column(high, turned[:, size_x + i :], i, 0)
         first[i] = jnp.where(odd, bottom, top)
         second[i] = jnp.where(odd, top, bottom)
 
@@ -59,20 +59,20 @@
     lax.fori_loop(0, size_x, plane, 0)
 
 
-def edge_kernel(position, masked, y_first, y_second, first, second):
+def edge_kernel(masked, y_first, y_second, first, second):
     size_x, size_y = masked.shape[:2]
     outer = size_y + 1
-    for face, plane in ((first, (size_x - 1) * (1 - position[4])), (second, (size_x - 1) * position[4])):
+    for face, plane in ((first, (size_x - 1) * (1 - lax.axis_index("wx"))), (second, (size_x - 1) * lax.axis_index("wx"))):
         face[1:outer] = masked[plane]
-        face[outer * (1 - position[3])] = y_first[plane]
-        face[outer * position[3]] = y_second[plane]
-
-
-def fill_row(position, padded, row, i, masked, y_first, y_second):
+        face[outer * (1 - lax.axis_index("nc"))] = y_first[plane]
+        face[outer * lax.axis_index("nc")] = y_second[plane]
+
+
+def fill_row(padded, row, i, masked, y_first, y_second):
     outer = masked.shape[1] + 1
     padded[row, 1:outer] = masked[i].astype(F32)
-    padded[row, outer * (1 - position[3])] = y_first[i].astype(F32)
-    padded[row, outer * position[3]] = y_second[i].astype(F32)
+    padded[row, outer * (1 - lax.axis_index("nc"))] = y_first[i].astype(F32)
+    padded[row, outer * lax.axis_index("nc")] = y_second[i].astype(F32)
 
 
 def stencil_plane(base, padded, conv, mixed, start):
@@ -111,7 +111,6 @@
 
 
 def inner_kernel(
-    position,
     masked,
     y_first,
     y_second,
@@ -141,7 +140,7 @@
         copy.start()
 
     def fill(i, carry):
-        fill_row(position, padded, i, i, masked, y_first, y_second)
+        fill_row(padded, i, i, masked, y_first, y_second)
         return carry
 
     lax.fori_loop(0, size_x, fill, 0)
@@ -160,66 +159,74 @@
     project_plane(last * cells, (last + 1) * cells, cells, mixed, weights, keys, values_t, query2_t)
 
 
-def score_weights(query_t, head_in_pair, head_size):
+def score_weights(query_t, head, columns):
+    head_size = LANES // 2
     factor = 1.8 / math.sqrt(head_size) * math.log2(math.e)
-    scaled = query_t.astype(F32) * factor
+    scaled = query_t[head * head_size : (head + 1) * head_size, columns].astype(F32) * factor
     high = scaled.astype(BF16)
     low = (scaled - high.astype(F32)).astype(BF16)
     blank = jnp.zeros_like(high)
-    if head_in_pair == 0:
+    if head % 2 == 0:
         return jnp.concatenate([high, blank, low, blank], axis=0)
     return jnp.concatenate([blank, high, blank, low], axis=0)
 
 
-def attention_scores(pair, head_in_pair, block, width, chunk, keys, query_t, scores):
-    head_size = LANES // 2
-    start = pl.multiple_of(pair * LANES, LANES) + head_in_pair * head_size
-    columns = pl.ds(pl.multiple_of(block * width, width), width)
-    right = score_weights(query_t[pl.ds(start, head_size), columns], head_in_pair, head_size)
-    top = None
+def chunks_of(pieces, axis, chunk):
+    found = []
     base = 0
-    for piece in keys:
-        for part in range(piece.shape[0] // chunk):
-            left = piece[pl.ds(part * chunk, chunk), pl.ds(pl.multiple_of(pair * LANES, LANES), LANES)]
-            found = dot(jnp.concatenate([left, left], axis=1), right)
-            scores[head_in_pair, pl.ds(base, chunk), :] = found
+    for piece in pieces:
+        for part in range(piece.shape[axis] // chunk):
+            found.append((piece, part * chunk, base))
             base += chunk
-            largest = jnp.max(found.reshape(chunk // 8, 8, width), axis=0)
-            top = largest if top is None else jnp.maximum(top, largest)
-    return jnp.max(top, axis=0, keepdims=True)
-
-
-def attention_sums(head, head_in_pair, chunk, values_t, scores, top):
-    total = None
-    base = 0
-    for piece in values_t:
-        for part in range(piece.shape[2] // chunk):
-            weights = jnp.exp2(scores[head_in_pair, pl.ds(base, chunk), :] - top).astype(BF16)
-            base += chunk
-            found = dot(piece[head, :, pl.ds(part * chunk, chunk)], weights)
-            total = found if total is None else total + found
-    return total
-
-
-def attention_loop(keys, query_t, values_t, scores, chunk, finish):
+    return found
+
+
+def score_chunk(place, head, right, chunk, scores, top):
+    piece, start, base = place
+    pair = head // 2
+    left = piece[start : start + chunk, pair * LANES : (pair + 1) * LANES]
+    found = dot(jnp.concatenate([left, left], axis=1), right)
+    scores[head % 2, base : base + chunk, :] = found
+    largest = jnp.max(found.reshape(chunk // 8, 8, found.shape[1]), axis=0)
+    return largest if top is None else jnp.maximum(top, largest)
+
+
+def sum_chunk(place, head, chunk, scores, top, total):
+    piece, start, base = place
+    weights = jnp.exp2(scores[head % 2, base : base + chunk, :] - top).astype(BF16)
+    found = dot(piece[head, :, start : start + chunk], weights)
+    return found if total is None else total + found
+
+
+def attention_loop(keys, query_t, values_t, scores, chunk, columns_of, finish):
     width = scores.shape[2]
     blocks = query_t.shape[1] // width
-    pairs = query_t.shape[0] // LANES
-    steps = pairs * blocks
-
-    def first(t):
-        return attention_scores(t % pairs, 0, t // pairs, width, chunk, keys, query_t, scores)
-
-    def step(t, top_even):
-        pair, block = t % pairs, t // pairs
-        top_odd = attention_scores(pair, 1, block, width, chunk, keys, query_t, scores)
-        even = attention_sums(2 * pair, 0, chunk, values_t, scores, top_even)
-        following = first(jnp.minimum(t + 1, steps - 1))
-        odd = attention_sums(2 * pair + 1, 1, chunk, values_t, scores, top_odd)
-        finish(pair, block, (even, odd), (top_even, top_odd))
-        return following
-
-    lax.fori_loop(0, steps, step, first(0))
+    key_chunks, value_chunks = chunks_of(keys, 0, chunk), chunks_of(values_t, 2, chunk)
+
+    def overall(top):
+        return jnp.max(top, axis=0, keepdims=True)
+
+    def first(block):
+        right = score_weights(query_t, 0, columns_of(block))
+        top = None
+        for place in key_chunks:
+            top = score_chunk(place, 0, right, chunk, scores, top)
+        return overall(top)
+
+    def step(block, top):
+        for head in range(HEADS):
+            following = block if head + 1 < HEADS else jnp.minimum(block + 1, blocks - 1)
+            ahead = (head + 1) % HEADS
+            right = score_weights(query_t, ahead, columns_of(following))
+            upcoming = total = None
+            for key_place, value_place in zip(key_chunks, value_chunks):
+                upcoming = score_chunk(key_place, ahead, right, chunk, scores, upcoming)
+                total = sum_chunk(value_place, head, chunk, scores, top, total)
+            finish(head, block, total, top)
+            top = overall(upcoming)
+        return top
+
+    lax.fori_loop(0, blocks, step, first(0))
 
 
 def split3(value):
@@ -234,7 +241,6 @@
 
 
 def read_kernel(
-    position,
     masked,
     x_first,
     x_second,
@@ -263,44 +269,40 @@
     cells = size_y * size_z
     last = size_x - 1
     for row, i in ((1, 0), (2, 1), (3, last - 1), (4, last)):
-        fill_row(position, padded, row, i, masked, y_first, y_second)
-    padded[5 * (1 - position[4])] = x_first[...].astype(F32)
-    padded[5 * position[4]] = x_second[...].astype(F32)
+        fill_row(padded, row, i, masked, y_first, y_second)
+    padded[5 * (1 - lax.axis_index("wx"))] = x_first[...].astype(F32)
+    padded[5 * lax.axis_index("wx")] = x_second[...].astype(F32)
     values_t[:, head_size:, :] = jnp.ones_like(values_t[:, head_size:, :])
     stats[...] = jnp.zeros_like(stats)
 
-    def plane(i, carry):
-        stencil_plane(3 * i, padded, conv, mixed, i * cells)
-        weights = (w_key1, w_value1, w_query2)
-        project_plane(i * cells, i * last * cells, cells, mixed, weights, keys, values_t, query2_t)
-        return carry
-
-    lax.fori_loop(0, 2, plane, 0)
-
-    core = position[0]
+    weights = (w_key1, w_value1, w_query2)
+    stencil_plane(0, padded, conv, mixed, 0)
+    project_plane(0, 0, cells, mixed, weights, keys, values_t, query2_t)
+    stencil_plane(3, padded, conv, mixed, cells)
+    project_plane(cells, last * cells, cells, mixed, weights, keys, values_t, query2_t)
+
+    core = lax.axis_index("nc")
     per_half = kept.shape[0]
     span = scores.shape[2]
-    ratio = span // LANES
-
-    def finish(pair, block, sums, tops):
-        both = jnp.concatenate([part[:head_size] for part in sums], axis=0).astype(BF16)
-        rows = pl.ds(pl.multiple_of(pair * LANES, LANES), LANES)
-        first = block * ratio
-        side = first // per_half
+
+    def columns_of(block):
+        return pl.ds(pl.multiple_of((block ^ (1 - core)) * span, span), span)
+
+    def finish(head, block, total, top):
+        rows = slice(head * head_size, (head + 1) * head_size)
 
         def write(target):
-            for k in range(ratio):
-                target[first - side * per_half + k, rows, :] = both[:, k * LANES : (k + 1) * LANES]
-
-        pl.when(side == core)(lambda: write(kept))
-        pl.when(side != core)(lambda: write(given))
-        columns = pl.ds(pl.multiple_of(block * span, span), span)
-        for head_in_pair in range(2):
-            values = stat_rows(tops[head_in_pair], sums[head_in_pair][head_size : head_size + 1])
-            for slot, row in enumerate(values):
-                stats[pl.ds(slot * HEADS + 2 * pair + head_in_pair, 1), columns] = row
-
-    attention_loop([inner_keys, keys], query1_t, [inner_values_t, values_t], scores, 256, finish)
+            for k in range(per_half):
+                target[k, rows, :] = total[:head_size, k * LANES : (k + 1) * LANES].astype(BF16)
+
+        pl.when(block == 1)(lambda: write(kept))
+        pl.when(block == 0)(lambda: write(given))
+        for slot, row in enumerate(stat_rows(top, total[head_size : head_size + 1])):
+            stats[slot * HEADS + head : slot * HEADS + head + 1, columns_of(block)] = row
+
+    attention_loop(
+        [inner_keys, keys], query1_t, [inner_values_t, values_t], scores, 256, columns_of, finish
+    )
     for target, side in ((kept, core), (given, 1 - core)):
         for k in range(per_half):
             columns = pl.ds(pl.multiple_of((side * per_half + k) * LANES, LANES), LANES)
@@ -328,15 +330,15 @@
     return jnp.concatenate(rows + [filler], axis=0)
 
 
-def merge_pair_kernel(position, kept, taken, *outs):
+def merge_pair_kernel(kept, taken, *outs):
     for distance, out in enumerate(outs):
-        index = position[1] ^ distance
+        index = lax.axis_index(("wx", "ny")) ^ distance
         sums, top, total = merge_blocks([ref[index].astype(F32) for ref in (kept, taken)])
         sums.append(all_stats(top, total, STAT_ROWS))
         out[...] = jnp.concatenate(sums, axis=0).astype(BF16)
 
 
-def merge_group_kernel(count, position, *refs):
+def merge_group_kernel(count, *refs):
     blocks, outs, turned = refs[:count], refs[count:-1], refs[-1]
     sums, top, total = merge_blocks([ref[...].astype(F32) for ref in blocks])
     width = turned.shape[1] - LANES
@@ -347,7 +349,7 @@
     turned[:, width:] = all_stats(top, total, LANES).T
     rows = outs[0].shape[0]
     for distance, out in enumerate(outs):
-        index = position[2] ^ distance
+        index = lax.axis_index("wz") ^ distance
         out[...] = turned[pl.ds(pl.multiple_of(index * rows, rows), rows), :].astype(BF16)
 
 
@@ -419,39 +421,34 @@
         values_t[:, :head_size, rows] = value_t.reshape(HEADS, head_size, half)
     span = scores.shape[2]
     blocks = out.shape[0] // span
-    last_pair = width // LANES - 1
 
     def send(block):
         slot = block % 2
         rows = pl.ds(pl.multiple_of(block * span, span), span)
         return pltpu.make_async_copy(buffers.at[slot], out.at[rows, :], sent.at[slot])
 
-    def finish(pair, block, sums, tops):
-        both = [part[:head_size] / part[head_size : head_size + 1] for part in sums]
-        rows = pl.ds(pl.multiple_of(pair * LANES, LANES), LANES)
-        read_t[rows, :] = jnp.concatenate(both, axis=0).astype(BF16)
-
-        @pl.when(pair == last_pair)
-        def _():
+    def columns_of(block):
+        return pl.ds(pl.multiple_of(block * span, span), span)
+
+    def finish(head, block, total, top):
+        rows = slice(head * head_size, (head + 1) * head_size)
+        read_t[rows, :] = (total[:head_size] / total[head_size : head_size + 1]).astype(BF16)
+        if head == HEADS - 1:
             pl.when(block >= 2)(lambda: send(block - 2).wait())
-            cells = pl.ds(pl.multiple_of(block * span, span), span)
             change = dot(read_t[...], w_out2[...], ((0,), (0,)))
-            buffers[block % 2] = masked[cells, :].astype(F32) + change
+            buffers[block % 2] = masked[columns_of(block), :].astype(F32) + change
             send(block).start()
 
-    attention_loop([keys], query2_t, [values_t], scores, 256, finish)
+    attention_loop([keys], query2_t, [values_t], scores, 256, columns_of, finish)
     for block in range(max(blocks - 2, 0), blocks):
         send(block).wait()
 
 
-def call(kernel, shapes, scratch, operands, limit, flops, name, position=None, far=(), aliases=None, out_space=pltpu.VMEM):
+def call(kernel, shapes, scratch, operands, limit, flops, name, far=(), aliases=None, out_space=pltpu.VMEM):
     vmem = pl.BlockSpec(memory_space=pltpu.VMEM)
     hbm = pl.BlockSpec(memory_space=pltpu.HBM)
     many = isinstance(shapes, (list, tuple))
     in_specs = [hbm if n in far else vmem for n in range(len(operands))]
-    if position is not None:
-        in_specs = [pl.BlockSpec(memory_space=pltpu.SMEM)] + in_specs
-        operands = [position] + list(operands)
     moved = sum(x.size * x.dtype.itemsize for x in operands)
     result = pl.pallas_call(
         kernel,
@@ -504,8 +501,6 @@
     group_size = lax.axis_size(group)
     far = lax.axis_size("wz")
     core, member, layer = lax.axis_index("nc"), lax.axis_index(group), lax.axis_index("wz")
-    column = lax.axis_index("wx")
-    position = jnp.stack([core, member, layer, core, column]).astype(jnp.int32)
     block_size = latent_count // (2 * group_size)
     rows = block_size // far
     shape = jax.ShapeDtypeStruct
@@ -521,7 +516,6 @@
         56,
         step,
         "face",
-        position,
         (0, 1),
     )
     y_first, y_second = pair_exchange(y_first, y_second, narrow)
@@ -539,7 +533,7 @@
     )
     side = shape((size_y + 2, size_z, width), BF16)
     x_first, x_second = call(
-        edge_kernel, [side, side], [], [masked, y_first, y_second], 12, step, "edge", position
+        edge_kernel, [side, side], [], [masked, y_first, y_second], 12, step, "edge"
     )
     x_first, x_second = pair_exchange(x_first, x_second, wide)
     weight = pltpu.VMEM((width, width), BF16)
@@ -562,7 +556,6 @@
         28,
         10 * step,
         "inner",
-        position,
         (4, 5, 6),
     )
     query2_t, kept, given = call(
@@ -594,13 +587,12 @@
         32,
         20 * step,
         "read",
-        position,
         (),
-        {13: 0},
+        {12: 0},
     )
     taken = flipped(given, "nc", 1)
     block = shape((width + STAT_ROWS, LANES), BF16)
-    blocks = call(merge_pair_kernel, [block] * group_size, [], [kept, taken], 16, step, "merge_pair", position)
+    blocks = call(merge_pair_kernel, [block] * group_size, [], [kept, taken], 16, step, "merge_pair")
     blocks = blocks[:1] + [flipped(blocks[d], group, d) for d in range(1, group_size)]
     parts = call(
         functools.partial(merge_group_kernel, group_size),
@@ -610,7 +602,6 @@
         16,
         step,
         "merge_group",
-        position,
     )
     parts = parts[:1] + [flipped(parts[d], "wz", d) for d in range(1, far)]
     start = ((core * group_size + member) * far + layer) * rows

time: 114 us -> 108 us (0.947)
  Pallas kernels: 63.6 us -> 57.5 us
    pallas_call x12, Pallas kernels: 63.6 us -> 57.5 us  [call(): pl.pallas_call(kernel, out_shape=shapes, in_specs=in_specs, out_specs=[vm...]
where the time goes in v5:
time: 108 us
  Pallas kernels  57.5 us (53%)
  starting transfers between devices  26.8 us (25%)
  waiting for transfers between devices  22.9 us (21%)
    pallas_call x12, Pallas kernels, call(): pl.pallas_call(kernel, out_shape=shapes, in_specs=in_specs, out_specs=[vm...  57.5 us
    ppermute x14, waiting for transfers between devices, flipped(): lax.ppermute(array, axis, [(i, i ^ distance) for i in range(lax.axis_size...  22.8 us
    ppermute x14, starting transfers between devices, flipped(): lax.ppermute(array, axis, [(i, i ^ distance) for i in range(lax.axis_size...  22.2 us
    ppermute x2, starting transfers between devices, pair_exchange(): return (lax.ppermute(first, axis, swaps[0]), other)  3.15 us
  transfers between devices with their start and end apart: 18, of which 13 were waited for; matrix products, arithmetic and copies ran while one was open for 0% of the time, Pallas kernels for 11%

profile of v5, /device:TPU:0, one launch (start us, length us, event | category | flops | bytes accessed | tf_op | source)
XLA Modules:
  0.0 107.8 jit_solution(7810330048094475407)
XLA Ops:
  0.0 2.0 %face.1 = (bf16[8,16,512]{2,1,0:T(8,128)(2,1)}, bf16[8,16,512]{2,1,0:T(8,128)(2,1)}) custom-call(bf16[8,16,16,512]{3,2,1,0:T(8,128)(2,1)} %flow.3, s32[8,16,16]{2,1,0:T(8,128)} %far_mask.1), custom_call_target="tpu_custom_call" | custom-call | flops 1000000000 | bytes 2105344 | tf_op jit(solution)/shard_map/face/pallas_call | solution.py:453
  2.1 0.6 collective-permute-start
  2.6 0.8 collective-permute-start.1
  3.4 1.5 %prepare.1.masked = bf16[8,16,16,512]{3,2,1,0:T(8,128)(2,1)S(1)} custom-call(bf16[8,16,16,512]{3,2,1,0:T(8,128)(2,1)S(1)} %copy-done.1, s32[8,16,16]{2,1,0:T(8,128)S(1)} %copy-done.10), custom_call_target="tpu_custom_call" | custom-call | flops 2000000000 | bytes 2105344 | tf_op jit(solution)/shard_map/prepare/pallas_call | solution.py:453
  4.9 0.7 latent_query.1.query1_t
  5.7 0.0 copy-start.3
  5.7 0.0 copy-start.4
  5.7 0.0 copy-start.5
  5.7 0.0 copy-start.11
  5.7 0.0 collective-permute-done.1.y_second
  5.8 0.1 edge.1
  5.8 2.6 %collective-permute-start.2 = (bf16[18,16,512]{2,1,0:T(8,128)(2,1)S(1)}, bf16[18,16,512]{2,1,0:T(8,128)(2,1)S(1)}, u32[]{:S(2)}, u32[]{:S(2)}) collective-permute-start(bf16[18,16,512]{2,1,0:T(8,128)(2,1)S(1)} %get-tuple-element.25), channel_id=1, source_target_pairs={{0,4},{4,0},{8,12},{12,8},{16,20},{20,16},{24,28},{28,24},{1,5},{5... | collective-permute-start | bytes 884744 | tf_op jit(solution)/shard_map/ppermute | solution.py:473
  8.4 0.7 collective-permute-start.3
  9.1 9.7 %inner.1 = (bf16[1536,512]{1,0:T(8,128)(2,1)S(1)}, bf16[8,80,1536]{2,1,0:T(8,128)(2,1)S(1)}, bf16[512,2048]{1,0:T(8,128)(2,1)S(1)}) custom-call(bf16[8,16,16,512]{3,2,1,0:T(8,128)(2,1)S(1)} %prepare.1.masked, bf16[8,16,512]{2,1,0:T(8,128)(2,1)S(1)} %collective-permute-done.y_first, bf16[8,16,512]{2,1,0:T(8,128)(2,1)S(1)} %collective-permute-done.1.y_second, ...), custom_call_target="tpu_custom_call" | custom-call | flops 10000000000 | bytes 3987456 | tf_op jit(solution)/shard_map/inner/pallas_call | solution.py:453
  18.8 0.0 collective-permute-done.2.x_first
  18.9 20.9 %read.1 = (bf16[512,2048]{1,0:T(8,128)(2,1)S(1)}, bf16[4,560,128]{2,1,0:T(8,128)(2,1)S(1)}, bf16[4,560,128]{2,1,0:T(8,128)(2,1)S(1)}) custom-call(bf16[8,16,16,512]{3,2,1,0:T(8,128)(2,1)S(1)} %prepare.1.masked, bf16[18,16,512]{2,1,0:T(8,128)(2,1)S(1)} %collective-permute-done.2.x_first, ...), custom_call_target="tpu_custom_call", output_to_operand_aliasing={{0}: (12, {})} | custom-call | flops 20000000000 | bytes 11261952 | tf_op jit(solution)/shard_map/read/pallas_call | solution.py:453
  39.8 0.0 copy-start.14
  39.8 4.0 %collective-permute-start.4 = (bf16[4,560,128]{2,1,0:T(8,128)(2,1)S(1)}, bf16[4,560,128]{2,1,0:T(8,128)(2,1)S(1)}, u32[]{:S(2)}, u32[]{:S(2)}) collective-permute-start(bf16[4,560,128]{2,1,0:T(8,128)(2,1)S(1)} %get-tuple-element.31), channel_id=1, source_target_pairs={{0,1},{1,0},{2,3},{3,2},{4,5},{5,4},{6,7},{7,6},{8,9},{9,8},{10,11... | collective-permute-start | bytes 1720328 | tf_op jit(solution)/shard_map/ppermute | solution.py:477
  43.8 1.6 %collective-permute-done.4.taken = bf16[4,560,128]{2,1,0:T(8,128)(2,1)S(1)} collective-permute-done((bf16[4,560,128]{2,1,0:T(8,128)(2,1)S(1)}, bf16[4,560,128]{2,1,0:T(8,128)(2,1)S(1)}, u32[]{:S(2)}, u32[]{:S(2)}) %collective-permute-start.4) | collective-permute-done | bytes 573472 | tf_op jit(solution)/shard_map/ppermute | solution.py:477
  45.4 0.2 merge_pair.1
  45.6 0.0 copy-start.6
  45.6 1.5 %collective-permute-start.5 = (bf16[560,128]{1,0:T(8,128)(2,1)S(1)}, bf16[560,128]{1,0:T(8,128)(2,1)S(1)}, u32[]{:S(2)}, u32[]{:S(2)}) collective-permute-start(bf16[560,128]{1,0:T(8,128)(2,1)S(1)} %get-tuple-element.33), channel_id=1, source_target_pairs={{0,2},{2,0},{4,6},{6,4},{1,3},{3,1},{5,7},{7,5},{8,10},{10,8},{12,... | collective-permute-start | bytes 430088 | tf_op jit(solution)/shard_map/ppermute | solution.py:477
  47.1 4.3 %collective-permute-start.6 = (bf16[560,128]{1,0:T(8,128)(2,1)S(1)}, bf16[560,128]{1,0:T(8,128)(2,1)S(1)}, u32[]{:S(2)}, u32[]{:S(2)}) collective-permute-start(bf16[560,128]{1,0:T(8,128)(2,1)S(1)} %get-tuple-element.34), channel_id=1, source_target_pairs={{0,4},{2,6},{4,0},{6,2},{1,5},{3,7},{5,1},{7,3},{8,12},{10,14},{12... | collective-permute-start | bytes 430088 | tf_op jit(solution)/shard_map/ppermute | solution.py:477
  51.4 0.3 collective-permute-done.5.refs_1_
  51.7 4.3 %collective-permute-done.6.refs_2_ = bf16[560,128]{1,0:T(8,128)(2,1)S(1)} collective-permute-done((bf16[560,128]{1,0:T(8,128)(2,1)S(1)}, bf16[560,128]{1,0:T(8,128)(2,1)S(1)}, u32[]{:S(2)}, u32[]{:S(2)}) %collective-permute-start.6) | collective-permute-done | bytes 143392 | tf_op jit(solution)/shard_map/ppermute | solution.py:477
  56.0 2.2 %collective-permute-done.7.refs_3_ = bf16[560,128]{1,0:T(8,128)(2,1)S(1)} collective-permute-done((bf16[560,128]{1,0:T(8,128)(2,1)S(1)}, bf16[560,128]{1,0:T(8,128)(2,1)S(1)}, u32[]{:S(2)}, u32[]{:S(2)}) %collective-permute-start.7) | collective-permute-done | bytes 143392 | tf_op jit(solution)/shard_map/ppermute | solution.py:477
  58.2 0.2 merge_group.1
  58.5 2.8 %collective-permute-start.10 = (bf16[32,640]{1,0:T(8,128)(2,1)S(1)}, bf16[32,640]{1,0:T(8,128)(2,1)S(1)}, u32[]{:S(2)}, u32[]{:S(2)}) collective-permute-start(bf16[32,640]{1,0:T(8,128)(2,1)S(1)} %get-tuple-element.39), channel_id=1, source_target_pairs={{0,24},{8,16},{16,8},{24,0},{1,25},{9,17},{17,9},{25,1},{2,26},{10... | collective-permute-start | bytes 122888 | tf_op jit(solution)/shard_map/ppermute | solution.py:477
  61.3 0.4 collective-permute-start.8
  61.7 1.2 %collective-permute-start.9 = (bf16[32,640]{1,0:T(8,128)(2,1)S(1)}, bf16[32,640]{1,0:T(8,128)(2,1)S(1)}, u32[]{:S(2)}, u32[]{:S(2)}) collective-permute-start(bf16[32,640]{1,0:T(8,128)(2,1)S(1)} %get-tuple-element.38), channel_id=1, source_target_pairs={{0,16},{8,24},{16,0},{24,8},{1,17},{9,25},{17,1},{25,9},{2,18},{10... | collective-permute-start | bytes 122888 | tf_op jit(solution)/shard_map/ppermute | solution.py:477
  62.9 1.4 %collective-permute-done.10.refs_3_ = bf16[32,640]{1,0:T(8,128)(2,1)S(1)} collective-permute-done((bf16[32,640]{1,0:T(8,128)(2,1)S(1)}, bf16[32,640]{1,0:T(8,128)(2,1)S(1)}, u32[]{:S(2)}, u32[]{:S(2)}) %collective-permute-start.10) | collective-permute-done | bytes 40992 | tf_op jit(solution)/shard_map/ppermute | solution.py:477
  64.4 0.9 collective-permute-done.8.refs_1_
  65.3 1.3 %collective-permute-done.9.refs_2_ = bf16[32,640]{1,0:T(8,128)(2,1)S(1)} collective-permute-done((bf16[32,640]{1,0:T(8,128)(2,1)S(1)}, bf16[32,640]{1,0:T(8,128)(2,1)S(1)}, u32[]{:S(2)}, u32[]{:S(2)}) %collective-permute-start.9) | collective-permute-done | bytes 40992 | tf_op jit(solution)/shard_map/ppermute | solution.py:477
  66.6 0.5 update.1.refs_0_
  67.2 1.6 %collective-permute-start.11 = (bf16[32,512]{1,0:T(8,128)(2,1)S(1)}, bf16[32,512]{1,0:T(8,128)(2,1)S(1)}, u32[]{:S(2)}, u32[]{:S(2)}) collective-permute-start(bf16[32,512]{1,0:T(8,128)(2,1)S(1)} %update.1.refs_0_), channel_id=1, source_target_pairs={{0,8},{8,0},{16,24},{24,16},{1,9},{9,1},{17,25},{25,17},{2,10},{10... | collective-permute-start | bytes 98312 | tf_op jit(solution)/shard_map/ppermute | solution.py:477
  68.8 0.3 collective-permute-start.12
  69.1 2.5 %collective-permute-start.13 = (bf16[32,512]{1,0:T(8,128)(2,1)S(1)}, bf16[32,512]{1,0:T(8,128)(2,1)S(1)}, u32[]{:S(2)}, u32[]{:S(2)}) collective-permute-start(bf16[32,512]{1,0:T(8,128)(2,1)S(1)} %update.1.refs_0_), channel_id=1, source_target_pairs={{0,24},{8,16},{16,8},{24,0},{1,25},{9,17},{17,9},{25,1},{2,26},{10... | collective-permute-start | bytes 98312 | tf_op jit(solution)/shard_map/ppermute | solution.py:477
  71.6 2.2 %collective-permute-done.12.refs_2_ = bf16[32,512]{1,0:T(8,128)(2,1)S(1)} collective-permute-done((bf16[32,512]{1,0:T(8,128)(2,1)S(1)}, bf16[32,512]{1,0:T(8,128)(2,1)S(1)}, u32[]{:S(2)}, u32[]{:S(2)}) %collective-permute-start.12) | collective-permute-done | bytes 32800 | tf_op jit(solution)/shard_map/ppermute | solution.py:477
  73.8 1.0 collective-permute-done.13.refs_3_
  74.8 1.5 %collective-permute-start.14 = (bf16[128,512]{1,0:T(8,128)(2,1)S(1)}, bf16[128,512]{1,0:T(8,128)(2,1)S(1)}, u32[]{:S(2)}, u32[]{:S(2)}) collective-permute-start(bf16[128,512]{1,0:T(8,128)(2,1)S(1)} %join_far.1.refs_0_), channel_id=1, source_target_pairs={{0,2},{2,0},{4,6},{6,4},{1,3},{3,1},{5,7},{7,5},{8,10},{10,8},{12,... | collective-permute-start | bytes 393224 | tf_op jit(solution)/shard_map/ppermute | solution.py:477
  76.4 1.7 %collective-permute-start.15 = (bf16[128,512]{1,0:T(8,128)(2,1)S(1)}, bf16[128,512]{1,0:T(8,128)(2,1)S(1)}, u32[]{:S(2)}, u32[]{:S(2)}) collective-permute-start(bf16[128,512]{1,0:T(8,128)(2,1)S(1)} %join_far.1.refs_0_), channel_id=1, source_target_pairs={{0,4},{2,6},{4,0},{6,2},{1,5},{3,7},{5,1},{7,3},{8,12},{10,14},{12... | collective-permute-start | bytes 393224 | tf_op jit(solution)/shard_map/ppermute | solution.py:477
  78.1 0.3 collective-permute-start.16
  78.4 2.1 %collective-permute-done.14.refs_1_ = bf16[128,512]{1,0:T(8,128)(2,1)S(1)} collective-permute-done((bf16[128,512]{1,0:T(8,128)(2,1)S(1)}, bf16[128,512]{1,0:T(8,128)(2,1)S(1)}, u32[]{:S(2)}, u32[]{:S(2)}) %collective-permute-start.14) | collective-permute-done | bytes 131104 | tf_op jit(solution)/shard_map/ppermute | solution.py:477
  80.5 0.9 collective-permute-done.15.refs_2_
  81.3 2.6 %collective-permute-done.16.refs_3_ = bf16[128,512]{1,0:T(8,128)(2,1)S(1)} collective-permute-done((bf16[128,512]{1,0:T(8,128)(2,1)S(1)}, bf16[128,512]{1,0:T(8,128)(2,1)S(1)}, u32[]{:S(2)}, u32[]{:S(2)}) %collective-permute-start.16) | collective-permute-done | bytes 131104 | tf_op jit(solution)/shard_map/ppermute | solution.py:477
  84.0 0.1 collective-permute-start.17
  84.1 1.9 %collective-permute-done.17.other_state = bf16[512,512]{1,0:T(8,128)(2,1)S(1)} collective-permute-done((bf16[512,512]{1,0:T(8,128)(2,1)S(1)}, bf16[512,512]{1,0:T(8,128)(2,1)S(1)}, u32[]{:S(2)}, u32[]{:S(2)}) %collective-permute-start.17) | collective-permute-done | bytes 524320 | tf_op jit(solution)/shard_map/ppermute | solution.py:477
  86.0 21.6 %write.1 = f32[2048,512]{1,0:T(8,128)} custom-call(bf16[512,512]{1,0:T(8,128)(2,1)S(1)} %join_group.1.own_state, bf16[512,512]{1,0:T(8,128)(2,1)S(1)} %collective-permute-done.17.other_state, bf16[512,2048]{1,0:T(8,128)(2,1)S(1)} %copy-done.15, bf16[2048,512]{1,0:T(8,128)(2,1)S(1)} %bitcast.2, bf16[512,512]{1,0:T(8,128)(2,1)S(1)} %copy-done.7, ...), custom_call_target="tpu_custom_call" | custom-call | flops 20000000000 | bytes 6815744 | tf_op jit(solution)/shard_map/write/pallas_call | solution.py:453
  (33 shorter events, 0.1 us)
Async XLA Ops:
  0.0 3.4 %copy-start.1 = (bf16[8,16,16,512]{3,2,1,0:T(8,128)(2,1)S(1)}, bf16[8,16,16,512]{3,2,1,0:T(8,128)(2,1)}, u32[]{:S(2)}) copy-start(bf16[8,16,16,512]{3,2,1,0:T(8,128)(2,1)} %flow.3) | copy-start | bytes 6291460
  0.0 3.4 %copy-start.10 = (s32[8,16,16]{2,1,0:T(8,128)S(1)}, s32[8,16,16]{2,1,0:T(8,128)}, u32[]{:S(2)}) copy-start(s32[8,16,16]{2,1,0:T(8,128)} %far_mask.1) | copy-start | bytes 24580
  2.1 3.7 %collective-permute-start = (bf16[8,16,512]{2,1,0:T(8,128)(2,1)}, bf16[8,16,512]{2,1,0:T(8,128)(2,1)S(1)}, u32[]{:S(2)}, u32[]{:S(2)}) collective-permute-start(bf16[8,16,512]{2,1,0:T(8,128)(2,1)} %get-tuple-element.23), channel_id=1, source_target_pairs={{0,1},{1,0},{2,3},{3,2},{4,5},{5,4},{6,7},{7,6},{8,9},{9,8},{10,11... | collective-permute-start | bytes 393224 | tf_op jit(solution)/shard_map/ppermute | solution.py:473
  2.6 2.3 %copy-start = (bf16[1024,512]{1,0:T(8,128)(2,1)S(1)}, bf16[1024,512]{1,0:T(8,128)(2,1)}, u32[]{:S(2)}) copy-start(bf16[1024,512]{1,0:T(8,128)(2,1)} %latents.1) | copy-start | bytes 3145732
  2.6 2.3 %copy-start.2 = (bf16[512,512]{1,0:T(8,128)(2,1)S(1)}, bf16[512,512]{1,0:T(8,128)(2,1)}, u32[]{:S(2)}) copy-start(bf16[512,512]{1,0:T(8,128)(2,1)} %w_query1.1) | copy-start | bytes 1572868
  2.6 3.1 %collective-permute-start.1 = (bf16[8,16,512]{2,1,0:T(8,128)(2,1)}, bf16[8,16,512]{2,1,0:T(8,128)(2,1)S(1)}, u32[]{:S(2)}, u32[]{:S(2)}) collective-permute-start(bf16[8,16,512]{2,1,0:T(8,128)(2,1)} %get-tuple-element.24), channel_id=1, source_target_pairs={{1,2},{2,1},{5,6},{6,5},{9,10},{10,9},{13,14},{14,13},{17,18},{18,... | collective-permute-start | bytes 393224 | tf_op jit(solution)/shard_map/ppermute | solution.py:472
  4.9 13.9 %copy-start.12 = (bf16[8,16,16,512]{3,2,1,0:T(8,128)(2,1)}, bf16[8,16,16,512]{3,2,1,0:T(8,128)(2,1)S(1)}, u32[]{:S(2)}) copy-start(bf16[8,16,16,512]{3,2,1,0:T(8,128)(2,1)S(1)} %prepare.1.masked) | copy-start | bytes 6291460
  5.7 3.4 %copy-start.3 = (bf16[512,512]{1,0:T(8,128)(2,1)S(1)}, bf16[512,512]{1,0:T(8,128)(2,1)}, u32[]{:S(2)}) copy-start(bf16[512,512]{1,0:T(8,128)(2,1)} %w_key1.1) | copy-start | bytes 1572868
  5.7 3.4 %copy-start.4 = (bf16[512,512]{1,0:T(8,128)(2,1)S(1)}, bf16[512,512]{1,0:T(8,128)(2,1)}, u32[]{:S(2)}) copy-start(bf16[512,512]{1,0:T(8,128)(2,1)} %w_value1.1) | copy-start | bytes 1572868
  5.7 3.4 %copy-start.5 = (bf16[512,512]{1,0:T(8,128)(2,1)S(1)}, bf16[512,512]{1,0:T(8,128)(2,1)}, u32[]{:S(2)}) copy-start(bf16[512,512]{1,0:T(8,128)(2,1)} %w_query2.1) | copy-start | bytes 1572868
  5.7 3.4 %copy-start.11 = (f32[27,512]{1,0:T(8,128)S(1)}, f32[27,512]{1,0:T(8,128)}, u32[]{:S(2)}) copy-start(f32[27,512]{1,0:T(8,128)} %conv.3) | copy-start | bytes 165892
  5.8 13.0 %collective-permute-start.2 = (bf16[18,16,512]{2,1,0:T(8,128)(2,1)S(1)}, bf16[18,16,512]{2,1,0:T(8,128)(2,1)S(1)}, u32[]{:S(2)}, u32[]{:S(2)}) collective-permute-start(bf16[18,16,512]{2,1,0:T(8,128)(2,1)S(1)} %get-tuple-element.25), channel_id=1, source_target_pairs={{0,4},{4,0},{8,12},{12,8},{16,20},{20,16},{24,28},{28,24},{1,5},{5... | collective-permute-start | bytes 884744 | tf_op jit(solution)/shard_map/ppermute | solution.py:473
  8.4 10.4 %collective-permute-start.3 = (bf16[18,16,512]{2,1,0:T(8,128)(2,1)S(1)}, bf16[18,16,512]{2,1,0:T(8,128)(2,1)S(1)}, u32[]{:S(2)}, u32[]{:S(2)}) collective-permute-start(bf16[18,16,512]{2,1,0:T(8,128)(2,1)S(1)} %get-tuple-element.26), channel_id=1, source_target_pairs={{4,8},{8,4},{12,16},{16,12},{20,24},{24,20},{5,9},{9,5},{13,17},{1... | collective-permute-start | bytes 884744 | tf_op jit(solution)/shard_map/ppermute | solution.py:472
  39.8 11.6 %copy-start.14 = (bf16[512,2048]{1,0:T(8,128)(2,1)}, bf16[512,2048]{1,0:T(8,128)(2,1)S(1)}, u32[]{:S(2)}) copy-start(bf16[512,2048]{1,0:T(8,128)(2,1)S(1)} %get-tuple-element.40.query2_t) | copy-start | bytes 6291460
  39.8 5.6 %collective-permute-start.4 = (bf16[4,560,128]{2,1,0:T(8,128)(2,1)S(1)}, bf16[4,560,128]{2,1,0:T(8,128)(2,1)S(1)}, u32[]{:S(2)}, u32[]{:S(2)}) collective-permute-start(bf16[4,560,128]{2,1,0:T(8,128)(2,1)S(1)} %get-tuple-element.31), channel_id=1, source_target_pairs={{0,1},{1,0},{2,3},{3,2},{4,5},{5,4},{6,7},{7,6},{8,9},{9,8},{10,11... | collective-permute-start | bytes 1720328 | tf_op jit(solution)/shard_map/ppermute | solution.py:477
  45.6 21.0 %copy-start.6 = (bf16[512,512]{1,0:T(8,128)(2,1)S(1)}, bf16[512,512]{1,0:T(8,128)(2,1)}, u32[]{:S(2)}) copy-start(bf16[512,512]{1,0:T(8,128)(2,1)} %w_out1.1) | copy-start | bytes 1572868
  45.6 6.1 %collective-permute-start.5 = (bf16[560,128]{1,0:T(8,128)(2,1)S(1)}, bf16[560,128]{1,0:T(8,128)(2,1)S(1)}, u32[]{:S(2)}, u32[]{:S(2)}) collective-permute-start(bf16[560,128]{1,0:T(8,128)(2,1)S(1)} %get-tuple-element.33), channel_id=1, source_target_pairs={{0,2},{2,0},{4,6},{6,4},{1,3},{3,1},{5,7},{7,5},{8,10},{10,8},{12,... | collective-permute-start | bytes 430088 | tf_op jit(solution)/shard_map/ppermute | solution.py:477
  47.1 8.9 %collective-permute-start.6 = (bf16[560,128]{1,0:T(8,128)(2,1)S(1)}, bf16[560,128]{1,0:T(8,128)(2,1)S(1)}, u32[]{:S(2)}, u32[]{:S(2)}) collective-permute-start(bf16[560,128]{1,0:T(8,128)(2,1)S(1)} %get-tuple-element.34), channel_id=1, source_target_pairs={{0,4},{2,6},{4,0},{6,2},{1,5},{3,7},{5,1},{7,3},{8,12},{10,14},{12... | collective-permute-start | bytes 430088 | tf_op jit(solution)/shard_map/ppermute | solution.py:477
  51.4 6.9 %collective-permute-start.7 = (bf16[560,128]{1,0:T(8,128)(2,1)S(1)}, bf16[560,128]{1,0:T(8,128)(2,1)S(1)}, u32[]{:S(2)}, u32[]{:S(2)}) collective-permute-start(bf16[560,128]{1,0:T(8,128)(2,1)S(1)} %get-tuple-element.35), channel_id=1, source_target_pairs={{0,6},{2,4},{4,2},{6,0},{1,7},{3,5},{5,3},{7,1},{8,14},{10,12},{12... | collective-permute-start | bytes 430088 | tf_op jit(solution)/shard_map/ppermute | solution.py:477
  58.2 27.7 %copy-start.15 = (bf16[512,2048]{1,0:T(8,128)(2,1)S(1)}, bf16[512,2048]{1,0:T(8,128)(2,1)}, u32[]{:S(2)}) copy-start(bf16[512,2048]{1,0:T(8,128)(2,1)} %copy-done.14) | copy-start | bytes 6291460
  58.5 5.9 %collective-permute-start.10 = (bf16[32,640]{1,0:T(8,128)(2,1)S(1)}, bf16[32,640]{1,0:T(8,128)(2,1)S(1)}, u32[]{:S(2)}, u32[]{:S(2)}) collective-permute-start(bf16[32,640]{1,0:T(8,128)(2,1)S(1)} %get-tuple-element.39), channel_id=1, source_target_pairs={{0,24},{8,16},{16,8},{24,0},{1,25},{9,17},{17,9},{25,1},{2,26},{10... | collective-permute-start | bytes 122888 | tf_op jit(solution)/shard_map/ppermute | solution.py:477
  61.3 4.0 %collective-permute-start.8 = (bf16[32,640]{1,0:T(8,128)(2,1)S(1)}, bf16[32,640]{1,0:T(8,128)(2,1)S(1)}, u32[]{:S(2)}, u32[]{:S(2)}) collective-permute-start(bf16[32,640]{1,0:T(8,128)(2,1)S(1)} %get-tuple-element.37), channel_id=1, source_target_pairs={{0,8},{8,0},{16,24},{24,16},{1,9},{9,1},{17,25},{25,17},{2,10},{10... | collective-permute-start | bytes 122888 | tf_op jit(solution)/shard_map/ppermute | solution.py:477
  61.7 4.9 %collective-permute-start.9 = (bf16[32,640]{1,0:T(8,128)(2,1)S(1)}, bf16[32,640]{1,0:T(8,128)(2,1)S(1)}, u32[]{:S(2)}, u32[]{:S(2)}) collective-permute-start(bf16[32,640]{1,0:T(8,128)(2,1)S(1)} %get-tuple-element.38), channel_id=1, source_target_pairs={{0,16},{8,24},{16,0},{24,8},{1,17},{9,25},{17,1},{25,9},{2,18},{10... | collective-permute-start | bytes 122888 | tf_op jit(solution)/shard_map/ppermute | solution.py:477
  66.6 19.4 %copy-start.7 = (bf16[512,512]{1,0:T(8,128)(2,1)S(1)}, bf16[512,512]{1,0:T(8,128)(2,1)}, u32[]{:S(2)}) copy-start(bf16[512,512]{1,0:T(8,128)(2,1)} %w_key2.1) | copy-start | bytes 1572868
  66.6 19.4 %copy-start.8 = (bf16[512,512]{1,0:T(8,128)(2,1)S(1)}, bf16[512,512]{1,0:T(8,128)(2,1)}, u32[]{:S(2)}) copy-start(bf16[512,512]{1,0:T(8,128)(2,1)} %w_value2.1) | copy-start | bytes 1572868
  66.6 19.4 %copy-start.9 = (bf16[512,512]{1,0:T(8,128)(2,1)S(1)}, bf16[512,512]{1,0:T(8,128)(2,1)}, u32[]{:S(2)}) copy-start(bf16[512,512]{1,0:T(8,128)(2,1)} %w_out2.1) | copy-start | bytes 1572868
  66.6 19.4 %copy-start.13 = (bf16[8,16,16,512]{3,2,1,0:T(8,128)(2,1)S(1)}, bf16[8,16,16,512]{3,2,1,0:T(8,128)(2,1)}, u32[]{:S(2)}) copy-start(bf16[8,16,16,512]{3,2,1,0:T(8,128)(2,1)} %copy-done.12) | copy-start | bytes 6291460
  67.2 4.4 %collective-permute-start.11 = (bf16[32,512]{1,0:T(8,128)(2,1)S(1)}, bf16[32,512]{1,0:T(8,128)(2,1)S(1)}, u32[]{:S(2)}, u32[]{:S(2)}) collective-permute-start(bf16[32,512]{1,0:T(8,128)(2,1)S(1)} %update.1.refs_0_), channel_id=1, source_target_pairs={{0,8},{8,0},{16,24},{24,16},{1,9},{9,1},{17,25},{25,17},{2,10},{10... | collective-permute-start | bytes 98312 | tf_op jit(solution)/shard_map/ppermute | solution.py:477
  68.8 5.0 %collective-permute-start.12 = (bf16[32,512]{1,0:T(8,128)(2,1)S(1)}, bf16[32,512]{1,0:T(8,128)(2,1)S(1)}, u32[]{:S(2)}, u32[]{:S(2)}) collective-permute-start(bf16[32,512]{1,0:T(8,128)(2,1)S(1)} %update.1.refs_0_), channel_id=1, source_target_pairs={{0,16},{8,24},{16,0},{24,8},{1,17},{9,25},{17,1},{25,9},{2,18},{10... | collective-permute-start | bytes 98312 | tf_op jit(solution)/shard_map/ppermute | solution.py:477
  69.1 5.7 %collective-permute-start.13 = (bf16[32,512]{1,0:T(8,128)(2,1)S(1)}, bf16[32,512]{1,0:T(8,128)(2,1)S(1)}, u32[]{:S(2)}, u32[]{:S(2)}) collective-permute-start(bf16[32,512]{1,0:T(8,128)(2,1)S(1)} %update.1.refs_0_), channel_id=1, source_target_pairs={{0,24},{8,16},{16,8},{24,0},{1,25},{9,17},{17,9},{25,1},{2,26},{10... | collective-permute-start | bytes 98312 | tf_op jit(solution)/shard_map/ppermute | solution.py:477
  74.8 5.6 %collective-permute-start.14 = (bf16[128,512]{1,0:T(8,128)(2,1)S(1)}, bf16[128,512]{1,0:T(8,128)(2,1)S(1)}, u32[]{:S(2)}, u32[]{:S(2)}) collective-permute-start(bf16[128,512]{1,0:T(8,128)(2,1)S(1)} %join_far.1.refs_0_), channel_id=1, source_target_pairs={{0,2},{2,0},{4,6},{6,4},{1,3},{3,1},{5,7},{7,5},{8,10},{10,8},{12,... | collective-permute-start | bytes 393224 | tf_op jit(solution)/shard_map/ppermute | solution.py:477
  76.4 5.0 %collective-permute-start.15 = (bf16[128,512]{1,0:T(8,128)(2,1)S(1)}, bf16[128,512]{1,0:T(8,128)(2,1)S(1)}, u32[]{:S(2)}, u32[]{:S(2)}) collective-permute-start(bf16[128,512]{1,0:T(8,128)(2,1)S(1)} %join_far.1.refs_0_), channel_id=1, source_target_pairs={{0,4},{2,6},{4,0},{6,2},{1,5},{3,7},{5,1},{7,3},{8,12},{10,14},{12... | collective-permute-start | bytes 393224 | tf_op jit(solution)/shard_map/ppermute | solution.py:477
  78.1 5.9 %collective-permute-start.16 = (bf16[128,512]{1,0:T(8,128)(2,1)S(1)}, bf16[128,512]{1,0:T(8,128)(2,1)S(1)}, u32[]{:S(2)}, u32[]{:S(2)}) collective-permute-start(bf16[128,512]{1,0:T(8,128)(2,1)S(1)} %join_far.1.refs_0_), channel_id=1, source_target_pairs={{0,6},{2,4},{4,2},{6,0},{1,7},{3,5},{5,3},{7,1},{8,14},{10,12},{12... | collective-permute-start | bytes 393224 | tf_op jit(solution)/shard_map/ppermute | solution.py:477
  84.0 2.0 %collective-permute-start.17 = (bf16[512,512]{1,0:T(8,128)(2,1)S(1)}, bf16[512,512]{1,0:T(8,128)(2,1)S(1)}, u32[]{:S(2)}, u32[]{:S(2)}) collective-permute-start(bf16[512,512]{1,0:T(8,128)(2,1)S(1)} %join_group.1.own_state), channel_id=1, source_target_pairs={{0,1},{1,0},{2,3},{3,2},{4,5},{5,4},{6,7},{7,6},{8,9},{9,8},{10,11... | collective-permute-start | bytes 1572872 | tf_op jit(solution)/shard_map/ppermute | solution.py:477

commit v6 on v5

--- a/solution.py
+++ b/solution.py
@@ -198,9 +198,7 @@
     return found if total is None else total + found
 
 
-def attention_loop(keys, query_t, values_t, scores, chunk, columns_of, finish):
-    width = scores.shape[2]
-    blocks = query_t.shape[1] // width
+def attention_loop(keys, query_t, values_t, scores, chunk, blocks, columns_of, finish):
     key_chunks, value_chunks = chunks_of(keys, 0, chunk), chunks_of(values_t, 2, chunk)
 
     def overall(top):
@@ -215,18 +213,23 @@
 
     def step(block, top):
         for head in range(HEADS):
-            following = block if head + 1 < HEADS else jnp.minimum(block + 1, blocks - 1)
             ahead = (head + 1) % HEADS
-            right = score_weights(query_t, ahead, columns_of(following))
+            wanted = ahead > 0 or blocks > 1
+            following = block if ahead else jnp.minimum(block + 1, blocks - 1)
+            right = score_weights(query_t, ahead, columns_of(following)) if wanted else None
             upcoming = total = None
             for key_place, value_place in zip(key_chunks, value_chunks):
-                upcoming = score_chunk(key_place, ahead, right, chunk, scores, upcoming)
+                if wanted:
+                    upcoming = score_chunk(key_place, ahead, right, chunk, scores, upcoming)
                 total = sum_chunk(value_place, head, chunk, scores, top, total)
             finish(head, block, total, top)
-            top = overall(upcoming)
+            top = overall(upcoming) if wanted else top
         return top
 
-    lax.fori_loop(0, blocks, step, first(0))
+    if blocks == 1:
+        step(0, first(0))
+    else:
+        lax.fori_loop(0, blocks, step, first(0))
 
 
 def split3(value):
@@ -238,6 +241,25 @@
 
 def stat_rows(top, total):
     return split3(top) + split3(total)[:2]
+
+
+def half_attention(side, keys, values_t, query1_t, target, scores, stats):
+    per_half = target.shape[0]
+    span = scores.shape[2]
+    head_size = query1_t.shape[0] // HEADS
+    width = query1_t.shape[0]
+    columns = pl.ds(pl.multiple_of(side * span, span), span)
+
+    def finish(head, block, total, top):
+        rows = slice(head * head_size, (head + 1) * head_size)
+        for k in range(per_half):
+            target[k, rows, :] = total[:head_size, k * LANES : (k + 1) * LANES].astype(BF16)
+        for slot, row in enumerate(stat_rows(top, total[head_size : head_size + 1])):
+            stats[slot * HEADS + head : slot * HEADS + head + 1, :] = row
+
+    attention_loop(keys, query1_t, values_t, scores, 256, 1, lambda block: columns, finish)
+    for k in range(per_half):
+        target[k, width:, :] = stats[:, k * LANES : (k + 1) * LANES].astype(BF16)
 
 
 def read_kernel(
@@ -255,12 +277,11 @@
     query1_t,
     inner_query2_t,
     query2_t,
-    kept,
     given,
+    keys,
+    values_t,
     padded,
     mixed,
-    keys,
-    values_t,
     scores,
     stats,
 ):
@@ -281,32 +302,14 @@
     stencil_plane(3, padded, conv, mixed, cells)
     project_plane(cells, last * cells, cells, mixed, weights, keys, values_t, query2_t)
 
-    core = lax.axis_index("nc")
-    per_half = kept.shape[0]
-    span = scores.shape[2]
-
-    def columns_of(block):
-        return pl.ds(pl.multiple_of((block ^ (1 - core)) * span, span), span)
-
-    def finish(head, block, total, top):
-        rows = slice(head * head_size, (head + 1) * head_size)
-
-        def write(target):
-            for k in range(per_half):
-                target[k, rows, :] = total[:head_size, k * LANES : (k + 1) * LANES].astype(BF16)
-
-        pl.when(block == 1)(lambda: write(kept))
-        pl.when(block == 0)(lambda: write(given))
-        for slot, row in enumerate(stat_rows(top, total[head_size : head_size + 1])):
-            stats[slot * HEADS + head : slot * HEADS + head + 1, columns_of(block)] = row
-
-    attention_loop(
-        [inner_keys, keys], query1_t, [inner_values_t, values_t], scores, 256, columns_of, finish
-    )
-    for target, side in ((kept, core), (given, 1 - core)):
-        for k in range(per_half):
-            columns = pl.ds(pl.multiple_of((side * per_half + k) * LANES, LANES), LANES)
-            target[k, width:, :] = stats[:, columns].astype(BF16)
+    side = 1 - lax.axis_index("nc")
+    half_attention(side, [inner_keys, keys], [inner_values_t, values_t], query1_t, given, scores, stats)
+
+
+def keep_kernel(inner_keys, keys, inner_values_t, values_t, query1_t, kept, scores, stats):
+    side = lax.axis_index("nc")
+    stats[...] = jnp.zeros_like(stats)
+    half_attention(side, [inner_keys, keys], [inner_values_t, values_t], query1_t, kept, scores, stats)
 
 
 def merge_blocks(blocks):
@@ -432,14 +435,15 @@
 
     def finish(head, block, total, top):
         rows = slice(head * head_size, (head + 1) * head_size)
-        read_t[rows, :] = (total[:head_size] / total[head_size : head_size + 1]).astype(BF16)
+        inverse = 1.0 / total[head_size : head_size + 1]
+        read_t[rows, :] = (total[:head_size] * inverse).astype(BF16)
         if head == HEADS - 1:
             pl.when(block >= 2)(lambda: send(block - 2).wait())
             change = dot(read_t[...], w_out2[...], ((0,), (0,)))
             buffers[block % 2] = masked[columns_of(block), :].astype(F32) + change
             send(block).start()
 
-    attention_loop([keys], query2_t, [values_t], scores, 256, columns_of, finish)
+    attention_loop([keys], query2_t, [values_t], scores, 256, blocks, columns_of, finish)
     for block in range(max(blocks - 2, 0), blocks):
         send(block).wait()
 
@@ -558,17 +562,24 @@
         "inner",
         (4, 5, 6),
     )
-    query2_t, kept, given = call(
+    part = shape((group_size, width + STAT_ROWS, LANES), BF16)
+    partial_scratch = [
+        pltpu.VMEM((2, cells, latent_count // 2), F32),
+        pltpu.VMEM((STAT_ROWS, latent_count // 2), F32),
+    ]
+    query2_t, given, outer_keys, outer_values_t = call(
         read_kernel,
-        [shape((width, cells), BF16)] + [shape((group_size, width + STAT_ROWS, LANES), BF16)] * 2,
+        [
+            shape((width, cells), BF16),
+            part,
+            shape((outer_cells, width), BF16),
+            shape((HEADS, head_size + ONES_ROWS, outer_cells), BF16),
+        ],
         [
             pltpu.VMEM((6, size_y + 2, size_z, width), F32),
             pltpu.VMEM((outer_cells, width), BF16),
-            pltpu.VMEM((outer_cells, width), BF16),
-            pltpu.VMEM((HEADS, head_size + ONES_ROWS, outer_cells), BF16),
-            pltpu.VMEM((2, cells, latent_count // 2), F32),
-            pltpu.VMEM((STAT_ROWS, latent_count), F32),
-        ],
+        ]
+        + partial_scratch,
         [
             masked,
             x_first,
@@ -591,9 +602,18 @@
         {12: 0},
     )
     taken = flipped(given, "nc", 1)
+    kept = call(
+        keep_kernel,
+        part,
+        partial_scratch,
+        [inner_keys, outer_keys, inner_values_t, outer_values_t, query1_t],
+        24,
+        10 * step,
+        "keep",
+    )
     block = shape((width + STAT_ROWS, LANES), BF16)
     blocks = call(merge_pair_kernel, [block] * group_size, [], [kept, taken], 16, step, "merge_pair")
-    blocks = blocks[:1] + [flipped(blocks[d], group, d) for d in range(1, group_size)]
+    blocks = [flipped(blocks[d], group, d) for d in range(group_size - 1, 0, -1)] + blocks[:1]
     parts = call(
         functools.partial(merge_group_kernel, group_size),
         [shape((rows, width + LANES), BF16)] * far,
@@ -603,12 +623,13 @@
         step,
         "merge_group",
     )
-    parts = parts[:1] + [flipped(parts[d], "wz", d) for d in range(1, far)]
+    order = list(range(far - 2, 0, -1)) + [far - 1]
+    parts = [flipped(parts[d], "wz", d) for d in order] + parts[:1]
     start = ((core * group_size + member) * far + layer) * rows
     own = lax.dynamic_slice_in_dim(latents, start, rows, 0)
     state = call(update_kernel, shape((rows, width), BF16), [], [own, w_out1] + parts, 16, step, "update")
-    state = join([state] + [flipped(state, "wz", d) for d in range(1, far)], "join_far")
-    state = join([state] + [flipped(state, group, d) for d in range(1, group_size)], "join_group")
+    state = join([flipped(state, "wz", d) for d in range(far - 1, 0, -1)] + [state], "join_far")
+    state = join([flipped(state, group, d) for d in range(group_size - 1, 0, -1)] + [state], "join_group")
     other = flipped(state, "nc", 1)
     span = 2 * plane_cells
 

time: 108 us -> 109 us (level)
  Pallas kernels: 57.5 us -> 63 us
  waiting for transfers between devices: 22.9 us -> 18.5 us
    pallas_call x12 -> x13, Pallas kernels: 57.5 us -> 63 us  [call(): pl.pallas_call(kernel, out_shape=shapes, in_specs=in_specs, out_specs=[vm...]
    ppermute x14, waiting for transfers between devices: 22.8 us -> 18.5 us  [flipped(): lax.ppermute(array, axis, [(i, i ^ distance) for i in range(lax.axis_size...]
  transfers between devices with their start and end apart: 18 -> 18, of which waited for: 13 -> 11; matrix products, arithmetic and copies ran while one was open for 0% -> 0% of each run, Pallas kernels for 11% -> 22%
where the time goes in v6:
time: 109 us
  Pallas kernels  63 us (58%)
  starting transfers between devices  26.6 us (24%)
  waiting for transfers between devices  18.5 us (17%)
    pallas_call x13, Pallas kernels, call(): pl.pallas_call(kernel, out_shape=shapes, in_specs=in_specs, out_specs=[vm...  63 us
    ppermute x14, starting transfers between devices, flipped(): lax.ppermute(array, axis, [(i, i ^ distance) for i in range(lax.axis_size...  22 us
    ppermute x14, waiting for transfers between devices, flipped(): lax.ppermute(array, axis, [(i, i ^ distance) for i in range(lax.axis_size...  18.5 us
    ppermute x2, starting transfers between devices, pair_exchange(): return (lax.ppermute(first, axis, swaps[0]), other)  3.15 us
  transfers between devices with their start and end apart: 18, of which 11 were waited for; matrix products, arithmetic and copies ran while one was open for 0% of the time, Pallas kernels for 22%

profile of v6, /device:TPU:0, one launch (start us, length us, event | category | flops | bytes accessed | tf_op | source)
XLA Modules:
  0.0 108.8 jit_solution(7793437313385633190)
XLA Ops:
  0.0 2.0 %face.1 = (bf16[8,16,512]{2,1,0:T(8,128)(2,1)}, bf16[8,16,512]{2,1,0:T(8,128)(2,1)}) custom-call(bf16[8,16,16,512]{3,2,1,0:T(8,128)(2,1)} %flow.3, s32[8,16,16]{2,1,0:T(8,128)} %far_mask.1), custom_call_target="tpu_custom_call" | custom-call | flops 1000000000 | bytes 2105344 | tf_op jit(solution)/shard_map/face/pallas_call | solution.py:457
  2.1 0.6 collective-permute-start
  2.6 0.8 collective-permute-start.1
  3.4 1.5 %prepare.1.masked = bf16[8,16,16,512]{3,2,1,0:T(8,128)(2,1)S(1)} custom-call(bf16[8,16,16,512]{3,2,1,0:T(8,128)(2,1)S(1)} %copy-done.1, s32[8,16,16]{2,1,0:T(8,128)S(1)} %copy-done.10), custom_call_target="tpu_custom_call" | custom-call | flops 2000000000 | bytes 2105344 | tf_op jit(solution)/shard_map/prepare/pallas_call | solution.py:457
  4.9 0.7 latent_query.1.query1_t
  5.7 0.0 copy-start.3
  5.7 0.0 copy-start.4
  5.7 0.0 copy-start.5
  5.7 0.0 copy-start.11
  5.7 0.0 collective-permute-done.y_first
  5.8 0.1 edge.1
  5.8 2.6 %collective-permute-start.2 = (bf16[18,16,512]{2,1,0:T(8,128)(2,1)S(1)}, bf16[18,16,512]{2,1,0:T(8,128)(2,1)S(1)}, u32[]{:S(2)}, u32[]{:S(2)}) collective-permute-start(bf16[18,16,512]{2,1,0:T(8,128)(2,1)S(1)} %get-tuple-element.27), channel_id=1, source_target_pairs={{0,4},{4,0},{8,12},{12,8},{16,20},{20,16},{24,28},{28,24},{1,5},{5... | collective-permute-start | bytes 884744 | tf_op jit(solution)/shard_map/ppermute | solution.py:477
  8.4 0.7 collective-permute-start.3
  9.1 9.9 %inner.1 = (bf16[1536,512]{1,0:T(8,128)(2,1)S(1)}, bf16[8,80,1536]{2,1,0:T(8,128)(2,1)S(1)}, bf16[512,2048]{1,0:T(8,128)(2,1)S(1)}) custom-call(bf16[8,16,16,512]{3,2,1,0:T(8,128)(2,1)S(1)} %prepare.1.masked, bf16[8,16,512]{2,1,0:T(8,128)(2,1)S(1)} %collective-permute-done.y_first, bf16[8,16,512]{2,1,0:T(8,128)(2,1)S(1)} %collective-permute-done.1.y_second, ...), custom_call_target="tpu_custom_call" | custom-call | flops 10000000000 | bytes 3987456 | tf_op jit(solution)/shard_map/inner/pallas_call | solution.py:457
  19.0 0.0 collective-permute-done.2.x_first
  19.0 14.7 %read.1 = (bf16[512,2048]{1,0:T(8,128)(2,1)S(1)}, bf16[4,560,128]{2,1,0:T(8,128)(2,1)S(1)}, bf16[512,512]{1,0:T(8,128)(2,1)S(1)}, bf16[8,80,512]{2,1,0:T(8,128)(2,1)S(1)}) custom-call(bf16[8,16,16,512]{3,2,1,0:T(8,128)(2,1)S(1)} %prepare.1.masked, bf16[18,16,512]{2,1,0:T(8,128)(2,1)S(1)} %collective-permute-done.2.x_first, ...), custom_call_target="tpu_custom_call", output_to_operand_aliasing={{0}: (12, {})} | custom-call | flops 20000000000 | bytes 11261952 | tf_op jit(solution)/shard_map/read/pallas_call | solution.py:457
  33.7 0.0 copy-start.14
  33.7 4.0 %collective-permute-start.4 = (bf16[4,560,128]{2,1,0:T(8,128)(2,1)S(1)}, bf16[4,560,128]{2,1,0:T(8,128)(2,1)S(1)}, u32[]{:S(2)}, u32[]{:S(2)}) collective-permute-start(bf16[4,560,128]{2,1,0:T(8,128)(2,1)S(1)} %get-tuple-element.33), channel_id=1, source_target_pairs={{0,1},{1,0},{2,3},{3,2},{4,5},{5,4},{6,7},{7,6},{8,9},{9,8},{10,11... | collective-permute-start | bytes 1720328 | tf_op jit(solution)/shard_map/ppermute | solution.py:481
  37.7 11.7 %keep.1.kept = bf16[4,560,128]{2,1,0:T(8,128)(2,1)S(1)} custom-call(bf16[1536,512]{1,0:T(8,128)(2,1)S(1)} %get-tuple-element.26.inner_keys, bf16[512,512]{1,0:T(8,128)(2,1)S(1)} %get-tuple-element.31.keys, bf16[8,80,1536]{2,1,0:T(8,128)(2,1)S(1)} %get-tuple-element.29.inner_values_t, bf16[8,80,512]{2,1,0:T(8,128)(2,1)S(1)} %get-tuple-element.32.values_t, ...), custom_call_target="tpu_custom_call" | custom-call | flops 10000000000 | bytes 5767168 | tf_op jit(solution)/shard_map/keep/pallas_call | solution.py:457
  49.4 0.3 merge_pair.1
  49.7 0.0 copy-start.6
  49.7 4.8 %collective-permute-start.5 = (bf16[560,128]{1,0:T(8,128)(2,1)S(1)}, bf16[560,128]{1,0:T(8,128)(2,1)S(1)}, u32[]{:S(2)}, u32[]{:S(2)}) collective-permute-start(bf16[560,128]{1,0:T(8,128)(2,1)S(1)} %get-tuple-element.34), channel_id=1, source_target_pairs={{0,6},{2,4},{4,2},{6,0},{1,7},{3,5},{5,3},{7,1},{8,14},{10,12},{12... | collective-permute-start | bytes 430088 | tf_op jit(solution)/shard_map/ppermute | solution.py:481
  54.6 0.7 collective-permute-start.7
  55.2 3.9 %collective-permute-done.5.refs_0_ = bf16[560,128]{1,0:T(8,128)(2,1)S(1)} collective-permute-done((bf16[560,128]{1,0:T(8,128)(2,1)S(1)}, bf16[560,128]{1,0:T(8,128)(2,1)S(1)}, u32[]{:S(2)}, u32[]{:S(2)}) %collective-permute-start.5) | collective-permute-done | bytes 143392 | tf_op jit(solution)/shard_map/ppermute | solution.py:481
  59.2 2.1 %collective-permute-done.6.refs_1_ = bf16[560,128]{1,0:T(8,128)(2,1)S(1)} collective-permute-done((bf16[560,128]{1,0:T(8,128)(2,1)S(1)}, bf16[560,128]{1,0:T(8,128)(2,1)S(1)}, u32[]{:S(2)}, u32[]{:S(2)}) %collective-permute-start.6) | collective-permute-done | bytes 143392 | tf_op jit(solution)/shard_map/ppermute | solution.py:481
  61.3 0.7 collective-permute-done.7.refs_2_
  62.0 0.2 merge_group.1
  62.2 2.8 %collective-permute-start.10 = (bf16[32,640]{1,0:T(8,128)(2,1)S(1)}, bf16[32,640]{1,0:T(8,128)(2,1)S(1)}, u32[]{:S(2)}, u32[]{:S(2)}) collective-permute-start(bf16[32,640]{1,0:T(8,128)(2,1)S(1)} %get-tuple-element.40), channel_id=1, source_target_pairs={{0,24},{8,16},{16,8},{24,0},{1,25},{9,17},{17,9},{25,1},{2,26},{10... | collective-permute-start | bytes 122888 | tf_op jit(solution)/shard_map/ppermute | solution.py:481
  65.1 0.3 collective-permute-start.8
  65.3 1.3 %collective-permute-start.9 = (bf16[32,640]{1,0:T(8,128)(2,1)S(1)}, bf16[32,640]{1,0:T(8,128)(2,1)S(1)}, u32[]{:S(2)}, u32[]{:S(2)}) collective-permute-start(bf16[32,640]{1,0:T(8,128)(2,1)S(1)} %get-tuple-element.39), channel_id=1, source_target_pairs={{0,8},{8,0},{16,24},{24,16},{1,9},{9,1},{17,25},{25,17},{2,10},{10... | collective-permute-start | bytes 122888 | tf_op jit(solution)/shard_map/ppermute | solution.py:481
  66.7 1.5 %collective-permute-done.10.refs_2_ = bf16[32,640]{1,0:T(8,128)(2,1)S(1)} collective-permute-done((bf16[32,640]{1,0:T(8,128)(2,1)S(1)}, bf16[32,640]{1,0:T(8,128)(2,1)S(1)}, u32[]{:S(2)}, u32[]{:S(2)}) %collective-permute-start.10) | collective-permute-done | bytes 40992 | tf_op jit(solution)/shard_map/ppermute | solution.py:481
  68.2 2.1 %collective-permute-done.8.refs_0_ = bf16[32,640]{1,0:T(8,128)(2,1)S(1)} collective-permute-done((bf16[32,640]{1,0:T(8,128)(2,1)S(1)}, bf16[32,640]{1,0:T(8,128)(2,1)S(1)}, u32[]{:S(2)}, u32[]{:S(2)}) %collective-permute-start.8) | collective-permute-done | bytes 40992 | tf_op jit(solution)/shard_map/ppermute | solution.py:481
  70.3 0.0 copy-start.8
  70.3 0.0 copy-start.9
  70.4 0.5 update.1.refs_3_
  70.9 1.9 %collective-permute-start.11 = (bf16[32,512]{1,0:T(8,128)(2,1)S(1)}, bf16[32,512]{1,0:T(8,128)(2,1)S(1)}, u32[]{:S(2)}, u32[]{:S(2)}) collective-permute-start(bf16[32,512]{1,0:T(8,128)(2,1)S(1)} %update.1.refs_3_), channel_id=1, source_target_pairs={{0,24},{8,16},{16,8},{24,0},{1,25},{9,17},{17,9},{25,1},{2,26},{10... | collective-permute-start | bytes 98312 | tf_op jit(solution)/shard_map/ppermute | solution.py:481
  72.8 2.5 %collective-permute-start.13 = (bf16[32,512]{1,0:T(8,128)(2,1)S(1)}, bf16[32,512]{1,0:T(8,128)(2,1)S(1)}, u32[]{:S(2)}, u32[]{:S(2)}) collective-permute-start(bf16[32,512]{1,0:T(8,128)(2,1)S(1)} %update.1.refs_3_), channel_id=1, source_target_pairs={{0,8},{8,0},{16,24},{24,16},{1,9},{9,1},{17,25},{25,17},{2,10},{10... | collective-permute-start | bytes 98312 | tf_op jit(solution)/shard_map/ppermute | solution.py:481
  75.3 1.7 %collective-permute-done.11.refs_0_ = bf16[32,512]{1,0:T(8,128)(2,1)S(1)} collective-permute-done((bf16[32,512]{1,0:T(8,128)(2,1)S(1)}, bf16[32,512]{1,0:T(8,128)(2,1)S(1)}, u32[]{:S(2)}, u32[]{:S(2)}) %collective-permute-start.11) | collective-permute-done | bytes 32800 | tf_op jit(solution)/shard_map/ppermute | solution.py:481
  77.0 0.8 collective-permute-done.12.refs_1_
  77.8 2.2 %collective-permute-start.14 = (bf16[128,512]{1,0:T(8,128)(2,1)S(1)}, bf16[128,512]{1,0:T(8,128)(2,1)S(1)}, u32[]{:S(2)}, u32[]{:S(2)}) collective-permute-start(bf16[128,512]{1,0:T(8,128)(2,1)S(1)} %join_far.1.refs_3_), channel_id=1, source_target_pairs={{0,6},{2,4},{4,2},{6,0},{1,7},{3,5},{5,3},{7,1},{8,14},{10,12},{12... | collective-permute-start | bytes 393224 | tf_op jit(solution)/shard_map/ppermute | solution.py:481
  80.0 0.2 collective-permute-start.15
  80.2 1.2 %collective-permute-start.16 = (bf16[128,512]{1,0:T(8,128)(2,1)S(1)}, bf16[128,512]{1,0:T(8,128)(2,1)S(1)}, u32[]{:S(2)}, u32[]{:S(2)}) collective-permute-start(bf16[128,512]{1,0:T(8,128)(2,1)S(1)} %join_far.1.refs_3_), channel_id=1, source_target_pairs={{0,2},{2,0},{4,6},{6,4},{1,3},{3,1},{5,7},{7,5},{8,10},{10,8},{12,... | collective-permute-start | bytes 393224 | tf_op jit(solution)/shard_map/ppermute | solution.py:481
  81.3 2.4 %collective-permute-done.14.refs_0_ = bf16[128,512]{1,0:T(8,128)(2,1)S(1)} collective-permute-done((bf16[128,512]{1,0:T(8,128)(2,1)S(1)}, bf16[128,512]{1,0:T(8,128)(2,1)S(1)}, u32[]{:S(2)}, u32[]{:S(2)}) %collective-permute-start.14) | collective-permute-done | bytes 131104 | tf_op jit(solution)/shard_map/ppermute | solution.py:481
  83.7 1.3 %collective-permute-done.15.refs_1_ = bf16[128,512]{1,0:T(8,128)(2,1)S(1)} collective-permute-done((bf16[128,512]{1,0:T(8,128)(2,1)S(1)}, bf16[128,512]{1,0:T(8,128)(2,1)S(1)}, u32[]{:S(2)}, u32[]{:S(2)}) %collective-permute-start.15) | collective-permute-done | bytes 131104 | tf_op jit(solution)/shard_map/ppermute | solution.py:481
  84.9 0.2 collective-permute-done.16.refs_2_
  85.2 0.1 collective-permute-start.17
  85.2 1.9 %collective-permute-done.17.other_state = bf16[512,512]{1,0:T(8,128)(2,1)S(1)} collective-permute-done((bf16[512,512]{1,0:T(8,128)(2,1)S(1)}, bf16[512,512]{1,0:T(8,128)(2,1)S(1)}, u32[]{:S(2)}, u32[]{:S(2)}) %collective-permute-start.17) | collective-permute-done | bytes 524320 | tf_op jit(solution)/shard_map/ppermute | solution.py:481
  87.2 21.4 %write.1 = f32[2048,512]{1,0:T(8,128)} custom-call(bf16[512,512]{1,0:T(8,128)(2,1)S(1)} %join_group.1.own_state, bf16[512,512]{1,0:T(8,128)(2,1)S(1)} %collective-permute-done.17.other_state, bf16[512,2048]{1,0:T(8,128)(2,1)S(1)} %copy-done.15, bf16[2048,512]{1,0:T(8,128)(2,1)S(1)} %bitcast.2, bf16[512,512]{1,0:T(8,128)(2,1)S(1)} %copy-done.7, ...), custom_call_target="tpu_custom_call" | custom-call | flops 20000000000 | bytes 6815744 | tf_op jit(solution)/shard_map/write/pallas_call | solution.py:457
  (34 shorter events, 0.1 us)
Async XLA Ops:
  0.0 3.4 %copy-start.1 = (bf16[8,16,16,512]{3,2,1,0:T(8,128)(2,1)S(1)}, bf16[8,16,16,512]{3,2,1,0:T(8,128)(2,1)}, u32[]{:S(2)}) copy-start(bf16[8,16,16,512]{3,2,1,0:T(8,128)(2,1)} %flow.3) | copy-start | bytes 6291460
  0.0 3.4 %copy-start.10 = (s32[8,16,16]{2,1,0:T(8,128)S(1)}, s32[8,16,16]{2,1,0:T(8,128)}, u32[]{:S(2)}) copy-start(s32[8,16,16]{2,1,0:T(8,128)} %far_mask.1) | copy-start | bytes 24580
  2.1 3.7 %collective-permute-start = (bf16[8,16,512]{2,1,0:T(8,128)(2,1)}, bf16[8,16,512]{2,1,0:T(8,128)(2,1)S(1)}, u32[]{:S(2)}, u32[]{:S(2)}) collective-permute-start(bf16[8,16,512]{2,1,0:T(8,128)(2,1)} %get-tuple-element.24), channel_id=1, source_target_pairs={{0,1},{1,0},{2,3},{3,2},{4,5},{5,4},{6,7},{7,6},{8,9},{9,8},{10,11... | collective-permute-start | bytes 393224 | tf_op jit(solution)/shard_map/ppermute | solution.py:477
  2.6 2.3 %copy-start = (bf16[1024,512]{1,0:T(8,128)(2,1)S(1)}, bf16[1024,512]{1,0:T(8,128)(2,1)}, u32[]{:S(2)}) copy-start(bf16[1024,512]{1,0:T(8,128)(2,1)} %latents.1) | copy-start | bytes 3145732
  2.6 2.3 %copy-start.2 = (bf16[512,512]{1,0:T(8,128)(2,1)S(1)}, bf16[512,512]{1,0:T(8,128)(2,1)}, u32[]{:S(2)}) copy-start(bf16[512,512]{1,0:T(8,128)(2,1)} %w_query1.1) | copy-start | bytes 1572868
  2.6 3.1 %collective-permute-start.1 = (bf16[8,16,512]{2,1,0:T(8,128)(2,1)}, bf16[8,16,512]{2,1,0:T(8,128)(2,1)S(1)}, u32[]{:S(2)}, u32[]{:S(2)}) collective-permute-start(bf16[8,16,512]{2,1,0:T(8,128)(2,1)} %get-tuple-element.25), channel_id=1, source_target_pairs={{1,2},{2,1},{5,6},{6,5},{9,10},{10,9},{13,14},{14,13},{17,18},{18,... | collective-permute-start | bytes 393224 | tf_op jit(solution)/shard_map/ppermute | solution.py:476
  4.9 14.1 %copy-start.12 = (bf16[8,16,16,512]{3,2,1,0:T(8,128)(2,1)}, bf16[8,16,16,512]{3,2,1,0:T(8,128)(2,1)S(1)}, u32[]{:S(2)}) copy-start(bf16[8,16,16,512]{3,2,1,0:T(8,128)(2,1)S(1)} %prepare.1.masked) | copy-start | bytes 6291460
  5.7 3.4 %copy-start.3 = (bf16[512,512]{1,0:T(8,128)(2,1)S(1)}, bf16[512,512]{1,0:T(8,128)(2,1)}, u32[]{:S(2)}) copy-start(bf16[512,512]{1,0:T(8,128)(2,1)} %w_key1.1) | copy-start | bytes 1572868
  5.7 3.4 %copy-start.4 = (bf16[512,512]{1,0:T(8,128)(2,1)S(1)}, bf16[512,512]{1,0:T(8,128)(2,1)}, u32[]{:S(2)}) copy-start(bf16[512,512]{1,0:T(8,128)(2,1)} %w_value1.1) | copy-start | bytes 1572868
  5.7 3.4 %copy-start.5 = (bf16[512,512]{1,0:T(8,128)(2,1)S(1)}, bf16[512,512]{1,0:T(8,128)(2,1)}, u32[]{:S(2)}) copy-start(bf16[512,512]{1,0:T(8,128)(2,1)} %w_query2.1) | copy-start | bytes 1572868
  5.7 3.4 %copy-start.11 = (f32[27,512]{1,0:T(8,128)S(1)}, f32[27,512]{1,0:T(8,128)}, u32[]{:S(2)}) copy-start(f32[27,512]{1,0:T(8,128)} %conv.3) | copy-start | bytes 165892
  5.8 13.2 %collective-permute-start.2 = (bf16[18,16,512]{2,1,0:T(8,128)(2,1)S(1)}, bf16[18,16,512]{2,1,0:T(8,128)(2,1)S(1)}, u32[]{:S(2)}, u32[]{:S(2)}) collective-permute-start(bf16[18,16,512]{2,1,0:T(8,128)(2,1)S(1)} %get-tuple-element.27), channel_id=1, source_target_pairs={{0,4},{4,0},{8,12},{12,8},{16,20},{20,16},{24,28},{28,24},{1,5},{5... | collective-permute-start | bytes 884744 | tf_op jit(solution)/shard_map/ppermute | solution.py:477
  8.4 10.6 %collective-permute-start.3 = (bf16[18,16,512]{2,1,0:T(8,128)(2,1)S(1)}, bf16[18,16,512]{2,1,0:T(8,128)(2,1)S(1)}, u32[]{:S(2)}, u32[]{:S(2)}) collective-permute-start(bf16[18,16,512]{2,1,0:T(8,128)(2,1)S(1)} %get-tuple-element.28), channel_id=1, source_target_pairs={{4,8},{8,4},{12,16},{16,12},{20,24},{24,20},{5,9},{9,5},{13,17},{1... | collective-permute-start | bytes 884744 | tf_op jit(solution)/shard_map/ppermute | solution.py:476
  33.7 15.7 %copy-start.14 = (bf16[512,2048]{1,0:T(8,128)(2,1)}, bf16[512,2048]{1,0:T(8,128)(2,1)S(1)}, u32[]{:S(2)}) copy-start(bf16[512,2048]{1,0:T(8,128)(2,1)S(1)} %get-tuple-element.42.query2_t) | copy-start | bytes 6291460
  33.7 15.7 %collective-permute-start.4 = (bf16[4,560,128]{2,1,0:T(8,128)(2,1)S(1)}, bf16[4,560,128]{2,1,0:T(8,128)(2,1)S(1)}, u32[]{:S(2)}, u32[]{:S(2)}) collective-permute-start(bf16[4,560,128]{2,1,0:T(8,128)(2,1)S(1)} %get-tuple-element.33), channel_id=1, source_target_pairs={{0,1},{1,0},{2,3},{3,2},{4,5},{5,4},{6,7},{7,6},{8,9},{9,8},{10,11... | collective-permute-start | bytes 1720328 | tf_op jit(solution)/shard_map/ppermute | solution.py:481
  49.7 20.6 %copy-start.6 = (bf16[512,512]{1,0:T(8,128)(2,1)S(1)}, bf16[512,512]{1,0:T(8,128)(2,1)}, u32[]{:S(2)}) copy-start(bf16[512,512]{1,0:T(8,128)(2,1)} %w_out1.1) | copy-start | bytes 1572868
  49.7 9.5 %collective-permute-start.5 = (bf16[560,128]{1,0:T(8,128)(2,1)S(1)}, bf16[560,128]{1,0:T(8,128)(2,1)S(1)}, u32[]{:S(2)}, u32[]{:S(2)}) collective-permute-start(bf16[560,128]{1,0:T(8,128)(2,1)S(1)} %get-tuple-element.34), channel_id=1, source_target_pairs={{0,6},{2,4},{4,2},{6,0},{1,7},{3,5},{5,3},{7,1},{8,14},{10,12},{12... | collective-permute-start | bytes 430088 | tf_op jit(solution)/shard_map/ppermute | solution.py:481
  54.6 6.7 %collective-permute-start.6 = (bf16[560,128]{1,0:T(8,128)(2,1)S(1)}, bf16[560,128]{1,0:T(8,128)(2,1)S(1)}, u32[]{:S(2)}, u32[]{:S(2)}) collective-permute-start(bf16[560,128]{1,0:T(8,128)(2,1)S(1)} %get-tuple-element.35), channel_id=1, source_target_pairs={{0,4},{2,6},{4,0},{6,2},{1,5},{3,7},{5,1},{7,3},{8,12},{10,14},{12... | collective-permute-start | bytes 430088 | tf_op jit(solution)/shard_map/ppermute | solution.py:481
  54.6 7.4 %collective-permute-start.7 = (bf16[560,128]{1,0:T(8,128)(2,1)S(1)}, bf16[560,128]{1,0:T(8,128)(2,1)S(1)}, u32[]{:S(2)}, u32[]{:S(2)}) collective-permute-start(bf16[560,128]{1,0:T(8,128)(2,1)S(1)} %get-tuple-element.36), channel_id=1, source_target_pairs={{0,2},{2,0},{4,6},{6,4},{1,3},{3,1},{5,7},{7,5},{8,10},{10,8},{12,... | collective-permute-start | bytes 430088 | tf_op jit(solution)/shard_map/ppermute | solution.py:481
  62.0 25.1 %copy-start.15 = (bf16[512,2048]{1,0:T(8,128)(2,1)S(1)}, bf16[512,2048]{1,0:T(8,128)(2,1)}, u32[]{:S(2)}) copy-start(bf16[512,2048]{1,0:T(8,128)(2,1)} %copy-done.14) | copy-start | bytes 6291460
  62.2 6.0 %collective-permute-start.10 = (bf16[32,640]{1,0:T(8,128)(2,1)S(1)}, bf16[32,640]{1,0:T(8,128)(2,1)S(1)}, u32[]{:S(2)}, u32[]{:S(2)}) collective-permute-start(bf16[32,640]{1,0:T(8,128)(2,1)S(1)} %get-tuple-element.40), channel_id=1, source_target_pairs={{0,24},{8,16},{16,8},{24,0},{1,25},{9,17},{17,9},{25,1},{2,26},{10... | collective-permute-start | bytes 122888 | tf_op jit(solution)/shard_map/ppermute | solution.py:481
  65.1 5.3 %collective-permute-start.8 = (bf16[32,640]{1,0:T(8,128)(2,1)S(1)}, bf16[32,640]{1,0:T(8,128)(2,1)S(1)}, u32[]{:S(2)}, u32[]{:S(2)}) collective-permute-start(bf16[32,640]{1,0:T(8,128)(2,1)S(1)} %get-tuple-element.38), channel_id=1, source_target_pairs={{0,16},{8,24},{16,0},{24,8},{1,17},{9,25},{17,1},{25,9},{2,18},{10... | collective-permute-start | bytes 122888 | tf_op jit(solution)/shard_map/ppermute | solution.py:481
  65.3 5.0 %collective-permute-start.9 = (bf16[32,640]{1,0:T(8,128)(2,1)S(1)}, bf16[32,640]{1,0:T(8,128)(2,1)S(1)}, u32[]{:S(2)}, u32[]{:S(2)}) collective-permute-start(bf16[32,640]{1,0:T(8,128)(2,1)S(1)} %get-tuple-element.39), channel_id=1, source_target_pairs={{0,8},{8,0},{16,24},{24,16},{1,9},{9,1},{17,25},{25,17},{2,10},{10... | collective-permute-start | bytes 122888 | tf_op jit(solution)/shard_map/ppermute | solution.py:481
  70.3 16.8 %copy-start.7 = (bf16[512,512]{1,0:T(8,128)(2,1)S(1)}, bf16[512,512]{1,0:T(8,128)(2,1)}, u32[]{:S(2)}) copy-start(bf16[512,512]{1,0:T(8,128)(2,1)} %w_key2.1) | copy-start | bytes 1572868
  70.3 16.8 %copy-start.8 = (bf16[512,512]{1,0:T(8,128)(2,1)S(1)}, bf16[512,512]{1,0:T(8,128)(2,1)}, u32[]{:S(2)}) copy-start(bf16[512,512]{1,0:T(8,128)(2,1)} %w_value2.1) | copy-start | bytes 1572868
  70.3 16.8 %copy-start.9 = (bf16[512,512]{1,0:T(8,128)(2,1)S(1)}, bf16[512,512]{1,0:T(8,128)(2,1)}, u32[]{:S(2)}) copy-start(bf16[512,512]{1,0:T(8,128)(2,1)} %w_out2.1) | copy-start | bytes 1572868
  70.4 16.8 %copy-start.13 = (bf16[8,16,16,512]{3,2,1,0:T(8,128)(2,1)S(1)}, bf16[8,16,16,512]{3,2,1,0:T(8,128)(2,1)}, u32[]{:S(2)}) copy-start(bf16[8,16,16,512]{3,2,1,0:T(8,128)(2,1)} %copy-done.12) | copy-start | bytes 6291460
  70.9 6.1 %collective-permute-start.11 = (bf16[32,512]{1,0:T(8,128)(2,1)S(1)}, bf16[32,512]{1,0:T(8,128)(2,1)S(1)}, u32[]{:S(2)}, u32[]{:S(2)}) collective-permute-start(bf16[32,512]{1,0:T(8,128)(2,1)S(1)} %update.1.refs_3_), channel_id=1, source_target_pairs={{0,24},{8,16},{16,8},{24,0},{1,25},{9,17},{17,9},{25,1},{2,26},{10... | collective-permute-start | bytes 98312 | tf_op jit(solution)/shard_map/ppermute | solution.py:481
  72.8 5.0 %collective-permute-start.12 = (bf16[32,512]{1,0:T(8,128)(2,1)S(1)}, bf16[32,512]{1,0:T(8,128)(2,1)S(1)}, u32[]{:S(2)}, u32[]{:S(2)}) collective-permute-start(bf16[32,512]{1,0:T(8,128)(2,1)S(1)} %update.1.refs_3_), channel_id=1, source_target_pairs={{0,16},{8,24},{16,0},{24,8},{1,17},{9,25},{17,1},{25,9},{2,18},{10... | collective-permute-start | bytes 98312 | tf_op jit(solution)/shard_map/ppermute | solution.py:481
  72.8 5.0 %collective-permute-start.13 = (bf16[32,512]{1,0:T(8,128)(2,1)S(1)}, bf16[32,512]{1,0:T(8,128)(2,1)S(1)}, u32[]{:S(2)}, u32[]{:S(2)}) collective-permute-start(bf16[32,512]{1,0:T(8,128)(2,1)S(1)} %update.1.refs_3_), channel_id=1, source_target_pairs={{0,8},{8,0},{16,24},{24,16},{1,9},{9,1},{17,25},{25,17},{2,10},{10... | collective-permute-start | bytes 98312 | tf_op jit(solution)/shard_map/ppermute | solution.py:481
  77.8 5.9 %collective-permute-start.14 = (bf16[128,512]{1,0:T(8,128)(2,1)S(1)}, bf16[128,512]{1,0:T(8,128)(2,1)S(1)}, u32[]{:S(2)}, u32[]{:S(2)}) collective-permute-start(bf16[128,512]{1,0:T(8,128)(2,1)S(1)} %join_far.1.refs_3_), channel_id=1, source_target_pairs={{0,6},{2,4},{4,2},{6,0},{1,7},{3,5},{5,3},{7,1},{8,14},{10,12},{12... | collective-permute-start | bytes 393224 | tf_op jit(solution)/shard_map/ppermute | solution.py:481
  80.0 5.0 %collective-permute-start.15 = (bf16[128,512]{1,0:T(8,128)(2,1)S(1)}, bf16[128,512]{1,0:T(8,128)(2,1)S(1)}, u32[]{:S(2)}, u32[]{:S(2)}) collective-permute-start(bf16[128,512]{1,0:T(8,128)(2,1)S(1)} %join_far.1.refs_3_), channel_id=1, source_target_pairs={{0,4},{2,6},{4,0},{6,2},{1,5},{3,7},{5,1},{7,3},{8,12},{10,14},{12... | collective-permute-start | bytes 393224 | tf_op jit(solution)/shard_map/ppermute | solution.py:481
  80.2 5.0 %collective-permute-start.16 = (bf16[128,512]{1,0:T(8,128)(2,1)S(1)}, bf16[128,512]{1,0:T(8,128)(2,1)S(1)}, u32[]{:S(2)}, u32[]{:S(2)}) collective-permute-start(bf16[128,512]{1,0:T(8,128)(2,1)S(1)} %join_far.1.refs_3_), channel_id=1, source_target_pairs={{0,2},{2,0},{4,6},{6,4},{1,3},{3,1},{5,7},{7,5},{8,10},{10,8},{12,... | collective-permute-start | bytes 393224 | tf_op jit(solution)/shard_map/ppermute | solution.py:481
  85.2 2.0 %collective-permute-start.17 = (bf16[512,512]{1,0:T(8,128)(2,1)S(1)}, bf16[512,512]{1,0:T(8,128)(2,1)S(1)}, u32[]{:S(2)}, u32[]{:S(2)}) collective-permute-start(bf16[512,512]{1,0:T(8,128)(2,1)S(1)} %join_group.1.own_state), channel_id=1, source_target_pairs={{0,1},{1,0},{2,3},{3,2},{4,5},{5,4},{6,7},{7,6},{8,9},{9,8},{10,11... | collective-permute-start | bytes 1572872 | tf_op jit(solution)/shard_map/ppermute | solution.py:481

commit v7 on v5

--- a/solution.py
+++ b/solution.py
@@ -145,18 +145,15 @@
 
     lax.fori_loop(0, size_x, fill, 0)
     values_t[:, head_size:, :] = jnp.ones_like(values_t[:, head_size:, :])
-    stencil_plane(0, padded, conv, mixed, 0)
     for copy in copies:
         copy.wait()
 
     def plane(i, carry):
-        project_plane((i - 1) * cells, i * cells, cells, mixed, weights, keys, values_t, query2_t)
         stencil_plane(i, padded, conv, mixed, i * cells)
+        project_plane(i * cells, (i + 1) * cells, cells, mixed, weights, keys, values_t, query2_t)
         return carry
 
-    lax.fori_loop(1, size_x - 2, plane, 0)
-    last = size_x - 3
-    project_plane(last * cells, (last + 1) * cells, cells, mixed, weights, keys, values_t, query2_t)
+    lax.fori_loop(0, size_x - 2, plane, 0)
 
 
 def score_weights(query_t, head, columns):
@@ -198,9 +195,7 @@
     return found if total is None else total + found
 
 
-def attention_loop(keys, query_t, values_t, scores, chunk, columns_of, finish):
-    width = scores.shape[2]
-    blocks = query_t.shape[1] // width
+def attention_loop(keys, query_t, values_t, scores, chunk, blocks, columns_of, finish):
     key_chunks, value_chunks = chunks_of(keys, 0, chunk), chunks_of(values_t, 2, chunk)
 
     def overall(top):
@@ -215,8 +210,8 @@
 
     def step(block, top):
         for head in range(HEADS):
-            following = block if head + 1 < HEADS else jnp.minimum(block + 1, blocks - 1)
             ahead = (head + 1) % HEADS
+            following = block if ahead else jnp.minimum(block + 1, blocks - 1)
             right = score_weights(query_t, ahead, columns_of(following))
             upcoming = total = None
             for key_place, value_place in zip(key_chunks, value_chunks):
@@ -276,10 +271,13 @@
     stats[...] = jnp.zeros_like(stats)
 
     weights = (w_key1, w_value1, w_query2)
-    stencil_plane(0, padded, conv, mixed, 0)
-    project_plane(0, 0, cells, mixed, weights, keys, values_t, query2_t)
-    stencil_plane(3, padded, conv, mixed, cells)
-    project_plane(cells, last * cells, cells, mixed, weights, keys, values_t, query2_t)
+
+    def plane(i, carry):
+        stencil_plane(3 * i, padded, conv, mixed, i * cells)
+        project_plane(i * cells, i * last * cells, cells, mixed, weights, keys, values_t, query2_t)
+        return carry
+
+    lax.fori_loop(0, 2, plane, 0)
 
     core = lax.axis_index("nc")
     per_half = kept.shape[0]
@@ -301,7 +299,7 @@
             stats[slot * HEADS + head : slot * HEADS + head + 1, columns_of(block)] = row
 
     attention_loop(
-        [inner_keys, keys], query1_t, [inner_values_t, values_t], scores, 256, columns_of, finish
+        [inner_keys, keys], query1_t, [inner_values_t, values_t], scores, 256, 2, columns_of, finish
     )
     for target, side in ((kept, core), (given, 1 - core)):
         for k in range(per_half):
@@ -432,14 +430,15 @@
 
     def finish(head, block, total, top):
         rows = slice(head * head_size, (head + 1) * head_size)
-        read_t[rows, :] = (total[:head_size] / total[head_size : head_size + 1]).astype(BF16)
+        inverse = 1.0 / total[head_size : head_size + 1]
+        read_t[rows, :] = (total[:head_size] * inverse).astype(BF16)
         if head == HEADS - 1:
             pl.when(block >= 2)(lambda: send(block - 2).wait())
             change = dot(read_t[...], w_out2[...], ((0,), (0,)))
             buffers[block % 2] = masked[columns_of(block), :].astype(F32) + change
             send(block).start()
 
-    attention_loop([keys], query2_t, [values_t], scores, 256, columns_of, finish)
+    attention_loop([keys], query2_t, [values_t], scores, 256, blocks, columns_of, finish)
     for block in range(max(blocks - 2, 0), blocks):
         send(block).wait()
 
@@ -593,7 +592,7 @@
     taken = flipped(given, "nc", 1)
     block = shape((width + STAT_ROWS, LANES), BF16)
     blocks = call(merge_pair_kernel, [block] * group_size, [], [kept, taken], 16, step, "merge_pair")
-    blocks = blocks[:1] + [flipped(blocks[d], group, d) for d in range(1, group_size)]
+    blocks = [flipped(blocks[d], group, d) for d in range(group_size - 1, 0, -1)] + blocks[:1]
     parts = call(
         functools.partial(merge_group_kernel, group_size),
         [shape((rows, width + LANES), BF16)] * far,
@@ -603,12 +602,13 @@
         step,
         "merge_group",
     )
-    parts = parts[:1] + [flipped(parts[d], "wz", d) for d in range(1, far)]
+    order = list(range(far - 2, 0, -1)) + [far - 1]
+    parts = [flipped(parts[d], "wz", d) for d in order] + parts[:1]
     start = ((core * group_size + member) * far + layer) * rows
     own = lax.dynamic_slice_in_dim(latents, start, rows, 0)
     state = call(update_kernel, shape((rows, width), BF16), [], [own, w_out1] + parts, 16, step, "update")
-    state = join([state] + [flipped(state, "wz", d) for d in range(1, far)], "join_far")
-    state = join([state] + [flipped(state, group, d) for d in range(1, group_size)], "join_group")
+    state = join([flipped(state, "wz", d) for d in range(far - 1, 0, -1)] + [state], "join_far")
+    state = join([flipped(state, group, d) for d in range(group_size - 1, 0, -1)] + [state], "join_group")
     other = flipped(state, "nc", 1)
     span = 2 * plane_cells
 

time: 108 us -> 106 us (0.981)
  waiting for transfers between devices: 22.9 us -> 20 us
    ppermute x14, waiting for transfers between devices: 22.8 us -> 19.9 us  [flipped(): lax.ppermute(array, axis, [(i, i ^ distance) for i in range(lax.axis_size...]
  transfers between devices with their start and end apart: 18 -> 18, of which waited for: 13 -> 12; matrix products, arithmetic and copies ran while one was open for 0% -> 0% of each run, Pallas kernels for 11% -> 12%
where the time goes in v7:
time: 106 us
  Pallas kernels  58.2 us (55%)
  starting transfers between devices  26.9 us (25%)
  waiting for transfers between devices  20 us (19%)
    pallas_call x12, Pallas kernels, call(): pl.pallas_call(kernel, out_shape=shapes, in_specs=in_specs, out_specs=[vm...  58.2 us
    ppermute x14, starting transfers between devices, flipped(): lax.ppermute(array, axis, [(i, i ^ distance) for i in range(lax.axis_size...  22.3 us
    ppermute x14, waiting for transfers between devices, flipped(): lax.ppermute(array, axis, [(i, i ^ distance) for i in range(lax.axis_size...  19.9 us
    ppermute x2, starting transfers between devices, pair_exchange(): return (lax.ppermute(first, axis, swaps[0]), other)  3.15 us
  transfers between devices with their start and end apart: 18, of which 12 were waited for; matrix products, arithmetic and copies ran while one was open for 0% of the time, Pallas kernels for 12%

profile of v7, /device:TPU:0, one launch (start us, length us, event | category | flops | bytes accessed | tf_op | source)
XLA Modules:
  0.0 105.6 jit_solution(6390761474432356585)
XLA Ops:
  0.0 2.0 %face.1 = (bf16[8,16,512]{2,1,0:T(8,128)(2,1)}, bf16[8,16,512]{2,1,0:T(8,128)(2,1)}) custom-call(bf16[8,16,16,512]{3,2,1,0:T(8,128)(2,1)} %flow.3, s32[8,16,16]{2,1,0:T(8,128)} %far_mask.1), custom_call_target="tpu_custom_call" | custom-call | flops 1000000000 | bytes 2105344 | tf_op jit(solution)/shard_map/face/pallas_call | solution.py:452
  2.1 0.6 collective-permute-start
  2.6 0.8 collective-permute-start.1
  3.4 1.5 %prepare.1.masked = bf16[8,16,16,512]{3,2,1,0:T(8,128)(2,1)S(1)} custom-call(bf16[8,16,16,512]{3,2,1,0:T(8,128)(2,1)S(1)} %copy-done.1, s32[8,16,16]{2,1,0:T(8,128)S(1)} %copy-done.10), custom_call_target="tpu_custom_call" | custom-call | flops 2000000000 | bytes 2105344 | tf_op jit(solution)/shard_map/prepare/pallas_call | solution.py:452
  4.9 0.7 latent_query.1.query1_t
  5.7 0.0 copy-start.3
  5.7 0.0 copy-start.4
  5.7 0.0 copy-start.5
  5.7 0.0 copy-start.11
  5.7 0.0 collective-permute-done.y_first
  5.7 0.0 collective-permute-done.1.y_second
  5.8 0.1 edge.1
  5.8 2.6 %collective-permute-start.2 = (bf16[18,16,512]{2,1,0:T(8,128)(2,1)S(1)}, bf16[18,16,512]{2,1,0:T(8,128)(2,1)S(1)}, u32[]{:S(2)}, u32[]{:S(2)}) collective-permute-start(bf16[18,16,512]{2,1,0:T(8,128)(2,1)S(1)} %get-tuple-element.25), channel_id=1, source_target_pairs={{0,4},{4,0},{8,12},{12,8},{16,20},{20,16},{24,28},{28,24},{1,5},{5... | collective-permute-start | bytes 884744 | tf_op jit(solution)/shard_map/ppermute | solution.py:472
  8.4 0.7 collective-permute-start.3
  9.1 10.1 %inner.1 = (bf16[1536,512]{1,0:T(8,128)(2,1)S(1)}, bf16[8,80,1536]{2,1,0:T(8,128)(2,1)S(1)}, bf16[512,2048]{1,0:T(8,128)(2,1)S(1)}) custom-call(bf16[8,16,16,512]{3,2,1,0:T(8,128)(2,1)S(1)} %prepare.1.masked, bf16[8,16,512]{2,1,0:T(8,128)(2,1)S(1)} %collective-permute-done.y_first, bf16[8,16,512]{2,1,0:T(8,128)(2,1)S(1)} %collective-permute-done.1.y_second, ...), custom_call_target="tpu_custom_call" | custom-call | flops 10000000000 | bytes 3987456 | tf_op jit(solution)/shard_map/inner/pallas_call | solution.py:452
  19.2 21.3 %read.1 = (bf16[512,2048]{1,0:T(8,128)(2,1)S(1)}, bf16[4,560,128]{2,1,0:T(8,128)(2,1)S(1)}, bf16[4,560,128]{2,1,0:T(8,128)(2,1)S(1)}) custom-call(bf16[8,16,16,512]{3,2,1,0:T(8,128)(2,1)S(1)} %prepare.1.masked, bf16[18,16,512]{2,1,0:T(8,128)(2,1)S(1)} %collective-permute-done.2.x_first, ...), custom_call_target="tpu_custom_call", output_to_operand_aliasing={{0}: (12, {})} | custom-call | flops 20000000000 | bytes 11261952 | tf_op jit(solution)/shard_map/read/pallas_call | solution.py:452
  40.5 0.0 copy-start.14
  40.6 4.0 %collective-permute-start.4 = (bf16[4,560,128]{2,1,0:T(8,128)(2,1)S(1)}, bf16[4,560,128]{2,1,0:T(8,128)(2,1)S(1)}, u32[]{:S(2)}, u32[]{:S(2)}) collective-permute-start(bf16[4,560,128]{2,1,0:T(8,128)(2,1)S(1)} %get-tuple-element.31), channel_id=1, source_target_pairs={{0,1},{1,0},{2,3},{3,2},{4,5},{5,4},{6,7},{7,6},{8,9},{9,8},{10,11... | collective-permute-start | bytes 1720328 | tf_op jit(solution)/shard_map/ppermute | solution.py:476
  44.6 1.6 %collective-permute-done.4.taken = bf16[4,560,128]{2,1,0:T(8,128)(2,1)S(1)} collective-permute-done((bf16[4,560,128]{2,1,0:T(8,128)(2,1)S(1)}, bf16[4,560,128]{2,1,0:T(8,128)(2,1)S(1)}, u32[]{:S(2)}, u32[]{:S(2)}) %collective-permute-start.4) | collective-permute-done | bytes 573472 | tf_op jit(solution)/shard_map/ppermute | solution.py:476
  46.2 0.2 merge_pair.1
  46.4 0.0 copy-start.6
  46.5 5.2 %collective-permute-start.5 = (bf16[560,128]{1,0:T(8,128)(2,1)S(1)}, bf16[560,128]{1,0:T(8,128)(2,1)S(1)}, u32[]{:S(2)}, u32[]{:S(2)}) collective-permute-start(bf16[560,128]{1,0:T(8,128)(2,1)S(1)} %get-tuple-element.32), channel_id=1, source_target_pairs={{0,6},{2,4},{4,2},{6,0},{1,7},{3,5},{5,3},{7,1},{8,14},{10,12},{12... | collective-permute-start | bytes 430088 | tf_op jit(solution)/shard_map/ppermute | solution.py:476
  51.6 0.6 collective-permute-start.7
  52.3 4.0 %collective-permute-done.5.refs_0_ = bf16[560,128]{1,0:T(8,128)(2,1)S(1)} collective-permute-done((bf16[560,128]{1,0:T(8,128)(2,1)S(1)}, bf16[560,128]{1,0:T(8,128)(2,1)S(1)}, u32[]{:S(2)}, u32[]{:S(2)}) %collective-permute-start.5) | collective-permute-done | bytes 143392 | tf_op jit(solution)/shard_map/ppermute | solution.py:476
  56.2 1.8 %collective-permute-done.6.refs_1_ = bf16[560,128]{1,0:T(8,128)(2,1)S(1)} collective-permute-done((bf16[560,128]{1,0:T(8,128)(2,1)S(1)}, bf16[560,128]{1,0:T(8,128)(2,1)S(1)}, u32[]{:S(2)}, u32[]{:S(2)}) %collective-permute-start.6) | collective-permute-done | bytes 143392 | tf_op jit(solution)/shard_map/ppermute | solution.py:476
  58.0 0.7 collective-permute-done.7.refs_2_
  58.7 0.2 merge_group.1
  59.0 2.8 %collective-permute-start.10 = (bf16[32,640]{1,0:T(8,128)(2,1)S(1)}, bf16[32,640]{1,0:T(8,128)(2,1)S(1)}, u32[]{:S(2)}, u32[]{:S(2)}) collective-permute-start(bf16[32,640]{1,0:T(8,128)(2,1)S(1)} %get-tuple-element.38), channel_id=1, source_target_pairs={{0,24},{8,16},{16,8},{24,0},{1,25},{9,17},{17,9},{25,1},{2,26},{10... | collective-permute-start | bytes 122888 | tf_op jit(solution)/shard_map/ppermute | solution.py:476
  61.8 0.3 collective-permute-start.8
  62.1 1.3 %collective-permute-start.9 = (bf16[32,640]{1,0:T(8,128)(2,1)S(1)}, bf16[32,640]{1,0:T(8,128)(2,1)S(1)}, u32[]{:S(2)}, u32[]{:S(2)}) collective-permute-start(bf16[32,640]{1,0:T(8,128)(2,1)S(1)} %get-tuple-element.37), channel_id=1, source_target_pairs={{0,8},{8,0},{16,24},{24,16},{1,9},{9,1},{17,25},{25,17},{2,10},{10... | collective-permute-start | bytes 122888 | tf_op jit(solution)/shard_map/ppermute | solution.py:476
  63.4 1.5 %collective-permute-done.10.refs_2_ = bf16[32,640]{1,0:T(8,128)(2,1)S(1)} collective-permute-done((bf16[32,640]{1,0:T(8,128)(2,1)S(1)}, bf16[32,640]{1,0:T(8,128)(2,1)S(1)}, u32[]{:S(2)}, u32[]{:S(2)}) %collective-permute-start.10) | collective-permute-done | bytes 40992 | tf_op jit(solution)/shard_map/ppermute | solution.py:476
  64.9 2.1 %collective-permute-done.8.refs_0_ = bf16[32,640]{1,0:T(8,128)(2,1)S(1)} collective-permute-done((bf16[32,640]{1,0:T(8,128)(2,1)S(1)}, bf16[32,640]{1,0:T(8,128)(2,1)S(1)}, u32[]{:S(2)}, u32[]{:S(2)}) %collective-permute-start.8) | collective-permute-done | bytes 40992 | tf_op jit(solution)/shard_map/ppermute | solution.py:476
  67.1 0.0 copy-start.8
  67.1 0.0 copy-start.9
  67.1 0.5 update.1.refs_3_
  67.6 2.1 %collective-permute-start.11 = (bf16[32,512]{1,0:T(8,128)(2,1)S(1)}, bf16[32,512]{1,0:T(8,128)(2,1)S(1)}, u32[]{:S(2)}, u32[]{:S(2)}) collective-permute-start(bf16[32,512]{1,0:T(8,128)(2,1)S(1)} %update.1.refs_3_), channel_id=1, source_target_pairs={{0,24},{8,16},{16,8},{24,0},{1,25},{9,17},{17,9},{25,1},{2,26},{10... | collective-permute-start | bytes 98312 | tf_op jit(solution)/shard_map/ppermute | solution.py:476
  69.8 2.3 %collective-permute-start.13 = (bf16[32,512]{1,0:T(8,128)(2,1)S(1)}, bf16[32,512]{1,0:T(8,128)(2,1)S(1)}, u32[]{:S(2)}, u32[]{:S(2)}) collective-permute-start(bf16[32,512]{1,0:T(8,128)(2,1)S(1)} %update.1.refs_3_), channel_id=1, source_target_pairs={{0,8},{8,0},{16,24},{24,16},{1,9},{9,1},{17,25},{25,17},{2,10},{10... | collective-permute-start | bytes 98312 | tf_op jit(solution)/shard_map/ppermute | solution.py:476
  72.0 1.3 %collective-permute-done.11.refs_0_ = bf16[32,512]{1,0:T(8,128)(2,1)S(1)} collective-permute-done((bf16[32,512]{1,0:T(8,128)(2,1)S(1)}, bf16[32,512]{1,0:T(8,128)(2,1)S(1)}, u32[]{:S(2)}, u32[]{:S(2)}) %collective-permute-start.11) | collective-permute-done | bytes 32800 | tf_op jit(solution)/shard_map/ppermute | solution.py:476
  73.3 1.2 %collective-permute-done.12.refs_1_ = bf16[32,512]{1,0:T(8,128)(2,1)S(1)} collective-permute-done((bf16[32,512]{1,0:T(8,128)(2,1)S(1)}, bf16[32,512]{1,0:T(8,128)(2,1)S(1)}, u32[]{:S(2)}, u32[]{:S(2)}) %collective-permute-start.12) | collective-permute-done | bytes 32800 | tf_op jit(solution)/shard_map/ppermute | solution.py:476
  74.6 2.1 %collective-permute-start.14 = (bf16[128,512]{1,0:T(8,128)(2,1)S(1)}, bf16[128,512]{1,0:T(8,128)(2,1)S(1)}, u32[]{:S(2)}, u32[]{:S(2)}) collective-permute-start(bf16[128,512]{1,0:T(8,128)(2,1)S(1)} %join_far.1.refs_3_), channel_id=1, source_target_pairs={{0,6},{2,4},{4,2},{6,0},{1,7},{3,5},{5,3},{7,1},{8,14},{10,12},{12... | collective-permute-start | bytes 393224 | tf_op jit(solution)/shard_map/ppermute | solution.py:476
  76.7 0.2 collective-permute-start.15
  76.9 1.3 %collective-permute-start.16 = (bf16[128,512]{1,0:T(8,128)(2,1)S(1)}, bf16[128,512]{1,0:T(8,128)(2,1)S(1)}, u32[]{:S(2)}, u32[]{:S(2)}) collective-permute-start(bf16[128,512]{1,0:T(8,128)(2,1)S(1)} %join_far.1.refs_3_), channel_id=1, source_target_pairs={{0,2},{2,0},{4,6},{6,4},{1,3},{3,1},{5,7},{7,5},{8,10},{10,8},{12,... | collective-permute-start | bytes 393224 | tf_op jit(solution)/shard_map/ppermute | solution.py:476
  78.2 2.4 %collective-permute-done.14.refs_0_ = bf16[128,512]{1,0:T(8,128)(2,1)S(1)} collective-permute-done((bf16[128,512]{1,0:T(8,128)(2,1)S(1)}, bf16[128,512]{1,0:T(8,128)(2,1)S(1)}, u32[]{:S(2)}, u32[]{:S(2)}) %collective-permute-start.14) | collective-permute-done | bytes 131104 | tf_op jit(solution)/shard_map/ppermute | solution.py:476
  80.5 1.1 %collective-permute-done.15.refs_1_ = bf16[128,512]{1,0:T(8,128)(2,1)S(1)} collective-permute-done((bf16[128,512]{1,0:T(8,128)(2,1)S(1)}, bf16[128,512]{1,0:T(8,128)(2,1)S(1)}, u32[]{:S(2)}, u32[]{:S(2)}) %collective-permute-start.15) | collective-permute-done | bytes 131104 | tf_op jit(solution)/shard_map/ppermute | solution.py:476
  81.7 0.3 collective-permute-done.16.refs_2_
  82.0 0.1 collective-permute-start.17
  82.1 1.9 %collective-permute-done.17.other_state = bf16[512,512]{1,0:T(8,128)(2,1)S(1)} collective-permute-done((bf16[512,512]{1,0:T(8,128)(2,1)S(1)}, bf16[512,512]{1,0:T(8,128)(2,1)S(1)}, u32[]{:S(2)}, u32[]{:S(2)}) %collective-permute-start.17) | collective-permute-done | bytes 524320 | tf_op jit(solution)/shard_map/ppermute | solution.py:476
  84.0 21.4 %write.1 = f32[2048,512]{1,0:T(8,128)} custom-call(bf16[512,512]{1,0:T(8,128)(2,1)S(1)} %join_group.1.own_state, bf16[512,512]{1,0:T(8,128)(2,1)S(1)} %collective-permute-done.17.other_state, bf16[512,2048]{1,0:T(8,128)(2,1)S(1)} %copy-done.15, bf16[2048,512]{1,0:T(8,128)(2,1)S(1)} %bitcast.2, bf16[512,512]{1,0:T(8,128)(2,1)S(1)} %copy-done.7, ...), custom_call_target="tpu_custom_call" | custom-call | flops 20000000000 | bytes 6815744 | tf_op jit(solution)/shard_map/write/pallas_call | solution.py:452
  (33 shorter events, 0.1 us)
Async XLA Ops:
  0.0 3.4 %copy-start.1 = (bf16[8,16,16,512]{3,2,1,0:T(8,128)(2,1)S(1)}, bf16[8,16,16,512]{3,2,1,0:T(8,128)(2,1)}, u32[]{:S(2)}) copy-start(bf16[8,16,16,512]{3,2,1,0:T(8,128)(2,1)} %flow.3) | copy-start | bytes 6291460
  0.0 3.4 %copy-start.10 = (s32[8,16,16]{2,1,0:T(8,128)S(1)}, s32[8,16,16]{2,1,0:T(8,128)}, u32[]{:S(2)}) copy-start(s32[8,16,16]{2,1,0:T(8,128)} %far_mask.1) | copy-start | bytes 24580
  2.1 3.7 %collective-permute-start = (bf16[8,16,512]{2,1,0:T(8,128)(2,1)}, bf16[8,16,512]{2,1,0:T(8,128)(2,1)S(1)}, u32[]{:S(2)}, u32[]{:S(2)}) collective-permute-start(bf16[8,16,512]{2,1,0:T(8,128)(2,1)} %get-tuple-element.23), channel_id=1, source_target_pairs={{0,1},{1,0},{2,3},{3,2},{4,5},{5,4},{6,7},{7,6},{8,9},{9,8},{10,11... | collective-permute-start | bytes 393224 | tf_op jit(solution)/shard_map/ppermute | solution.py:472
  2.6 2.3 %copy-start = (bf16[1024,512]{1,0:T(8,128)(2,1)S(1)}, bf16[1024,512]{1,0:T(8,128)(2,1)}, u32[]{:S(2)}) copy-start(bf16[1024,512]{1,0:T(8,128)(2,1)} %latents.1) | copy-start | bytes 3145732
  2.6 2.3 %copy-start.2 = (bf16[512,512]{1,0:T(8,128)(2,1)S(1)}, bf16[512,512]{1,0:T(8,128)(2,1)}, u32[]{:S(2)}) copy-start(bf16[512,512]{1,0:T(8,128)(2,1)} %w_query1.1) | copy-start | bytes 1572868
  2.6 3.1 %collective-permute-start.1 = (bf16[8,16,512]{2,1,0:T(8,128)(2,1)}, bf16[8,16,512]{2,1,0:T(8,128)(2,1)S(1)}, u32[]{:S(2)}, u32[]{:S(2)}) collective-permute-start(bf16[8,16,512]{2,1,0:T(8,128)(2,1)} %get-tuple-element.24), channel_id=1, source_target_pairs={{1,2},{2,1},{5,6},{6,5},{9,10},{10,9},{13,14},{14,13},{17,18},{18,... | collective-permute-start | bytes 393224 | tf_op jit(solution)/shard_map/ppermute | solution.py:471
  4.9 14.3 %copy-start.12 = (bf16[8,16,16,512]{3,2,1,0:T(8,128)(2,1)}, bf16[8,16,16,512]{3,2,1,0:T(8,128)(2,1)S(1)}, u32[]{:S(2)}) copy-start(bf16[8,16,16,512]{3,2,1,0:T(8,128)(2,1)S(1)} %prepare.1.masked) | copy-start | bytes 6291460
  5.7 3.4 %copy-start.3 = (bf16[512,512]{1,0:T(8,128)(2,1)S(1)}, bf16[512,512]{1,0:T(8,128)(2,1)}, u32[]{:S(2)}) copy-start(bf16[512,512]{1,0:T(8,128)(2,1)} %w_key1.1) | copy-start | bytes 1572868
  5.7 3.4 %copy-start.4 = (bf16[512,512]{1,0:T(8,128)(2,1)S(1)}, bf16[512,512]{1,0:T(8,128)(2,1)}, u32[]{:S(2)}) copy-start(bf16[512,512]{1,0:T(8,128)(2,1)} %w_value1.1) | copy-start | bytes 1572868
  5.7 3.4 %copy-start.5 = (bf16[512,512]{1,0:T(8,128)(2,1)S(1)}, bf16[512,512]{1,0:T(8,128)(2,1)}, u32[]{:S(2)}) copy-start(bf16[512,512]{1,0:T(8,128)(2,1)} %w_query2.1) | copy-start | bytes 1572868
  5.7 3.4 %copy-start.11 = (f32[27,512]{1,0:T(8,128)S(1)}, f32[27,512]{1,0:T(8,128)}, u32[]{:S(2)}) copy-start(f32[27,512]{1,0:T(8,128)} %conv.3) | copy-start | bytes 165892
  5.8 13.4 %collective-permute-start.2 = (bf16[18,16,512]{2,1,0:T(8,128)(2,1)S(1)}, bf16[18,16,512]{2,1,0:T(8,128)(2,1)S(1)}, u32[]{:S(2)}, u32[]{:S(2)}) collective-permute-start(bf16[18,16,512]{2,1,0:T(8,128)(2,1)S(1)} %get-tuple-element.25), channel_id=1, source_target_pairs={{0,4},{4,0},{8,12},{12,8},{16,20},{20,16},{24,28},{28,24},{1,5},{5... | collective-permute-start | bytes 884744 | tf_op jit(solution)/shard_map/ppermute | solution.py:472
  8.4 10.8 %collective-permute-start.3 = (bf16[18,16,512]{2,1,0:T(8,128)(2,1)S(1)}, bf16[18,16,512]{2,1,0:T(8,128)(2,1)S(1)}, u32[]{:S(2)}, u32[]{:S(2)}) collective-permute-start(bf16[18,16,512]{2,1,0:T(8,128)(2,1)S(1)} %get-tuple-element.26), channel_id=1, source_target_pairs={{4,8},{8,4},{12,16},{16,12},{20,24},{24,20},{5,9},{9,5},{13,17},{1... | collective-permute-start | bytes 884744 | tf_op jit(solution)/shard_map/ppermute | solution.py:471
  40.5 11.7 %copy-start.14 = (bf16[512,2048]{1,0:T(8,128)(2,1)}, bf16[512,2048]{1,0:T(8,128)(2,1)S(1)}, u32[]{:S(2)}) copy-start(bf16[512,2048]{1,0:T(8,128)(2,1)S(1)} %get-tuple-element.40.query2_t) | copy-start | bytes 6291460
  40.6 5.6 %collective-permute-start.4 = (bf16[4,560,128]{2,1,0:T(8,128)(2,1)S(1)}, bf16[4,560,128]{2,1,0:T(8,128)(2,1)S(1)}, u32[]{:S(2)}, u32[]{:S(2)}) collective-permute-start(bf16[4,560,128]{2,1,0:T(8,128)(2,1)S(1)} %get-tuple-element.31), channel_id=1, source_target_pairs={{0,1},{1,0},{2,3},{3,2},{4,5},{5,4},{6,7},{7,6},{8,9},{9,8},{10,11... | collective-permute-start | bytes 1720328 | tf_op jit(solution)/shard_map/ppermute | solution.py:476
  46.4 20.6 %copy-start.6 = (bf16[512,512]{1,0:T(8,128)(2,1)S(1)}, bf16[512,512]{1,0:T(8,128)(2,1)}, u32[]{:S(2)}) copy-start(bf16[512,512]{1,0:T(8,128)(2,1)} %w_out1.1) | copy-start | bytes 1572868
  46.5 9.8 %collective-permute-start.5 = (bf16[560,128]{1,0:T(8,128)(2,1)S(1)}, bf16[560,128]{1,0:T(8,128)(2,1)S(1)}, u32[]{:S(2)}, u32[]{:S(2)}) collective-permute-start(bf16[560,128]{1,0:T(8,128)(2,1)S(1)} %get-tuple-element.32), channel_id=1, source_target_pairs={{0,6},{2,4},{4,2},{6,0},{1,7},{3,5},{5,3},{7,1},{8,14},{10,12},{12... | collective-permute-start | bytes 430088 | tf_op jit(solution)/shard_map/ppermute | solution.py:476
  51.6 6.4 %collective-permute-start.6 = (bf16[560,128]{1,0:T(8,128)(2,1)S(1)}, bf16[560,128]{1,0:T(8,128)(2,1)S(1)}, u32[]{:S(2)}, u32[]{:S(2)}) collective-permute-start(bf16[560,128]{1,0:T(8,128)(2,1)S(1)} %get-tuple-element.33), channel_id=1, source_target_pairs={{0,4},{2,6},{4,0},{6,2},{1,5},{3,7},{5,1},{7,3},{8,12},{10,14},{12... | collective-permute-start | bytes 430088 | tf_op jit(solution)/shard_map/ppermute | solution.py:476
  51.6 7.1 %collective-permute-start.7 = (bf16[560,128]{1,0:T(8,128)(2,1)S(1)}, bf16[560,128]{1,0:T(8,128)(2,1)S(1)}, u32[]{:S(2)}, u32[]{:S(2)}) collective-permute-start(bf16[560,128]{1,0:T(8,128)(2,1)S(1)} %get-tuple-element.34), channel_id=1, source_target_pairs={{0,2},{2,0},{4,6},{6,4},{1,3},{3,1},{5,7},{7,5},{8,10},{10,8},{12,... | collective-permute-start | bytes 430088 | tf_op jit(solution)/shard_map/ppermute | solution.py:476
  58.7 25.2 %copy-start.15 = (bf16[512,2048]{1,0:T(8,128)(2,1)S(1)}, bf16[512,2048]{1,0:T(8,128)(2,1)}, u32[]{:S(2)}) copy-start(bf16[512,2048]{1,0:T(8,128)(2,1)} %copy-done.14) | copy-start | bytes 6291460
  59.0 6.0 %collective-permute-start.10 = (bf16[32,640]{1,0:T(8,128)(2,1)S(1)}, bf16[32,640]{1,0:T(8,128)(2,1)S(1)}, u32[]{:S(2)}, u32[]{:S(2)}) collective-permute-start(bf16[32,640]{1,0:T(8,128)(2,1)S(1)} %get-tuple-element.38), channel_id=1, source_target_pairs={{0,24},{8,16},{16,8},{24,0},{1,25},{9,17},{17,9},{25,1},{2,26},{10... | collective-permute-start | bytes 122888 | tf_op jit(solution)/shard_map/ppermute | solution.py:476
  61.8 5.2 %collective-permute-start.8 = (bf16[32,640]{1,0:T(8,128)(2,1)S(1)}, bf16[32,640]{1,0:T(8,128)(2,1)S(1)}, u32[]{:S(2)}, u32[]{:S(2)}) collective-permute-start(bf16[32,640]{1,0:T(8,128)(2,1)S(1)} %get-tuple-element.36), channel_id=1, source_target_pairs={{0,16},{8,24},{16,0},{24,8},{1,17},{9,25},{17,1},{25,9},{2,18},{10... | collective-permute-start | bytes 122888 | tf_op jit(solution)/shard_map/ppermute | solution.py:476
  62.1 5.0 %collective-permute-start.9 = (bf16[32,640]{1,0:T(8,128)(2,1)S(1)}, bf16[32,640]{1,0:T(8,128)(2,1)S(1)}, u32[]{:S(2)}, u32[]{:S(2)}) collective-permute-start(bf16[32,640]{1,0:T(8,128)(2,1)S(1)} %get-tuple-element.37), channel_id=1, source_target_pairs={{0,8},{8,0},{16,24},{24,16},{1,9},{9,1},{17,25},{25,17},{2,10},{10... | collective-permute-start | bytes 122888 | tf_op jit(solution)/shard_map/ppermute | solution.py:476
  67.0 16.9 %copy-start.7 = (bf16[512,512]{1,0:T(8,128)(2,1)S(1)}, bf16[512,512]{1,0:T(8,128)(2,1)}, u32[]{:S(2)}) copy-start(bf16[512,512]{1,0:T(8,128)(2,1)} %w_key2.1) | copy-start | bytes 1572868
  67.1 16.9 %copy-start.8 = (bf16[512,512]{1,0:T(8,128)(2,1)S(1)}, bf16[512,512]{1,0:T(8,128)(2,1)}, u32[]{:S(2)}) copy-start(bf16[512,512]{1,0:T(8,128)(2,1)} %w_value2.1) | copy-start | bytes 1572868
  67.1 16.9 %copy-start.9 = (bf16[512,512]{1,0:T(8,128)(2,1)S(1)}, bf16[512,512]{1,0:T(8,128)(2,1)}, u32[]{:S(2)}) copy-start(bf16[512,512]{1,0:T(8,128)(2,1)} %w_out2.1) | copy-start | bytes 1572868
  67.1 16.9 %copy-start.13 = (bf16[8,16,16,512]{3,2,1,0:T(8,128)(2,1)S(1)}, bf16[8,16,16,512]{3,2,1,0:T(8,128)(2,1)}, u32[]{:S(2)}) copy-start(bf16[8,16,16,512]{3,2,1,0:T(8,128)(2,1)} %copy-done.12) | copy-start | bytes 6291460
  67.6 5.7 %collective-permute-start.11 = (bf16[32,512]{1,0:T(8,128)(2,1)S(1)}, bf16[32,512]{1,0:T(8,128)(2,1)S(1)}, u32[]{:S(2)}, u32[]{:S(2)}) collective-permute-start(bf16[32,512]{1,0:T(8,128)(2,1)S(1)} %update.1.refs_3_), channel_id=1, source_target_pairs={{0,24},{8,16},{16,8},{24,0},{1,25},{9,17},{17,9},{25,1},{2,26},{10... | collective-permute-start | bytes 98312 | tf_op jit(solution)/shard_map/ppermute | solution.py:476
  69.8 4.8 %collective-permute-start.12 = (bf16[32,512]{1,0:T(8,128)(2,1)S(1)}, bf16[32,512]{1,0:T(8,128)(2,1)S(1)}, u32[]{:S(2)}, u32[]{:S(2)}) collective-permute-start(bf16[32,512]{1,0:T(8,128)(2,1)S(1)} %update.1.refs_3_), channel_id=1, source_target_pairs={{0,16},{8,24},{16,0},{24,8},{1,17},{9,25},{17,1},{25,9},{2,18},{10... | collective-permute-start | bytes 98312 | tf_op jit(solution)/shard_map/ppermute | solution.py:476
  69.8 4.8 %collective-permute-start.13 = (bf16[32,512]{1,0:T(8,128)(2,1)S(1)}, bf16[32,512]{1,0:T(8,128)(2,1)S(1)}, u32[]{:S(2)}, u32[]{:S(2)}) collective-permute-start(bf16[32,512]{1,0:T(8,128)(2,1)S(1)} %update.1.refs_3_), channel_id=1, source_target_pairs={{0,8},{8,0},{16,24},{24,16},{1,9},{9,1},{17,25},{25,17},{2,10},{10... | collective-permute-start | bytes 98312 | tf_op jit(solution)/shard_map/ppermute | solution.py:476
  74.6 5.9 %collective-permute-start.14 = (bf16[128,512]{1,0:T(8,128)(2,1)S(1)}, bf16[128,512]{1,0:T(8,128)(2,1)S(1)}, u32[]{:S(2)}, u32[]{:S(2)}) collective-permute-start(bf16[128,512]{1,0:T(8,128)(2,1)S(1)} %join_far.1.refs_3_), channel_id=1, source_target_pairs={{0,6},{2,4},{4,2},{6,0},{1,7},{3,5},{5,3},{7,1},{8,14},{10,12},{12... | collective-permute-start | bytes 393224 | tf_op jit(solution)/shard_map/ppermute | solution.py:476
  76.7 5.0 %collective-permute-start.15 = (bf16[128,512]{1,0:T(8,128)(2,1)S(1)}, bf16[128,512]{1,0:T(8,128)(2,1)S(1)}, u32[]{:S(2)}, u32[]{:S(2)}) collective-permute-start(bf16[128,512]{1,0:T(8,128)(2,1)S(1)} %join_far.1.refs_3_), channel_id=1, source_target_pairs={{0,4},{2,6},{4,0},{6,2},{1,5},{3,7},{5,1},{7,3},{8,12},{10,14},{12... | collective-permute-start | bytes 393224 | tf_op jit(solution)/shard_map/ppermute | solution.py:476
  76.9 5.0 %collective-permute-start.16 = (bf16[128,512]{1,0:T(8,128)(2,1)S(1)}, bf16[128,512]{1,0:T(8,128)(2,1)S(1)}, u32[]{:S(2)}, u32[]{:S(2)}) collective-permute-start(bf16[128,512]{1,0:T(8,128)(2,1)S(1)} %join_far.1.refs_3_), channel_id=1, source_target_pairs={{0,2},{2,0},{4,6},{6,4},{1,3},{3,1},{5,7},{7,5},{8,10},{10,8},{12,... | collective-permute-start | bytes 393224 | tf_op jit(solution)/shard_map/ppermute | solution.py:476
  82.0 2.0 %collective-permute-start.17 = (bf16[512,512]{1,0:T(8,128)(2,1)S(1)}, bf16[512,512]{1,0:T(8,128)(2,1)S(1)}, u32[]{:S(2)}, u32[]{:S(2)}) collective-permute-start(bf16[512,512]{1,0:T(8,128)(2,1)S(1)} %join_group.1.own_state), channel_id=1, source_target_pairs={{0,1},{1,0},{2,3},{3,2},{4,5},{5,4},{6,7},{7,6},{8,9},{9,8},{10,11... | collective-permute-start | bytes 1572872 | tf_op jit(solution)/shard_map/ppermute | solution.py:476

commit v8 on v7

--- a/solution.py
+++ b/solution.py
@@ -75,13 +75,16 @@
     padded[row, outer * lax.axis_index("nc")] = y_second[i].astype(F32)
 
 
-def stencil_plane(base, padded, conv, mixed, start):
+def stencil_plane(base, padded, conv, mixed, start, others=()):
     size_y, size_z, width = padded.shape[1] - 2, padded.shape[2], padded.shape[3]
     row_of = lax.broadcasted_iota(jnp.int32, (size_z, LANES), 0)
+    others = list(others)
     for tile in range(width // LANES):
         lanes = slice(tile * LANES, (tile + 1) * LANES)
         taps = [jnp.broadcast_to(conv[n : n + 1, lanes], (size_z, LANES)) for n in range(27)]
         for j in range(size_y):
+            if others and j % (size_y // 2) == 0:
+                others.pop(0)()
             sums = [None] * 3
             for a in range(3):
                 for b in range(3):
@@ -93,17 +96,36 @@
             above = jnp.where(row_of == size_z - 1, 0.0, pltpu.roll(sums[2], size_z - 1, 0))
             total = padded[base + 1, j + 1, :, lanes] + sums[1] + below + above
             mixed[pl.ds(pl.multiple_of(start + j * size_z, size_z), size_z), lanes] = total.astype(BF16)
-
-
-def project_plane(start, target, cells, mixed, weights, keys, values_t, query2_t):
+    for other in others:
+        other()
+
+
+def projections(start, target, cells, mixed, weights, keys, values_t, query2_t):
     w_key1, w_value1, w_query2 = weights
-    head_size = mixed.shape[1] // HEADS
+    width = mixed.shape[1]
+    head_size = width // HEADS
     rows = pl.ds(pl.multiple_of(start, cells), cells)
-    block = mixed[rows, :]
-    keys[rows, :] = dot(block, w_key1[...]).astype(BF16)
-    value_t = dot(w_value1[...], block, ((0,), (1,))).astype(BF16)
-    values_t[:, :head_size, rows] = value_t.reshape(HEADS, head_size, cells)
-    query2_t[:, pl.ds(pl.multiple_of(target, cells), cells)] = dot(w_query2[...], block, ((0,), (1,))).astype(BF16)
+    columns = pl.ds(pl.multiple_of(target, cells), cells)
+    work = []
+    for part in range(2):
+
+        def key_part(part=part):
+            some = pl.ds(pl.multiple_of(start + part * (cells // 2), cells // 2), cells // 2)
+            keys[some, :] = dot(mixed[some, :], w_key1[...]).astype(BF16)
+
+        def value_part(part=part):
+            channels = slice(part * (width // 2), (part + 1) * (width // 2))
+            value_t = dot(w_value1[channels, :], mixed[rows, :], ((1,), (1,))).astype(BF16)
+            heads = slice(part * (HEADS // 2), (part + 1) * (HEADS // 2))
+            values_t[heads, :head_size, rows] = value_t.reshape(HEADS // 2, head_size, cells)
+
+        def query_part(part=part):
+            channels = slice(part * (width // 2), (part + 1) * (width // 2))
+            found = dot(w_query2[channels, :], mixed[rows, :], ((1,), (1,)))
+            query2_t[channels, columns] = found.astype(BF16)
+
+        work += [key_part, value_part, query_part]
+    return work
 
 
 def latent_query_kernel(latents, w_query1, query1_t):
@@ -121,6 +143,8 @@
     keys,
     values_t,
     query2_t,
+    turned_value1,
+    turned_query2,
     padded,
     mixed,
     w_key1,
@@ -131,10 +155,10 @@
     size_x, size_y, size_z, width = masked.shape
     head_size = width // HEADS
     cells = size_y * size_z
-    weights = (w_key1, w_value1, w_query2)
+    weights = (w_key1, turned_value1, turned_query2)
     copies = [
         pltpu.make_async_copy(source, target, arrived.at[n])
-        for n, (source, target) in enumerate(zip((far_key1, far_value1, far_query2), weights))
+        for n, (source, target) in enumerate(zip((far_key1, far_value1, far_query2), (w_key1, w_value1, w_query2)))
     ]
     for copy in copies:
         copy.start()
@@ -147,13 +171,21 @@
     values_t[:, head_size:, :] = jnp.ones_like(values_t[:, head_size:, :])
     for copy in copies:
         copy.wait()
+    turned_value1[...] = w_value1[...].T
+    turned_query2[...] = w_query2[...].T
+
+    def work(i):
+        return projections(i * cells, (i + 1) * cells, cells, mixed, weights, keys, values_t, query2_t)
+
+    stencil_plane(0, padded, conv, mixed, 0)
 
     def plane(i, carry):
-        stencil_plane(i, padded, conv, mixed, i * cells)
-        project_plane(i * cells, (i + 1) * cells, cells, mixed, weights, keys, values_t, query2_t)
+        stencil_plane(i, padded, conv, mixed, i * cells, work(i - 1))
         return carry
 
-    lax.fori_loop(0, size_x - 2, plane, 0)
+    lax.fori_loop(1, size_x - 2, plane, 0)
+    for product in work(size_x - 3):
+        product()
 
 
 def score_weights(query_t, head, columns):
@@ -272,12 +304,14 @@
 
     weights = (w_key1, w_value1, w_query2)
 
-    def plane(i, carry):
-        stencil_plane(3 * i, padded, conv, mixed, i * cells)
-        project_plane(i * cells, i * last * cells, cells, mixed, weights, keys, values_t, query2_t)
-        return carry
-
-    lax.fori_loop(0, 2, plane, 0)
+
+    def work(i):
+        return projections(i * cells, i * last * cells, cells, mixed, weights, keys, values_t, query2_t)
+
+    stencil_plane(0, padded, conv, mixed, 0)
+    stencil_plane(3, padded, conv, mixed, cells, work(0))
+    for product in work(1):
+        product()
 
     core = lax.axis_index("nc")
     per_half = kept.shape[0]
@@ -536,12 +570,14 @@
     )
     x_first, x_second = pair_exchange(x_first, x_second, wide)
     weight = pltpu.VMEM((width, width), BF16)
-    inner_keys, inner_values_t, query2_t = call(
+    inner_keys, inner_values_t, query2_t, turned_value1, turned_query2 = call(
         inner_kernel,
         [
             shape((inner_cells, width), BF16),
             shape((HEADS, head_size + ONES_ROWS, inner_cells), BF16),
             shape((width, cells), BF16),
+            shape((width, width), BF16),
+            shape((width, width), BF16),
         ],
         [
             pltpu.VMEM((size_x, size_y + 2, size_z, width), F32),
@@ -576,8 +612,8 @@
             y_second,
             conv_weight,
             w_key1,
-            w_value1,
-            w_query2,
+            turned_value1,
+            turned_query2,
             inner_keys,
             inner_values_t,
             query1_t,

time: 106 us -> 105 us (level)
  transfers between devices with their start and end apart: 18 -> 18, of which waited for: 12 -> 12; matrix products, arithmetic and copies ran while one was open for 0% -> 0% of each run, Pallas kernels for 12% -> 11%
where the time goes in v8:
time: 105 us
  Pallas kernels  57.9 us (55%)
  starting transfers between devices  26.9 us (26%)
  waiting for transfers between devices  19.9 us (19%)
    pallas_call x12, Pallas kernels, call(): pl.pallas_call(kernel, out_shape=shapes, in_specs=in_specs, out_specs=[vm...  57.9 us
    ppermute x14, starting transfers between devices, flipped(): lax.ppermute(array, axis, [(i, i ^ distance) for i in range(lax.axis_size...  22.3 us
    ppermute x14, waiting for transfers between devices, flipped(): lax.ppermute(array, axis, [(i, i ^ distance) for i in range(lax.axis_size...  19.9 us
    ppermute x2, starting transfers between devices, pair_exchange(): return (lax.ppermute(first, axis, swaps[0]), other)  3.15 us
  transfers between devices with their start and end apart: 18, of which 12 were waited for; matrix products, arithmetic and copies ran while one was open for 0% of the time, Pallas kernels for 11%

profile of v8, /device:TPU:0, one launch (start us, length us, event | category | flops | bytes accessed | tf_op | source)
XLA Modules:
  0.0 105.3 jit_solution(7181091374077223492)
XLA Ops:
  0.0 2.0 %face.1 = (bf16[8,16,512]{2,1,0:T(8,128)(2,1)}, bf16[8,16,512]{2,1,0:T(8,128)(2,1)}) custom-call(bf16[8,16,16,512]{3,2,1,0:T(8,128)(2,1)} %flow.3, s32[8,16,16]{2,1,0:T(8,128)} %far_mask.1), custom_call_target="tpu_custom_call" | custom-call | flops 1000000000 | bytes 2105344 | tf_op jit(solution)/shard_map/face/pallas_call | solution.py:486
  2.1 0.6 collective-permute-start
  2.6 0.8 collective-permute-start.1
  3.4 1.5 %prepare.1.masked = bf16[8,16,16,512]{3,2,1,0:T(8,128)(2,1)S(1)} custom-call(bf16[8,16,16,512]{3,2,1,0:T(8,128)(2,1)S(1)} %copy-done.1, s32[8,16,16]{2,1,0:T(8,128)S(1)} %copy-done.10), custom_call_target="tpu_custom_call" | custom-call | flops 2000000000 | bytes 2105344 | tf_op jit(solution)/shard_map/prepare/pallas_call | solution.py:486
  4.9 0.7 latent_query.1.query1_t
  5.7 0.0 copy-start.3
  5.7 0.0 copy-start.4
  5.7 0.0 copy-start.5
  5.7 0.0 copy-start.11
  5.7 0.0 collective-permute-done.y_first
  5.8 0.1 edge.1
  5.8 2.6 %collective-permute-start.2 = (bf16[18,16,512]{2,1,0:T(8,128)(2,1)S(1)}, bf16[18,16,512]{2,1,0:T(8,128)(2,1)S(1)}, u32[]{:S(2)}, u32[]{:S(2)}) collective-permute-start(bf16[18,16,512]{2,1,0:T(8,128)(2,1)S(1)} %get-tuple-element.27), channel_id=1, source_target_pairs={{0,4},{4,0},{8,12},{12,8},{16,20},{20,16},{24,28},{28,24},{1,5},{5... | collective-permute-start | bytes 884744 | tf_op jit(solution)/shard_map/ppermute | solution.py:506
  8.4 0.7 collective-permute-start.3
  9.1 9.9 %inner.1 = (bf16[1536,512]{1,0:T(8,128)(2,1)S(1)}, bf16[8,80,1536]{2,1,0:T(8,128)(2,1)S(1)}, bf16[512,2048]{1,0:T(8,128)(2,1)S(1)}, bf16[512,512]{1,0:T(8,128)(2,1)S(1)}, bf16[512,512]{1,0:T(8,128)(2,1)S(1)}) custom-call(bf16[8,16,16,512]{3,2,1,0:T(8,128)(2,1)S(1)} %prepare.1.masked, bf16[8,16,512]{2,1,0:T(8,128)(2,1)S(1)} %collective-permute-done.y_first, ...), custom_call_target="tpu_custom_call" | custom-call | flops 10000000000 | bytes 3987456 | tf_op jit(solution)/shard_map/inner/pallas_call | solution.py:486
  19.0 0.0 collective-permute-done.2.x_first
  19.0 21.0 %read.1 = (bf16[512,2048]{1,0:T(8,128)(2,1)S(1)}, bf16[4,560,128]{2,1,0:T(8,128)(2,1)S(1)}, bf16[4,560,128]{2,1,0:T(8,128)(2,1)S(1)}) custom-call(bf16[8,16,16,512]{3,2,1,0:T(8,128)(2,1)S(1)} %prepare.1.masked, bf16[18,16,512]{2,1,0:T(8,128)(2,1)S(1)} %collective-permute-done.2.x_first, ...), custom_call_target="tpu_custom_call", output_to_operand_aliasing={{0}: (12, {})} | custom-call | flops 20000000000 | bytes 11261952 | tf_op jit(solution)/shard_map/read/pallas_call | solution.py:486
  40.1 0.0 copy-start.14
  40.1 4.0 %collective-permute-start.4 = (bf16[4,560,128]{2,1,0:T(8,128)(2,1)S(1)}, bf16[4,560,128]{2,1,0:T(8,128)(2,1)S(1)}, u32[]{:S(2)}, u32[]{:S(2)}) collective-permute-start(bf16[4,560,128]{2,1,0:T(8,128)(2,1)S(1)} %get-tuple-element.35), channel_id=1, source_target_pairs={{0,1},{1,0},{2,3},{3,2},{4,5},{5,4},{6,7},{7,6},{8,9},{9,8},{10,11... | collective-permute-start | bytes 1720328 | tf_op jit(solution)/shard_map/ppermute | solution.py:510
  44.1 1.6 %collective-permute-done.4.taken = bf16[4,560,128]{2,1,0:T(8,128)(2,1)S(1)} collective-permute-done((bf16[4,560,128]{2,1,0:T(8,128)(2,1)S(1)}, bf16[4,560,128]{2,1,0:T(8,128)(2,1)S(1)}, u32[]{:S(2)}, u32[]{:S(2)}) %collective-permute-start.4) | collective-permute-done | bytes 573472 | tf_op jit(solution)/shard_map/ppermute | solution.py:510
  45.7 0.2 merge_pair.1
  45.9 0.0 copy-start.6
  45.9 5.2 %collective-permute-start.5 = (bf16[560,128]{1,0:T(8,128)(2,1)S(1)}, bf16[560,128]{1,0:T(8,128)(2,1)S(1)}, u32[]{:S(2)}, u32[]{:S(2)}) collective-permute-start(bf16[560,128]{1,0:T(8,128)(2,1)S(1)} %get-tuple-element.36), channel_id=1, source_target_pairs={{0,6},{2,4},{4,2},{6,0},{1,7},{3,5},{5,3},{7,1},{8,14},{10,12},{12... | collective-permute-start | bytes 430088 | tf_op jit(solution)/shard_map/ppermute | solution.py:510
  51.2 0.6 collective-permute-start.7
  51.8 4.0 %collective-permute-done.5.refs_0_ = bf16[560,128]{1,0:T(8,128)(2,1)S(1)} collective-permute-done((bf16[560,128]{1,0:T(8,128)(2,1)S(1)}, bf16[560,128]{1,0:T(8,128)(2,1)S(1)}, u32[]{:S(2)}, u32[]{:S(2)}) %collective-permute-start.5) | collective-permute-done | bytes 143392 | tf_op jit(solution)/shard_map/ppermute | solution.py:510
  55.8 1.8 %collective-permute-done.6.refs_1_ = bf16[560,128]{1,0:T(8,128)(2,1)S(1)} collective-permute-done((bf16[560,128]{1,0:T(8,128)(2,1)S(1)}, bf16[560,128]{1,0:T(8,128)(2,1)S(1)}, u32[]{:S(2)}, u32[]{:S(2)}) %collective-permute-start.6) | collective-permute-done | bytes 143392 | tf_op jit(solution)/shard_map/ppermute | solution.py:510
  57.6 0.7 collective-permute-done.7.refs_2_
  58.3 0.2 merge_group.1
  58.5 2.8 %collective-permute-start.10 = (bf16[32,640]{1,0:T(8,128)(2,1)S(1)}, bf16[32,640]{1,0:T(8,128)(2,1)S(1)}, u32[]{:S(2)}, u32[]{:S(2)}) collective-permute-start(bf16[32,640]{1,0:T(8,128)(2,1)S(1)} %get-tuple-element.42), channel_id=1, source_target_pairs={{0,24},{8,16},{16,8},{24,0},{1,25},{9,17},{17,9},{25,1},{2,26},{10... | collective-permute-start | bytes 122888 | tf_op jit(solution)/shard_map/ppermute | solution.py:510
  61.3 0.3 collective-permute-start.8
  61.7 1.3 %collective-permute-start.9 = (bf16[32,640]{1,0:T(8,128)(2,1)S(1)}, bf16[32,640]{1,0:T(8,128)(2,1)S(1)}, u32[]{:S(2)}, u32[]{:S(2)}) collective-permute-start(bf16[32,640]{1,0:T(8,128)(2,1)S(1)} %get-tuple-element.41), channel_id=1, source_target_pairs={{0,8},{8,0},{16,24},{24,16},{1,9},{9,1},{17,25},{25,17},{2,10},{10... | collective-permute-start | bytes 122888 | tf_op jit(solution)/shard_map/ppermute | solution.py:510
  63.0 1.5 %collective-permute-done.10.refs_2_ = bf16[32,640]{1,0:T(8,128)(2,1)S(1)} collective-permute-done((bf16[32,640]{1,0:T(8,128)(2,1)S(1)}, bf16[32,640]{1,0:T(8,128)(2,1)S(1)}, u32[]{:S(2)}, u32[]{:S(2)}) %collective-permute-start.10) | collective-permute-done | bytes 40992 | tf_op jit(solution)/shard_map/ppermute | solution.py:510
  64.5 2.1 %collective-permute-done.8.refs_0_ = bf16[32,640]{1,0:T(8,128)(2,1)S(1)} collective-permute-done((bf16[32,640]{1,0:T(8,128)(2,1)S(1)}, bf16[32,640]{1,0:T(8,128)(2,1)S(1)}, u32[]{:S(2)}, u32[]{:S(2)}) %collective-permute-start.8) | collective-permute-done | bytes 40992 | tf_op jit(solution)/shard_map/ppermute | solution.py:510
  66.6 0.0 copy-start.8
  66.6 0.0 copy-start.9
  66.7 0.5 update.1.refs_3_
  67.2 2.1 %collective-permute-start.11 = (bf16[32,512]{1,0:T(8,128)(2,1)S(1)}, bf16[32,512]{1,0:T(8,128)(2,1)S(1)}, u32[]{:S(2)}, u32[]{:S(2)}) collective-permute-start(bf16[32,512]{1,0:T(8,128)(2,1)S(1)} %update.1.refs_3_), channel_id=1, source_target_pairs={{0,24},{8,16},{16,8},{24,0},{1,25},{9,17},{17,9},{25,1},{2,26},{10... | collective-permute-start | bytes 98312 | tf_op jit(solution)/shard_map/ppermute | solution.py:510
  69.3 2.3 %collective-permute-start.13 = (bf16[32,512]{1,0:T(8,128)(2,1)S(1)}, bf16[32,512]{1,0:T(8,128)(2,1)S(1)}, u32[]{:S(2)}, u32[]{:S(2)}) collective-permute-start(bf16[32,512]{1,0:T(8,128)(2,1)S(1)} %update.1.refs_3_), channel_id=1, source_target_pairs={{0,8},{8,0},{16,24},{24,16},{1,9},{9,1},{17,25},{25,17},{2,10},{10... | collective-permute-start | bytes 98312 | tf_op jit(solution)/shard_map/ppermute | solution.py:510
  71.6 1.3 %collective-permute-done.11.refs_0_ = bf16[32,512]{1,0:T(8,128)(2,1)S(1)} collective-permute-done((bf16[32,512]{1,0:T(8,128)(2,1)S(1)}, bf16[32,512]{1,0:T(8,128)(2,1)S(1)}, u32[]{:S(2)}, u32[]{:S(2)}) %collective-permute-start.11) | collective-permute-done | bytes 32800 | tf_op jit(solution)/shard_map/ppermute | solution.py:510
  72.9 1.2 %collective-permute-done.12.refs_1_ = bf16[32,512]{1,0:T(8,128)(2,1)S(1)} collective-permute-done((bf16[32,512]{1,0:T(8,128)(2,1)S(1)}, bf16[32,512]{1,0:T(8,128)(2,1)S(1)}, u32[]{:S(2)}, u32[]{:S(2)}) %collective-permute-start.12) | collective-permute-done | bytes 32800 | tf_op jit(solution)/shard_map/ppermute | solution.py:510
  74.1 2.1 %collective-permute-start.14 = (bf16[128,512]{1,0:T(8,128)(2,1)S(1)}, bf16[128,512]{1,0:T(8,128)(2,1)S(1)}, u32[]{:S(2)}, u32[]{:S(2)}) collective-permute-start(bf16[128,512]{1,0:T(8,128)(2,1)S(1)} %join_far.1.refs_3_), channel_id=1, source_target_pairs={{0,6},{2,4},{4,2},{6,0},{1,7},{3,5},{5,3},{7,1},{8,14},{10,12},{12... | collective-permute-start | bytes 393224 | tf_op jit(solution)/shard_map/ppermute | solution.py:510
  76.3 0.2 collective-permute-start.15
  76.4 1.2 %collective-permute-start.16 = (bf16[128,512]{1,0:T(8,128)(2,1)S(1)}, bf16[128,512]{1,0:T(8,128)(2,1)S(1)}, u32[]{:S(2)}, u32[]{:S(2)}) collective-permute-start(bf16[128,512]{1,0:T(8,128)(2,1)S(1)} %join_far.1.refs_3_), channel_id=1, source_target_pairs={{0,2},{2,0},{4,6},{6,4},{1,3},{3,1},{5,7},{7,5},{8,10},{10,8},{12,... | collective-permute-start | bytes 393224 | tf_op jit(solution)/shard_map/ppermute | solution.py:510
  77.7 2.4 %collective-permute-done.14.refs_0_ = bf16[128,512]{1,0:T(8,128)(2,1)S(1)} collective-permute-done((bf16[128,512]{1,0:T(8,128)(2,1)S(1)}, bf16[128,512]{1,0:T(8,128)(2,1)S(1)}, u32[]{:S(2)}, u32[]{:S(2)}) %collective-permute-start.14) | collective-permute-done | bytes 131104 | tf_op jit(solution)/shard_map/ppermute | solution.py:510
  80.1 1.2 %collective-permute-done.15.refs_1_ = bf16[128,512]{1,0:T(8,128)(2,1)S(1)} collective-permute-done((bf16[128,512]{1,0:T(8,128)(2,1)S(1)}, bf16[128,512]{1,0:T(8,128)(2,1)S(1)}, u32[]{:S(2)}, u32[]{:S(2)}) %collective-permute-start.15) | collective-permute-done | bytes 131104 | tf_op jit(solution)/shard_map/ppermute | solution.py:510
  81.2 0.2 collective-permute-done.16.refs_2_
  81.5 0.1 collective-permute-start.17
  81.6 1.9 %collective-permute-done.17.other_state = bf16[512,512]{1,0:T(8,128)(2,1)S(1)} collective-permute-done((bf16[512,512]{1,0:T(8,128)(2,1)S(1)}, bf16[512,512]{1,0:T(8,128)(2,1)S(1)}, u32[]{:S(2)}, u32[]{:S(2)}) %collective-permute-start.17) | collective-permute-done | bytes 524320 | tf_op jit(solution)/shard_map/ppermute | solution.py:510
  83.5 21.6 %write.1 = f32[2048,512]{1,0:T(8,128)} custom-call(bf16[512,512]{1,0:T(8,128)(2,1)S(1)} %join_group.1.own_state, bf16[512,512]{1,0:T(8,128)(2,1)S(1)} %collective-permute-done.17.other_state, bf16[512,2048]{1,0:T(8,128)(2,1)S(1)} %copy-done.15, bf16[2048,512]{1,0:T(8,128)(2,1)S(1)} %bitcast.2, bf16[512,512]{1,0:T(8,128)(2,1)S(1)} %copy-done.7, ...), custom_call_target="tpu_custom_call" | custom-call | flops 20000000000 | bytes 6815744 | tf_op jit(solution)/shard_map/write/pallas_call | solution.py:486
  (33 shorter events, 0.1 us)
Async XLA Ops:
  0.0 3.4 %copy-start.1 = (bf16[8,16,16,512]{3,2,1,0:T(8,128)(2,1)S(1)}, bf16[8,16,16,512]{3,2,1,0:T(8,128)(2,1)}, u32[]{:S(2)}) copy-start(bf16[8,16,16,512]{3,2,1,0:T(8,128)(2,1)} %flow.3) | copy-start | bytes 6291460
  0.0 3.4 %copy-start.10 = (s32[8,16,16]{2,1,0:T(8,128)S(1)}, s32[8,16,16]{2,1,0:T(8,128)}, u32[]{:S(2)}) copy-start(s32[8,16,16]{2,1,0:T(8,128)} %far_mask.1) | copy-start | bytes 24580
  2.1 3.7 %collective-permute-start = (bf16[8,16,512]{2,1,0:T(8,128)(2,1)}, bf16[8,16,512]{2,1,0:T(8,128)(2,1)S(1)}, u32[]{:S(2)}, u32[]{:S(2)}) collective-permute-start(bf16[8,16,512]{2,1,0:T(8,128)(2,1)} %get-tuple-element.25), channel_id=1, source_target_pairs={{0,1},{1,0},{2,3},{3,2},{4,5},{5,4},{6,7},{7,6},{8,9},{9,8},{10,11... | collective-permute-start | bytes 393224 | tf_op jit(solution)/shard_map/ppermute | solution.py:506
  2.6 2.3 %copy-start = (bf16[1024,512]{1,0:T(8,128)(2,1)S(1)}, bf16[1024,512]{1,0:T(8,128)(2,1)}, u32[]{:S(2)}) copy-start(bf16[1024,512]{1,0:T(8,128)(2,1)} %latents.1) | copy-start | bytes 3145732
  2.6 2.3 %copy-start.2 = (bf16[512,512]{1,0:T(8,128)(2,1)S(1)}, bf16[512,512]{1,0:T(8,128)(2,1)}, u32[]{:S(2)}) copy-start(bf16[512,512]{1,0:T(8,128)(2,1)} %w_query1.1) | copy-start | bytes 1572868
  2.6 3.1 %collective-permute-start.1 = (bf16[8,16,512]{2,1,0:T(8,128)(2,1)}, bf16[8,16,512]{2,1,0:T(8,128)(2,1)S(1)}, u32[]{:S(2)}, u32[]{:S(2)}) collective-permute-start(bf16[8,16,512]{2,1,0:T(8,128)(2,1)} %get-tuple-element.26), channel_id=1, source_target_pairs={{1,2},{2,1},{5,6},{6,5},{9,10},{10,9},{13,14},{14,13},{17,18},{18,... | collective-permute-start | bytes 393224 | tf_op jit(solution)/shard_map/ppermute | solution.py:505
  4.9 14.1 %copy-start.12 = (bf16[8,16,16,512]{3,2,1,0:T(8,128)(2,1)}, bf16[8,16,16,512]{3,2,1,0:T(8,128)(2,1)S(1)}, u32[]{:S(2)}) copy-start(bf16[8,16,16,512]{3,2,1,0:T(8,128)(2,1)S(1)} %prepare.1.masked) | copy-start | bytes 6291460
  5.7 3.4 %copy-start.3 = (bf16[512,512]{1,0:T(8,128)(2,1)S(1)}, bf16[512,512]{1,0:T(8,128)(2,1)}, u32[]{:S(2)}) copy-start(bf16[512,512]{1,0:T(8,128)(2,1)} %far_value1.1) | copy-start | bytes 1572868
  5.7 3.4 %copy-start.4 = (bf16[512,512]{1,0:T(8,128)(2,1)S(1)}, bf16[512,512]{1,0:T(8,128)(2,1)}, u32[]{:S(2)}) copy-start(bf16[512,512]{1,0:T(8,128)(2,1)} %far_query2.1) | copy-start | bytes 1572868
  5.7 3.4 %copy-start.5 = (bf16[512,512]{1,0:T(8,128)(2,1)S(1)}, bf16[512,512]{1,0:T(8,128)(2,1)}, u32[]{:S(2)}) copy-start(bf16[512,512]{1,0:T(8,128)(2,1)} %w_key1.1) | copy-start | bytes 1572868
  5.7 3.4 %copy-start.11 = (f32[27,512]{1,0:T(8,128)S(1)}, f32[27,512]{1,0:T(8,128)}, u32[]{:S(2)}) copy-start(f32[27,512]{1,0:T(8,128)} %conv.3) | copy-start | bytes 165892
  5.8 13.2 %collective-permute-start.2 = (bf16[18,16,512]{2,1,0:T(8,128)(2,1)S(1)}, bf16[18,16,512]{2,1,0:T(8,128)(2,1)S(1)}, u32[]{:S(2)}, u32[]{:S(2)}) collective-permute-start(bf16[18,16,512]{2,1,0:T(8,128)(2,1)S(1)} %get-tuple-element.27), channel_id=1, source_target_pairs={{0,4},{4,0},{8,12},{12,8},{16,20},{20,16},{24,28},{28,24},{1,5},{5... | collective-permute-start | bytes 884744 | tf_op jit(solution)/shard_map/ppermute | solution.py:506
  8.4 10.6 %collective-permute-start.3 = (bf16[18,16,512]{2,1,0:T(8,128)(2,1)S(1)}, bf16[18,16,512]{2,1,0:T(8,128)(2,1)S(1)}, u32[]{:S(2)}, u32[]{:S(2)}) collective-permute-start(bf16[18,16,512]{2,1,0:T(8,128)(2,1)S(1)} %get-tuple-element.28), channel_id=1, source_target_pairs={{4,8},{8,4},{12,16},{16,12},{20,24},{24,20},{5,9},{9,5},{13,17},{1... | collective-permute-start | bytes 884744 | tf_op jit(solution)/shard_map/ppermute | solution.py:505
  40.1 11.7 %copy-start.14 = (bf16[512,2048]{1,0:T(8,128)(2,1)}, bf16[512,2048]{1,0:T(8,128)(2,1)S(1)}, u32[]{:S(2)}) copy-start(bf16[512,2048]{1,0:T(8,128)(2,1)S(1)} %get-tuple-element.44.query2_t) | copy-start | bytes 6291460
  40.1 5.6 %collective-permute-start.4 = (bf16[4,560,128]{2,1,0:T(8,128)(2,1)S(1)}, bf16[4,560,128]{2,1,0:T(8,128)(2,1)S(1)}, u32[]{:S(2)}, u32[]{:S(2)}) collective-permute-start(bf16[4,560,128]{2,1,0:T(8,128)(2,1)S(1)} %get-tuple-element.35), channel_id=1, source_target_pairs={{0,1},{1,0},{2,3},{3,2},{4,5},{5,4},{6,7},{7,6},{8,9},{9,8},{10,11... | collective-permute-start | bytes 1720328 | tf_op jit(solution)/shard_map/ppermute | solution.py:510
  45.9 20.7 %copy-start.6 = (bf16[512,512]{1,0:T(8,128)(2,1)S(1)}, bf16[512,512]{1,0:T(8,128)(2,1)}, u32[]{:S(2)}) copy-start(bf16[512,512]{1,0:T(8,128)(2,1)} %w_out1.1) | copy-start | bytes 1572868
  45.9 9.8 %collective-permute-start.5 = (bf16[560,128]{1,0:T(8,128)(2,1)S(1)}, bf16[560,128]{1,0:T(8,128)(2,1)S(1)}, u32[]{:S(2)}, u32[]{:S(2)}) collective-permute-start(bf16[560,128]{1,0:T(8,128)(2,1)S(1)} %get-tuple-element.36), channel_id=1, source_target_pairs={{0,6},{2,4},{4,2},{6,0},{1,7},{3,5},{5,3},{7,1},{8,14},{10,12},{12... | collective-permute-start | bytes 430088 | tf_op jit(solution)/shard_map/ppermute | solution.py:510
  51.2 6.4 %collective-permute-start.6 = (bf16[560,128]{1,0:T(8,128)(2,1)S(1)}, bf16[560,128]{1,0:T(8,128)(2,1)S(1)}, u32[]{:S(2)}, u32[]{:S(2)}) collective-permute-start(bf16[560,128]{1,0:T(8,128)(2,1)S(1)} %get-tuple-element.37), channel_id=1, source_target_pairs={{0,4},{2,6},{4,0},{6,2},{1,5},{3,7},{5,1},{7,3},{8,12},{10,14},{12... | collective-permute-start | bytes 430088 | tf_op jit(solution)/shard_map/ppermute | solution.py:510
  51.2 7.1 %collective-permute-start.7 = (bf16[560,128]{1,0:T(8,128)(2,1)S(1)}, bf16[560,128]{1,0:T(8,128)(2,1)S(1)}, u32[]{:S(2)}, u32[]{:S(2)}) collective-permute-start(bf16[560,128]{1,0:T(8,128)(2,1)S(1)} %get-tuple-element.38), channel_id=1, source_target_pairs={{0,2},{2,0},{4,6},{6,4},{1,3},{3,1},{5,7},{7,5},{8,10},{10,8},{12,... | collective-permute-start | bytes 430088 | tf_op jit(solution)/shard_map/ppermute | solution.py:510
  58.3 25.2 %copy-start.15 = (bf16[512,2048]{1,0:T(8,128)(2,1)S(1)}, bf16[512,2048]{1,0:T(8,128)(2,1)}, u32[]{:S(2)}) copy-start(bf16[512,2048]{1,0:T(8,128)(2,1)} %copy-done.14) | copy-start | bytes 6291460
  58.5 6.0 %collective-permute-start.10 = (bf16[32,640]{1,0:T(8,128)(2,1)S(1)}, bf16[32,640]{1,0:T(8,128)(2,1)S(1)}, u32[]{:S(2)}, u32[]{:S(2)}) collective-permute-start(bf16[32,640]{1,0:T(8,128)(2,1)S(1)} %get-tuple-element.42), channel_id=1, source_target_pairs={{0,24},{8,16},{16,8},{24,0},{1,25},{9,17},{17,9},{25,1},{2,26},{10... | collective-permute-start | bytes 122888 | tf_op jit(solution)/shard_map/ppermute | solution.py:510
  61.3 5.3 %collective-permute-start.8 = (bf16[32,640]{1,0:T(8,128)(2,1)S(1)}, bf16[32,640]{1,0:T(8,128)(2,1)S(1)}, u32[]{:S(2)}, u32[]{:S(2)}) collective-permute-start(bf16[32,640]{1,0:T(8,128)(2,1)S(1)} %get-tuple-element.40), channel_id=1, source_target_pairs={{0,16},{8,24},{16,0},{24,8},{1,17},{9,25},{17,1},{25,9},{2,18},{10... | collective-permute-start | bytes 122888 | tf_op jit(solution)/shard_map/ppermute | solution.py:510
  61.7 5.0 %collective-permute-start.9 = (bf16[32,640]{1,0:T(8,128)(2,1)S(1)}, bf16[32,640]{1,0:T(8,128)(2,1)S(1)}, u32[]{:S(2)}, u32[]{:S(2)}) collective-permute-start(bf16[32,640]{1,0:T(8,128)(2,1)S(1)} %get-tuple-element.41), channel_id=1, source_target_pairs={{0,8},{8,0},{16,24},{24,16},{1,9},{9,1},{17,25},{25,17},{2,10},{10... | collective-permute-start | bytes 122888 | tf_op jit(solution)/shard_map/ppermute | solution.py:510
  66.6 16.9 %copy-start.7 = (bf16[512,512]{1,0:T(8,128)(2,1)S(1)}, bf16[512,512]{1,0:T(8,128)(2,1)}, u32[]{:S(2)}) copy-start(bf16[512,512]{1,0:T(8,128)(2,1)} %w_key2.1) | copy-start | bytes 1572868
  66.6 16.9 %copy-start.8 = (bf16[512,512]{1,0:T(8,128)(2,1)S(1)}, bf16[512,512]{1,0:T(8,128)(2,1)}, u32[]{:S(2)}) copy-start(bf16[512,512]{1,0:T(8,128)(2,1)} %w_value2.1) | copy-start | bytes 1572868
  66.6 16.9 %copy-start.9 = (bf16[512,512]{1,0:T(8,128)(2,1)S(1)}, bf16[512,512]{1,0:T(8,128)(2,1)}, u32[]{:S(2)}) copy-start(bf16[512,512]{1,0:T(8,128)(2,1)} %w_out2.1) | copy-start | bytes 1572868
  66.6 16.9 %copy-start.13 = (bf16[8,16,16,512]{3,2,1,0:T(8,128)(2,1)S(1)}, bf16[8,16,16,512]{3,2,1,0:T(8,128)(2,1)}, u32[]{:S(2)}) copy-start(bf16[8,16,16,512]{3,2,1,0:T(8,128)(2,1)} %copy-done.12) | copy-start | bytes 6291460
  67.2 5.7 %collective-permute-start.11 = (bf16[32,512]{1,0:T(8,128)(2,1)S(1)}, bf16[32,512]{1,0:T(8,128)(2,1)S(1)}, u32[]{:S(2)}, u32[]{:S(2)}) collective-permute-start(bf16[32,512]{1,0:T(8,128)(2,1)S(1)} %update.1.refs_3_), channel_id=1, source_target_pairs={{0,24},{8,16},{16,8},{24,0},{1,25},{9,17},{17,9},{25,1},{2,26},{10... | collective-permute-start | bytes 98312 | tf_op jit(solution)/shard_map/ppermute | solution.py:510
  69.3 4.8 %collective-permute-start.12 = (bf16[32,512]{1,0:T(8,128)(2,1)S(1)}, bf16[32,512]{1,0:T(8,128)(2,1)S(1)}, u32[]{:S(2)}, u32[]{:S(2)}) collective-permute-start(bf16[32,512]{1,0:T(8,128)(2,1)S(1)} %update.1.refs_3_), channel_id=1, source_target_pairs={{0,16},{8,24},{16,0},{24,8},{1,17},{9,25},{17,1},{25,9},{2,18},{10... | collective-permute-start | bytes 98312 | tf_op jit(solution)/shard_map/ppermute | solution.py:510
  69.3 4.8 %collective-permute-start.13 = (bf16[32,512]{1,0:T(8,128)(2,1)S(1)}, bf16[32,512]{1,0:T(8,128)(2,1)S(1)}, u32[]{:S(2)}, u32[]{:S(2)}) collective-permute-start(bf16[32,512]{1,0:T(8,128)(2,1)S(1)} %update.1.refs_3_), channel_id=1, source_target_pairs={{0,8},{8,0},{16,24},{24,16},{1,9},{9,1},{17,25},{25,17},{2,10},{10... | collective-permute-start | bytes 98312 | tf_op jit(solution)/shard_map/ppermute | solution.py:510
  74.1 5.9 %collective-permute-start.14 = (bf16[128,512]{1,0:T(8,128)(2,1)S(1)}, bf16[128,512]{1,0:T(8,128)(2,1)S(1)}, u32[]{:S(2)}, u32[]{:S(2)}) collective-permute-start(bf16[128,512]{1,0:T(8,128)(2,1)S(1)} %join_far.1.refs_3_), channel_id=1, source_target_pairs={{0,6},{2,4},{4,2},{6,0},{1,7},{3,5},{5,3},{7,1},{8,14},{10,12},{12... | collective-permute-start | bytes 393224 | tf_op jit(solution)/shard_map/ppermute | solution.py:510
  76.3 5.0 %collective-permute-start.15 = (bf16[128,512]{1,0:T(8,128)(2,1)S(1)}, bf16[128,512]{1,0:T(8,128)(2,1)S(1)}, u32[]{:S(2)}, u32[]{:S(2)}) collective-permute-start(bf16[128,512]{1,0:T(8,128)(2,1)S(1)} %join_far.1.refs_3_), channel_id=1, source_target_pairs={{0,4},{2,6},{4,0},{6,2},{1,5},{3,7},{5,1},{7,3},{8,12},{10,14},{12... | collective-permute-start | bytes 393224 | tf_op jit(solution)/shard_map/ppermute | solution.py:510
  76.4 5.0 %collective-permute-start.16 = (bf16[128,512]{1,0:T(8,128)(2,1)S(1)}, bf16[128,512]{1,0:T(8,128)(2,1)S(1)}, u32[]{:S(2)}, u32[]{:S(2)}) collective-permute-start(bf16[128,512]{1,0:T(8,128)(2,1)S(1)} %join_far.1.refs_3_), channel_id=1, source_target_pairs={{0,2},{2,0},{4,6},{6,4},{1,3},{3,1},{5,7},{7,5},{8,10},{10,8},{12,... | collective-permute-start | bytes 393224 | tf_op jit(solution)/shard_map/ppermute | solution.py:510
  81.5 2.0 %collective-permute-start.17 = (bf16[512,512]{1,0:T(8,128)(2,1)S(1)}, bf16[512,512]{1,0:T(8,128)(2,1)S(1)}, u32[]{:S(2)}, u32[]{:S(2)}) collective-permute-start(bf16[512,512]{1,0:T(8,128)(2,1)S(1)} %join_group.1.own_state), channel_id=1, source_target_pairs={{0,1},{1,0},{2,3},{3,2},{4,5},{5,4},{6,7},{7,6},{8,9},{9,8},{10,11... | collective-permute-start | bytes 1572872 | tf_op jit(solution)/shard_map/ppermute | solution.py:510

commit v9 on v5

--- a/solution.py
+++ b/solution.py
@@ -59,7 +59,7 @@
     lax.fori_loop(0, size_x, plane, 0)
 
 
-def edge_kernel(masked, y_first, y_second, first, second):
+def edge_kernel(masked, y_second, y_first, first, second):
     size_x, size_y = masked.shape[:2]
     outer = size_y + 1
     for face, plane in ((first, (size_x - 1) * (1 - lax.axis_index("wx"))), (second, (size_x - 1) * lax.axis_index("wx"))):
@@ -432,7 +432,8 @@
 
     def finish(head, block, total, top):
         rows = slice(head * head_size, (head + 1) * head_size)
-        read_t[rows, :] = (total[:head_size] / total[head_size : head_size + 1]).astype(BF16)
+        inverse = 1.0 / total[head_size : head_size + 1]
+        read_t[rows, :] = (total[:head_size] * inverse).astype(BF16)
         if head == HEADS - 1:
             pl.when(block >= 2)(lambda: send(block - 2).wait())
             change = dot(read_t[...], w_out2[...], ((0,), (0,)))
@@ -533,7 +534,7 @@
     )
     side = shape((size_y + 2, size_z, width), BF16)
     x_first, x_second = call(
-        edge_kernel, [side, side], [], [masked, y_first, y_second], 12, step, "edge"
+        edge_kernel, [side, side], [], [masked, y_second, y_first], 12, step, "edge"
     )
     x_first, x_second = pair_exchange(x_first, x_second, wide)
     weight = pltpu.VMEM((width, width), BF16)
@@ -593,7 +594,7 @@
     taken = flipped(given, "nc", 1)
     block = shape((width + STAT_ROWS, LANES), BF16)
     blocks = call(merge_pair_kernel, [block] * group_size, [], [kept, taken], 16, step, "merge_pair")
-    blocks = blocks[:1] + [flipped(blocks[d], group, d) for d in range(1, group_size)]
+    blocks = [flipped(blocks[d], group, d) for d in range(group_size - 1, 0, -1)] + blocks[:1]
     parts = call(
         functools.partial(merge_group_kernel, group_size),
         [shape((rows, width + LANES), BF16)] * far,
@@ -603,12 +604,13 @@
         step,
         "merge_group",
     )
-    parts = parts[:1] + [flipped(parts[d], "wz", d) for d in range(1, far)]
+    order = list(range(far - 2, 0, -1)) + [far - 1]
+    parts = [flipped(parts[d], "wz", d) for d in order] + parts[:1]
     start = ((core * group_size + member) * far + layer) * rows
     own = lax.dynamic_slice_in_dim(latents, start, rows, 0)
     state = call(update_kernel, shape((rows, width), BF16), [], [own, w_out1] + parts, 16, step, "update")
-    state = join([state] + [flipped(state, "wz", d) for d in range(1, far)], "join_far")
-    state = join([state] + [flipped(state, group, d) for d in range(1, group_size)], "join_group")
+    state = join([flipped(state, "wz", d) for d in range(far - 1, 0, -1)] + [state], "join_far")
+    state = join([flipped(state, group, d) for d in range(group_size - 1, 0, -1)] + [state], "join_group")
     other = flipped(state, "nc", 1)
     span = 2 * plane_cells
 

time: 108 us -> 106 us (0.981)
  starting transfers between devices: 26.8 us -> 24.3 us
    ppermute x14, starting transfers between devices: 22.2 us -> 17 us  [flipped(): lax.ppermute(array, axis, [(i, i ^ distance) for i in range(lax.axis_size...]
    ppermute x2, starting transfers between devices: 3.15 us -> 5.96 us  [pair_exchange(): return (lax.ppermute(first, axis, swaps[0]), other)]
    ppermute x2, waiting for transfers between devices: 0.01 us -> 2.75 us  [pair_exchange(): return (lax.ppermute(first, axis, swaps[0]), other)]
    ppermute x14, waiting for transfers between devices: 22.8 us -> 20.4 us  [flipped(): lax.ppermute(array, axis, [(i, i ^ distance) for i in range(lax.axis_size...]
where the time goes in v9:
time: 106 us
  Pallas kernels  57.6 us (54%)
  starting transfers between devices  24.3 us (23%)
  waiting for transfers between devices  23.1 us (22%)
    pallas_call x12, Pallas kernels, call(): pl.pallas_call(kernel, out_shape=shapes, in_specs=in_specs, out_specs=[vm...  57.6 us
    ppermute x14, waiting for transfers between devices, flipped(): lax.ppermute(array, axis, [(i, i ^ distance) for i in range(lax.axis_size...  20.4 us
    ppermute x14, starting transfers between devices, flipped(): lax.ppermute(array, axis, [(i, i ^ distance) for i in range(lax.axis_size...  17 us
    ppermute x2, starting transfers between devices, pair_exchange(): return (lax.ppermute(first, axis, swaps[0]), other)  5.96 us
    ppermute x2, waiting for transfers between devices, pair_exchange(): return (lax.ppermute(first, axis, swaps[0]), other)  2.75 us
  transfers between devices with their start and end apart: 18, of which 13 were waited for; matrix products, arithmetic and copies ran while one was open for 0% of the time, Pallas kernels for 11%

profile of v9, /device:TPU:0, one launch (start us, length us, event | category | flops | bytes accessed | tf_op | source)
XLA Modules:
  0.0 105.6 jit_solution(5435032011676131094)
XLA Ops:
  0.0 2.0 %face.1 = (bf16[8,16,512]{2,1,0:T(8,128)(2,1)}, bf16[8,16,512]{2,1,0:T(8,128)(2,1)}) custom-call(bf16[8,16,16,512]{3,2,1,0:T(8,128)(2,1)} %flow.3, s32[8,16,16]{2,1,0:T(8,128)} %far_mask.1), custom_call_target="tpu_custom_call" | custom-call | flops 1000000000 | bytes 2105344 | tf_op jit(solution)/shard_map/face/pallas_call | solution.py:454
  2.1 0.7 collective-permute-start
  2.7 0.0 copy-start
  2.7 0.0 copy-start.2
  2.8 4.4 %collective-permute-start.1 = (bf16[8,16,512]{2,1,0:T(8,128)(2,1)}, bf16[8,16,512]{2,1,0:T(8,128)(2,1)S(1)}, u32[]{:S(2)}, u32[]{:S(2)}) collective-permute-start(bf16[8,16,512]{2,1,0:T(8,128)(2,1)} %get-tuple-element.24), channel_id=1, source_target_pairs={{0,1},{1,0},{2,3},{3,2},{4,5},{5,4},{6,7},{7,6},{8,9},{9,8},{10,11... | collective-permute-start | bytes 393224 | tf_op jit(solution)/shard_map/ppermute | solution.py:474
  7.2 1.5 %prepare.1.masked = bf16[8,16,16,512]{3,2,1,0:T(8,128)(2,1)S(1)} custom-call(bf16[8,16,16,512]{3,2,1,0:T(8,128)(2,1)S(1)} %copy-done.1, s32[8,16,16]{2,1,0:T(8,128)S(1)} %copy-done.10), custom_call_target="tpu_custom_call" | custom-call | flops 2000000000 | bytes 2105344 | tf_op jit(solution)/shard_map/prepare/pallas_call | solution.py:454
  8.7 0.8 latent_query.1.query1_t
  9.4 0.0 copy-start.3
  9.5 0.0 copy-start.4
  9.5 0.0 copy-start.11
  9.5 0.1 edge.1
  9.6 1.5 %collective-permute-start.2 = (bf16[18,16,512]{2,1,0:T(8,128)(2,1)S(1)}, bf16[18,16,512]{2,1,0:T(8,128)(2,1)S(1)}, u32[]{:S(2)}, u32[]{:S(2)}) collective-permute-start(bf16[18,16,512]{2,1,0:T(8,128)(2,1)S(1)} %get-tuple-element.25), channel_id=1, source_target_pairs={{0,4},{4,0},{8,12},{12,8},{16,20},{20,16},{24,28},{28,24},{1,5},{5... | collective-permute-start | bytes 884744 | tf_op jit(solution)/shard_map/ppermute | solution.py:474
  11.1 0.7 collective-permute-start.3
  11.8 9.7 %inner.1 = (bf16[1536,512]{1,0:T(8,128)(2,1)S(1)}, bf16[8,80,1536]{2,1,0:T(8,128)(2,1)S(1)}, bf16[512,2048]{1,0:T(8,128)(2,1)S(1)}) custom-call(bf16[8,16,16,512]{3,2,1,0:T(8,128)(2,1)S(1)} %prepare.1.masked, bf16[8,16,512]{2,1,0:T(8,128)(2,1)S(1)} %collective-permute-done.1.y_first, bf16[8,16,512]{2,1,0:T(8,128)(2,1)S(1)} %collective-permute-done.y_second, ...), custom_call_target="tpu_custom_call" | custom-call | flops 10000000000 | bytes 3987456 | tf_op jit(solution)/shard_map/inner/pallas_call | solution.py:454
  21.5 2.7 %collective-permute-done.2.x_first = bf16[18,16,512]{2,1,0:T(8,128)(2,1)S(1)} collective-permute-done((bf16[18,16,512]{2,1,0:T(8,128)(2,1)S(1)}, bf16[18,16,512]{2,1,0:T(8,128)(2,1)S(1)}, u32[]{:S(2)}, u32[]{:S(2)}) %collective-permute-start.2) | collective-permute-done | bytes 294944 | tf_op jit(solution)/shard_map/ppermute | solution.py:474
  24.3 20.9 %read.1 = (bf16[512,2048]{1,0:T(8,128)(2,1)S(1)}, bf16[4,560,128]{2,1,0:T(8,128)(2,1)S(1)}, bf16[4,560,128]{2,1,0:T(8,128)(2,1)S(1)}) custom-call(bf16[8,16,16,512]{3,2,1,0:T(8,128)(2,1)S(1)} %prepare.1.masked, bf16[18,16,512]{2,1,0:T(8,128)(2,1)S(1)} %collective-permute-done.2.x_first, ...), custom_call_target="tpu_custom_call", output_to_operand_aliasing={{0}: (12, {})} | custom-call | flops 20000000000 | bytes 11261952 | tf_op jit(solution)/shard_map/read/pallas_call | solution.py:454
  45.2 0.0 copy-start.14
  45.2 0.1 collective-permute-start.4
  45.3 2.0 %collective-permute-done.4.taken = bf16[4,560,128]{2,1,0:T(8,128)(2,1)S(1)} collective-permute-done((bf16[4,560,128]{2,1,0:T(8,128)(2,1)S(1)}, bf16[4,560,128]{2,1,0:T(8,128)(2,1)S(1)}, u32[]{:S(2)}, u32[]{:S(2)}) %collective-permute-start.4) | collective-permute-done | bytes 573472 | tf_op jit(solution)/shard_map/ppermute | solution.py:478
  47.2 0.2 merge_pair.1
  47.5 0.0 copy-start.6
  47.5 3.1 %collective-permute-start.5 = (bf16[560,128]{1,0:T(8,128)(2,1)S(1)}, bf16[560,128]{1,0:T(8,128)(2,1)S(1)}, u32[]{:S(2)}, u32[]{:S(2)}) collective-permute-start(bf16[560,128]{1,0:T(8,128)(2,1)S(1)} %get-tuple-element.32), channel_id=1, source_target_pairs={{0,6},{2,4},{4,2},{6,0},{1,7},{3,5},{5,3},{7,1},{8,14},{10,12},{12... | collective-permute-start | bytes 430088 | tf_op jit(solution)/shard_map/ppermute | solution.py:478
  50.6 0.9 collective-permute-start.7
  51.5 3.7 %collective-permute-done.5.refs_0_ = bf16[560,128]{1,0:T(8,128)(2,1)S(1)} collective-permute-done((bf16[560,128]{1,0:T(8,128)(2,1)S(1)}, bf16[560,128]{1,0:T(8,128)(2,1)S(1)}, u32[]{:S(2)}, u32[]{:S(2)}) %collective-permute-start.5) | collective-permute-done | bytes 143392 | tf_op jit(solution)/shard_map/ppermute | solution.py:478
  55.2 1.9 %collective-permute-done.6.refs_1_ = bf16[560,128]{1,0:T(8,128)(2,1)S(1)} collective-permute-done((bf16[560,128]{1,0:T(8,128)(2,1)S(1)}, bf16[560,128]{1,0:T(8,128)(2,1)S(1)}, u32[]{:S(2)}, u32[]{:S(2)}) %collective-permute-start.6) | collective-permute-done | bytes 143392 | tf_op jit(solution)/shard_map/ppermute | solution.py:478
  57.2 0.6 collective-permute-done.7.refs_2_
  57.8 0.2 merge_group.1
  58.0 4.3 %collective-permute-start.10 = (bf16[32,640]{1,0:T(8,128)(2,1)S(1)}, bf16[32,640]{1,0:T(8,128)(2,1)S(1)}, u32[]{:S(2)}, u32[]{:S(2)}) collective-permute-start(bf16[32,640]{1,0:T(8,128)(2,1)S(1)} %get-tuple-element.38), channel_id=1, source_target_pairs={{0,24},{8,16},{16,8},{24,0},{1,25},{9,17},{17,9},{25,1},{2,26},{10... | collective-permute-start | bytes 122888 | tf_op jit(solution)/shard_map/ppermute | solution.py:478
  62.3 0.6 collective-permute-start.9
  62.9 1.3 %collective-permute-done.10.refs_2_ = bf16[32,640]{1,0:T(8,128)(2,1)S(1)} collective-permute-done((bf16[32,640]{1,0:T(8,128)(2,1)S(1)}, bf16[32,640]{1,0:T(8,128)(2,1)S(1)}, u32[]{:S(2)}, u32[]{:S(2)}) %collective-permute-start.10) | collective-permute-done | bytes 40992 | tf_op jit(solution)/shard_map/ppermute | solution.py:478
  64.2 2.9 %collective-permute-done.8.refs_0_ = bf16[32,640]{1,0:T(8,128)(2,1)S(1)} collective-permute-done((bf16[32,640]{1,0:T(8,128)(2,1)S(1)}, bf16[32,640]{1,0:T(8,128)(2,1)S(1)}, u32[]{:S(2)}, u32[]{:S(2)}) %collective-permute-start.8) | collective-permute-done | bytes 40992 | tf_op jit(solution)/shard_map/ppermute | solution.py:478
  67.2 0.0 copy-start.9
  67.2 0.5 update.1.refs_3_
  67.7 1.7 %collective-permute-start.11 = (bf16[32,512]{1,0:T(8,128)(2,1)S(1)}, bf16[32,512]{1,0:T(8,128)(2,1)S(1)}, u32[]{:S(2)}, u32[]{:S(2)}) collective-permute-start(bf16[32,512]{1,0:T(8,128)(2,1)S(1)} %update.1.refs_3_), channel_id=1, source_target_pairs={{0,24},{8,16},{16,8},{24,0},{1,25},{9,17},{17,9},{25,1},{2,26},{10... | collective-permute-start | bytes 98312 | tf_op jit(solution)/shard_map/ppermute | solution.py:478
  69.4 0.4 collective-permute-start.12
  69.8 2.3 %collective-permute-start.13 = (bf16[32,512]{1,0:T(8,128)(2,1)S(1)}, bf16[32,512]{1,0:T(8,128)(2,1)S(1)}, u32[]{:S(2)}, u32[]{:S(2)}) collective-permute-start(bf16[32,512]{1,0:T(8,128)(2,1)S(1)} %update.1.refs_3_), channel_id=1, source_target_pairs={{0,8},{8,0},{16,24},{24,16},{1,9},{9,1},{17,25},{25,17},{2,10},{10... | collective-permute-start | bytes 98312 | tf_op jit(solution)/shard_map/ppermute | solution.py:478
  72.1 1.3 %collective-permute-done.11.refs_0_ = bf16[32,512]{1,0:T(8,128)(2,1)S(1)} collective-permute-done((bf16[32,512]{1,0:T(8,128)(2,1)S(1)}, bf16[32,512]{1,0:T(8,128)(2,1)S(1)}, u32[]{:S(2)}, u32[]{:S(2)}) %collective-permute-start.11) | collective-permute-done | bytes 32800 | tf_op jit(solution)/shard_map/ppermute | solution.py:478
  73.5 0.9 collective-permute-done.12.refs_1_
  74.3 0.0 collective-permute-done.13.refs_2_
  74.4 1.8 %collective-permute-start.14 = (bf16[128,512]{1,0:T(8,128)(2,1)S(1)}, bf16[128,512]{1,0:T(8,128)(2,1)S(1)}, u32[]{:S(2)}, u32[]{:S(2)}) collective-permute-start(bf16[128,512]{1,0:T(8,128)(2,1)S(1)} %join_far.1.refs_3_), channel_id=1, source_target_pairs={{0,6},{2,4},{4,2},{6,0},{1,7},{3,5},{5,3},{7,1},{8,14},{10,12},{12... | collective-permute-start | bytes 393224 | tf_op jit(solution)/shard_map/ppermute | solution.py:478
  76.2 0.3 collective-permute-start.15
  76.5 1.4 %collective-permute-start.16 = (bf16[128,512]{1,0:T(8,128)(2,1)S(1)}, bf16[128,512]{1,0:T(8,128)(2,1)S(1)}, u32[]{:S(2)}, u32[]{:S(2)}) collective-permute-start(bf16[128,512]{1,0:T(8,128)(2,1)S(1)} %join_far.1.refs_3_), channel_id=1, source_target_pairs={{0,2},{2,0},{4,6},{6,4},{1,3},{3,1},{5,7},{7,5},{8,10},{10,8},{12,... | collective-permute-start | bytes 393224 | tf_op jit(solution)/shard_map/ppermute | solution.py:478
  78.0 2.4 %collective-permute-done.14.refs_0_ = bf16[128,512]{1,0:T(8,128)(2,1)S(1)} collective-permute-done((bf16[128,512]{1,0:T(8,128)(2,1)S(1)}, bf16[128,512]{1,0:T(8,128)(2,1)S(1)}, u32[]{:S(2)}, u32[]{:S(2)}) %collective-permute-start.14) | collective-permute-done | bytes 131104 | tf_op jit(solution)/shard_map/ppermute | solution.py:478
  80.4 0.8 collective-permute-done.15.refs_1_
  81.2 0.6 collective-permute-done.16.refs_2_
  81.8 0.1 collective-permute-start.17
  81.8 1.9 %collective-permute-done.17.other_state = bf16[512,512]{1,0:T(8,128)(2,1)S(1)} collective-permute-done((bf16[512,512]{1,0:T(8,128)(2,1)S(1)}, bf16[512,512]{1,0:T(8,128)(2,1)S(1)}, u32[]{:S(2)}, u32[]{:S(2)}) %collective-permute-start.17) | collective-permute-done | bytes 524320 | tf_op jit(solution)/shard_map/ppermute | solution.py:478
  83.8 21.6 %write.1 = f32[2048,512]{1,0:T(8,128)} custom-call(bf16[512,512]{1,0:T(8,128)(2,1)S(1)} %join_group.1.own_state, bf16[512,512]{1,0:T(8,128)(2,1)S(1)} %collective-permute-done.17.other_state, bf16[512,2048]{1,0:T(8,128)(2,1)S(1)} %copy-done.15, bf16[2048,512]{1,0:T(8,128)(2,1)S(1)} %bitcast.2, bf16[512,512]{1,0:T(8,128)(2,1)S(1)} %copy-done.7, ...), custom_call_target="tpu_custom_call" | custom-call | flops 20000000000 | bytes 6815744 | tf_op jit(solution)/shard_map/write/pallas_call | solution.py:454
  (33 shorter events, 0.1 us)
Async XLA Ops:
  0.0 7.2 %copy-start.1 = (bf16[8,16,16,512]{3,2,1,0:T(8,128)(2,1)S(1)}, bf16[8,16,16,512]{3,2,1,0:T(8,128)(2,1)}, u32[]{:S(2)}) copy-start(bf16[8,16,16,512]{3,2,1,0:T(8,128)(2,1)} %flow.3) | copy-start | bytes 6291460
  0.0 7.2 %copy-start.10 = (s32[8,16,16]{2,1,0:T(8,128)S(1)}, s32[8,16,16]{2,1,0:T(8,128)}, u32[]{:S(2)}) copy-start(s32[8,16,16]{2,1,0:T(8,128)} %far_mask.1) | copy-start | bytes 24580
  2.1 7.4 %collective-permute-start = (bf16[8,16,512]{2,1,0:T(8,128)(2,1)}, bf16[8,16,512]{2,1,0:T(8,128)(2,1)S(1)}, u32[]{:S(2)}, u32[]{:S(2)}) collective-permute-start(bf16[8,16,512]{2,1,0:T(8,128)(2,1)} %get-tuple-element.23), channel_id=1, source_target_pairs={{1,2},{2,1},{5,6},{6,5},{9,10},{10,9},{13,14},{14,13},{17,18},{18,... | collective-permute-start | bytes 393224 | tf_op jit(solution)/shard_map/ppermute | solution.py:473
  2.7 5.9 %copy-start = (bf16[1024,512]{1,0:T(8,128)(2,1)S(1)}, bf16[1024,512]{1,0:T(8,128)(2,1)}, u32[]{:S(2)}) copy-start(bf16[1024,512]{1,0:T(8,128)(2,1)} %latents.1) | copy-start | bytes 3145732
  2.7 5.9 %copy-start.2 = (bf16[512,512]{1,0:T(8,128)(2,1)S(1)}, bf16[512,512]{1,0:T(8,128)(2,1)}, u32[]{:S(2)}) copy-start(bf16[512,512]{1,0:T(8,128)(2,1)} %w_query1.1) | copy-start | bytes 1572868
  2.8 6.7 %collective-permute-start.1 = (bf16[8,16,512]{2,1,0:T(8,128)(2,1)}, bf16[8,16,512]{2,1,0:T(8,128)(2,1)S(1)}, u32[]{:S(2)}, u32[]{:S(2)}) collective-permute-start(bf16[8,16,512]{2,1,0:T(8,128)(2,1)} %get-tuple-element.24), channel_id=1, source_target_pairs={{0,1},{1,0},{2,3},{3,2},{4,5},{5,4},{6,7},{7,6},{8,9},{9,8},{10,11... | collective-permute-start | bytes 393224 | tf_op jit(solution)/shard_map/ppermute | solution.py:474
  8.7 15.6 %copy-start.12 = (bf16[8,16,16,512]{3,2,1,0:T(8,128)(2,1)}, bf16[8,16,16,512]{3,2,1,0:T(8,128)(2,1)S(1)}, u32[]{:S(2)}) copy-start(bf16[8,16,16,512]{3,2,1,0:T(8,128)(2,1)S(1)} %prepare.1.masked) | copy-start | bytes 6291460
  9.4 2.4 %copy-start.3 = (bf16[512,512]{1,0:T(8,128)(2,1)S(1)}, bf16[512,512]{1,0:T(8,128)(2,1)}, u32[]{:S(2)}) copy-start(bf16[512,512]{1,0:T(8,128)(2,1)} %w_key1.1) | copy-start | bytes 1572868
  9.5 2.4 %copy-start.4 = (bf16[512,512]{1,0:T(8,128)(2,1)S(1)}, bf16[512,512]{1,0:T(8,128)(2,1)}, u32[]{:S(2)}) copy-start(bf16[512,512]{1,0:T(8,128)(2,1)} %w_value1.1) | copy-start | bytes 1572868
  9.5 2.4 %copy-start.5 = (bf16[512,512]{1,0:T(8,128)(2,1)S(1)}, bf16[512,512]{1,0:T(8,128)(2,1)}, u32[]{:S(2)}) copy-start(bf16[512,512]{1,0:T(8,128)(2,1)} %w_query2.1) | copy-start | bytes 1572868
  9.5 2.3 %copy-start.11 = (f32[27,512]{1,0:T(8,128)S(1)}, f32[27,512]{1,0:T(8,128)}, u32[]{:S(2)}) copy-start(f32[27,512]{1,0:T(8,128)} %conv.3) | copy-start | bytes 165892
  9.6 14.7 %collective-permute-start.2 = (bf16[18,16,512]{2,1,0:T(8,128)(2,1)S(1)}, bf16[18,16,512]{2,1,0:T(8,128)(2,1)S(1)}, u32[]{:S(2)}, u32[]{:S(2)}) collective-permute-start(bf16[18,16,512]{2,1,0:T(8,128)(2,1)S(1)} %get-tuple-element.25), channel_id=1, source_target_pairs={{0,4},{4,0},{8,12},{12,8},{16,20},{20,16},{24,28},{28,24},{1,5},{5... | collective-permute-start | bytes 884744 | tf_op jit(solution)/shard_map/ppermute | solution.py:474
  11.1 13.2 %collective-permute-start.3 = (bf16[18,16,512]{2,1,0:T(8,128)(2,1)S(1)}, bf16[18,16,512]{2,1,0:T(8,128)(2,1)S(1)}, u32[]{:S(2)}, u32[]{:S(2)}) collective-permute-start(bf16[18,16,512]{2,1,0:T(8,128)(2,1)S(1)} %get-tuple-element.26), channel_id=1, source_target_pairs={{4,8},{8,4},{12,16},{16,12},{20,24},{24,20},{5,9},{9,5},{13,17},{1... | collective-permute-start | bytes 884744 | tf_op jit(solution)/shard_map/ppermute | solution.py:473
  45.2 6.3 %copy-start.14 = (bf16[512,2048]{1,0:T(8,128)(2,1)}, bf16[512,2048]{1,0:T(8,128)(2,1)S(1)}, u32[]{:S(2)}) copy-start(bf16[512,2048]{1,0:T(8,128)(2,1)S(1)} %get-tuple-element.40.query2_t) | copy-start | bytes 6291460
  45.2 2.0 %collective-permute-start.4 = (bf16[4,560,128]{2,1,0:T(8,128)(2,1)S(1)}, bf16[4,560,128]{2,1,0:T(8,128)(2,1)S(1)}, u32[]{:S(2)}, u32[]{:S(2)}) collective-permute-start(bf16[4,560,128]{2,1,0:T(8,128)(2,1)S(1)} %get-tuple-element.31), channel_id=1, source_target_pairs={{0,1},{1,0},{2,3},{3,2},{4,5},{5,4},{6,7},{7,6},{8,9},{9,8},{10,11... | collective-permute-start | bytes 1720328 | tf_op jit(solution)/shard_map/ppermute | solution.py:478
  47.5 19.7 %copy-start.6 = (bf16[512,512]{1,0:T(8,128)(2,1)S(1)}, bf16[512,512]{1,0:T(8,128)(2,1)}, u32[]{:S(2)}) copy-start(bf16[512,512]{1,0:T(8,128)(2,1)} %w_out1.1) | copy-start | bytes 1572868
  47.5 7.7 %collective-permute-start.5 = (bf16[560,128]{1,0:T(8,128)(2,1)S(1)}, bf16[560,128]{1,0:T(8,128)(2,1)S(1)}, u32[]{:S(2)}, u32[]{:S(2)}) collective-permute-start(bf16[560,128]{1,0:T(8,128)(2,1)S(1)} %get-tuple-element.32), channel_id=1, source_target_pairs={{0,6},{2,4},{4,2},{6,0},{1,7},{3,5},{5,3},{7,1},{8,14},{10,12},{12... | collective-permute-start | bytes 430088 | tf_op jit(solution)/shard_map/ppermute | solution.py:478
  50.6 6.5 %collective-permute-start.6 = (bf16[560,128]{1,0:T(8,128)(2,1)S(1)}, bf16[560,128]{1,0:T(8,128)(2,1)S(1)}, u32[]{:S(2)}, u32[]{:S(2)}) collective-permute-start(bf16[560,128]{1,0:T(8,128)(2,1)S(1)} %get-tuple-element.33), channel_id=1, source_target_pairs={{0,4},{2,6},{4,0},{6,2},{1,5},{3,7},{5,1},{7,3},{8,12},{10,14},{12... | collective-permute-start | bytes 430088 | tf_op jit(solution)/shard_map/ppermute | solution.py:478
  50.6 7.1 %collective-permute-start.7 = (bf16[560,128]{1,0:T(8,128)(2,1)S(1)}, bf16[560,128]{1,0:T(8,128)(2,1)S(1)}, u32[]{:S(2)}, u32[]{:S(2)}) collective-permute-start(bf16[560,128]{1,0:T(8,128)(2,1)S(1)} %get-tuple-element.34), channel_id=1, source_target_pairs={{0,2},{2,0},{4,6},{6,4},{1,3},{3,1},{5,7},{7,5},{8,10},{10,8},{12,... | collective-permute-start | bytes 430088 | tf_op jit(solution)/shard_map/ppermute | solution.py:478
  57.8 26.0 %copy-start.15 = (bf16[512,2048]{1,0:T(8,128)(2,1)S(1)}, bf16[512,2048]{1,0:T(8,128)(2,1)}, u32[]{:S(2)}) copy-start(bf16[512,2048]{1,0:T(8,128)(2,1)} %copy-done.14) | copy-start | bytes 6291460
  58.0 6.2 %collective-permute-start.10 = (bf16[32,640]{1,0:T(8,128)(2,1)S(1)}, bf16[32,640]{1,0:T(8,128)(2,1)S(1)}, u32[]{:S(2)}, u32[]{:S(2)}) collective-permute-start(bf16[32,640]{1,0:T(8,128)(2,1)S(1)} %get-tuple-element.38), channel_id=1, source_target_pairs={{0,24},{8,16},{16,8},{24,0},{1,25},{9,17},{17,9},{25,1},{2,26},{10... | collective-permute-start | bytes 122888 | tf_op jit(solution)/shard_map/ppermute | solution.py:478
  62.3 4.9 %collective-permute-start.8 = (bf16[32,640]{1,0:T(8,128)(2,1)S(1)}, bf16[32,640]{1,0:T(8,128)(2,1)S(1)}, u32[]{:S(2)}, u32[]{:S(2)}) collective-permute-start(bf16[32,640]{1,0:T(8,128)(2,1)S(1)} %get-tuple-element.36), channel_id=1, source_target_pairs={{0,16},{8,24},{16,0},{24,8},{1,17},{9,25},{17,1},{25,9},{2,18},{10... | collective-permute-start | bytes 122888 | tf_op jit(solution)/shard_map/ppermute | solution.py:478
  62.3 4.9 %collective-permute-start.9 = (bf16[32,640]{1,0:T(8,128)(2,1)S(1)}, bf16[32,640]{1,0:T(8,128)(2,1)S(1)}, u32[]{:S(2)}, u32[]{:S(2)}) collective-permute-start(bf16[32,640]{1,0:T(8,128)(2,1)S(1)} %get-tuple-element.37), channel_id=1, source_target_pairs={{0,8},{8,0},{16,24},{24,16},{1,9},{9,1},{17,25},{25,17},{2,10},{10... | collective-permute-start | bytes 122888 | tf_op jit(solution)/shard_map/ppermute | solution.py:478
  67.2 16.6 %copy-start.7 = (bf16[512,512]{1,0:T(8,128)(2,1)S(1)}, bf16[512,512]{1,0:T(8,128)(2,1)}, u32[]{:S(2)}) copy-start(bf16[512,512]{1,0:T(8,128)(2,1)} %w_key2.1) | copy-start | bytes 1572868
  67.2 16.6 %copy-start.8 = (bf16[512,512]{1,0:T(8,128)(2,1)S(1)}, bf16[512,512]{1,0:T(8,128)(2,1)}, u32[]{:S(2)}) copy-start(bf16[512,512]{1,0:T(8,128)(2,1)} %w_value2.1) | copy-start | bytes 1572868
  67.2 16.6 %copy-start.9 = (bf16[512,512]{1,0:T(8,128)(2,1)S(1)}, bf16[512,512]{1,0:T(8,128)(2,1)}, u32[]{:S(2)}) copy-start(bf16[512,512]{1,0:T(8,128)(2,1)} %w_out2.1) | copy-start | bytes 1572868
  67.2 16.6 %copy-start.13 = (bf16[8,16,16,512]{3,2,1,0:T(8,128)(2,1)S(1)}, bf16[8,16,16,512]{3,2,1,0:T(8,128)(2,1)}, u32[]{:S(2)}) copy-start(bf16[8,16,16,512]{3,2,1,0:T(8,128)(2,1)} %copy-done.12) | copy-start | bytes 6291460
  67.7 5.7 %collective-permute-start.11 = (bf16[32,512]{1,0:T(8,128)(2,1)S(1)}, bf16[32,512]{1,0:T(8,128)(2,1)S(1)}, u32[]{:S(2)}, u32[]{:S(2)}) collective-permute-start(bf16[32,512]{1,0:T(8,128)(2,1)S(1)} %update.1.refs_3_), channel_id=1, source_target_pairs={{0,24},{8,16},{16,8},{24,0},{1,25},{9,17},{17,9},{25,1},{2,26},{10... | collective-permute-start | bytes 98312 | tf_op jit(solution)/shard_map/ppermute | solution.py:478
  69.4 4.9 %collective-permute-start.12 = (bf16[32,512]{1,0:T(8,128)(2,1)S(1)}, bf16[32,512]{1,0:T(8,128)(2,1)S(1)}, u32[]{:S(2)}, u32[]{:S(2)}) collective-permute-start(bf16[32,512]{1,0:T(8,128)(2,1)S(1)} %update.1.refs_3_), channel_id=1, source_target_pairs={{0,16},{8,24},{16,0},{24,8},{1,17},{9,25},{17,1},{25,9},{2,18},{10... | collective-permute-start | bytes 98312 | tf_op jit(solution)/shard_map/ppermute | solution.py:478
  69.8 4.6 %collective-permute-start.13 = (bf16[32,512]{1,0:T(8,128)(2,1)S(1)}, bf16[32,512]{1,0:T(8,128)(2,1)S(1)}, u32[]{:S(2)}, u32[]{:S(2)}) collective-permute-start(bf16[32,512]{1,0:T(8,128)(2,1)S(1)} %update.1.refs_3_), channel_id=1, source_target_pairs={{0,8},{8,0},{16,24},{24,16},{1,9},{9,1},{17,25},{25,17},{2,10},{10... | collective-permute-start | bytes 98312 | tf_op jit(solution)/shard_map/ppermute | solution.py:478
  74.4 6.0 %collective-permute-start.14 = (bf16[128,512]{1,0:T(8,128)(2,1)S(1)}, bf16[128,512]{1,0:T(8,128)(2,1)S(1)}, u32[]{:S(2)}, u32[]{:S(2)}) collective-permute-start(bf16[128,512]{1,0:T(8,128)(2,1)S(1)} %join_far.1.refs_3_), channel_id=1, source_target_pairs={{0,6},{2,4},{4,2},{6,0},{1,7},{3,5},{5,3},{7,1},{8,14},{10,12},{12... | collective-permute-start | bytes 393224 | tf_op jit(solution)/shard_map/ppermute | solution.py:478
  76.2 5.0 %collective-permute-start.15 = (bf16[128,512]{1,0:T(8,128)(2,1)S(1)}, bf16[128,512]{1,0:T(8,128)(2,1)S(1)}, u32[]{:S(2)}, u32[]{:S(2)}) collective-permute-start(bf16[128,512]{1,0:T(8,128)(2,1)S(1)} %join_far.1.refs_3_), channel_id=1, source_target_pairs={{0,4},{2,6},{4,0},{6,2},{1,5},{3,7},{5,1},{7,3},{8,12},{10,14},{12... | collective-permute-start | bytes 393224 | tf_op jit(solution)/shard_map/ppermute | solution.py:478
  76.5 5.2 %collective-permute-start.16 = (bf16[128,512]{1,0:T(8,128)(2,1)S(1)}, bf16[128,512]{1,0:T(8,128)(2,1)S(1)}, u32[]{:S(2)}, u32[]{:S(2)}) collective-permute-start(bf16[128,512]{1,0:T(8,128)(2,1)S(1)} %join_far.1.refs_3_), channel_id=1, source_target_pairs={{0,2},{2,0},{4,6},{6,4},{1,3},{3,1},{5,7},{7,5},{8,10},{10,8},{12,... | collective-permute-start | bytes 393224 | tf_op jit(solution)/shard_map/ppermute | solution.py:478
  81.8 2.0 %collective-permute-start.17 = (bf16[512,512]{1,0:T(8,128)(2,1)S(1)}, bf16[512,512]{1,0:T(8,128)(2,1)S(1)}, u32[]{:S(2)}, u32[]{:S(2)}) collective-permute-start(bf16[512,512]{1,0:T(8,128)(2,1)S(1)} %join_group.1.own_state), channel_id=1, source_target_pairs={{0,1},{1,0},{2,3},{3,2},{4,5},{5,4},{6,7},{7,6},{8,9},{9,8},{10,11... | collective-permute-start | bytes 1572872 | tf_op jit(solution)/shard_map/ppermute | solution.py:478

commit v10 on v9

--- a/solution.py
+++ b/solution.py
@@ -59,7 +59,7 @@
     lax.fori_loop(0, size_x, plane, 0)
 
 
-def edge_kernel(masked, y_second, y_first, first, second):
+def edge_kernel(masked, y_first, y_second, first, second):
     size_x, size_y = masked.shape[:2]
     outer = size_y + 1
     for face, plane in ((first, (size_x - 1) * (1 - lax.axis_index("wx"))), (second, (size_x - 1) * lax.axis_index("wx"))):
@@ -534,7 +534,7 @@
     )
     side = shape((size_y + 2, size_z, width), BF16)
     x_first, x_second = call(
-        edge_kernel, [side, side], [], [masked, y_second, y_first], 12, step, "edge"
+        edge_kernel, [side, side], [], [masked, y_first, y_second], 12, step, "edge"
     )
     x_first, x_second = pair_exchange(x_first, x_second, wide)
     weight = pltpu.VMEM((width, width), BF16)

time: 106 us -> 105 us (level)
  waiting for transfers between devices: 23.1 us -> 19.9 us
  starting transfers between devices: 24.3 us -> 26.9 us
    ppermute x14, starting transfers between devices: 17 us -> 22.3 us  [flipped(): lax.ppermute(array, axis, [(i, i ^ distance) for i in range(lax.axis_size...]
    ppermute x2, starting transfers between devices: 5.96 us -> 3.15 us  [pair_exchange(): return (lax.ppermute(first, axis, swaps[0]), other)]
    ppermute x2, waiting for transfers between devices: 2.75 us -> 0.01 us  [pair_exchange(): return (lax.ppermute(first, axis, swaps[0]), other)]
  transfers between devices with their start and end apart: 18 -> 18, of which waited for: 13 -> 12; matrix products, arithmetic and copies ran while one was open for 0% -> 0% of each run, Pallas kernels for 11% -> 11%
where the time goes in v10:
time: 105 us
  Pallas kernels  57.6 us (55%)
  starting transfers between devices  26.9 us (26%)
  waiting for transfers between devices  19.9 us (19%)
    pallas_call x12, Pallas kernels, call(): pl.pallas_call(kernel, out_shape=shapes, in_specs=in_specs, out_specs=[vm...  57.6 us
    ppermute x14, starting transfers between devices, flipped(): lax.ppermute(array, axis, [(i, i ^ distance) for i in range(lax.axis_size...  22.3 us
    ppermute x14, waiting for transfers between devices, flipped(): lax.ppermute(array, axis, [(i, i ^ distance) for i in range(lax.axis_size...  19.9 us
    ppermute x2, starting transfers between devices, pair_exchange(): return (lax.ppermute(first, axis, swaps[0]), other)  3.15 us
  transfers between devices with their start and end apart: 18, of which 12 were waited for; matrix products, arithmetic and copies ran while one was open for 0% of the time, Pallas kernels for 11%

profile of v10, /device:TPU:0, one launch (start us, length us, event | category | flops | bytes accessed | tf_op | source)
XLA Modules:
  0.0 105.0 jit_solution(18229629575645546076)
XLA Ops:
  0.0 2.0 %face.1 = (bf16[8,16,512]{2,1,0:T(8,128)(2,1)}, bf16[8,16,512]{2,1,0:T(8,128)(2,1)}) custom-call(bf16[8,16,16,512]{3,2,1,0:T(8,128)(2,1)} %flow.3, s32[8,16,16]{2,1,0:T(8,128)} %far_mask.1), custom_call_target="tpu_custom_call" | custom-call | flops 1000000000 | bytes 2105344 | tf_op jit(solution)/shard_map/face/pallas_call | solution.py:454
  2.1 0.6 collective-permute-start
  2.6 0.8 collective-permute-start.1
  3.4 1.5 %prepare.1.masked = bf16[8,16,16,512]{3,2,1,0:T(8,128)(2,1)S(1)} custom-call(bf16[8,16,16,512]{3,2,1,0:T(8,128)(2,1)S(1)} %copy-done.1, s32[8,16,16]{2,1,0:T(8,128)S(1)} %copy-done.10), custom_call_target="tpu_custom_call" | custom-call | flops 2000000000 | bytes 2105344 | tf_op jit(solution)/shard_map/prepare/pallas_call | solution.py:454
  4.9 0.7 latent_query.1.query1_t
  5.7 0.0 copy-start.3
  5.7 0.0 copy-start.4
  5.7 0.0 copy-start.5
  5.7 0.0 copy-start.11
  5.7 0.0 collective-permute-done.y_first
  5.8 0.1 edge.1
  5.8 2.6 %collective-permute-start.2 = (bf16[18,16,512]{2,1,0:T(8,128)(2,1)S(1)}, bf16[18,16,512]{2,1,0:T(8,128)(2,1)S(1)}, u32[]{:S(2)}, u32[]{:S(2)}) collective-permute-start(bf16[18,16,512]{2,1,0:T(8,128)(2,1)S(1)} %get-tuple-element.25), channel_id=1, source_target_pairs={{0,4},{4,0},{8,12},{12,8},{16,20},{20,16},{24,28},{28,24},{1,5},{5... | collective-permute-start | bytes 884744 | tf_op jit(solution)/shard_map/ppermute | solution.py:474
  8.4 0.7 collective-permute-start.3
  9.1 9.7 %inner.1 = (bf16[1536,512]{1,0:T(8,128)(2,1)S(1)}, bf16[8,80,1536]{2,1,0:T(8,128)(2,1)S(1)}, bf16[512,2048]{1,0:T(8,128)(2,1)S(1)}) custom-call(bf16[8,16,16,512]{3,2,1,0:T(8,128)(2,1)S(1)} %prepare.1.masked, bf16[8,16,512]{2,1,0:T(8,128)(2,1)S(1)} %collective-permute-done.y_first, bf16[8,16,512]{2,1,0:T(8,128)(2,1)S(1)} %collective-permute-done.1.y_second, ...), custom_call_target="tpu_custom_call" | custom-call | flops 10000000000 | bytes 3987456 | tf_op jit(solution)/shard_map/inner/pallas_call | solution.py:454
  18.8 0.0 collective-permute-done.2.x_first
  18.9 20.9 %read.1 = (bf16[512,2048]{1,0:T(8,128)(2,1)S(1)}, bf16[4,560,128]{2,1,0:T(8,128)(2,1)S(1)}, bf16[4,560,128]{2,1,0:T(8,128)(2,1)S(1)}) custom-call(bf16[8,16,16,512]{3,2,1,0:T(8,128)(2,1)S(1)} %prepare.1.masked, bf16[18,16,512]{2,1,0:T(8,128)(2,1)S(1)} %collective-permute-done.2.x_first, ...), custom_call_target="tpu_custom_call", output_to_operand_aliasing={{0}: (12, {})} | custom-call | flops 20000000000 | bytes 11261952 | tf_op jit(solution)/shard_map/read/pallas_call | solution.py:454
  39.8 0.0 copy-start.14
  39.8 4.0 %collective-permute-start.4 = (bf16[4,560,128]{2,1,0:T(8,128)(2,1)S(1)}, bf16[4,560,128]{2,1,0:T(8,128)(2,1)S(1)}, u32[]{:S(2)}, u32[]{:S(2)}) collective-permute-start(bf16[4,560,128]{2,1,0:T(8,128)(2,1)S(1)} %get-tuple-element.31), channel_id=1, source_target_pairs={{0,1},{1,0},{2,3},{3,2},{4,5},{5,4},{6,7},{7,6},{8,9},{9,8},{10,11... | collective-permute-start | bytes 1720328 | tf_op jit(solution)/shard_map/ppermute | solution.py:478
  43.8 1.6 %collective-permute-done.4.taken = bf16[4,560,128]{2,1,0:T(8,128)(2,1)S(1)} collective-permute-done((bf16[4,560,128]{2,1,0:T(8,128)(2,1)S(1)}, bf16[4,560,128]{2,1,0:T(8,128)(2,1)S(1)}, u32[]{:S(2)}, u32[]{:S(2)}) %collective-permute-start.4) | collective-permute-done | bytes 573472 | tf_op jit(solution)/shard_map/ppermute | solution.py:478
  45.4 0.2 merge_pair.1
  45.6 0.0 copy-start.6
  45.6 5.2 %collective-permute-start.5 = (bf16[560,128]{1,0:T(8,128)(2,1)S(1)}, bf16[560,128]{1,0:T(8,128)(2,1)S(1)}, u32[]{:S(2)}, u32[]{:S(2)}) collective-permute-start(bf16[560,128]{1,0:T(8,128)(2,1)S(1)} %get-tuple-element.32), channel_id=1, source_target_pairs={{0,6},{2,4},{4,2},{6,0},{1,7},{3,5},{5,3},{7,1},{8,14},{10,12},{12... | collective-permute-start | bytes 430088 | tf_op jit(solution)/shard_map/ppermute | solution.py:478
  50.8 0.6 collective-permute-start.7
  51.5 4.0 %collective-permute-done.5.refs_0_ = bf16[560,128]{1,0:T(8,128)(2,1)S(1)} collective-permute-done((bf16[560,128]{1,0:T(8,128)(2,1)S(1)}, bf16[560,128]{1,0:T(8,128)(2,1)S(1)}, u32[]{:S(2)}, u32[]{:S(2)}) %collective-permute-start.5) | collective-permute-done | bytes 143392 | tf_op jit(solution)/shard_map/ppermute | solution.py:478
  55.4 1.8 %collective-permute-done.6.refs_1_ = bf16[560,128]{1,0:T(8,128)(2,1)S(1)} collective-permute-done((bf16[560,128]{1,0:T(8,128)(2,1)S(1)}, bf16[560,128]{1,0:T(8,128)(2,1)S(1)}, u32[]{:S(2)}, u32[]{:S(2)}) %collective-permute-start.6) | collective-permute-done | bytes 143392 | tf_op jit(solution)/shard_map/ppermute | solution.py:478
  57.2 0.7 collective-permute-done.7.refs_2_
  58.0 0.2 merge_group.1
  58.2 2.8 %collective-permute-start.10 = (bf16[32,640]{1,0:T(8,128)(2,1)S(1)}, bf16[32,640]{1,0:T(8,128)(2,1)S(1)}, u32[]{:S(2)}, u32[]{:S(2)}) collective-permute-start(bf16[32,640]{1,0:T(8,128)(2,1)S(1)} %get-tuple-element.38), channel_id=1, source_target_pairs={{0,24},{8,16},{16,8},{24,0},{1,25},{9,17},{17,9},{25,1},{2,26},{10... | collective-permute-start | bytes 122888 | tf_op jit(solution)/shard_map/ppermute | solution.py:478
  61.0 0.3 collective-permute-start.8
  61.3 1.3 %collective-permute-start.9 = (bf16[32,640]{1,0:T(8,128)(2,1)S(1)}, bf16[32,640]{1,0:T(8,128)(2,1)S(1)}, u32[]{:S(2)}, u32[]{:S(2)}) collective-permute-start(bf16[32,640]{1,0:T(8,128)(2,1)S(1)} %get-tuple-element.37), channel_id=1, source_target_pairs={{0,8},{8,0},{16,24},{24,16},{1,9},{9,1},{17,25},{25,17},{2,10},{10... | collective-permute-start | bytes 122888 | tf_op jit(solution)/shard_map/ppermute | solution.py:478
  62.7 1.5 %collective-permute-done.10.refs_2_ = bf16[32,640]{1,0:T(8,128)(2,1)S(1)} collective-permute-done((bf16[32,640]{1,0:T(8,128)(2,1)S(1)}, bf16[32,640]{1,0:T(8,128)(2,1)S(1)}, u32[]{:S(2)}, u32[]{:S(2)}) %collective-permute-start.10) | collective-permute-done | bytes 40992 | tf_op jit(solution)/shard_map/ppermute | solution.py:478
  64.2 2.1 %collective-permute-done.8.refs_0_ = bf16[32,640]{1,0:T(8,128)(2,1)S(1)} collective-permute-done((bf16[32,640]{1,0:T(8,128)(2,1)S(1)}, bf16[32,640]{1,0:T(8,128)(2,1)S(1)}, u32[]{:S(2)}, u32[]{:S(2)}) %collective-permute-start.8) | collective-permute-done | bytes 40992 | tf_op jit(solution)/shard_map/ppermute | solution.py:478
  66.3 0.0 copy-start.8
  66.3 0.0 copy-start.9
  66.3 0.5 update.1.refs_3_
  66.8 2.1 %collective-permute-start.11 = (bf16[32,512]{1,0:T(8,128)(2,1)S(1)}, bf16[32,512]{1,0:T(8,128)(2,1)S(1)}, u32[]{:S(2)}, u32[]{:S(2)}) collective-permute-start(bf16[32,512]{1,0:T(8,128)(2,1)S(1)} %update.1.refs_3_), channel_id=1, source_target_pairs={{0,24},{8,16},{16,8},{24,0},{1,25},{9,17},{17,9},{25,1},{2,26},{10... | collective-permute-start | bytes 98312 | tf_op jit(solution)/shard_map/ppermute | solution.py:478
  69.0 2.3 %collective-permute-start.13 = (bf16[32,512]{1,0:T(8,128)(2,1)S(1)}, bf16[32,512]{1,0:T(8,128)(2,1)S(1)}, u32[]{:S(2)}, u32[]{:S(2)}) collective-permute-start(bf16[32,512]{1,0:T(8,128)(2,1)S(1)} %update.1.refs_3_), channel_id=1, source_target_pairs={{0,8},{8,0},{16,24},{24,16},{1,9},{9,1},{17,25},{25,17},{2,10},{10... | collective-permute-start | bytes 98312 | tf_op jit(solution)/shard_map/ppermute | solution.py:478
  71.2 1.3 %collective-permute-done.11.refs_0_ = bf16[32,512]{1,0:T(8,128)(2,1)S(1)} collective-permute-done((bf16[32,512]{1,0:T(8,128)(2,1)S(1)}, bf16[32,512]{1,0:T(8,128)(2,1)S(1)}, u32[]{:S(2)}, u32[]{:S(2)}) %collective-permute-start.11) | collective-permute-done | bytes 32800 | tf_op jit(solution)/shard_map/ppermute | solution.py:478
  72.6 1.2 %collective-permute-done.12.refs_1_ = bf16[32,512]{1,0:T(8,128)(2,1)S(1)} collective-permute-done((bf16[32,512]{1,0:T(8,128)(2,1)S(1)}, bf16[32,512]{1,0:T(8,128)(2,1)S(1)}, u32[]{:S(2)}, u32[]{:S(2)}) %collective-permute-start.12) | collective-permute-done | bytes 32800 | tf_op jit(solution)/shard_map/ppermute | solution.py:478
  73.8 2.1 %collective-permute-start.14 = (bf16[128,512]{1,0:T(8,128)(2,1)S(1)}, bf16[128,512]{1,0:T(8,128)(2,1)S(1)}, u32[]{:S(2)}, u32[]{:S(2)}) collective-permute-start(bf16[128,512]{1,0:T(8,128)(2,1)S(1)} %join_far.1.refs_3_), channel_id=1, source_target_pairs={{0,6},{2,4},{4,2},{6,0},{1,7},{3,5},{5,3},{7,1},{8,14},{10,12},{12... | collective-permute-start | bytes 393224 | tf_op jit(solution)/shard_map/ppermute | solution.py:478
  75.9 0.2 collective-permute-start.15
  76.1 1.3 %collective-permute-start.16 = (bf16[128,512]{1,0:T(8,128)(2,1)S(1)}, bf16[128,512]{1,0:T(8,128)(2,1)S(1)}, u32[]{:S(2)}, u32[]{:S(2)}) collective-permute-start(bf16[128,512]{1,0:T(8,128)(2,1)S(1)} %join_far.1.refs_3_), channel_id=1, source_target_pairs={{0,2},{2,0},{4,6},{6,4},{1,3},{3,1},{5,7},{7,5},{8,10},{10,8},{12,... | collective-permute-start | bytes 393224 | tf_op jit(solution)/shard_map/ppermute | solution.py:478
  77.4 2.4 %collective-permute-done.14.refs_0_ = bf16[128,512]{1,0:T(8,128)(2,1)S(1)} collective-permute-done((bf16[128,512]{1,0:T(8,128)(2,1)S(1)}, bf16[128,512]{1,0:T(8,128)(2,1)S(1)}, u32[]{:S(2)}, u32[]{:S(2)}) %collective-permute-start.14) | collective-permute-done | bytes 131104 | tf_op jit(solution)/shard_map/ppermute | solution.py:478
  79.8 1.2 %collective-permute-done.15.refs_1_ = bf16[128,512]{1,0:T(8,128)(2,1)S(1)} collective-permute-done((bf16[128,512]{1,0:T(8,128)(2,1)S(1)}, bf16[128,512]{1,0:T(8,128)(2,1)S(1)}, u32[]{:S(2)}, u32[]{:S(2)}) %collective-permute-start.15) | collective-permute-done | bytes 131104 | tf_op jit(solution)/shard_map/ppermute | solution.py:478
  80.9 0.2 collective-permute-done.16.refs_2_
  81.2 0.1 collective-permute-start.17
  81.3 1.9 %collective-permute-done.17.other_state = bf16[512,512]{1,0:T(8,128)(2,1)S(1)} collective-permute-done((bf16[512,512]{1,0:T(8,128)(2,1)S(1)}, bf16[512,512]{1,0:T(8,128)(2,1)S(1)}, u32[]{:S(2)}, u32[]{:S(2)}) %collective-permute-start.17) | collective-permute-done | bytes 524320 | tf_op jit(solution)/shard_map/ppermute | solution.py:478
  83.2 21.6 %write.1 = f32[2048,512]{1,0:T(8,128)} custom-call(bf16[512,512]{1,0:T(8,128)(2,1)S(1)} %join_group.1.own_state, bf16[512,512]{1,0:T(8,128)(2,1)S(1)} %collective-permute-done.17.other_state, bf16[512,2048]{1,0:T(8,128)(2,1)S(1)} %copy-done.15, bf16[2048,512]{1,0:T(8,128)(2,1)S(1)} %bitcast.2, bf16[512,512]{1,0:T(8,128)(2,1)S(1)} %copy-done.7, ...), custom_call_target="tpu_custom_call" | custom-call | flops 20000000000 | bytes 6815744 | tf_op jit(solution)/shard_map/write/pallas_call | solution.py:454
  (33 shorter events, 0.1 us)
Async XLA Ops:
  0.0 3.4 %copy-start.1 = (bf16[8,16,16,512]{3,2,1,0:T(8,128)(2,1)S(1)}, bf16[8,16,16,512]{3,2,1,0:T(8,128)(2,1)}, u32[]{:S(2)}) copy-start(bf16[8,16,16,512]{3,2,1,0:T(8,128)(2,1)} %flow.3) | copy-start | bytes 6291460
  0.0 3.4 %copy-start.10 = (s32[8,16,16]{2,1,0:T(8,128)S(1)}, s32[8,16,16]{2,1,0:T(8,128)}, u32[]{:S(2)}) copy-start(s32[8,16,16]{2,1,0:T(8,128)} %far_mask.1) | copy-start | bytes 24580
  2.1 3.7 %collective-permute-start = (bf16[8,16,512]{2,1,0:T(8,128)(2,1)}, bf16[8,16,512]{2,1,0:T(8,128)(2,1)S(1)}, u32[]{:S(2)}, u32[]{:S(2)}) collective-permute-start(bf16[8,16,512]{2,1,0:T(8,128)(2,1)} %get-tuple-element.23), channel_id=1, source_target_pairs={{0,1},{1,0},{2,3},{3,2},{4,5},{5,4},{6,7},{7,6},{8,9},{9,8},{10,11... | collective-permute-start | bytes 393224 | tf_op jit(solution)/shard_map/ppermute | solution.py:474
  2.6 2.3 %copy-start = (bf16[1024,512]{1,0:T(8,128)(2,1)S(1)}, bf16[1024,512]{1,0:T(8,128)(2,1)}, u32[]{:S(2)}) copy-start(bf16[1024,512]{1,0:T(8,128)(2,1)} %latents.1) | copy-start | bytes 3145732
  2.6 2.3 %copy-start.2 = (bf16[512,512]{1,0:T(8,128)(2,1)S(1)}, bf16[512,512]{1,0:T(8,128)(2,1)}, u32[]{:S(2)}) copy-start(bf16[512,512]{1,0:T(8,128)(2,1)} %w_query1.1) | copy-start | bytes 1572868
  2.6 3.1 %collective-permute-start.1 = (bf16[8,16,512]{2,1,0:T(8,128)(2,1)}, bf16[8,16,512]{2,1,0:T(8,128)(2,1)S(1)}, u32[]{:S(2)}, u32[]{:S(2)}) collective-permute-start(bf16[8,16,512]{2,1,0:T(8,128)(2,1)} %get-tuple-element.24), channel_id=1, source_target_pairs={{1,2},{2,1},{5,6},{6,5},{9,10},{10,9},{13,14},{14,13},{17,18},{18,... | collective-permute-start | bytes 393224 | tf_op jit(solution)/shard_map/ppermute | solution.py:473
  4.9 13.9 %copy-start.12 = (bf16[8,16,16,512]{3,2,1,0:T(8,128)(2,1)}, bf16[8,16,16,512]{3,2,1,0:T(8,128)(2,1)S(1)}, u32[]{:S(2)}) copy-start(bf16[8,16,16,512]{3,2,1,0:T(8,128)(2,1)S(1)} %prepare.1.masked) | copy-start | bytes 6291460
  5.7 3.4 %copy-start.3 = (bf16[512,512]{1,0:T(8,128)(2,1)S(1)}, bf16[512,512]{1,0:T(8,128)(2,1)}, u32[]{:S(2)}) copy-start(bf16[512,512]{1,0:T(8,128)(2,1)} %w_key1.1) | copy-start | bytes 1572868
  5.7 3.4 %copy-start.4 = (bf16[512,512]{1,0:T(8,128)(2,1)S(1)}, bf16[512,512]{1,0:T(8,128)(2,1)}, u32[]{:S(2)}) copy-start(bf16[512,512]{1,0:T(8,128)(2,1)} %w_value1.1) | copy-start | bytes 1572868
  5.7 3.4 %copy-start.5 = (bf16[512,512]{1,0:T(8,128)(2,1)S(1)}, bf16[512,512]{1,0:T(8,128)(2,1)}, u32[]{:S(2)}) copy-start(bf16[512,512]{1,0:T(8,128)(2,1)} %w_query2.1) | copy-start | bytes 1572868
  5.7 3.4 %copy-start.11 = (f32[27,512]{1,0:T(8,128)S(1)}, f32[27,512]{1,0:T(8,128)}, u32[]{:S(2)}) copy-start(f32[27,512]{1,0:T(8,128)} %conv.3) | copy-start | bytes 165892
  5.8 13.0 %collective-permute-start.2 = (bf16[18,16,512]{2,1,0:T(8,128)(2,1)S(1)}, bf16[18,16,512]{2,1,0:T(8,128)(2,1)S(1)}, u32[]{:S(2)}, u32[]{:S(2)}) collective-permute-start(bf16[18,16,512]{2,1,0:T(8,128)(2,1)S(1)} %get-tuple-element.25), channel_id=1, source_target_pairs={{0,4},{4,0},{8,12},{12,8},{16,20},{20,16},{24,28},{28,24},{1,5},{5... | collective-permute-start | bytes 884744 | tf_op jit(solution)/shard_map/ppermute | solution.py:474
  8.4 10.4 %collective-permute-start.3 = (bf16[18,16,512]{2,1,0:T(8,128)(2,1)S(1)}, bf16[18,16,512]{2,1,0:T(8,128)(2,1)S(1)}, u32[]{:S(2)}, u32[]{:S(2)}) collective-permute-start(bf16[18,16,512]{2,1,0:T(8,128)(2,1)S(1)} %get-tuple-element.26), channel_id=1, source_target_pairs={{4,8},{8,4},{12,16},{16,12},{20,24},{24,20},{5,9},{9,5},{13,17},{1... | collective-permute-start | bytes 884744 | tf_op jit(solution)/shard_map/ppermute | solution.py:473
  39.8 11.7 %copy-start.14 = (bf16[512,2048]{1,0:T(8,128)(2,1)}, bf16[512,2048]{1,0:T(8,128)(2,1)S(1)}, u32[]{:S(2)}) copy-start(bf16[512,2048]{1,0:T(8,128)(2,1)S(1)} %get-tuple-element.40.query2_t) | copy-start | bytes 6291460
  39.8 5.6 %collective-permute-start.4 = (bf16[4,560,128]{2,1,0:T(8,128)(2,1)S(1)}, bf16[4,560,128]{2,1,0:T(8,128)(2,1)S(1)}, u32[]{:S(2)}, u32[]{:S(2)}) collective-permute-start(bf16[4,560,128]{2,1,0:T(8,128)(2,1)S(1)} %get-tuple-element.31), channel_id=1, source_target_pairs={{0,1},{1,0},{2,3},{3,2},{4,5},{5,4},{6,7},{7,6},{8,9},{9,8},{10,11... | collective-permute-start | bytes 1720328 | tf_op jit(solution)/shard_map/ppermute | solution.py:478
  45.6 20.6 %copy-start.6 = (bf16[512,512]{1,0:T(8,128)(2,1)S(1)}, bf16[512,512]{1,0:T(8,128)(2,1)}, u32[]{:S(2)}) copy-start(bf16[512,512]{1,0:T(8,128)(2,1)} %w_out1.1) | copy-start | bytes 1572868
  45.6 9.8 %collective-permute-start.5 = (bf16[560,128]{1,0:T(8,128)(2,1)S(1)}, bf16[560,128]{1,0:T(8,128)(2,1)S(1)}, u32[]{:S(2)}, u32[]{:S(2)}) collective-permute-start(bf16[560,128]{1,0:T(8,128)(2,1)S(1)} %get-tuple-element.32), channel_id=1, source_target_pairs={{0,6},{2,4},{4,2},{6,0},{1,7},{3,5},{5,3},{7,1},{8,14},{10,12},{12... | collective-permute-start | bytes 430088 | tf_op jit(solution)/shard_map/ppermute | solution.py:478
  50.8 6.4 %collective-permute-start.6 = (bf16[560,128]{1,0:T(8,128)(2,1)S(1)}, bf16[560,128]{1,0:T(8,128)(2,1)S(1)}, u32[]{:S(2)}, u32[]{:S(2)}) collective-permute-start(bf16[560,128]{1,0:T(8,128)(2,1)S(1)} %get-tuple-element.33), channel_id=1, source_target_pairs={{0,4},{2,6},{4,0},{6,2},{1,5},{3,7},{5,1},{7,3},{8,12},{10,14},{12... | collective-permute-start | bytes 430088 | tf_op jit(solution)/shard_map/ppermute | solution.py:478
  50.8 7.1 %collective-permute-start.7 = (bf16[560,128]{1,0:T(8,128)(2,1)S(1)}, bf16[560,128]{1,0:T(8,128)(2,1)S(1)}, u32[]{:S(2)}, u32[]{:S(2)}) collective-permute-start(bf16[560,128]{1,0:T(8,128)(2,1)S(1)} %get-tuple-element.34), channel_id=1, source_target_pairs={{0,2},{2,0},{4,6},{6,4},{1,3},{3,1},{5,7},{7,5},{8,10},{10,8},{12,... | collective-permute-start | bytes 430088 | tf_op jit(solution)/shard_map/ppermute | solution.py:478
  58.0 25.2 %copy-start.15 = (bf16[512,2048]{1,0:T(8,128)(2,1)S(1)}, bf16[512,2048]{1,0:T(8,128)(2,1)}, u32[]{:S(2)}) copy-start(bf16[512,2048]{1,0:T(8,128)(2,1)} %copy-done.14) | copy-start | bytes 6291460
  58.2 6.0 %collective-permute-start.10 = (bf16[32,640]{1,0:T(8,128)(2,1)S(1)}, bf16[32,640]{1,0:T(8,128)(2,1)S(1)}, u32[]{:S(2)}, u32[]{:S(2)}) collective-permute-start(bf16[32,640]{1,0:T(8,128)(2,1)S(1)} %get-tuple-element.38), channel_id=1, source_target_pairs={{0,24},{8,16},{16,8},{24,0},{1,25},{9,17},{17,9},{25,1},{2,26},{10... | collective-permute-start | bytes 122888 | tf_op jit(solution)/shard_map/ppermute | solution.py:478
  61.0 5.3 %collective-permute-start.8 = (bf16[32,640]{1,0:T(8,128)(2,1)S(1)}, bf16[32,640]{1,0:T(8,128)(2,1)S(1)}, u32[]{:S(2)}, u32[]{:S(2)}) collective-permute-start(bf16[32,640]{1,0:T(8,128)(2,1)S(1)} %get-tuple-element.36), channel_id=1, source_target_pairs={{0,16},{8,24},{16,0},{24,8},{1,17},{9,25},{17,1},{25,9},{2,18},{10... | collective-permute-start | bytes 122888 | tf_op jit(solution)/shard_map/ppermute | solution.py:478
  61.3 4.9 %collective-permute-start.9 = (bf16[32,640]{1,0:T(8,128)(2,1)S(1)}, bf16[32,640]{1,0:T(8,128)(2,1)S(1)}, u32[]{:S(2)}, u32[]{:S(2)}) collective-permute-start(bf16[32,640]{1,0:T(8,128)(2,1)S(1)} %get-tuple-element.37), channel_id=1, source_target_pairs={{0,8},{8,0},{16,24},{24,16},{1,9},{9,1},{17,25},{25,17},{2,10},{10... | collective-permute-start | bytes 122888 | tf_op jit(solution)/shard_map/ppermute | solution.py:478
  66.3 16.9 %copy-start.7 = (bf16[512,512]{1,0:T(8,128)(2,1)S(1)}, bf16[512,512]{1,0:T(8,128)(2,1)}, u32[]{:S(2)}) copy-start(bf16[512,512]{1,0:T(8,128)(2,1)} %w_key2.1) | copy-start | bytes 1572868
  66.3 16.9 %copy-start.8 = (bf16[512,512]{1,0:T(8,128)(2,1)S(1)}, bf16[512,512]{1,0:T(8,128)(2,1)}, u32[]{:S(2)}) copy-start(bf16[512,512]{1,0:T(8,128)(2,1)} %w_value2.1) | copy-start | bytes 1572868
  66.3 16.9 %copy-start.9 = (bf16[512,512]{1,0:T(8,128)(2,1)S(1)}, bf16[512,512]{1,0:T(8,128)(2,1)}, u32[]{:S(2)}) copy-start(bf16[512,512]{1,0:T(8,128)(2,1)} %w_out2.1) | copy-start | bytes 1572868
  66.3 16.9 %copy-start.13 = (bf16[8,16,16,512]{3,2,1,0:T(8,128)(2,1)S(1)}, bf16[8,16,16,512]{3,2,1,0:T(8,128)(2,1)}, u32[]{:S(2)}) copy-start(bf16[8,16,16,512]{3,2,1,0:T(8,128)(2,1)} %copy-done.12) | copy-start | bytes 6291460
  66.8 5.7 %collective-permute-start.11 = (bf16[32,512]{1,0:T(8,128)(2,1)S(1)}, bf16[32,512]{1,0:T(8,128)(2,1)S(1)}, u32[]{:S(2)}, u32[]{:S(2)}) collective-permute-start(bf16[32,512]{1,0:T(8,128)(2,1)S(1)} %update.1.refs_3_), channel_id=1, source_target_pairs={{0,24},{8,16},{16,8},{24,0},{1,25},{9,17},{17,9},{25,1},{2,26},{10... | collective-permute-start | bytes 98312 | tf_op jit(solution)/shard_map/ppermute | solution.py:478
  69.0 4.8 %collective-permute-start.12 = (bf16[32,512]{1,0:T(8,128)(2,1)S(1)}, bf16[32,512]{1,0:T(8,128)(2,1)S(1)}, u32[]{:S(2)}, u32[]{:S(2)}) collective-permute-start(bf16[32,512]{1,0:T(8,128)(2,1)S(1)} %update.1.refs_3_), channel_id=1, source_target_pairs={{0,16},{8,24},{16,0},{24,8},{1,17},{9,25},{17,1},{25,9},{2,18},{10... | collective-permute-start | bytes 98312 | tf_op jit(solution)/shard_map/ppermute | solution.py:478
  69.0 4.8 %collective-permute-start.13 = (bf16[32,512]{1,0:T(8,128)(2,1)S(1)}, bf16[32,512]{1,0:T(8,128)(2,1)S(1)}, u32[]{:S(2)}, u32[]{:S(2)}) collective-permute-start(bf16[32,512]{1,0:T(8,128)(2,1)S(1)} %update.1.refs_3_), channel_id=1, source_target_pairs={{0,8},{8,0},{16,24},{24,16},{1,9},{9,1},{17,25},{25,17},{2,10},{10... | collective-permute-start | bytes 98312 | tf_op jit(solution)/shard_map/ppermute | solution.py:478
  73.8 5.9 %collective-permute-start.14 = (bf16[128,512]{1,0:T(8,128)(2,1)S(1)}, bf16[128,512]{1,0:T(8,128)(2,1)S(1)}, u32[]{:S(2)}, u32[]{:S(2)}) collective-permute-start(bf16[128,512]{1,0:T(8,128)(2,1)S(1)} %join_far.1.refs_3_), channel_id=1, source_target_pairs={{0,6},{2,4},{4,2},{6,0},{1,7},{3,5},{5,3},{7,1},{8,14},{10,12},{12... | collective-permute-start | bytes 393224 | tf_op jit(solution)/shard_map/ppermute | solution.py:478
  75.9 5.0 %collective-permute-start.15 = (bf16[128,512]{1,0:T(8,128)(2,1)S(1)}, bf16[128,512]{1,0:T(8,128)(2,1)S(1)}, u32[]{:S(2)}, u32[]{:S(2)}) collective-permute-start(bf16[128,512]{1,0:T(8,128)(2,1)S(1)} %join_far.1.refs_3_), channel_id=1, source_target_pairs={{0,4},{2,6},{4,0},{6,2},{1,5},{3,7},{5,1},{7,3},{8,12},{10,14},{12... | collective-permute-start | bytes 393224 | tf_op jit(solution)/shard_map/ppermute | solution.py:478
  76.1 5.0 %collective-permute-start.16 = (bf16[128,512]{1,0:T(8,128)(2,1)S(1)}, bf16[128,512]{1,0:T(8,128)(2,1)S(1)}, u32[]{:S(2)}, u32[]{:S(2)}) collective-permute-start(bf16[128,512]{1,0:T(8,128)(2,1)S(1)} %join_far.1.refs_3_), channel_id=1, source_target_pairs={{0,2},{2,0},{4,6},{6,4},{1,3},{3,1},{5,7},{7,5},{8,10},{10,8},{12,... | collective-permute-start | bytes 393224 | tf_op jit(solution)/shard_map/ppermute | solution.py:478
  81.2 2.0 %collective-permute-start.17 = (bf16[512,512]{1,0:T(8,128)(2,1)S(1)}, bf16[512,512]{1,0:T(8,128)(2,1)S(1)}, u32[]{:S(2)}, u32[]{:S(2)}) collective-permute-start(bf16[512,512]{1,0:T(8,128)(2,1)S(1)} %join_group.1.own_state), channel_id=1, source_target_pairs={{0,1},{1,0},{2,3},{3,2},{4,5},{5,4},{6,7},{7,6},{8,9},{9,8},{10,11... | collective-permute-start | bytes 1572872 | tf_op jit(solution)/shard_map/ppermute | solution.py:478
